TPU v7x, 256 devices: a whole 4x4x8 slice. The times are simulated.
256 devices in a mesh: grp: 2 (over core), gx: 8 (over x_hi, y), gy: 16 (over x_lo, z).
Axes of the slice: x: 4 (x_hi: 2, x_lo: 2; x = x_hi * 2 + x_lo), y: 4, z: 8, core: 2. Of those that a mesh axis runs over, the one named last changes fastest.
Arguments:
- right_side: float32 [128, 256, 256], P('gx', 'gy', 'grp'), may hold values from -6 to 6
- coefficient: float32 [128, 256, 256], P('gx', 'gy', 'grp'), may hold values from 0.2 to 5
Outputs:
- solution_field: float32 [128, 256, 256], P('gx', 'gy', 'grp')
- residual: float32 [128, 256, 256], P('gx', 'gy', 'grp')
All inputs are finite; a program needn't handle non-finite values.
Results may differ from a plain program's by a relative error of at most 0.0001.
Values sent between devices are 32-bit elements; how exact they have to be, the bound alone decides.
No kernel may reach another device: no remote copies, remote signals or barrier semaphores. Data moves between devices by JAX's collectives and lax.ppermute only.
A program may use at most 64 MiB of HBM per device.

v0:
```python
import jax
import jax.numpy as jnp
from jax import lax
from jax.sharding import PartitionSpec as P

FINE_DEGREE = 5
COARSE_DEGREE = 16
OUTER = 2


LOW_FINE = 0.2
LOW_COARSE = 0.02
HIGH_BOUND = 2.0
DAMPING = 0.5


def with_halo(x, sides, width):
    edges = {}
    for axis, dim in sides:
        size, length = (lax.axis_size(axis), x.shape[dim])
        up = [(i, (i + 1) % size) for i in range(size - 1)]
        last = lax.slice_in_dim(x, length - width, length, axis=dim)
        first = lax.slice_in_dim(x, 0, width, axis=dim)
        edges[dim] = (
            lax.ppermute(last, axis, up),
            lax.ppermute(first, axis, [(b, a) for a, b in up]),
        )
    done = []
    for _, dim in sides:
        low, high = edges[dim]
        around = [(width, width) if d in done else (0, 0) for d in range(x.ndim)]
        x = jnp.concatenate([jnp.pad(low, around), x, jnp.pad(high, around)], axis=dim)
        done.append(dim)
    return x


def face_parts(padded):
    center = padded[1:-1, 1:-1, 1:-1]
    return (
        0.5 * (center + padded[:-2, 1:-1, 1:-1]),
        0.5 * (center + padded[2:, 1:-1, 1:-1]),
        0.5 * (center + padded[1:-1, :-2, 1:-1]),
        0.5 * (center + padded[1:-1, 2:, 1:-1]),
        0.5 * (center + padded[1:-1, 1:-1, :-2]),
        0.5 * (center + padded[1:-1, 1:-1, 2:]),
    )


def diagonal_of(parts):
    return parts[0] + parts[1] + parts[2] + parts[3] + parts[4] + parts[5]


def stencil(padded, parts, scale):
    center = padded[1:-1, 1:-1, 1:-1]
    nearby = parts[0] * padded[:-2, 1:-1, 1:-1] + parts[1] * padded[2:, 1:-1, 1:-1]
    nearby = nearby + parts[2] * padded[1:-1, :-2, 1:-1] + parts[3] * padded[1:-1, 2:, 1:-1]
    nearby = nearby + parts[4] * padded[1:-1, 1:-1, :-2] + parts[5] * padded[1:-1, 1:-1, 2:]
    return scale * (diagonal_of(parts) * center - nearby)


def restrict(field):
    size_a, size_b, size_c = field.shape
    return field.reshape(size_a // 2, 2, size_b // 2, 2, size_c // 2, 2).mean(axis=(1, 3, 5))


def prolong(field):
    return jnp.repeat(jnp.repeat(jnp.repeat(field, 2, 0), 2, 1), 2, 2)


def cheb_steps(degree, low, high):
    theta = (high + low) / 2.0
    delta = (high - low) / 2.0
    sigma = theta / delta
    rho = 1.0 / sigma
    keeps = []
    pushes = []
    for step in range(degree - 1):
        rho_new = 1.0 / (2.0 * sigma - rho)
        keeps.append(rho_new * rho)
        pushes.append(2.0 * rho_new / delta)
        rho = rho_new
    return (1.0 / theta, keeps, pushes)


def chebyshev(rhs, inverse_diag, apply_fn, degree, low, high):
    inv_theta, keeps, pushes = cheb_steps(degree, low, high)
    keep_table = jnp.array(keeps, jnp.float32)
    push_table = jnp.array(pushes, jnp.float32)
    first = inverse_diag * rhs * inv_theta

    def advance(step, carry):
        resid, update, total = carry
        resid = resid - apply_fn(update)
        update = keep_table[step] * update + push_table[step] * (inverse_diag * resid)
        return (resid, update, total + update)

    return lax.fori_loop(0, degree - 1, advance, (rhs, first, first))[2]


def field_halo(field):
    return with_halo(field, (("grp", 2), ("gx", 0), ("gy", 1)), 1)


def coef_faces(field):
    return face_parts(with_halo(field, (("grp", 2), ("gx", 0), ("gy", 1)), 1))


def collect(block):
    size_a, size_b, size_c = block.shape
    whole = lax.all_gather(block.reshape(-1), ("grp", "gx", "gy"), axis=0, tiled=True)
    whole = whole.reshape(
        lax.axis_size("grp"), lax.axis_size("gx"), lax.axis_size("gy"), size_a, size_b, size_c
    )
    whole = whole.transpose(1, 3, 2, 4, 0, 5)
    return whole.reshape(
        lax.axis_size("gx") * size_a, lax.axis_size("gy") * size_b, lax.axis_size("grp") * size_c
    )


def on_device(right_side, coefficient):
    scales = [1.0, 0.25, 0.0625, 0.015625]
    coefs = [coefficient]
    for level in range(3):
        coefs.append(restrict(coefs[-1]))
    parts_all = [coef_faces(coefs[level]) for level in range(3)]
    base_shape = coefs[3].shape
    whole_coef = collect(coefs[3])
    parts_all.append(face_parts(jnp.pad(whole_coef, 1)))
    inverses = [1.0 / (scales[level] * diagonal_of(parts_all[level])) for level in range(4)]

    def make_apply(level):
        return lambda field: stencil(field_halo(field), parts_all[level], scales[level])

    solution_field = jnp.zeros_like(right_side)
    residual = right_side
    for outer in range(OUTER):
        rhs_list = [residual]
        for level in range(3):
            rhs_list.append(restrict(rhs_list[-1]))
        corrections = [
            chebyshev(residual, inverses[0], make_apply(0), FINE_DEGREE, LOW_FINE, HIGH_BOUND)
        ]
        for level in range(1, 3):
            corrections.append(
                chebyshev(
                    rhs_list[level],
                    inverses[level],
                    make_apply(level),
                    FINE_DEGREE,
                    LOW_FINE,
                    HIGH_BOUND,
                )
            )
        whole_rhs = collect(rhs_list[3])
        whole_corr = chebyshev(
            whole_rhs,
            inverses[3],
            lambda field: stencil(jnp.pad(field, 1), parts_all[3], scales[3]),
            COARSE_DEGREE,
            LOW_COARSE,
            HIGH_BOUND,
        )
        corner = (
            lax.axis_index("gx") * base_shape[0],
            lax.axis_index("gy") * base_shape[1],
            lax.axis_index("grp") * base_shape[2],
        )
        corrections.append(lax.dynamic_slice(whole_corr, corner, base_shape))
        combined = corrections[2] + prolong(corrections[3])
        combined = corrections[1] + prolong(combined)
        combined = corrections[0] + prolong(combined)
        solution_field = solution_field + DAMPING * combined
        residual = right_side - stencil(field_halo(solution_field), parts_all[0], 1.0)
    return (solution_field, residual)


def solution(mesh):
    placed = (P("gx", "gy", "grp"), P("gx", "gy", "grp"))
    return jax.shard_map(
        on_device,
        mesh=mesh,
        in_specs=placed,
        out_specs=(P("gx", "gy", "grp"), P("gx", "gy", "grp")),
        check_vma=False,
    )
```

profile of v0, /device:TPU:27, one launch (start us, length us, event | category | flops | bytes accessed | tf_op | source)
XLA Modules:
  0.0 1566.8 jit_solution(8455548241867140102)
XLA Ops:
  7.2 10.6 reshape.122
  38.5 9.8 reshape.121
  106.6 241.0 %all-reduce.56.cloned.1.call-done = (f32[16384]{0:T(1024)}, f32[16384]{0:T(1024)}) async-done(((f32[16384]{0:T(1024)}, f32[16384]{0:T(1024)}), (f32[16384]{0:T(1024)}, f32[16384]{0:T(1024)})) %all-reduce.56.cloned.1.call-update) | async-done | bytes 131088
  354.9 92.7 %while.163 = (s32[]{:T(128)}, f32[16,32,32]{2,1,0:T(8,128)}, f32[16,32,32]{2,1,0:T(8,128)S(1)}, f32[16,32,32]{2,1,0:T(8,128)}, f32[16,32,32]{2,1,0:T(8,128)S(1)}...) while((s32[]{:T(128)}, f32[16,32,32]{2,1,0:T(8,128)}, ...), condition=%wide.region_13.14_spmd.clone, body=%wide.region_12.13_spmd.sunk.clone.sunk | while | flops 327682 | bytes 1048757 | solution.py:97
  448.6 108.0 %while.162 = (s32[]{:T(128)}, f32[4,4,32]{2,1,0:T(4,128)}, f32[4,4,32]{2,1,0:T(4,128)}, f32[4,4,32]{2,1,0:T(4,128)}, f32[4,4,32]{2,1,0:T(4,128)S(1)}, /*index=5*...) while((s32[]{:T(128)}, f32[4,4,32]{2,1,0:T(4,128)}, ...), condition=%wide.region_9.10_spmd.clone, body=%wide.region_8.9_spmd.sunk.clone.sunk | while | flops 22530 | bytes 50613 | solution.py:97
  484.1 7.0 collective-permute-start.16
  539.3 7.0 collective-permute-start.16
  561.2 126.6 %while.161 = (s32[]{:T(128)}, f32[8,8,64]{2,1,0:T(8,128)}, f32[8,8,64]{2,1,0:T(8,128)}, f32[8,8,64]{2,1,0:T(8,128)}, f32[8,8,64]{2,1,0:T(8,128)}, /*index=5*/f32...) while((s32[]{:T(128)}, f32[8,8,64]{2,1,0:T(8,128)}, ...), condition=%wide.region_5.6_spmd.clone, body=%wide.region_4.5_spmd.sunk.clone.sunk | while | flops 180226 | bytes 340177 | solution.py:97
  570.6 7.0 collective-permute-start.10
  601.8 7.0 collective-permute-start.10
  633.7 7.0 collective-permute-start.10
  665.6 7.0 collective-permute-start.10
  694.1 129.1 %while.160 = (s32[]{:T(128)}, f32[16,16,128]{2,1,0:T(8,128)}, f32[16,16,128]{2,1,0:T(8,128)S(1)}, f32[16,16,128]{2,1,0:T(8,128)S(1)}, f32[16,16,128]{2,1,0:T(8,1...) while((s32[]{:T(128)}, f32[16,16,128]{2,1,0:T(8,128)}, ...), condition=%wide.region_1.0_spmd.clone, body=%wide.region_0.0_spmd.sunk.clone.sunk | while | flops 1409026 | bytes 2407377 | solution.py:97
  703.0 7.0 collective-permute-start.4
  734.6 7.0 collective-permute-start.4
  767.1 7.0 collective-permute-start.4
  799.6 7.0 collective-permute-start.4
  831.9 7.0 collective-permute-start.54
  849.9 9.8 reshape.136
  870.3 236.0 %all-reduce.54.cloned.1.call-done = f32[16384]{0:T(1024)} async-done(((f32[16384]{0:T(1024)}), f32[16384]{0:T(1024)}) %all-reduce.54.cloned.1.call-update) | async-done | bytes 65552
  1114.7 89.9 %while.167 = (s32[]{:T(128)}, f32[16,32,32]{2,1,0:T(8,128)}, f32[16,32,32]{2,1,0:T(8,128)S(1)}, f32[16,32,32]{2,1,0:T(8,128)}, f32[16,32,32]{2,1,0:T(8,128)S(1)}...) while((s32[]{:T(128)}, f32[16,32,32]{2,1,0:T(8,128)}, ...), condition=%wide.region_24.25_spmd.clone, body=%wide.region_23.24_spmd.sunk.clone.sunk | while | flops 327682 | bytes 1048757 | solution.py:97
  1205.7 106.6 %while.166 = (s32[]{:T(128)}, f32[4,4,32]{2,1,0:T(4,128)}, f32[4,4,32]{2,1,0:T(4,128)}, f32[4,4,32]{2,1,0:T(4,128)}, f32[4,4,32]{2,1,0:T(4,128)S(1)}, /*index=5*...) while((s32[]{:T(128)}, f32[4,4,32]{2,1,0:T(4,128)}, ...), condition=%wide.region_21.22_spmd.clone, body=%wide.region_20.21_spmd.sunk.clone.sunk | while | flops 22530 | bytes 50613 | solution.py:97
  1313.2 115.7 %while.165 = (s32[]{:T(128)}, f32[8,8,64]{2,1,0:T(8,128)}, f32[8,8,64]{2,1,0:T(8,128)}, f32[8,8,64]{2,1,0:T(8,128)}, f32[8,8,64]{2,1,0:T(8,128)}, /*index=5*/f32...) while((s32[]{:T(128)}, f32[8,8,64]{2,1,0:T(8,128)}, ...), condition=%wide.region_18.19_spmd.clone, body=%wide.region_17.18_spmd.sunk.clone.sunk | while | flops 180226 | bytes 331957 | solution.py:97
  1430.6 104.5 %while.164 = (s32[]{:T(128)}, f32[16,16,128]{2,1,0:T(8,128)S(1)}, f32[16,16,128]{2,1,0:T(8,128)S(1)}, f32[16,16,128]{2,1,0:T(8,128)S(1)}, f32[16,16,128]{2,1,0:T...) while((s32[]{:T(128)}, f32[16,16,128]{2,1,0:T(8,128)S(1)}, ...), condition=%wide.region_15.16_spmd.clone, body=%wide.region_14.15_spmd.sunk.clone.sunk | while | flops 1409026 | bytes 2374581 | solution.py:97
  (866 shorter events, 966.0 us)
Async XLA Ops:
  7.2 340.4 %all-reduce.56.cloned.1.call-start = ((), (), s32[]{:S(2)}) async-start(), calls=%async_computation.1 | async-start | bytes 262144
  21.9 56.3 %collective-permute-start.45 = (f32[1,8,64]{2,1,0:T(8,128)S(1)}, f32[1,8,64]{2,1,0:T(8,128)S(1)}, u32[]{:S(2)}, u32[]{:S(2)}) collective-permute-start(f32[1,8,64]{2,1,0:T(8,128)S(1)} %get-tuple-element.3340), channel_id=1, source_target_pairs={{16,0},{32,16},{48,32},{64,48},{80,64},{96,80},{112,96},{17,1},{33... | collective-permute-start | bytes 6152 | tf_op jit(solution)/shard_map/ppermute | solution.py:26
  25.5 31.0 %collective-permute-start.51 = (f32[1,4,32]{2,1,0:T(4,128)S(1)}, f32[1,4,32]{2,1,0:T(4,128)S(1)}, u32[]{:S(2)}, u32[]{:S(2)}) collective-permute-start(f32[1,4,32]{2,1,0:T(4,128)S(1)} %get-tuple-element.3350), channel_id=1, source_target_pairs={{16,0},{32,16},{48,32},{64,48},{80,64},{96,80},{112,96},{17,1},{33... | collective-permute-start | bytes 1544 | tf_op jit(solution)/shard_map/ppermute | solution.py:26
  27.7 36.1 %collective-permute-start.50 = (f32[4,4,1]{2,1,0:T(4,128)S(1)}, f32[4,4,1]{2,1,0:T(4,128)S(1)}, u32[]{:S(2)}, u32[]{:S(2)}) collective-permute-start(f32[4,4,1]{2,1,0:T(4,128)S(1)} %get-tuple-element.3352), channel_id=1, source_target_pairs={{128,0},{129,1},{130,2},{131,3},{132,4},{133,5},{134,6},{135,7},{1... | collective-permute-start | bytes 200 | tf_op jit(solution)/shard_map/ppermute | solution.py:26
  30.8 31.6 %collective-permute-start.48 = (f32[1,4,32]{2,1,0:T(4,128)S(1)}, f32[1,4,32]{2,1,0:T(4,128)S(1)}, u32[]{:S(2)}, u32[]{:S(2)}) collective-permute-start(f32[1,4,32]{2,1,0:T(4,128)S(1)} %get-tuple-element.3349), channel_id=1, source_target_pairs={{0,16},{16,32},{32,48},{48,64},{64,80},{80,96},{96,112},{1,17},{17... | collective-permute-start | bytes 1544 | tf_op jit(solution)/shard_map/ppermute | solution.py:25
  68.0 25.1 %collective-permute-start.47 = (f32[8,1,64]{2,1,0:T(1,128)S(1)}, f32[8,1,64]{2,1,0:T(1,128)S(1)}, u32[]{:S(2)}, u32[]{:S(2)}) collective-permute-start(f32[8,1,64]{2,1,0:T(1,128)S(1)} %get-tuple-element.3337), channel_id=1, source_target_pairs={{1,0},{2,1},{3,2},{4,3},{5,4},{6,5},{7,6},{8,7},{9,8},{10,9},{11,1... | collective-permute-start | bytes 6152 | tf_op jit(solution)/shard_map/ppermute | solution.py:26
  105.1 1001.1 %all-reduce.54.cloned.1.call-start = ((), (), s32[]{:S(2)}) async-start(), calls=%async_computation | async-start | bytes 131072
  562.6 26.6 %collective-permute-start.8 = (f32[8,1,64]{2,1,0:T(1,128)}, f32[8,1,64]{2,1,0:T(1,128)}, u32[]{:S(2)}, u32[]{:S(2)}) collective-permute-start(f32[8,1,64]{2,1,0:T(1,128)} %get-tuple-element.3936), channel_id=1, source_target_pairs={{1,0},{2,1},{3,2},{4,3},{5,4},{6,5},{7,6},{8,7},{9,8},{10,9},{11,1... | collective-permute-start | bytes 6152 | tf_op jit(solution)/shard_map/while/body/eval_jaxpr/ppermute | solution.py:26
  593.5 27.6 %collective-permute-start.8 = (f32[8,1,64]{2,1,0:T(1,128)}, f32[8,1,64]{2,1,0:T(1,128)}, u32[]{:S(2)}, u32[]{:S(2)}) collective-permute-start(f32[8,1,64]{2,1,0:T(1,128)} %get-tuple-element.3936), channel_id=1, source_target_pairs={{1,0},{2,1},{3,2},{4,3},{5,4},{6,5},{7,6},{8,7},{9,8},{10,9},{11,1... | collective-permute-start | bytes 6152 | tf_op jit(solution)/shard_map/while/body/eval_jaxpr/ppermute | solution.py:26
  625.4 27.6 %collective-permute-start.8 = (f32[8,1,64]{2,1,0:T(1,128)}, f32[8,1,64]{2,1,0:T(1,128)}, u32[]{:S(2)}, u32[]{:S(2)}) collective-permute-start(f32[8,1,64]{2,1,0:T(1,128)} %get-tuple-element.3936), channel_id=1, source_target_pairs={{1,0},{2,1},{3,2},{4,3},{5,4},{6,5},{7,6},{8,7},{9,8},{10,9},{11,1... | collective-permute-start | bytes 6152 | tf_op jit(solution)/shard_map/while/body/eval_jaxpr/ppermute | solution.py:26
  657.3 27.6 %collective-permute-start.8 = (f32[8,1,64]{2,1,0:T(1,128)}, f32[8,1,64]{2,1,0:T(1,128)}, u32[]{:S(2)}, u32[]{:S(2)}) collective-permute-start(f32[8,1,64]{2,1,0:T(1,128)} %get-tuple-element.3936), channel_id=1, source_target_pairs={{1,0},{2,1},{3,2},{4,3},{5,4},{6,5},{7,6},{8,7},{9,8},{10,9},{11,1... | collective-permute-start | bytes 6152 | tf_op jit(solution)/shard_map/while/body/eval_jaxpr/ppermute | solution.py:26
  694.8 27.5 %collective-permute-start.2 = (f32[16,1,128]{2,1,0:T(1,128)}, f32[16,1,128]{2,1,0:T(1,128)}, u32[]{:S(2)}, u32[]{:S(2)}) collective-permute-start(f32[16,1,128]{2,1,0:T(1,128)} %get-tuple-element.3915), channel_id=1, source_target_pairs={{1,0},{2,1},{3,2},{4,3},{5,4},{6,5},{7,6},{8,7},{9,8},{10,9},{11,1... | collective-permute-start | bytes 24584 | tf_op jit(solution)/shard_map/while/body/eval_jaxpr/ppermute | solution.py:26
  726.3 28.4 %collective-permute-start.2 = (f32[16,1,128]{2,1,0:T(1,128)}, f32[16,1,128]{2,1,0:T(1,128)}, u32[]{:S(2)}, u32[]{:S(2)}) collective-permute-start(f32[16,1,128]{2,1,0:T(1,128)} %get-tuple-element.3915), channel_id=1, source_target_pairs={{1,0},{2,1},{3,2},{4,3},{5,4},{6,5},{7,6},{8,7},{9,8},{10,9},{11,1... | collective-permute-start | bytes 24584 | tf_op jit(solution)/shard_map/while/body/eval_jaxpr/ppermute | solution.py:26
  758.8 28.4 %collective-permute-start.2 = (f32[16,1,128]{2,1,0:T(1,128)}, f32[16,1,128]{2,1,0:T(1,128)}, u32[]{:S(2)}, u32[]{:S(2)}) collective-permute-start(f32[16,1,128]{2,1,0:T(1,128)} %get-tuple-element.3915), channel_id=1, source_target_pairs={{1,0},{2,1},{3,2},{4,3},{5,4},{6,5},{7,6},{8,7},{9,8},{10,9},{11,1... | collective-permute-start | bytes 24584 | tf_op jit(solution)/shard_map/while/body/eval_jaxpr/ppermute | solution.py:26
  791.3 28.4 %collective-permute-start.2 = (f32[16,1,128]{2,1,0:T(1,128)}, f32[16,1,128]{2,1,0:T(1,128)}, u32[]{:S(2)}, u32[]{:S(2)}) collective-permute-start(f32[16,1,128]{2,1,0:T(1,128)} %get-tuple-element.3915), channel_id=1, source_target_pairs={{1,0},{2,1},{3,2},{4,3},{5,4},{6,5},{7,6},{8,7},{9,8},{10,9},{11,1... | collective-permute-start | bytes 24584 | tf_op jit(solution)/shard_map/while/body/eval_jaxpr/ppermute | solution.py:26
  824.2 24.5 %collective-permute-start.59 = (f32[16,1,128]{2,0,1:T(8,128)S(1)}, f32[16,1,128]{2,0,1:T(8,128)S(1)}, u32[]{:S(2)}, u32[]{:S(2)}) collective-permute-start(f32[16,1,128]{2,0,1:T(8,128)S(1)} %bitcast.113), channel_id=1, source_target_pairs={{1,0},{2,1},{3,2},{4,3},{5,4},{6,5},{7,6},{8,7},{9,8},{10,9},{11,1... | collective-permute-start | bytes 24584 | tf_op jit(solution)/shard_map/ppermute | solution.py:26
  1314.0 25.0 %collective-permute-start.26 = (f32[8,1,64]{2,1,0:T(1,128)S(1)}, f32[8,1,64]{2,1,0:T(1,128)S(1)}, u32[]{:S(2)}, u32[]{:S(2)}) collective-permute-start(f32[8,1,64]{2,1,0:T(1,128)S(1)} %get-tuple-element.4014), channel_id=1, source_target_pairs={{1,0},{2,1},{3,2},{4,3},{5,4},{6,5},{7,6},{8,7},{9,8},{10,9},{11,1... | collective-permute-start | bytes 6152 | tf_op jit(solution)/shard_map/while/body/eval_jaxpr/ppermute | solution.py:26
  1342.7 25.3 %collective-permute-start.26 = (f32[8,1,64]{2,1,0:T(1,128)S(1)}, f32[8,1,64]{2,1,0:T(1,128)S(1)}, u32[]{:S(2)}, u32[]{:S(2)}) collective-permute-start(f32[8,1,64]{2,1,0:T(1,128)S(1)} %get-tuple-element.4014), channel_id=1, source_target_pairs={{1,0},{2,1},{3,2},{4,3},{5,4},{6,5},{7,6},{8,7},{9,8},{10,9},{11,1... | collective-permute-start | bytes 6152 | tf_op jit(solution)/shard_map/while/body/eval_jaxpr/ppermute | solution.py:26
  1371.7 25.3 %collective-permute-start.26 = (f32[8,1,64]{2,1,0:T(1,128)S(1)}, f32[8,1,64]{2,1,0:T(1,128)S(1)}, u32[]{:S(2)}, u32[]{:S(2)}) collective-permute-start(f32[8,1,64]{2,1,0:T(1,128)S(1)} %get-tuple-element.4014), channel_id=1, source_target_pairs={{1,0},{2,1},{3,2},{4,3},{5,4},{6,5},{7,6},{8,7},{9,8},{10,9},{11,1... | collective-permute-start | bytes 6152 | tf_op jit(solution)/shard_map/while/body/eval_jaxpr/ppermute | solution.py:26
  1400.7 25.3 %collective-permute-start.26 = (f32[8,1,64]{2,1,0:T(1,128)S(1)}, f32[8,1,64]{2,1,0:T(1,128)S(1)}, u32[]{:S(2)}, u32[]{:S(2)}) collective-permute-start(f32[8,1,64]{2,1,0:T(1,128)S(1)} %get-tuple-element.4014), channel_id=1, source_target_pairs={{1,0},{2,1},{3,2},{4,3},{5,4},{6,5},{7,6},{8,7},{9,8},{10,9},{11,1... | collective-permute-start | bytes 6152 | tf_op jit(solution)/shard_map/while/body/eval_jaxpr/ppermute | solution.py:26
  1456.0 24.6 %collective-permute-start.20 = (f32[16,1,128]{2,1,0:T(1,128)S(1)}, f32[16,1,128]{2,1,0:T(1,128)S(1)}, u32[]{:S(2)}, u32[]{:S(2)}) collective-permute-start(f32[16,1,128]{2,1,0:T(1,128)S(1)} %get-tuple-element.3993), channel_id=1, source_target_pairs={{1,0},{2,1},{3,2},{4,3},{5,4},{6,5},{7,6},{8,7},{9,8},{10,9},{11,1... | collective-permute-start | bytes 24584 | tf_op jit(solution)/shard_map/while/body/eval_jaxpr/ppermute | solution.py:26
  1482.4 24.6 %collective-permute-start.20 = (f32[16,1,128]{2,1,0:T(1,128)S(1)}, f32[16,1,128]{2,1,0:T(1,128)S(1)}, u32[]{:S(2)}, u32[]{:S(2)}) collective-permute-start(f32[16,1,128]{2,1,0:T(1,128)S(1)} %get-tuple-element.3993), channel_id=1, source_target_pairs={{1,0},{2,1},{3,2},{4,3},{5,4},{6,5},{7,6},{8,7},{9,8},{10,9},{11,1... | collective-permute-start | bytes 24584 | tf_op jit(solution)/shard_map/while/body/eval_jaxpr/ppermute | solution.py:26
  1508.8 24.6 %collective-permute-start.20 = (f32[16,1,128]{2,1,0:T(1,128)S(1)}, f32[16,1,128]{2,1,0:T(1,128)S(1)}, u32[]{:S(2)}, u32[]{:S(2)}) collective-permute-start(f32[16,1,128]{2,1,0:T(1,128)S(1)} %get-tuple-element.3993), channel_id=1, source_target_pairs={{1,0},{2,1},{3,2},{4,3},{5,4},{6,5},{7,6},{8,7},{9,8},{10,9},{11,1... | collective-permute-start | bytes 24584 | tf_op jit(solution)/shard_map/while/body/eval_jaxpr/ppermute | solution.py:26
  1535.2 23.8 %collective-permute-start.65 = (f32[16,1,128]{2,0,1:T(8,128)S(1)}, f32[16,1,128]{2,0,1:T(8,128)S(1)}, u32[]{:S(2)}, u32[]{:S(2)}) collective-permute-start(f32[16,1,128]{2,0,1:T(8,128)S(1)} %bitcast.112), channel_id=1, source_target_pairs={{1,0},{2,1},{3,2},{4,3},{5,4},{6,5},{7,6},{8,7},{9,8},{10,9},{11,1... | collective-permute-start | bytes 24584 | tf_op jit(solution)/shard_map/ppermute | solution.py:26
  (183 other events, 4521.8 us)
Sparse Core Ops, SparseCore 0:
  105.3 242.2 all-reduce.55
  868.6 237.6 all-reduce.53
where the time goes:
time: 1580 us; the launch traced here: 1570 us
  starting transfers between devices  600 us (38%)
  waiting for transfers between devices  501 us (32%)
  local copies, waits for them, and re-layouts  253 us (16%)
  other arithmetic  195 us (12%)
    unnamed x4, waiting for transfers between devices  477 us
    ppermute x87, starting transfers between devices, with_halo(): lax.ppermute(first, axis, [(b, a) for a, b in up])  307 us
    ppermute x87, starting transfers between devices, with_halo(): lax.ppermute(last, axis, up)  293 us
    add x54, other arithmetic, advance(): return (resid, update, total + update)  171 us
    dynamic_slice x54, local copies, waits for them, and re-layouts, advance(): keep_table[step] * update + push_table[step] * (inverse_diag * resid)  70 us
    dynamic_slice x54, local copies, waits for them, and re-layouts, advance(): push_table[step] * (inverse_diag * resid)  68.9 us
  transfers between devices with their start and end apart: 176, of which 20 were waited for; matrix products, arithmetic and copies ran while one was open for 7% of the time, Pallas kernels for 0%

commit v1 on v0

v1 whole, which is shorter than its diff:
```python
import functools

import jax
import jax.numpy as jnp
from jax import lax
from jax.experimental import pallas as pl
from jax.experimental.pallas import tpu as pltpu
from jax.sharding import PartitionSpec as P

FINE_DEGREE = 5
COARSE_DEGREE = 16
LOW_FINE = 0.2
LOW_COARSE = 0.02
HIGH_BOUND = 2.0
DAMPING = 0.5

F32 = jnp.float32
INTERPRET = False
LANES_X = {1: 1, 2: 2, 3: 4}
BLOCKS = {1: 28, 2: 10, 3: 5}
ROWS = {1: 32, 2: 24, 3: 24}
SCALE = {1: 1.0, 2: 0.25, 3: 0.0625, 4: 0.015625}


def cheb_steps(degree, low, high):
    theta = (high + low) / 2.0
    delta = (high - low) / 2.0
    sigma = theta / delta
    rho = 1.0 / sigma
    keeps = []
    pushes = []
    for step in range(degree - 1):
        rho_new = 1.0 / (2.0 * sigma - rho)
        keeps.append(rho_new * rho)
        pushes.append(2.0 * rho_new / delta)
        rho = rho_new
    return (1.0 / theta, keeps, pushes)


def roll(x, shift, axis):
    size = x.shape[axis]
    return pltpu.roll(x, shift % size, axis)


def lane_iota(shape):
    return lax.broadcasted_iota(jnp.int32, shape, len(shape) - 1)


def dot(x, m):
    return jnp.dot(x, m, precision=lax.Precision.HIGHEST, preferred_element_type=F32)


def select_matrix(fn, value):
    row = lax.broadcasted_iota(jnp.int32, (128, 128), 0)
    col = lax.broadcasted_iota(jnp.int32, (128, 128), 1)
    return jnp.where(fn(row, col), value, 0.0).astype(F32)


def x_up(q, here, after):
    if q == 1:
        return after
    zz = 128 // q
    lane = lane_iota(here.shape)
    return jnp.where(lane < 128 - zz, roll(here, -zz, 2), roll(after, -zz, 2))


def x_dn(q, here, before):
    if q == 1:
        return before
    zz = 128 // q
    lane = lane_iota(here.shape)
    return jnp.where(lane >= zz, roll(here, zz, 2), roll(before, zz, 2))


def z_up(q, v):
    zz = 128 // q
    moved = roll(v, -1, 2)
    wrap = moved if q == 1 else roll(v, zz - 1, 2)
    swapped = jnp.concatenate([wrap[1:], wrap[:1]], axis=0)
    edge = lane_iota(v.shape) % zz == zz - 1
    return jnp.where(edge, swapped, moved)


def z_dn(q, v):
    zz = 128 // q
    moved = roll(v, 1, 2)
    wrap = moved if q == 1 else roll(v, -(zz - 1), 2)
    swapped = jnp.concatenate([wrap[1:], wrap[:1]], axis=0)
    edge = lane_iota(v.shape) % zz == 0
    return jnp.where(edge, swapped, moved)


def faces(level, a, fx, fy, fz, inv, diag_ref):
    q, nb, rows = LANES_X[level], BLOCKS[level], ROWS[level]
    zz = 128 // q
    shape = (2, rows, 128)

    def body(i, _):
        here = a[:, i]
        half = 0.5 * here
        after = a[:, jnp.minimum(i + 1, nb - 1)]
        fxv = half + 0.5 * x_up(q, here, after)
        fx[:, i] = fxv
        fyv = half + 0.5 * roll(here, -1, 1)
        fy[:, i] = fyv
        core = lax.broadcasted_iota(jnp.int32, shape, 0)
        lane = lane_iota(shape) % zz
        top = (core == 1) & (lane == zz - 1)
        bottom = (core == 0) & (lane == 0)
        inner = half + 0.5 * z_up(q, here)
        fzv = jnp.where(top, 0.0, inner)
        fz[:, i] = fzv
        before = fx[:, jnp.maximum(i - 1, 0)]
        total = fxv + x_dn(q, fxv, before) + fyv + roll(fyv, 1, 1)
        total = total + jnp.where(top, half, inner) + jnp.where(bottom, half, z_dn(q, fzv))
        inv[:, i] = jnp.where(here > 0.0, 1.0 / total, 0.0)
        if diag_ref is not None:
            diag_ref[:, i] = total
        return 0

    lax.fori_loop(0, nb, body, 0)


def nearby(q, i, nb, v, fx, fy, fz):
    here = v[:, i]
    before_i = jnp.maximum(i - 1, 0)
    after = v[:, jnp.minimum(i + 1, nb - 1)]
    before = v[:, before_i]
    fxv = fx[:, i]
    fyv = fy[:, i]
    fzv = fz[:, i]
    total = fxv * x_up(q, here, after) + x_dn(q, fxv * here, fx[:, before_i] * before)
    total = total + fyv * roll(here, -1, 1) + roll(fyv * here, 1, 1)
    total = total + fzv * z_up(q, here) + z_dn(q, fzv * here)
    return here, total


def smooth(level, b, fx, fy, fz, inv, e, d, x):
    q, nb = LANES_X[level], BLOCKS[level]
    first, keeps, pushes = cheb_steps(FINE_DEGREE, LOW_FINE, HIGH_BOUND)

    def start(i, _):
        ev = b[:, i] * inv[:, i] * (1.0 / SCALE[level])
        e[:, i] = ev
        d[0, :, i] = ev * first
        x[:, i] = ev * first
        return 0

    lax.fori_loop(0, nb, start, 0)
    for step in range(FINE_DEGREE - 1):
        src, dst = d.at[step % 2], d.at[1 - step % 2]
        margin = step + 1 if level == 1 else 0

        def body(i, _):
            here, near = nearby(q, i, nb, src, fx, fy, fz)
            ev = e[:, i] - here + inv[:, i] * near
            new = keeps[step] * here + pushes[step] * ev
            e[:, i] = ev
            dst[:, i] = new
            x[:, i] = x[:, i] + new
            return 0

        lax.fori_loop(margin, nb - margin, body, 0)


def x_up4(v):
    moved = roll(v, -32, 2)
    after = jnp.concatenate([moved[1:], moved[:1]], axis=0)
    return jnp.where(lane_iota(v.shape) < 96, moved, after)


def x_dn4(v):
    moved = roll(v, 32, 2)
    before = jnp.concatenate([moved[-1:], moved[:-1]], axis=0)
    return jnp.where(lane_iota(v.shape) >= 32, moved, before)


def faces4(a, fx, fy, fz, inv):
    nb, rows, _ = a.shape
    blk = lax.broadcasted_iota(jnp.int32, a.shape, 0)
    row = lax.broadcasted_iota(jnp.int32, a.shape, 1)
    lane = lane_iota(a.shape)
    half = 0.5 * a
    total = jnp.zeros_like(a)
    for up, dn, last, start, out in (
        (x_up4, x_dn4, (blk == nb - 1) & (lane >= 96), (blk == 0) & (lane < 32), fx),
        (lambda v: roll(v, -1, 1), lambda v: roll(v, 1, 1), row == rows - 1, row == 0, fy),
        (lambda v: roll(v, -1, 2), lambda v: roll(v, 1, 2), lane % 32 == 31, lane % 32 == 0, fz),
    ):
        inner = half + 0.5 * up(a)
        off = jnp.where(last, 0.0, inner)
        out[...] = off
        total = total + jnp.where(last, half, inner) + jnp.where(start, half, dn(off))
    inv[...] = 1.0 / total


def smooth4(table, b, fx, fy, fz, inv):
    first = cheb_steps(COARSE_DEGREE, LOW_COARSE, HIGH_BOUND)[0]
    e = b * inv[...] * (1.0 / SCALE[4])
    d = e * first

    def body(step, carry):
        e, d, x = carry
        gx, gy, gz = fx[...], fy[...], fz[...]
        near = gx * x_up4(d) + x_dn4(gx * d)
        near = near + gy * roll(d, -1, 1) + roll(gy * d, 1, 1)
        near = near + gz * roll(d, -1, 2) + roll(gz * d, 1, 2)
        e = e - d + inv[...] * near
        d = table[0, step] * d + table[1, step] * e
        return e, d, x + d

    return lax.fori_loop(0, COARSE_DEGREE - 1, body, (e, d, d))[2]


def build4(src, stride, offset, core, gx_n, gy_n):
    count = gx_n * gy_n * 2
    gap = stride // 2
    pairs = src[pl.ds(offset, count, stride), :] + src[pl.ds(offset + gap, count, stride), :]
    pairs = pairs.reshape(gx_n // 2, 2, gy_n * 2, 128)
    out = None
    for odd in range(2):
        mat = select_matrix(
            lambda r, c: c == odd * 64 + (r // 64) * 32 + core * 16 + (r % 32) // 2, 0.125
        )
        part = dot(pairs[:, odd].reshape(gx_n * gy_n, 128), mat)
        out = part if out is None else out + part
    return out.reshape(gx_n // 2, gy_n * 2, 128)


def window3(src, dst, field, fields, core, pos, gx_n, gy_n):
    for bx in range(5):
        for by in range(6):
            ix = pos[1] + (bx - 2)
            iy = pos[2] + (by - 2)
            ok = (ix >= 0) & (ix < gx_n) & (iy >= 0) & (iy < gy_n)
            at = jnp.clip(ix, 0, gx_n - 1) * gy_n + jnp.clip(iy, 0, gy_n - 1)
            if fields == 1:
                tile = src[at]
            else:
                tile = src[at, pl.ds(field, 4, fields), :]
            dst[core, bx, by * 4:by * 4 + 4, :] = jnp.where(ok, tile, 0.0)


def restrict_to2(read_pair, out):
    even = jnp.concatenate([read_pair(2 * k) for k in range(4)], axis=0)
    odd = jnp.concatenate([read_pair(2 * k + 1) for k in range(4)], axis=0)
    low = select_matrix(lambda r, c: c == r // 2, 0.125)
    high = select_matrix(lambda r, c: c == 64 + r // 2, 0.125)
    both = dot(even, low) + dot(odd, high)
    for k in range(4):
        out(k, both[k * 8:k * 8 + 8])


def restrict_to3(read_rows):
    total = None
    for k in range(4):
        mat = select_matrix(lambda r, c: c == k * 32 + (r % 64) // 2, 0.125)
        part = dot(read_rows(k), mat)
        total = part if total is None else total + part
    return total


def prepare_kernel(a, b, own, up, down, slot):
    for f, src in enumerate((a, b)):
        for t in range(2):
            own[pl.ds(f * 32 + t, 16, 2)] = src[:, t * 8:t * 8 + 8, :]
            up[pl.ds(f * 12 + t, 6, 2)] = src[10:16, t * 8:t * 8 + 8, :]
            down[pl.ds(f * 12 + t, 6, 2)] = src[0:6, t * 8:t * 8 + 8, :]

        def read_pair(k):
            total = None
            for x in (2 * k, 2 * k + 1):
                part = src[x, pl.ds(0, 8, 2), :] + src[x, pl.ds(1, 8, 2), :]
                total = part if total is None else total + part
            return total

        def out(k, value):
            own[64 + f * 4 + k] = value
            if k >= 1:
                up[24 + f * 3 + k - 1] = value
            if k <= 2:
                down[24 + f * 3 + k] = value

        restrict_to2(read_pair, out)
        slot[pl.ds(f, 4, 2), :] = restrict_to3(
            lambda k: own[64 + f * 4 + k, pl.ds(0, 4, 2), :] + own[64 + f * 4 + k, pl.ds(1, 4, 2), :]
        )


def sides_kernel(nf, pos, own, lower, upper, up, down):
    c = pos[0]
    for f in range(nf):
        for out, t in ((up, 1), (down, 0)):
            for i in range(6):
                out[f * 28 + i] = lower[f * 12 + 2 * i + t]
                out[f * 28 + 22 + i] = upper[f * 12 + 2 * i + t]
            for i in range(16):
                out[f * 28 + 6 + i] = own[c, f * 32 + 2 * i + t]
            base = nf * 28 + f * 10
            for i in range(3):
                out[base + i] = lower[nf * 12 + f * 3 + i]
                out[base + 7 + i] = upper[nf * 12 + f * 3 + i]
            for i in range(4):
                out[base + 3 + i] = own[c, nf * 32 + f * 4 + i]


def spread(nf, f, core, own, xm, xp, ym, yp, fine, mid):
    for i in range(28):
        fine[core, i, 0:8, :] = ym[f * 28 + i]
        fine[core, i, 24:32, :] = yp[f * 28 + i]
        for t in range(2):
            if i < 6:
                tile = xm[f * 12 + 2 * i + t]
            elif i >= 22:
                tile = xp[f * 12 + 2 * (i - 22) + t]
            else:
                tile = own[f * 32 + 2 * (i - 6) + t]
            fine[core, i, 8 + 8 * t:16 + 8 * t, :] = tile
    base = nf * 28 + f * 10
    for i in range(10):
        mid[core, i, 0:8, :] = ym[base + i]
        mid[core, i, 16:24, :] = yp[base + i]
        if i < 3:
            tile = xm[nf * 12 + f * 3 + i]
        elif i >= 7:
            tile = xp[nf * 12 + f * 3 + i - 7]
        else:
            tile = own[nf * 32 + f * 4 + i - 3]
        mid[core, i, 8:16, :] = tile


def combine(pos, gx_n, gy_n, x4, x3, x2, tmp3, tmp2):
    gx, gy = pos[1], pos[2]
    yrow = lax.broadcasted_iota(jnp.int32, (24, gy_n * 2), 0)
    ycol = lax.broadcasted_iota(jnp.int32, (24, gy_n * 2), 1)
    rows = jnp.where(ycol == (4 * gy - 8 + yrow + 1024) // 2 - 512, 1.0, 0.0).astype(F32)
    for bx in (1, 2, 3):
        ix = gx + (bx - 2)
        ok = (ix >= 0) & (ix < gx_n)
        at = jnp.clip(ix, 0, gx_n - 1)
        odd = lax.rem(at, 2)
        spread_rows = dot(rows, x4[lax.div(at, 2)])
        for c in range(2):
            mat = select_matrix(
                lambda r, k: r == odd * 64 + (k // 64) * 32 + c * 16 + (k % 32) // 2, 1.0
            )
            part = jnp.where(ok, dot(spread_rows, mat), 0.0)
            x3[c, bx] = x3[c, bx] + part
    for c in range(2):
        for bx in (1, 2, 3):
            tmp3[c, bx, pl.ds(0, 12, 2), :] = x3[c, bx, 4:16, :]
            tmp3[c, bx, pl.ds(1, 12, 2), :] = x3[c, bx, 4:16, :]
    for low in range(4):
        blocks = [i for i in range(2, 8) if (i + 5) % 4 == low]
        mat = select_matrix(lambda r, k: r == low * 32 + (k % 64) // 2, 1.0)
        for i in blocks:
            bx = (i + 5) // 4
            part = dot(tmp3[:, bx].reshape(48, 128), mat).reshape(2, 24, 128)
            x2[:, i] = x2[:, i] + part
    for low in range(2):
        mat = select_matrix(lambda r, k: r == low * 64 + k // 2, 1.0)
        part = dot(x2[:, 2:8].reshape(2 * 6 * 24, 128), mat).reshape(2, 6, 24, 128)
        for i in range(6):
            piece = part[:, i, 4:20, :]
            tmp2[:, 2 * i + low, pl.ds(0, 16, 2), :] = piece
            tmp2[:, 2 * i + low, pl.ds(1, 16, 2), :] = piece


def first_kernel(
    gx_n, gy_n, pos, table,
    own_a, xm_a, xp_a, ym_a, yp_a, own_b, xm_b, xp_b, ym_b, yp_b,
    r3_a, r3_b, r3f_a, r3f_b,
    fx1, fy1, fz1, inv1, diag1, fx2, fy2, fz2, inv2, fx3, fy3, fz3, inv3, fx4, fy4, fz4, inv4,
    x1, right, own, up, down, slot,
    a1, b1, e1, d1, a2, b2, e2, d2, c2, a3, b3, e3, d3, c3, x4, tmp3, tmp2, rest,
):
    core = pos[0]
    mine = ((core, own_a, xm_a, xp_a, ym_a, yp_a), (1 - core, own_b, xm_b, xp_b, ym_b, yp_b))
    for c, *parts in mine:
        spread(2, 0, c, *parts, a1, a2)
        spread(2, 1, c, *parts, b1, b2)
    for c, src in ((core, r3_a), (1 - core, r3_b)):
        window3(src, a3, 0, 2, c, pos, gx_n, gy_n)
        window3(src, b3, 1, 2, c, pos, gx_n, gy_n)
    a4 = build4(r3f_a, 4, 0, core, gx_n, gy_n) + build4(r3f_b, 4, 0, 1 - core, gx_n, gy_n)
    b4 = build4(r3f_a, 4, 1, core, gx_n, gy_n) + build4(r3f_b, 4, 1, 1 - core, gx_n, gy_n)
    faces4(a4, fx4, fy4, fz4, inv4)
    faces(1, a1, fx1, fy1, fz1, inv1, diag1)
    faces(2, a2, fx2, fy2, fz2, inv2, None)
    faces(3, a3, fx3, fy3, fz3, inv3, None)
    x4[...] = smooth4(table, b4, fx4, fy4, fz4, inv4)
    smooth(3, b3, fx3, fy3, fz3, inv3, e3, d3, c3)
    smooth(2, b2, fx2, fy2, fz2, inv2, e2, d2, c2)
    smooth(1, b1, fx1, fy1, fz1, inv1, e1, d1, x1)
    combine(pos, gx_n, gy_n, x4, c3, c2, tmp3, tmp2)

    def finish(i, _):
        x1[:, i] = DAMPING * (x1[:, i] + tmp2[:, i // 2 - 1])
        return 0

    lax.fori_loop(4, 24, finish, 0)

    def residual(i, _):
        here, near = nearby(1, i + 6, 28, x1, fx1, fy1, fz1)
        bv = b1[:, i + 6]
        right[:, i] = bv[:, 8:24, :]
        res = bv - (diag1[:, i + 6] * here - near)
        rest[:, i] = res[:, 8:24, :]
        return 0

    lax.fori_loop(0, 16, residual, 0)
    for c in range(2):
        for t in range(2):
            own[c, pl.ds(t, 16, 2)] = rest[c, :, t * 8:t * 8 + 8, :]

        def read_pair(k):
            total = None
            for x in (2 * k, 2 * k + 1):
                part = rest[c, x, pl.ds(0, 8, 2), :] + rest[c, x, pl.ds(1, 8, 2), :]
                total = part if total is None else total + part
            return total

        def out(k, value):
            own[c, 32 + k] = value

        restrict_to2(read_pair, out)
    for i in range(6):
        for t in range(2):
            up[2 * i + t] = own[core, 2 * (10 + i) + t]
            down[2 * i + t] = own[core, 2 * i + t]
    for i in range(3):
        up[12 + i] = own[core, 33 + i]
        down[12 + i] = own[core, 32 + i]
    slot[...] = restrict_to3(
        lambda k: own[core, 32 + k, pl.ds(0, 4, 2), :] + own[core, 32 + k, pl.ds(1, 4, 2), :]
    )


def second_kernel(
    gx_n, gy_n, pos, table,
    own, xm_a, xp_a, ym_a, yp_a, xm_b, xp_b, ym_b, yp_b, r3_a, r3_b, r3f_a, r3f_b,
    fx1, fy1, fz1, inv1, diag1, fx2, fy2, fz2, inv2, fx3, fy3, fz3, inv3, fx4, fy4, fz4, inv4,
    x1, right, out_x, out_r,
    b1, e1, d1, c1, b2, e2, d2, c2, b3, e3, d3, c3, x4, tmp3, tmp2, rest,
):
    core = pos[0]
    spread(1, 0, core, own.at[core], xm_a, xp_a, ym_a, yp_a, b1, b2)
    spread(1, 0, 1 - core, own.at[1 - core], xm_b, xp_b, ym_b, yp_b, b1, b2)
    window3(r3_a, b3, 0, 1, core, pos, gx_n, gy_n)
    window3(r3_b, b3, 0, 1, 1 - core, pos, gx_n, gy_n)
    b4 = build4(r3f_a, 2, 0, core, gx_n, gy_n) + build4(r3f_b, 2, 0, 1 - core, gx_n, gy_n)
    x4[...] = smooth4(table, b4, fx4, fy4, fz4, inv4)
    smooth(3, b3, fx3, fy3, fz3, inv3, e3, d3, c3)
    smooth(2, b2, fx2, fy2, fz2, inv2, e2, d2, c2)
    smooth(1, b1, fx1, fy1, fz1, inv1, e1, d1, c1)
    combine(pos, gx_n, gy_n, x4, c3, c2, tmp3, tmp2)

    def finish(i, _):
        c1[:, i] = x1[:, i] + DAMPING * (c1[:, i] + tmp2[:, i // 2 - 1])
        return 0

    lax.fori_loop(4, 24, finish, 0)

    def residual(i, _):
        here, near = nearby(1, i + 6, 28, c1, fx1, fy1, fz1)
        res = diag1[:, i + 6] * here - near
        rest[:, i] = right[:, i] - res[:, 8:24, :]
        return 0

    lax.fori_loop(0, 16, residual, 0)
    out_r[...] = rest[core]
    out_x[...] = c1[core, 6:22, 8:24, :]


def call(kernel, outs, scratch, *args):
    smem = pl.BlockSpec(memory_space=pltpu.SMEM)
    vmem = pl.BlockSpec(memory_space=pltpu.VMEM)
    return pl.pallas_call(
        kernel,
        out_shape=[jax.ShapeDtypeStruct(s, F32) for s in outs],
        in_specs=[smem if a.ndim < 3 and a.shape[-1] != 128 else vmem for a in args],
        out_specs=[vmem for _ in outs],
        scratch_shapes=[pltpu.VMEM(s, F32) for s in scratch],
        compiler_params=pltpu.CompilerParams(vmem_limit_bytes=56 * 1024 * 1024),
        interpret=INTERPRET,
    )(*args)


def shift(x, axis, step):
    size = lax.axis_size(axis)
    return lax.ppermute(x, axis, [(i, i + step) for i in range(size) if 0 <= i + step < size])


def swap(x):
    return lax.ppermute(x, "grp", [(0, 1), (1, 0)])


def everywhere(slot):
    gx_n, gy_n = lax.axis_size("gx"), lax.axis_size("gy")
    copies = jnp.broadcast_to(slot[None], (gx_n * gy_n,) + slot.shape)
    return lax.all_to_all(copies, ("gx", "gy"), 0, 0, tiled=True)


def on_device(right_side, coefficient):
    gx_n, gy_n = lax.axis_size("gx"), lax.axis_size("gy")
    pos = jnp.stack([lax.axis_index("grp"), lax.axis_index("gx"), lax.axis_index("gy")])
    pos = pos.astype(jnp.int32)
    _, keeps, pushes = cheb_steps(COARSE_DEGREE, LOW_COARSE, HIGH_BOUND)
    table = jnp.array([keeps, pushes], F32)

    own, up, down, slot = call(
        prepare_kernel, [(72, 8, 128), (30, 8, 128), (30, 8, 128), (8, 128)], [],
        coefficient, right_side,
    )
    own_o = swap(own)
    xm, xp = shift(up, "gx", 1), shift(down, "gx", -1)
    r3 = everywhere(slot)
    xm_o, xp_o = swap(xm), swap(xp)
    r3_o = swap(r3)
    zero = pos * 0
    up, down = call(
        functools.partial(sides_kernel, 2), [(76, 8, 128)] * 2, [], zero, own[None], xm, xp
    )
    ym, yp = shift(up, "gy", 1), shift(down, "gy", -1)
    ym_o, yp_o = swap(ym), swap(yp)

    s1, s2, s3 = (2, 28, 32, 128), (2, 10, 24, 128), (2, 5, 24, 128)
    s4 = (gx_n // 2, gy_n * 2, 128)
    coarse = (gx_n * gy_n * 8, 128)
    outs = [s1] * 5 + [s2] * 4 + [s3] * 4 + [s4] * 4
    outs += [s1, (2, 16, 16, 128), (2, 36, 8, 128), (15, 8, 128), (15, 8, 128), (4, 128)]
    *coefs, x1, right, own, up, down, slot = call(
        functools.partial(first_kernel, gx_n, gy_n), outs,
        [s1, s1, s1, (2,) + s1, s2, s2, s2, (2,) + s2, s2, s3, s3, s3, (2,) + s3, s3,
         s4, s3, (2, 12, 32, 128), (2, 16, 16, 128)],
        pos, table, own, xm, xp, ym, yp, own_o, xm_o, xp_o, ym_o, yp_o,
        r3, r3_o, r3.reshape(coarse), r3_o.reshape(coarse),
    )
    xm, xp = shift(up, "gx", 1), shift(down, "gx", -1)
    r3 = everywhere(slot)
    xm_o, xp_o = swap(xm), swap(xp)
    r3_o = swap(r3)
    up, down = call(
        functools.partial(sides_kernel, 1), [(38, 8, 128)] * 2, [], pos, own, xm, xp
    )
    ym, yp = shift(up, "gy", 1), shift(down, "gy", -1)
    ym_o, yp_o = swap(ym), swap(yp)
    coarse = (gx_n * gy_n * 4, 128)
    solution_field, residual = call(
        functools.partial(second_kernel, gx_n, gy_n), [(16, 16, 128)] * 2,
        [s1, s1, (2,) + s1, s1, s2, s2, (2,) + s2, s2, s3, s3, (2,) + s3, s3,
         s4, s3, (2, 12, 32, 128), (2, 16, 16, 128)],
        pos, table, own, xm, xp, ym, yp, xm_o, xp_o, ym_o, yp_o,
        r3, r3_o, r3.reshape(coarse), r3_o.reshape(coarse), *coefs, x1, right,
    )
    return solution_field, residual


def solution(mesh):
    placed = P("gx", "gy", "grp")
    return jax.shard_map(
        on_device, mesh=mesh, in_specs=(placed, placed), out_specs=(placed, placed),
        check_vma=False,
    )
```

time: 1580 us -> 165 us (0.10)
  starting transfers between devices: 600 us -> 65.9 us
  waiting for transfers between devices: 501 us -> 19.7 us
  local copies, waits for them, and re-layouts: 253 us -> 6.16 us
  other arithmetic: 195 us -> 0.56 us
  Pallas kernels: 0 us -> 69.8 us
    ppermute x174 -> x19, starting transfers between devices: 600 us -> 40.2 us  [the longest x8 26.3 us: shift(): lax.ppermute(x, axis, [(i, i + step) for i in range(size) if 0 <= i + ste...]
    unnamed x4 -> x0, waiting for transfers between devices: 477 us -> none
    add x60 -> x0, other arithmetic: 174 us -> none  [the longest x54 171 us: advance(): return (resid, update, total + update)]
    dynamic_slice x110 -> x0, local copies, waits for them, and re-layouts: 140 us -> none  [the longest x54 70 us: advance(): keep_table[step] * update + push_table[step] * (inverse_diag * resid)]
    pallas_call x0 -> x5, Pallas kernels: none -> 69.8 us  [call(): pl.pallas_call(kernel, out_shape=[jax.ShapeDtypeStruct(s, F32) for s in o...]
    reshape x21 -> x0, local copies, waits for them, and re-layouts: 46.2 us -> none  [the longest x3 30.1 us: restrict(): field.reshape(size_a // 2, 2, size_b // 2, 2, size_c // 2, 2)]
    all_to_all x0 -> x2, starting transfers between devices: none -> 25.7 us  [everywhere(): return lax.all_to_all(copies, ('gx', 'gy'), 0, 0, tiled=True)]
    slice x87 -> x0, local copies, waits for them, and re-layouts: 16.7 us -> none  [the longest x84 16.6 us: with_halo(): last = lax.slice_in_dim(x, length - width, length, axis=dim)]
  transfers between devices with their start and end apart: 176 -> 21, of which waited for: 20 -> 8; matrix products, arithmetic and copies ran while one was open for 7% -> 1% of each run, Pallas kernels for 0% -> 2%
where the time goes in v1:
time: 165 us; the launch traced here: 163 us
  Pallas kernels  69.8 us (42%)
  starting transfers between devices  65.9 us (40%)
  waiting for transfers between devices  19.7 us (12%)
  local copies, waits for them, and re-layouts  6.16 us (4%)
    pallas_call x5, Pallas kernels, call(): pl.pallas_call(kernel, out_shape=[jax.ShapeDtypeStruct(s, F32) for s in o...  69.8 us
    ppermute x8, starting transfers between devices, shift(): lax.ppermute(x, axis, [(i, i + step) for i in range(size) if 0 <= i + ste...  26.3 us
    all_to_all x2, starting transfers between devices, everywhere(): return lax.all_to_all(copies, ('gx', 'gy'), 0, 0, tiled=True)  25.7 us
    ppermute x8, waiting for transfers between devices, shift(): lax.ppermute(x, axis, [(i, i + step) for i in range(size) if 0 <= i + ste...  16.6 us
    ppermute x11, starting transfers between devices, swap(): return lax.ppermute(x, 'grp', [(0, 1), (1, 0)])  13.8 us
  transfers between devices with their start and end apart: 21, of which 8 were waited for; matrix products, arithmetic and copies ran while one was open for 1% of the time, Pallas kernels for 2%

profile of v1, /device:TPU:27, one launch (start us, length us, event | category | flops | bytes accessed | tf_op | source)
XLA Modules:
  0.0 163.2 jit_solution(17232611558981378534)
XLA Ops:
  0.6 2.5 %shard_map.50 = (f32[72,8,128]{2,1,0:T(8,128)}, f32[30,8,128]{2,1,0:T(8,128)}, f32[30,8,128]{2,1,0:T(8,128)}, f32[8,128]{1,0:T(8,128)}) custom-call(f32[16,16,128]{2,1,0:T(8,128)} %a.1, f32[16,16,128]{2,1,0:T(8,128)} %b.1), custom_call_target="tpu_custom_call" | custom-call | tf_op jit(solution)/shard_map/pallas_call | solution.py:478
  3.1 1.5 broadcast_in_dim.7
  4.7 14.9 %all-to-all-start = ((f32[128,8,128]{2,1,0:T(8,128)}), f32[128,8,128]{2,1,0:T(8,128)S(1)}, u32[]{:S(2)}, u32[]{:S(2)}) async-start(f32[128,8,128]{2,1,0:T(8,128)} %broadcast_in_dim.7), calls=%async_computation | async-start | bytes 1048576 | tf_op jit(solution)/shard_map/all_to_all | solution.py:501
  19.6 3.9 %collective-permute-start = (f32[30,8,128]{2,1,0:T(8,128)S(1)}, f32[30,8,128]{2,1,0:T(8,128)S(1)}, u32[]{:S(2)}, u32[]{:S(2)}) collective-permute-start(f32[30,8,128]{2,1,0:T(8,128)S(1)} %copy-done.23), channel_id=1, source_target_pairs={{0,16},{16,32},{32,48},{48,64},{64,80},{80,96},{96,112},{1,17},{17... | collective-permute-start | bytes 368648 | tf_op jit(solution)/shard_map/ppermute | solution.py:491
  23.6 1.9 %collective-permute-start.1 = (f32[30,8,128]{2,1,0:T(8,128)S(1)}, f32[30,8,128]{2,1,0:T(8,128)S(1)}, u32[]{:S(2)}, u32[]{:S(2)}) collective-permute-start(f32[30,8,128]{2,1,0:T(8,128)S(1)} %copy-done.22), channel_id=1, source_target_pairs={{16,0},{32,16},{48,32},{64,48},{80,64},{96,80},{112,96},{17,1},{33... | collective-permute-start | bytes 368648 | tf_op jit(solution)/shard_map/ppermute | solution.py:491
  25.5 1.9 %collective-permute-done.lower.xm_a = f32[30,8,128]{2,1,0:T(8,128)S(1)} collective-permute-done((f32[30,8,128]{2,1,0:T(8,128)S(1)}, f32[30,8,128]{2,1,0:T(8,128)S(1)}, u32[]{:S(2)}, u32[]{:S(2)}) %collective-permute-start) | collective-permute-done | bytes 122912 | tf_op jit(solution)/shard_map/ppermute | solution.py:491
  27.4 6.7 %collective-permute-done.1.upper.xp_a = f32[30,8,128]{2,1,0:T(8,128)S(1)} collective-permute-done((f32[30,8,128]{2,1,0:T(8,128)S(1)}, f32[30,8,128]{2,1,0:T(8,128)S(1)}, u32[]{:S(2)}, u32[]{:S(2)}) %collective-permute-start.1) | collective-permute-done | bytes 122912 | tf_op jit(solution)/shard_map/ppermute | solution.py:491
  34.8 1.9 %shard_map.51 = (f32[76,8,128]{2,1,0:T(8,128)}, f32[76,8,128]{2,1,0:T(8,128)}) custom-call(s32[3]{0:T(128)} %broadcast_1_pos.2.pos, f32[1,72,8,128]{3,2,1,0:T(8,128)} %bitcast.11, f32[30,8,128]{2,1,0:T(8,128)} %copy-done.5, f32[30,8,128]{2,1,0:T(8,128)} %copy-done.6), custom_call_target="tpu_custom_call" | custom-call | tf_op jit(solution)/shard_map/pallas_call | solution.py:478
  36.7 2.8 %collective-permute-start.2 = (f32[76,8,128]{2,1,0:T(8,128)}, f32[76,8,128]{2,1,0:T(8,128)S(1)}, u32[]{:S(2)}, u32[]{:S(2)}) collective-permute-start(f32[76,8,128]{2,1,0:T(8,128)} %get-tuple-element.36), channel_id=1, source_target_pairs={{0,1},{1,2},{2,3},{3,4},{4,5},{5,6},{6,7},{7,8},{8,9},{9,10},{10,1... | collective-permute-start | bytes 933896 | tf_op jit(solution)/shard_map/ppermute | solution.py:491
  39.6 4.5 %collective-permute-start.3 = (f32[76,8,128]{2,1,0:T(8,128)}, f32[76,8,128]{2,1,0:T(8,128)S(1)}, u32[]{:S(2)}, u32[]{:S(2)}) collective-permute-start(f32[76,8,128]{2,1,0:T(8,128)} %get-tuple-element.37), channel_id=1, source_target_pairs={{1,0},{2,1},{3,2},{4,3},{5,4},{6,5},{7,6},{8,7},{9,8},{10,9},{11,1... | collective-permute-start | bytes 933896 | tf_op jit(solution)/shard_map/ppermute | solution.py:491
  44.1 2.7 %collective-permute-start.9 = (f32[128,8,128]{2,1,0:T(8,128)S(1)}, f32[128,8,128]{2,1,0:T(8,128)S(1)}, u32[]{:S(2)}, u32[]{:S(2)}) collective-permute-start(f32[128,8,128]{2,1,0:T(8,128)S(1)} %all-to-all-done.r3_a), channel_id=1, source_target_pairs={{0,128},{128,0},{1,129},{129,1},{2,130},{130,2},{3,131},{131,3},{4... | collective-permute-start | bytes 1572872 | tf_op jit(solution)/shard_map/ppermute | solution.py:495
  47.8 2.9 %collective-permute-start.7 = (f32[76,8,128]{2,1,0:T(8,128)S(1)}, f32[76,8,128]{2,1,0:T(8,128)S(1)}, u32[]{:S(2)}, u32[]{:S(2)}) collective-permute-start(f32[76,8,128]{2,1,0:T(8,128)S(1)} %collective-permute-done.2.ym_a), channel_id=1, source_target_pairs={{0,128},{128,0},{1,129},{129,1},{2,130},{130,2},{3,131},{131,3},{4... | collective-permute-start | bytes 933896 | tf_op jit(solution)/shard_map/ppermute | solution.py:495
  56.5 36.3 %shard_map.52 = (f32[2,28,32,128]{3,2,1,0:T(8,128)}, f32[2,28,32,128]{3,2,1,0:T(8,128)}, f32[2,28,32,128]{3,2,1,0:T(8,128)}, f32[2,28,32,128]{3,2,1,0:T(8,128)},...) custom-call(s32[3]{0:T(128)} %pad_add_fusion.pos, ...), custom_call_target="tpu_custom_call" | custom-call | tf_op jit(solution)/shard_map/pallas_call | solution.py:478
  92.8 1.4 broadcast_in_dim.8
  94.2 10.8 %all-to-all-start.1 = ((f32[128,4,128]{2,1,0:T(4,128)}), f32[128,4,128]{2,1,0:T(4,128)S(1)}, u32[]{:S(2)}, u32[]{:S(2)}) async-start(f32[128,4,128]{2,1,0:T(4,128)} %broadcast_in_dim.8), calls=%async_computation.1 | async-start | bytes 524288 | tf_op jit(solution)/shard_map/all_to_all | solution.py:501
  105.1 3.8 %collective-permute-start.10 = (f32[15,8,128]{2,1,0:T(8,128)S(1)}, f32[15,8,128]{2,1,0:T(8,128)S(1)}, u32[]{:S(2)}, u32[]{:S(2)}) collective-permute-start(f32[15,8,128]{2,1,0:T(8,128)S(1)} %copy-done.25), channel_id=1, source_target_pairs={{0,16},{16,32},{32,48},{48,64},{64,80},{80,96},{96,112},{1,17},{17... | collective-permute-start | bytes 184328 | tf_op jit(solution)/shard_map/ppermute | solution.py:491
  108.9 1.9 %collective-permute-start.11 = (f32[15,8,128]{2,1,0:T(8,128)S(1)}, f32[15,8,128]{2,1,0:T(8,128)S(1)}, u32[]{:S(2)}, u32[]{:S(2)}) collective-permute-start(f32[15,8,128]{2,1,0:T(8,128)S(1)} %copy-done.24), channel_id=1, source_target_pairs={{16,0},{32,16},{48,32},{64,48},{80,64},{96,80},{112,96},{17,1},{33... | collective-permute-start | bytes 184328 | tf_op jit(solution)/shard_map/ppermute | solution.py:491
  110.9 7.0 %collective-permute-done.11.upper.xp_a = f32[15,8,128]{2,1,0:T(8,128)S(1)} collective-permute-done((f32[15,8,128]{2,1,0:T(8,128)S(1)}, f32[15,8,128]{2,1,0:T(8,128)S(1)}, u32[]{:S(2)}, u32[]{:S(2)}) %collective-permute-start.11) | collective-permute-done | bytes 61472 | tf_op jit(solution)/shard_map/ppermute | solution.py:491
  118.5 1.8 %shard_map.53 = (f32[38,8,128]{2,1,0:T(8,128)}, f32[38,8,128]{2,1,0:T(8,128)}) custom-call(s32[3]{0:T(128)} %pad_add_fusion.pos, f32[2,36,8,128]{3,2,1,0:T(8,128)} %get-tuple-element.39.own, f32[15,8,128]{2,1,0:T(8,128)} %copy-done.12, f32[15,8,128]{2,1,0:T(8,128)} %copy-done.13), custom_call_target="tpu_custom_call" | custom-call | tf_op jit(solution)/shard_map/pallas_call | solution.py:478
  120.2 3.0 %collective-permute-start.12 = (f32[38,8,128]{2,1,0:T(8,128)}, f32[38,8,128]{2,1,0:T(8,128)S(1)}, u32[]{:S(2)}, u32[]{:S(2)}) collective-permute-start(f32[38,8,128]{2,1,0:T(8,128)} %get-tuple-element.42), channel_id=1, source_target_pairs={{0,1},{1,2},{2,3},{3,4},{4,5},{5,6},{6,7},{7,8},{8,9},{9,10},{10,1... | collective-permute-start | bytes 466952 | tf_op jit(solution)/shard_map/ppermute | solution.py:491
  123.3 4.3 %collective-permute-start.13 = (f32[38,8,128]{2,1,0:T(8,128)}, f32[38,8,128]{2,1,0:T(8,128)S(1)}, u32[]{:S(2)}, u32[]{:S(2)}) collective-permute-start(f32[38,8,128]{2,1,0:T(8,128)} %get-tuple-element.43), channel_id=1, source_target_pairs={{1,0},{2,1},{3,2},{4,3},{5,4},{6,5},{7,6},{8,7},{9,8},{10,9},{11,1... | collective-permute-start | bytes 466952 | tf_op jit(solution)/shard_map/ppermute | solution.py:491
  127.7 2.6 %collective-permute-start.18 = (f32[128,4,128]{2,1,0:T(4,128)S(1)}, f32[128,4,128]{2,1,0:T(4,128)S(1)}, u32[]{:S(2)}, u32[]{:S(2)}) collective-permute-start(f32[128,4,128]{2,1,0:T(4,128)S(1)} %all-to-all-done.1.r3_a), channel_id=1, source_target_pairs={{0,128},{128,0},{1,129},{129,1},{2,130},{130,2},{3,131},{131,3},{4... | collective-permute-start | bytes 786440 | tf_op jit(solution)/shard_map/ppermute | solution.py:495
  131.7 1.6 collective-permute-start.17
  135.7 27.3 %shard_map.54 = (f32[16,16,128]{2,1,0:T(8,128)}, f32[16,16,128]{2,1,0:T(8,128)}) custom-call(s32[3]{0:T(128)} %pad_add_fusion.pos, f32[2,15]{1,0:T(2,128)} %constant.18.clone.table, f32[2,36,8,128]{3,2,1,0:T(8,128)} %get-tuple-element.39.own, f32[15,8,128]{2,1,0:T(8,128)} %copy-done.12, f32[15,8,128]{2,1,0:T(8,128)} %copy-done.13, f32[38,8,128]{2,1,0:T(8,128)} %copy-done.14, ...), custom_call_target="tpu_custom_call" | custom-call | tf_op jit(solution)/shard_map/pallas_call | solution.py:478
  (79 shorter events, 11.9 us)
Async XLA Ops:
  4.7 14.9 %copy-start.23 = (f32[30,8,128]{2,1,0:T(8,128)S(1)}, f32[30,8,128]{2,1,0:T(8,128)}, u32[]{:S(2)}) copy-start(f32[30,8,128]{2,1,0:T(8,128)} %get-tuple-element.34) | copy-start | bytes 368644
  4.7 18.9 %copy-start.22 = (f32[30,8,128]{2,1,0:T(8,128)S(1)}, f32[30,8,128]{2,1,0:T(8,128)}, u32[]{:S(2)}) copy-start(f32[30,8,128]{2,1,0:T(8,128)} %get-tuple-element.35) | copy-start | bytes 368644
  4.7 39.4 %all-to-all-start = ((f32[128,8,128]{2,1,0:T(8,128)}), f32[128,8,128]{2,1,0:T(8,128)S(1)}, u32[]{:S(2)}, u32[]{:S(2)}) async-start(f32[128,8,128]{2,1,0:T(8,128)} %broadcast_in_dim.7), calls=%async_computation | async-start | bytes 1048576 | tf_op jit(solution)/shard_map/all_to_all | solution.py:501
  19.6 32.4 %copy-start.3 = (f32[72,8,128]{2,1,0:T(8,128)S(1)}, f32[72,8,128]{2,1,0:T(8,128)}, u32[]{:S(2)}) copy-start(f32[72,8,128]{2,1,0:T(8,128)} %get-tuple-element.33.own_a) | copy-start | bytes 884740
  19.6 7.8 %collective-permute-start = (f32[30,8,128]{2,1,0:T(8,128)S(1)}, f32[30,8,128]{2,1,0:T(8,128)S(1)}, u32[]{:S(2)}, u32[]{:S(2)}) collective-permute-start(f32[30,8,128]{2,1,0:T(8,128)S(1)} %copy-done.23), channel_id=1, source_target_pairs={{0,16},{16,32},{32,48},{48,64},{64,80},{80,96},{96,112},{1,17},{17... | collective-permute-start | bytes 368648 | tf_op jit(solution)/shard_map/ppermute | solution.py:491
  23.6 10.6 %collective-permute-start.1 = (f32[30,8,128]{2,1,0:T(8,128)S(1)}, f32[30,8,128]{2,1,0:T(8,128)S(1)}, u32[]{:S(2)}, u32[]{:S(2)}) collective-permute-start(f32[30,8,128]{2,1,0:T(8,128)S(1)} %copy-done.22), channel_id=1, source_target_pairs={{16,0},{32,16},{48,32},{64,48},{80,64},{96,80},{112,96},{17,1},{33... | collective-permute-start | bytes 368648 | tf_op jit(solution)/shard_map/ppermute | solution.py:491
  36.7 11.1 %collective-permute-start.2 = (f32[76,8,128]{2,1,0:T(8,128)}, f32[76,8,128]{2,1,0:T(8,128)S(1)}, u32[]{:S(2)}, u32[]{:S(2)}) collective-permute-start(f32[76,8,128]{2,1,0:T(8,128)} %get-tuple-element.36), channel_id=1, source_target_pairs={{0,1},{1,2},{2,3},{3,4},{4,5},{5,6},{6,7},{7,8},{8,9},{9,10},{10,1... | collective-permute-start | bytes 933896 | tf_op jit(solution)/shard_map/ppermute | solution.py:491
  39.6 11.1 %collective-permute-start.3 = (f32[76,8,128]{2,1,0:T(8,128)}, f32[76,8,128]{2,1,0:T(8,128)S(1)}, u32[]{:S(2)}, u32[]{:S(2)}) collective-permute-start(f32[76,8,128]{2,1,0:T(8,128)} %get-tuple-element.37), channel_id=1, source_target_pairs={{1,0},{2,1},{3,2},{4,3},{5,4},{6,5},{7,6},{8,7},{9,8},{10,9},{11,1... | collective-permute-start | bytes 933896 | tf_op jit(solution)/shard_map/ppermute | solution.py:491
  44.1 11.3 %collective-permute-start.9 = (f32[128,8,128]{2,1,0:T(8,128)S(1)}, f32[128,8,128]{2,1,0:T(8,128)S(1)}, u32[]{:S(2)}, u32[]{:S(2)}) collective-permute-start(f32[128,8,128]{2,1,0:T(8,128)S(1)} %all-to-all-done.r3_a), channel_id=1, source_target_pairs={{0,128},{128,0},{1,129},{129,1},{2,130},{130,2},{3,131},{131,3},{4... | collective-permute-start | bytes 1572872 | tf_op jit(solution)/shard_map/ppermute | solution.py:495
  47.8 7.6 %collective-permute-start.7 = (f32[76,8,128]{2,1,0:T(8,128)S(1)}, f32[76,8,128]{2,1,0:T(8,128)S(1)}, u32[]{:S(2)}, u32[]{:S(2)}) collective-permute-start(f32[76,8,128]{2,1,0:T(8,128)S(1)} %collective-permute-done.2.ym_a), channel_id=1, source_target_pairs={{0,128},{128,0},{1,129},{129,1},{2,130},{130,2},{3,131},{131,3},{4... | collective-permute-start | bytes 933896 | tf_op jit(solution)/shard_map/ppermute | solution.py:495
  50.7 4.7 %collective-permute-start.8 = (f32[76,8,128]{2,1,0:T(8,128)S(1)}, f32[76,8,128]{2,1,0:T(8,128)S(1)}, u32[]{:S(2)}, u32[]{:S(2)}) collective-permute-start(f32[76,8,128]{2,1,0:T(8,128)S(1)} %collective-permute-done.3.yp_a), channel_id=1, source_target_pairs={{0,128},{128,0},{1,129},{129,1},{2,130},{130,2},{3,131},{131,3},{4... | collective-permute-start | bytes 933896 | tf_op jit(solution)/shard_map/ppermute | solution.py:495
  52.0 3.4 %collective-permute-start.4 = (f32[72,8,128]{2,1,0:T(8,128)S(1)}, f32[72,8,128]{2,1,0:T(8,128)S(1)}, u32[]{:S(2)}, u32[]{:S(2)}) collective-permute-start(f32[72,8,128]{2,1,0:T(8,128)S(1)} %copy-done.3), channel_id=1, source_target_pairs={{0,128},{128,0},{1,129},{129,1},{2,130},{130,2},{3,131},{131,3},{4... | collective-permute-start | bytes 884744 | tf_op jit(solution)/shard_map/ppermute | solution.py:495
  52.0 1.8 %collective-permute-start.5 = (f32[30,8,128]{2,1,0:T(8,128)}, f32[30,8,128]{2,1,0:T(8,128)S(1)}, u32[]{:S(2)}, u32[]{:S(2)}) collective-permute-start(f32[30,8,128]{2,1,0:T(8,128)} %copy-done.5), channel_id=1, source_target_pairs={{0,128},{128,0},{1,129},{129,1},{2,130},{130,2},{3,131},{131,3},{4... | collective-permute-start | bytes 368648 | tf_op jit(solution)/shard_map/ppermute | solution.py:495
  53.8 1.6 collective-permute-start.6
  94.2 33.4 %all-to-all-start.1 = ((f32[128,4,128]{2,1,0:T(4,128)}), f32[128,4,128]{2,1,0:T(4,128)S(1)}, u32[]{:S(2)}, u32[]{:S(2)}) async-start(f32[128,4,128]{2,1,0:T(4,128)} %broadcast_in_dim.8), calls=%async_computation.1 | async-start | bytes 524288 | tf_op jit(solution)/shard_map/all_to_all | solution.py:501
  105.1 5.8 %collective-permute-start.10 = (f32[15,8,128]{2,1,0:T(8,128)S(1)}, f32[15,8,128]{2,1,0:T(8,128)S(1)}, u32[]{:S(2)}, u32[]{:S(2)}) collective-permute-start(f32[15,8,128]{2,1,0:T(8,128)S(1)} %copy-done.25), channel_id=1, source_target_pairs={{0,16},{16,32},{32,48},{48,64},{64,80},{80,96},{96,112},{1,17},{17... | collective-permute-start | bytes 184328 | tf_op jit(solution)/shard_map/ppermute | solution.py:491
  108.9 8.9 %collective-permute-start.11 = (f32[15,8,128]{2,1,0:T(8,128)S(1)}, f32[15,8,128]{2,1,0:T(8,128)S(1)}, u32[]{:S(2)}, u32[]{:S(2)}) collective-permute-start(f32[15,8,128]{2,1,0:T(8,128)S(1)} %copy-done.24), channel_id=1, source_target_pairs={{16,0},{32,16},{48,32},{64,48},{80,64},{96,80},{112,96},{17,1},{33... | collective-permute-start | bytes 184328 | tf_op jit(solution)/shard_map/ppermute | solution.py:491
  120.2 10.1 %collective-permute-start.12 = (f32[38,8,128]{2,1,0:T(8,128)}, f32[38,8,128]{2,1,0:T(8,128)S(1)}, u32[]{:S(2)}, u32[]{:S(2)}) collective-permute-start(f32[38,8,128]{2,1,0:T(8,128)} %get-tuple-element.42), channel_id=1, source_target_pairs={{0,1},{1,2},{2,3},{3,4},{4,5},{5,6},{6,7},{7,8},{8,9},{9,10},{10,1... | collective-permute-start | bytes 466952 | tf_op jit(solution)/shard_map/ppermute | solution.py:491
  123.3 8.4 %collective-permute-start.13 = (f32[38,8,128]{2,1,0:T(8,128)}, f32[38,8,128]{2,1,0:T(8,128)S(1)}, u32[]{:S(2)}, u32[]{:S(2)}) collective-permute-start(f32[38,8,128]{2,1,0:T(8,128)} %get-tuple-element.43), channel_id=1, source_target_pairs={{1,0},{2,1},{3,2},{4,3},{5,4},{6,5},{7,6},{8,7},{9,8},{10,9},{11,1... | collective-permute-start | bytes 466952 | tf_op jit(solution)/shard_map/ppermute | solution.py:491
  127.7 7.2 %collective-permute-start.18 = (f32[128,4,128]{2,1,0:T(4,128)S(1)}, f32[128,4,128]{2,1,0:T(4,128)S(1)}, u32[]{:S(2)}, u32[]{:S(2)}) collective-permute-start(f32[128,4,128]{2,1,0:T(4,128)S(1)} %all-to-all-done.1.r3_a), channel_id=1, source_target_pairs={{0,128},{128,0},{1,129},{129,1},{2,130},{130,2},{3,131},{131,3},{4... | collective-permute-start | bytes 786440 | tf_op jit(solution)/shard_map/ppermute | solution.py:495
  130.3 4.6 %collective-permute-start.16 = (f32[38,8,128]{2,1,0:T(8,128)S(1)}, f32[38,8,128]{2,1,0:T(8,128)S(1)}, u32[]{:S(2)}, u32[]{:S(2)}) collective-permute-start(f32[38,8,128]{2,1,0:T(8,128)S(1)} %collective-permute-done.12.ym_a), channel_id=1, source_target_pairs={{0,128},{128,0},{1,129},{129,1},{2,130},{130,2},{3,131},{131,3},{4... | collective-permute-start | bytes 466952 | tf_op jit(solution)/shard_map/ppermute | solution.py:495
  131.7 3.2 %collective-permute-start.17 = (f32[38,8,128]{2,1,0:T(8,128)S(1)}, f32[38,8,128]{2,1,0:T(8,128)S(1)}, u32[]{:S(2)}, u32[]{:S(2)}) collective-permute-start(f32[38,8,128]{2,1,0:T(8,128)S(1)} %collective-permute-done.13.yp_a), channel_id=1, source_target_pairs={{0,128},{128,0},{1,129},{129,1},{2,130},{130,2},{3,131},{131,3},{4... | collective-permute-start | bytes 466952 | tf_op jit(solution)/shard_map/ppermute | solution.py:495
  133.2 1.5 collective-permute-start.14
  133.2 1.6 collective-permute-start.15
  (23 other events, 89.5 us)

commit v2 on v1

v2 whole, which is shorter than its diff:
```python
import functools

import jax
import jax.numpy as jnp
from jax import lax
from jax.experimental import pallas as pl
from jax.experimental.pallas import tpu as pltpu
from jax.sharding import PartitionSpec as P

FINE_DEGREE = 5
COARSE_DEGREE = 16
LOW_FINE = 0.2
LOW_COARSE = 0.02
HIGH_BOUND = 2.0
DAMPING = 0.5

F32 = jnp.float32
INTERPRET = False
LANES_X = {1: 1, 2: 2, 3: 4}
ROWS = {1: 32, 2: 24, 3: 24}
HELD = {1: (1, 27), 2: (0, 10), 3: (0, 5)}
STEPS = {
    1: ((2, 26), (3, 25), (4, 24), (5, 23)),
    2: ((1, 9), (1, 9), (2, 8), (2, 8)),
    3: ((1, 4),) * 4,
}
CHUNK = {1: 2, 2: 2, 3: 3}
PAD = {1: 0, 2: 1, 3: 1}
SCALE = {1: 1.0, 2: 0.25, 3: 0.0625, 4: 0.015625}


def cheb_steps(degree, low, high):
    theta = (high + low) / 2.0
    delta = (high - low) / 2.0
    sigma = theta / delta
    rho = 1.0 / sigma
    keeps = []
    pushes = []
    for step in range(degree - 1):
        rho_new = 1.0 / (2.0 * sigma - rho)
        keeps.append(rho_new * rho)
        pushes.append(2.0 * rho_new / delta)
        rho = rho_new
    return (1.0 / theta, keeps, pushes)


def roll(x, shift, axis):
    size = x.shape[axis]
    return pltpu.roll(x, shift % size, axis)


def lane_iota(shape):
    return lax.broadcasted_iota(jnp.int32, shape, len(shape) - 1)


def dot(x, m):
    high = x.astype(jnp.bfloat16)
    rest = x - high.astype(F32)
    mid = rest.astype(jnp.bfloat16)
    low = (rest - mid.astype(F32)).astype(jnp.bfloat16)
    m = m.astype(jnp.bfloat16)
    mul = lambda v: jnp.dot(v, m, preferred_element_type=F32)
    return mul(high) + (mul(mid) + mul(low))


def select_matrix(fn, value):
    row = lax.broadcasted_iota(jnp.int32, (128, 128), 0)
    col = lax.broadcasted_iota(jnp.int32, (128, 128), 1)
    return jnp.where(fn(row, col), value, 0.0).astype(F32)


def neighbours(q, v):
    zz = 128 // q
    mid = v[:, 1:-1]
    lane = lane_iota(mid.shape)
    if q == 1:
        x_up, x_dn = v[:, 2:], v[:, :-2]
        for_up = for_dn = mid
    else:
        ups = roll(v[:, 1:], -zz, 3)
        dns = roll(v[:, :-1], zz, 3)
        x_up = jnp.where(lane < 128 - zz, ups[:, :-1], ups[:, 1:])
        x_dn = jnp.where(lane >= zz, dns[:, 1:], dns[:, :-1])
        for_up, for_dn = dns[:, 1:], ups[:, :-1]
    other = lambda w: jnp.concatenate([w[1:], w[:1]], axis=0)
    inner = lane % zz
    z_up = roll(jnp.where(inner == 0, other(for_up), mid), -1, 3)
    z_dn = roll(jnp.where(inner == zz - 1, other(for_dn), mid), 1, 3)
    return mid, (x_up, x_dn, roll(mid, -1, 2), roll(mid, 1, 2), z_up, z_dn)


def blocks(start, stop, step, body):
    if stop - start == step:
        body(start)
        return

    def run(n, _):
        body(start + n * step)
        return 0

    lax.fori_loop(0, (stop - start) // step, run, 0)


def faces(level, a, weights, inv, diag_ref):
    q, pad = LANES_X[level], PAD[level]
    zz = 128 // q
    first, last = HELD[level]
    step = 5 if level == 3 else 2

    def body(i):
        mid, near = neighbours(q, a[:, pl.ds(i + pad - 1, step + 2)])
        core = lax.broadcasted_iota(jnp.int32, mid.shape, 0)
        lane = lane_iota(mid.shape) % zz
        top = (core == 1) & (lane == zz - 1)
        bottom = (core == 0) & (lane == 0)
        x_up, x_dn, y_up, y_dn, z_up, z_dn = near
        z_up = jnp.where(top, 0.0, z_up)
        z_dn = jnp.where(bottom, 0.0, z_dn)
        near = (x_up, x_dn, y_up, y_dn, z_up, z_dn)
        total = 3.0 * mid + 0.5 * ((x_up + x_dn) + (y_up + y_dn) + (z_up + z_dn))
        inverse = jnp.where(mid > 0.0, 1.0 / total, 0.0)
        at = pl.ds(i, step)
        inv[:, at] = inverse
        half = 0.5 * inverse
        for k in range(6):
            w = half * (mid + near[k])
            if k == 4:
                w = jnp.where(top, 0.0, w)
            if k == 5:
                w = jnp.where(bottom, 0.0, w)
            weights[k][:, at] = w
        if diag_ref is not None:
            diag_ref[:, at] = total

    blocks(first, last, step, body)


def weighted(q, i, step, v, weights):
    mid, near = neighbours(q, v[:, pl.ds(i - 1, step + 2)])
    at = pl.ds(i, step)
    terms = [weights[k][:, at] * near[k] for k in range(6)]
    return mid, (terms[0] + terms[1]) + (terms[2] + terms[3]) + (terms[4] + terms[5])


def smooth(level, b, weights, inv, e, d, other, x):
    q = LANES_X[level]
    first, keeps, pushes = cheb_steps(FINE_DEGREE, LOW_FINE, HIGH_BOUND)
    step = CHUNK[level]

    def start(i):
        at = pl.ds(i, 5 if level == 3 else 2)
        ev = b[:, at] * inv[:, at] * (1.0 / SCALE[level])
        e[:, at] = ev
        d[:, at] = ev * first
        x[:, at] = ev * first

    blocks(*HELD[level], 5 if level == 3 else 2, start)
    for n in range(FINE_DEGREE - 1):
        src, dst = (d, other) if n % 2 == 0 else (other, d)

        def body(i):
            at = pl.ds(i, step)
            mid, near = weighted(q, i, step, src, weights)
            ev = (e[:, at] - mid) + near
            new = keeps[n] * mid + pushes[n] * ev
            x[:, at] = x[:, at] + new
            if n < FINE_DEGREE - 2:
                e[:, at] = ev
                dst[:, at] = new

        blocks(*STEPS[level][n], step, body)


def x_up4(v):
    moved = roll(v, -32, 2)
    after = jnp.concatenate([moved[1:], moved[:1]], axis=0)
    return jnp.where(lane_iota(v.shape) < 96, moved, after)


def x_dn4(v):
    moved = roll(v, 32, 2)
    before = jnp.concatenate([moved[-1:], moved[:-1]], axis=0)
    return jnp.where(lane_iota(v.shape) >= 32, moved, before)


def faces4(a, fx, fy, fz, inv):
    nb, rows, _ = a.shape
    blk = lax.broadcasted_iota(jnp.int32, a.shape, 0)
    row = lax.broadcasted_iota(jnp.int32, a.shape, 1)
    lane = lane_iota(a.shape)
    half = 0.5 * a
    total = jnp.zeros_like(a)
    for up, dn, last, start, out in (
        (x_up4, x_dn4, (blk == nb - 1) & (lane >= 96), (blk == 0) & (lane < 32), fx),
        (lambda v: roll(v, -1, 1), lambda v: roll(v, 1, 1), row == rows - 1, row == 0, fy),
        (lambda v: roll(v, -1, 2), lambda v: roll(v, 1, 2), lane % 32 == 31, lane % 32 == 0, fz),
    ):
        inner = half + 0.5 * up(a)
        off = jnp.where(last, 0.0, inner)
        out[...] = off
        total = total + jnp.where(last, half, inner) + jnp.where(start, half, dn(off))
    inv[...] = 1.0 / total


def smooth4(table, b, fx, fy, fz, inv):
    first = cheb_steps(COARSE_DEGREE, LOW_COARSE, HIGH_BOUND)[0]
    e = b * inv[...] * (1.0 / SCALE[4])
    d = e * first

    def body(step, carry):
        e, d, x = carry
        gx, gy, gz = fx[...], fy[...], fz[...]
        near = gx * x_up4(d) + x_dn4(gx * d)
        near = near + gy * roll(d, -1, 1) + roll(gy * d, 1, 1)
        near = near + gz * roll(d, -1, 2) + roll(gz * d, 1, 2)
        e = e - d + inv[...] * near
        d = table[0, step] * d + table[1, step] * e
        return e, d, x + d

    return lax.fori_loop(0, COARSE_DEGREE - 1, body, (e, d, d))[2]


def build4(src, stride, offset, core, gx_n, gy_n):
    count = gx_n * gy_n * 2
    gap = stride // 2
    pairs = src[pl.ds(offset, count, stride), :] + src[pl.ds(offset + gap, count, stride), :]
    pairs = pairs.reshape(gx_n // 2, 2, gy_n * 2, 128)
    out = None
    for odd in range(2):
        mat = select_matrix(
            lambda r, c: c == odd * 64 + (r // 64) * 32 + core * 16 + (r % 32) // 2, 0.125
        )
        part = dot(pairs[:, odd].reshape(gx_n * gy_n, 128), mat)
        out = part if out is None else out + part
    return out.reshape(gx_n // 2, gy_n * 2, 128)


def window3(src, dst, field, fields, core, pos, gx_n, gy_n, pad):
    for bx in range(5):
        for by in range(6):
            ix = pos[1] + (bx - 2)
            iy = pos[2] + (by - 2)
            ok = (ix >= 0) & (ix < gx_n) & (iy >= 0) & (iy < gy_n)
            at = jnp.clip(ix, 0, gx_n - 1) * gy_n + jnp.clip(iy, 0, gy_n - 1)
            if fields == 1:
                tile = src[at]
            else:
                tile = src[at, pl.ds(field, 4, fields), :]
            dst[core, bx + pad, by * 4:by * 4 + 4, :] = jnp.where(ok, tile, 0.0)


def restrict_to2(read_pair, out):
    even = jnp.concatenate([read_pair(2 * k) for k in range(4)], axis=0)
    odd = jnp.concatenate([read_pair(2 * k + 1) for k in range(4)], axis=0)
    low = select_matrix(lambda r, c: c == r // 2, 0.125)
    high = select_matrix(lambda r, c: c == 64 + r // 2, 0.125)
    both = dot(even, low) + dot(odd, high)
    for k in range(4):
        out(k, both[k * 8:k * 8 + 8])


def restrict_to3(read_rows):
    total = None
    for k in range(4):
        mat = select_matrix(lambda r, c: c == k * 32 + (r % 64) // 2, 0.125)
        part = dot(read_rows(k), mat)
        total = part if total is None else total + part
    return total


def position():
    return tuple(lax.axis_index(name) for name in ("grp", "gx", "gy"))


def put_pair(even, first, second, at, up, down):
    first[at] = jnp.where(even, up, down)
    second[at] = jnp.where(even, down, up)


def is_even(index):
    return lax.rem(index, 2) == 0


def prepare_kernel(a, b, own, first, second, slots):
    even = is_even(position()[1])
    slot = None
    for f, src in enumerate((a, b)):
        for t in range(2):
            own[pl.ds(f * 32 + t, 16, 2)] = src[:, t * 8:t * 8 + 8, :]
            put_pair(
                even, first, second, pl.ds(f * 12 + t, 6, 2),
                src[10:16, t * 8:t * 8 + 8, :], src[0:6, t * 8:t * 8 + 8, :],
            )

        def read_pair(k):
            total = None
            for x in (2 * k, 2 * k + 1):
                part = src[x, pl.ds(0, 8, 2), :] + src[x, pl.ds(1, 8, 2), :]
                total = part if total is None else total + part
            return total

        values = []

        def out(k, value):
            own[64 + f * 4 + k] = value
            values.append(value)

        restrict_to2(read_pair, out)
        for k in range(3):
            put_pair(even, first, second, 24 + f * 3 + k, values[k + 1], values[k])
        slots[0, pl.ds(f, 4, 2), :] = restrict_to3(
            lambda k: own[64 + f * 4 + k, pl.ds(0, 4, 2), :] + own[64 + f * 4 + k, pl.ds(1, 4, 2), :]
        )
    slots[1:] = jnp.broadcast_to(slots[0:1], (slots.shape[0] - 1, 8, 128))


def sides_kernel(nf, own, one, two, first, second):
    core, gx, gy = position()
    even_x, even_y = is_even(gx), is_even(gy)
    if nf == 2:
        mine = lambda i: own[i]
    else:
        mine = lambda i: own[core, i]

    def lower(i):
        return jnp.where(even_x, two[i], one[i])

    def upper(i):
        return jnp.where(even_x, one[i], two[i])

    for f in range(nf):
        for i in range(28):
            if i < 6:
                low, high = lower(f * 12 + 2 * i), lower(f * 12 + 2 * i + 1)
            elif i >= 22:
                low, high = upper(f * 12 + 2 * (i - 22)), upper(f * 12 + 2 * (i - 22) + 1)
            else:
                low, high = mine(f * 32 + 2 * (i - 6)), mine(f * 32 + 2 * (i - 6) + 1)
            put_pair(even_y, first, second, f * 28 + i, high, low)
        for i in range(10):
            if i < 3:
                tile = lower(nf * 12 + f * 3 + i)
            elif i >= 7:
                tile = upper(nf * 12 + f * 3 + i - 7)
            else:
                tile = mine(nf * 32 + f * 4 + i - 3)
            first[nf * 28 + f * 10 + i] = tile
            second[nf * 28 + f * 10 + i] = tile


def spread(nf, f, core, even_x, even_y, own, x_one, x_two, y_one, y_two, fine, mid, pad):
    lower = lambda i: jnp.where(even_x, x_two[i], x_one[i])
    upper = lambda i: jnp.where(even_x, x_one[i], x_two[i])
    below = lambda i: jnp.where(even_y, y_two[i], y_one[i])
    above = lambda i: jnp.where(even_y, y_one[i], y_two[i])
    for i in range(28):
        fine[core, i, 0:8, :] = below(f * 28 + i)
        fine[core, i, 24:32, :] = above(f * 28 + i)
        for t in range(2):
            if i < 6:
                tile = lower(f * 12 + 2 * i + t)
            elif i >= 22:
                tile = upper(f * 12 + 2 * (i - 22) + t)
            else:
                tile = own[f * 32 + 2 * (i - 6) + t]
            fine[core, i, 8 + 8 * t:16 + 8 * t, :] = tile
    base = nf * 28 + f * 10
    for i in range(10):
        mid[core, i + pad, 0:8, :] = below(base + i)
        mid[core, i + pad, 16:24, :] = above(base + i)
        if i < 3:
            tile = lower(nf * 12 + f * 3 + i)
        elif i >= 7:
            tile = upper(nf * 12 + f * 3 + i - 7)
        else:
            tile = own[nf * 32 + f * 4 + i - 3]
        mid[core, i + pad, 8:16, :] = tile


def add_coarsest(pos, gx_n, gy_n, x4, x3, out):
    gx, gy = pos[1], pos[2]
    yrow = lax.broadcasted_iota(jnp.int32, (24, gy_n * 2), 0)
    ycol = lax.broadcasted_iota(jnp.int32, (24, gy_n * 2), 1)
    rows = jnp.where(ycol == (4 * gy - 8 + yrow + 1024) // 2 - 512, 1.0, 0.0).astype(F32)
    for bx in (1, 2, 3):
        ix = gx + (bx - 2)
        ok = (ix >= 0) & (ix < gx_n)
        at = jnp.clip(ix, 0, gx_n - 1)
        odd = lax.rem(at, 2)
        picked = select_rows(rows, x4[lax.div(at, 2)])
        for c in range(2):
            mat = select_matrix(
                lambda r, k: r == odd * 64 + (k // 64) * 32 + c * 16 + (k % 32) // 2, 1.0
            )
            out[c, bx - 1] = x3[c, bx] + jnp.where(ok, dot(picked, mat), 0.0)


def select_rows(rows, v):
    high = v.astype(jnp.bfloat16)
    rest = v - high.astype(F32)
    mid = rest.astype(jnp.bfloat16)
    low = (rest - mid.astype(F32)).astype(jnp.bfloat16)
    rows = rows.astype(jnp.bfloat16)
    mul = lambda w: jnp.dot(rows, w, preferred_element_type=F32)
    return mul(high) + (mul(mid) + mul(low))


def combine(sum3, x2, tmp3, tmp2):
    for c in range(2):
        for bx in range(3):
            tmp3[c, bx, pl.ds(0, 12, 2), :] = sum3[c, bx, 4:16, :]
            tmp3[c, bx, pl.ds(1, 12, 2), :] = sum3[c, bx, 4:16, :]
    for low in range(4):
        mat = select_matrix(lambda r, k: r == low * 32 + (k % 64) // 2, 1.0)
        for i in [i for i in range(2, 8) if (i + 5) % 4 == low]:
            bx = (i + 5) // 4 - 1
            part = dot(tmp3[:, bx].reshape(48, 128), mat).reshape(2, 24, 128)
            x2[:, i] = x2[:, i] + part
    for low in range(2):
        mat = select_matrix(lambda r, k: r == low * 64 + k // 2, 1.0)
        part = dot(x2[:, 2:8].reshape(2 * 6 * 24, 128), mat).reshape(2, 6, 24, 128)
        for i in range(6):
            piece = part[:, i, 4:20, :]
            tmp2[:, 2 * i + low, pl.ds(0, 16, 2), :] = piece
            tmp2[:, 2 * i + low, pl.ds(1, 16, 2), :] = piece


def coarse_kernel(gx_n, gy_n, build, table, r3_a, r3_b, r3f_a, r3f_b, *refs):
    pos = position()
    core = pos[0]
    *weights3, inv3, fx4, fy4, fz4, inv4 = refs[:11]
    if build:
        sum3, a3, b3, e3, d3, o3, c3, x4 = refs[11:]
        for c in range(2):
            a3[c, 0] = jnp.zeros((24, 128), F32)
            a3[c, 6] = jnp.zeros((24, 128), F32)
        for c, src in ((core, r3_a), (1 - core, r3_b)):
            window3(src, a3, 0, 2, c, pos, gx_n, gy_n, 1)
            window3(src, b3, 1, 2, c, pos, gx_n, gy_n, 0)
        a4 = build4(r3f_a, 4, 0, core, gx_n, gy_n) + build4(r3f_b, 4, 0, 1 - core, gx_n, gy_n)
        b4 = build4(r3f_a, 4, 1, core, gx_n, gy_n) + build4(r3f_b, 4, 1, 1 - core, gx_n, gy_n)
        faces4(a4, fx4, fy4, fz4, inv4)
        faces(3, a3, weights3, inv3, None)
    else:
        sum3, b3, e3, d3, o3, c3, x4 = refs[11:]
        window3(r3_a, b3, 0, 1, core, pos, gx_n, gy_n, 0)
        window3(r3_b, b3, 0, 1, 1 - core, pos, gx_n, gy_n, 0)
        b4 = build4(r3f_a, 2, 0, core, gx_n, gy_n) + build4(r3f_b, 2, 0, 1 - core, gx_n, gy_n)
    x4[...] = smooth4(table, b4, fx4, fy4, fz4, inv4)
    smooth(3, b3, weights3, inv3, e3, d3, o3, c3)
    add_coarsest(pos, gx_n, gy_n, x4, c3, sum3)


def first_kernel(*refs):
    core, gx, gy = position()
    halves = ((core, refs[:5]), (1 - core, refs[5:10]))
    sum3 = refs[10]
    weights1, inv1, diag1 = refs[11:17], refs[17], refs[18]
    weights2, inv2 = refs[19:25], refs[25]
    x1, right, own, first, second, slots = refs[26:32]
    a1, b1, e1, d1, o1, a2, b2, e2, d2, o2, c2, tmp3, tmp2, rest = refs[32:]
    even_x, even_y = is_even(gx), is_even(gy)
    for c in range(2):
        a2[c, 0] = jnp.zeros((24, 128), F32)
        a2[c, 11] = jnp.zeros((24, 128), F32)
    for c, parts in halves:
        spread(2, 0, c, even_x, even_y, *parts, a1, a2, 1)
        spread(2, 1, c, even_x, even_y, *parts, b1, b2, 0)
    faces(1, a1, weights1, inv1, diag1)
    faces(2, a2, weights2, inv2, None)
    smooth(2, b2, weights2, inv2, e2, d2, o2, c2)
    smooth(1, b1, weights1, inv1, e1, d1, o1, x1)
    combine(sum3, c2, tmp3, tmp2)

    def finish(i, _):
        x1[:, i] = DAMPING * (x1[:, i] + tmp2[:, i // 2 - 1])
        return 0

    lax.fori_loop(5, 23, finish, 0)

    def residual(i):
        mid, near = weighted(1, i, 2, x1, weights1)
        at = pl.ds(i, 2)
        bv = b1[:, at]
        right[:, pl.ds(i - 6, 2)] = bv[:, :, 8:24, :]
        res = bv - diag1[:, at] * (mid - near)
        rest[:, pl.ds(i - 6, 2)] = res[:, :, 8:24, :]

    blocks(6, 22, 2, residual)
    for c in range(2):
        for t in range(2):
            own[c, pl.ds(t, 16, 2)] = rest[c, :, t * 8:t * 8 + 8, :]

        def read_pair(k):
            total = None
            for x in (2 * k, 2 * k + 1):
                part = rest[c, x, pl.ds(0, 8, 2), :] + rest[c, x, pl.ds(1, 8, 2), :]
                total = part if total is None else total + part
            return total

        def out(k, value):
            own[c, 32 + k] = value

        restrict_to2(read_pair, out)
    for i in range(12):
        put_pair(even_x, first, second, i, own[core, 20 + i], own[core, i])
    for i in range(3):
        put_pair(even_x, first, second, 12 + i, own[core, 33 + i], own[core, 32 + i])
    slots[0] = restrict_to3(
        lambda k: own[core, 32 + k, pl.ds(0, 4, 2), :] + own[core, 32 + k, pl.ds(1, 4, 2), :]
    )
    slots[1:] = jnp.broadcast_to(slots[0:1], (slots.shape[0] - 1, 4, 128))


def second_kernel(*refs):
    core, gx, gy = position()
    own, mine, theirs, sum3 = refs[0], refs[1:5], refs[5:9], refs[9]
    weights1, inv1, diag1 = refs[10:16], refs[16], refs[17]
    weights2, inv2 = refs[18:24], refs[24]
    x1, right, out_x, out_r = refs[25:29]
    b1, e1, d1, o1, c1, b2, e2, d2, o2, c2, tmp3, tmp2, rest = refs[29:]
    even_x, even_y = is_even(gx), is_even(gy)
    for c, parts in ((core, mine), (1 - core, theirs)):
        spread(1, 0, c, even_x, even_y, own.at[c], *parts, b1, b2, 0)
    smooth(2, b2, weights2, inv2, e2, d2, o2, c2)
    smooth(1, b1, weights1, inv1, e1, d1, o1, c1)
    combine(sum3, c2, tmp3, tmp2)

    def finish(i, _):
        c1[:, i] = x1[:, i] + DAMPING * (c1[:, i] + tmp2[:, i // 2 - 1])
        return 0

    lax.fori_loop(5, 23, finish, 0)

    def residual(i):
        mid, near = weighted(1, i, 2, c1, weights1)
        res = diag1[:, pl.ds(i, 2)] * (mid - near)
        at = pl.ds(i - 6, 2)
        rest[:, at] = right[:, at] - res[:, :, 8:24, :]

    blocks(6, 22, 2, residual)
    out_r[...] = rest[core]
    out_x[...] = c1[core, 6:22, 8:24, :]


def call(name, kernel, outs, scratch, *args):
    smem = pl.BlockSpec(memory_space=pltpu.SMEM)
    vmem = pl.BlockSpec(memory_space=pltpu.VMEM)
    return pl.pallas_call(
        kernel,
        out_shape=[jax.ShapeDtypeStruct(s, F32) for s in outs],
        in_specs=[smem if a.shape[-1] != 128 else vmem for a in args],
        out_specs=[vmem for _ in outs],
        scratch_shapes=[pltpu.VMEM(s, F32) for s in scratch],
        compiler_params=pltpu.CompilerParams(vmem_limit_bytes=56 * 1024 * 1024),
        interpret=INTERPRET,
        name=name,
    )(*args)


def trade(first, second, axis):
    size = lax.axis_size(axis)
    pairs = [(i, i ^ 1) for i in range(size)]
    others = [(i, i - 1 if i % 2 == 0 else i + 1) for i in range(1, size - 1)]
    return lax.ppermute(first, axis, pairs), lax.ppermute(second, axis, others)


def swap(x):
    return lax.ppermute(x, "grp", [(0, 1), (1, 0)])


def everywhere(slots):
    return lax.all_to_all(slots, ("gx", "gy"), 0, 0, tiled=True)


def on_device(right_side, coefficient):
    gx_n, gy_n = lax.axis_size("gx"), lax.axis_size("gy")
    count = gx_n * gy_n
    _, keeps, pushes = cheb_steps(COARSE_DEGREE, LOW_COARSE, HIGH_BOUND)
    table = jnp.array([keeps, pushes], F32)
    s1, s2, s3 = (2, 28, 32, 128), (2, 10, 24, 128), (2, 5, 24, 128)
    p2, p3 = (2, 12, 24, 128), (2, 7, 24, 128)
    s4 = (gx_n // 2, gy_n * 2, 128)
    sum3 = (2, 3, 24, 128)
    tmps = [sum3, (2, 12, 32, 128), (2, 16, 16, 128)]

    own, first, second, slots = call(
        "prepare", prepare_kernel,
        [(72, 8, 128), (30, 8, 128), (30, 8, 128), (count, 8, 128)], [], coefficient, right_side,
    )
    own_o = swap(own)
    x_one, x_two = trade(first, second, "gx")
    r3 = everywhere(slots)
    x_one_o, x_two_o = swap(x_one), swap(x_two)
    r3_o = swap(r3)
    first, second = call(
        "sides_a", functools.partial(sides_kernel, 2), [(76, 8, 128)] * 2, [], own, x_one, x_two
    )
    y_one, y_two = trade(first, second, "gy")
    flat = (count * 8, 128)
    *coarse, c3 = call(
        "coarse_a", functools.partial(coarse_kernel, gx_n, gy_n, True),
        [s3] * 7 + [s4] * 4 + [sum3], [p3, s3, s3, s3, s3, s3, s4],
        table, r3, r3_o, r3.reshape(flat), r3_o.reshape(flat),
    )
    y_one_o, y_two_o = swap(y_one), swap(y_two)
    outs = [s1] * 8 + [s2] * 7
    outs += [s1, (2, 16, 16, 128), (2, 36, 8, 128), (15, 8, 128), (15, 8, 128), (count, 4, 128)]
    *coefs, x1, right, own, first, second, slots = call(
        "fine_a", first_kernel, outs,
        [s1, s1, s1, s1, s1, p2, s2, s2, s2, s2, s2] + tmps,
        own, x_one, x_two, y_one, y_two, own_o, x_one_o, x_two_o, y_one_o, y_two_o, c3,
    )
    x_one, x_two = trade(first, second, "gx")
    r3 = everywhere(slots)
    x_one_o, x_two_o = swap(x_one), swap(x_two)
    r3_o = swap(r3)
    first, second = call(
        "sides_b", functools.partial(sides_kernel, 1), [(38, 8, 128)] * 2, [], own, x_one, x_two
    )
    y_one, y_two = trade(first, second, "gy")
    flat = (count * 4, 128)
    (c3,) = call(
        "coarse_b", functools.partial(coarse_kernel, gx_n, gy_n, False),
        [sum3], [s3, s3, s3, s3, s3, s4],
        table, r3, r3_o, r3.reshape(flat), r3_o.reshape(flat), *coarse,
    )
    y_one_o, y_two_o = swap(y_one), swap(y_two)
    solution_field, residual = call(
        "fine_b", second_kernel, [(16, 16, 128)] * 2,
        [s1, s1, s1, s1, s1, s2, s2, s2, s2, s2] + tmps,
        own, x_one, x_two, y_one, y_two, x_one_o, x_two_o, y_one_o, y_two_o, c3,
        *coefs, x1, right,
    )
    return solution_field, residual


def solution(mesh):
    placed = P("gx", "gy", "grp")
    return jax.shard_map(
        on_device, mesh=mesh, in_specs=(placed, placed), out_specs=(placed, placed),
        check_vma=False,
    )
```

time: 165 us -> 136 us (0.82)
  Pallas kernels: 69.8 us -> 49.2 us
  starting transfers between devices: 65.9 us -> 52.8 us
  waiting for transfers between devices: 19.7 us -> 26.6 us
  local copies, waits for them, and re-layouts: 6.16 us -> 4.41 us
    pallas_call x5 -> x7, Pallas kernels: 69.8 us -> 49.2 us  [call(): pl.pallas_call(kernel, out_shape=[jax.ShapeDtypeStruct(s, F32) for s in o...]
    all_to_all x2, waiting for transfers between devices: 0.01 us -> 11.6 us  [everywhere(): return lax.all_to_all(slots, ('gx', 'gy'), 0, 0, tiled=True)]
    ppermute x8, starting transfers between devices: 26.3 us -> 19.3 us  [the longest x4 16.3 us: trade(): lax.ppermute(second, axis, others)]
    all_to_all x2, starting transfers between devices: 25.7 us -> 22 us  [everywhere(): return lax.all_to_all(slots, ('gx', 'gy'), 0, 0, tiled=True)]
    ppermute x11, waiting for transfers between devices: 3.07 us -> 0.03 us  [swap(): return lax.ppermute(x, 'grp', [(0, 1), (1, 0)])]
    broadcast_in_dim x2 -> x0, local copies, waits for them, and re-layouts: 2.94 us -> none  [everywhere(): copies = jnp.broadcast_to(slot[None], (gx_n * gy_n,) + slot.shape)]
    ppermute x11, starting transfers between devices: 13.8 us -> 11.5 us  [swap(): return lax.ppermute(x, 'grp', [(0, 1), (1, 0)])]
    unnamed x52, local copies, waits for them, and re-layouts: 2.7 us -> 4.41 us
  transfers between devices with their start and end apart: 21 -> 21, of which waited for: 8 -> 5; matrix products, arithmetic and copies ran while one was open for 1% -> 0% of each run, Pallas kernels for 2% -> 11%
where the time goes in v2:
time: 136 us; the launch traced here: 134 us
  starting transfers between devices  52.8 us (39%)
  Pallas kernels  49.2 us (36%)
  waiting for transfers between devices  26.6 us (20%)
  local copies, waits for them, and re-layouts  4.41 us (3%)
    pallas_call x7, Pallas kernels, call(): pl.pallas_call(kernel, out_shape=[jax.ShapeDtypeStruct(s, F32) for s in o...  49.2 us
    all_to_all x2, starting transfers between devices, everywhere(): return lax.all_to_all(slots, ('gx', 'gy'), 0, 0, tiled=True)  22 us
    ppermute x4, starting transfers between devices, trade(): lax.ppermute(second, axis, others)  16.3 us
    all_to_all x2, waiting for transfers between devices, everywhere(): return lax.all_to_all(slots, ('gx', 'gy'), 0, 0, tiled=True)  11.6 us
    ppermute x11, starting transfers between devices, swap(): return lax.ppermute(x, 'grp', [(0, 1), (1, 0)])  11.5 us
    ppermute x4, waiting for transfers between devices, trade(): lax.ppermute(second, axis, others)  9.42 us
    ppermute x4, waiting for transfers between devices, trade(): lax.ppermute(first, axis, pairs)  5.53 us
    unnamed x52, local copies, waits for them, and re-layouts  4.41 us
  transfers between devices with their start and end apart: 21, of which 5 were waited for; matrix products, arithmetic and copies ran while one was open for 0% of the time, Pallas kernels for 11%

profile of v2, /device:TPU:27, one launch (start us, length us, event | category | flops | bytes accessed | tf_op | source)
XLA Modules:
  0.0 134.1 jit_solution(4471961559397637947)
XLA Ops:
  0.6 2.4 %prepare.1 = (f32[72,8,128]{2,1,0:T(8,128)}, f32[30,8,128]{2,1,0:T(8,128)}, f32[30,8,128]{2,1,0:T(8,128)}, f32[128,8,128]{2,1,0:T(8,128)}) custom-call(f32[16,16,128]{2,1,0:T(8,128)} %a.1, f32[16,16,128]{2,1,0:T(8,128)} %b.1), custom_call_target="tpu_custom_call" | custom-call | tf_op jit(solution)/shard_map/prepare/pallas_call | solution.py:549
  3.0 14.9 %all-to-all-start = ((f32[128,8,128]{2,1,0:T(8,128)}), f32[128,8,128]{2,1,0:T(8,128)S(1)}, u32[]{:S(2)}, u32[]{:S(2)}) async-start(f32[128,8,128]{2,1,0:T(8,128)} %get-tuple-element.48), calls=%async_computation | async-start | bytes 1048576 | tf_op jit(solution)/shard_map/all_to_all | solution.py:573
  18.5 4.6 %collective-permute-start.1 = (f32[30,8,128]{2,1,0:T(8,128)S(1)}, f32[30,8,128]{2,1,0:T(8,128)S(1)}, u32[]{:S(2)}, u32[]{:S(2)}) collective-permute-start(f32[30,8,128]{2,1,0:T(8,128)S(1)} %copy-done.22), channel_id=1, source_target_pairs={{16,32},{32,16},{48,64},{64,48},{80,96},{96,80},{17,33},{33,17},{4... | collective-permute-start | bytes 368648 | tf_op jit(solution)/shard_map/ppermute | solution.py:565
  23.1 11.6 %all-to-all-done.r3_a = f32[128,8,128]{2,1,0:T(8,128)S(1)} async-done(((f32[128,8,128]{2,1,0:T(8,128)}), f32[128,8,128]{2,1,0:T(8,128)S(1)}, u32[]{:S(2)}, u32[]{:S(2)}) %all-to-all-start) | async-done | bytes 524320 | tf_op jit(solution)/shard_map/all_to_all | solution.py:573
  34.7 2.5 %collective-permute-start.9 = (f32[128,8,128]{2,1,0:T(8,128)S(1)}, f32[128,8,128]{2,1,0:T(8,128)S(1)}, u32[]{:S(2)}, u32[]{:S(2)}) collective-permute-start(f32[128,8,128]{2,1,0:T(8,128)S(1)} %all-to-all-done.r3_a), channel_id=1, source_target_pairs={{0,128},{128,0},{1,129},{129,1},{2,130},{130,2},{3,131},{131,3},{4... | collective-permute-start | bytes 1572872 | tf_op jit(solution)/shard_map/ppermute | solution.py:569
  37.9 2.0 %sides_a.1 = (f32[76,8,128]{2,1,0:T(8,128)}, f32[76,8,128]{2,1,0:T(8,128)}) custom-call(f32[72,8,128]{2,1,0:T(8,128)} %get-tuple-element.43.own.refs_0_, f32[30,8,128]{2,1,0:T(8,128)} %copy-done.5, f32[30,8,128]{2,1,0:T(8,128)} %copy-done.6), custom_call_target="tpu_custom_call" | custom-call | tf_op jit(solution)/shard_map/sides_a/pallas_call | solution.py:549
  40.6 2.8 %collective-permute-start.3 = (f32[76,8,128]{2,1,0:T(8,128)}, f32[76,8,128]{2,1,0:T(8,128)S(1)}, u32[]{:S(2)}, u32[]{:S(2)}) collective-permute-start(f32[76,8,128]{2,1,0:T(8,128)} %get-tuple-element.47), channel_id=1, source_target_pairs={{1,2},{2,1},{3,4},{4,3},{5,6},{6,5},{7,8},{8,7},{9,10},{10,9},{11,... | collective-permute-start | bytes 933896 | tf_op jit(solution)/shard_map/ppermute | solution.py:565
  43.4 5.5 %collective-permute-done.2.refs_3_ = f32[76,8,128]{2,1,0:T(8,128)S(1)} collective-permute-done((f32[76,8,128]{2,1,0:T(8,128)}, f32[76,8,128]{2,1,0:T(8,128)S(1)}, u32[]{:S(2)}, u32[]{:S(2)}) %collective-permute-start.2) | collective-permute-done | bytes 311328 | tf_op jit(solution)/shard_map/ppermute | solution.py:565
  48.9 0.9 collective-permute-start.7
  49.9 3.6 %collective-permute-done.3.refs_4_ = f32[76,8,128]{2,1,0:T(8,128)S(1)} collective-permute-done((f32[76,8,128]{2,1,0:T(8,128)}, f32[76,8,128]{2,1,0:T(8,128)S(1)}, u32[]{:S(2)}, u32[]{:S(2)}) %collective-permute-start.3) | collective-permute-done | bytes 311328 | tf_op jit(solution)/shard_map/ppermute | solution.py:565
  53.4 1.2 collective-permute-start.8
  55.9 5.9 %coarse_a.1 = (f32[2,5,24,128]{3,2,1,0:T(8,128)}, f32[2,5,24,128]{3,2,1,0:T(8,128)}, f32[2,5,24,128]{3,2,1,0:T(8,128)}, f32[2,5,24,128]{3,2,1,0:T(8,128)}, f32[2...) custom-call(f32[2,15]{1,0:T(2,128)} %constant.2.clone.table, ...), custom_call_target="tpu_custom_call" | custom-call | tf_op jit(solution)/shard_map/coarse_a/pallas_call | solution.py:549
  62.8 17.5 %fine_a.1 = (f32[2,28,32,128]{3,2,1,0:T(8,128)}, f32[2,28,32,128]{3,2,1,0:T(8,128)}, f32[2,28,32,128]{3,2,1,0:T(8,128)}, f32[2,28,32,128]{3,2,1,0:T(8,128)}, f32...) custom-call(f32[72,8,128]{2,1,0:T(8,128)} %get-tuple-element.43.own., ...), custom_call_target="tpu_custom_call" | custom-call | tf_op jit(solution)/shard_map/fine_a/pallas_call | solution.py:549
  80.4 7.1 %all-to-all-start.1 = ((f32[128,4,128]{2,1,0:T(4,128)}), f32[128,4,128]{2,1,0:T(4,128)S(1)}, u32[]{:S(2)}, u32[]{:S(2)}) async-start(f32[128,4,128]{2,1,0:T(4,128)} %get-tuple-element.55), calls=%async_computation.1 | async-start | bytes 524288 | tf_op jit(solution)/shard_map/all_to_all | solution.py:573
  88.1 4.6 %collective-permute-start.11 = (f32[15,8,128]{2,1,0:T(8,128)S(1)}, f32[15,8,128]{2,1,0:T(8,128)S(1)}, u32[]{:S(2)}, u32[]{:S(2)}) collective-permute-start(f32[15,8,128]{2,1,0:T(8,128)S(1)} %copy-done.24), channel_id=1, source_target_pairs={{16,32},{32,16},{48,64},{64,48},{80,96},{96,80},{17,33},{33,17},{4... | collective-permute-start | bytes 184328 | tf_op jit(solution)/shard_map/ppermute | solution.py:565
  92.7 4.4 %collective-permute-done.11.two.refs_2_ = f32[15,8,128]{2,1,0:T(8,128)S(1)} collective-permute-done((f32[15,8,128]{2,1,0:T(8,128)S(1)}, f32[15,8,128]{2,1,0:T(8,128)S(1)}, u32[]{:S(2)}, u32[]{:S(2)}) %collective-permute-start.11) | collective-permute-done | bytes 61472 | tf_op jit(solution)/shard_map/ppermute | solution.py:565
  97.7 1.7 %sides_b.1 = (f32[38,8,128]{2,1,0:T(8,128)}, f32[38,8,128]{2,1,0:T(8,128)}) custom-call(f32[2,36,8,128]{3,2,1,0:T(8,128)} %get-tuple-element.50.own.refs_0_, f32[15,8,128]{2,1,0:T(8,128)} %copy-done.12, f32[15,8,128]{2,1,0:T(8,128)} %copy-done.13), custom_call_target="tpu_custom_call" | custom-call | tf_op jit(solution)/shard_map/sides_b/pallas_call | solution.py:549
  99.5 1.1 collective-permute-start.12
  100.6 4.3 %collective-permute-start.13 = (f32[38,8,128]{2,1,0:T(8,128)}, f32[38,8,128]{2,1,0:T(8,128)S(1)}, u32[]{:S(2)}, u32[]{:S(2)}) collective-permute-start(f32[38,8,128]{2,1,0:T(8,128)} %get-tuple-element.54), channel_id=1, source_target_pairs={{1,2},{2,1},{3,4},{4,3},{5,6},{6,5},{7,8},{8,7},{9,10},{10,9},{11,... | collective-permute-start | bytes 466952 | tf_op jit(solution)/shard_map/ppermute | solution.py:565
  104.9 2.4 %collective-permute-start.18 = (f32[128,4,128]{2,1,0:T(4,128)S(1)}, f32[128,4,128]{2,1,0:T(4,128)S(1)}, u32[]{:S(2)}, u32[]{:S(2)}) collective-permute-start(f32[128,4,128]{2,1,0:T(4,128)S(1)} %all-to-all-done.1.r3_a), channel_id=1, source_target_pairs={{0,128},{128,0},{1,129},{129,1},{2,130},{130,2},{3,131},{131,3},{4... | collective-permute-start | bytes 786440 | tf_op jit(solution)/shard_map/ppermute | solution.py:569
  107.4 1.5 %collective-permute-done.13.refs_4_ = f32[38,8,128]{2,1,0:T(8,128)S(1)} collective-permute-done((f32[38,8,128]{2,1,0:T(8,128)}, f32[38,8,128]{2,1,0:T(8,128)S(1)}, u32[]{:S(2)}, u32[]{:S(2)}) %collective-permute-start.13) | collective-permute-done | bytes 155680 | tf_op jit(solution)/shard_map/ppermute | solution.py:565
  108.9 3.2 %collective-permute-start.17 = (f32[38,8,128]{2,1,0:T(8,128)S(1)}, f32[38,8,128]{2,1,0:T(8,128)S(1)}, u32[]{:S(2)}, u32[]{:S(2)}) collective-permute-start(f32[38,8,128]{2,1,0:T(8,128)S(1)} %collective-permute-done.13.refs_4_), channel_id=1, source_target_pairs={{0,128},{128,0},{1,129},{129,1},{2,130},{130,2},{3,131},{131,3},{4... | collective-permute-start | bytes 466952 | tf_op jit(solution)/shard_map/ppermute | solution.py:569
  113.4 5.6 %coarse_b.1.refs_9_ = f32[2,3,24,128]{3,2,1,0:T(8,128)} custom-call(f32[2,15]{1,0:T(2,128)} %constant.2.clone.table, f32[128,4,128]{2,1,0:T(4,128)} %copy-done.1, f32[128,4,128]{2,1,0:T(4,128)} %copy-done.4, f32[512,128]{1,0:T(8,128)} %bitcast.5, f32[512,128]{1,0:T(8,128)} %bitcast.7, f32[2,5,24,128]{3,2,1,0:T(8,128)} %get-tuple-element.56.refs_0_, ...), custom_call_target="tpu_custom_call" | custom-call | tf_op jit(solution)/shard_map/coarse_b/pallas_call | solution.py:549
  119.8 14.1 %fine_b.1 = (f32[16,16,128]{2,1,0:T(8,128)}, f32[16,16,128]{2,1,0:T(8,128)}) custom-call(f32[2,36,8,128]{3,2,1,0:T(8,128)} %get-tuple-element.50.own.refs_0_, f32[15,8,128]{2,1,0:T(8,128)} %copy-done.12, f32[15,8,128]{2,1,0:T(8,128)} %copy-done.13, f32[38,8,128]{2,1,0:T(8,128)} %copy-done.14, f32[38,8,128]{2,1,0:T(8,128)} %copy-done.15, ...), custom_call_target="tpu_custom_call" | custom-call | tf_op jit(solution)/shard_map/fine_b/pallas_call | solution.py:549
  (77 shorter events, 7.6 us)
Async XLA Ops:
  3.0 15.5 %copy-start.22 = (f32[30,8,128]{2,1,0:T(8,128)S(1)}, f32[30,8,128]{2,1,0:T(8,128)}, u32[]{:S(2)}) copy-start(f32[30,8,128]{2,1,0:T(8,128)} %get-tuple-element.45) | copy-start | bytes 368644
  3.0 31.7 %all-to-all-start = ((f32[128,8,128]{2,1,0:T(8,128)}), f32[128,8,128]{2,1,0:T(8,128)S(1)}, u32[]{:S(2)}, u32[]{:S(2)}) async-start(f32[128,8,128]{2,1,0:T(8,128)} %get-tuple-element.48), calls=%async_computation | async-start | bytes 1048576 | tf_op jit(solution)/shard_map/all_to_all | solution.py:573
  17.9 36.7 %copy-start.3 = (f32[72,8,128]{2,1,0:T(8,128)S(1)}, f32[72,8,128]{2,1,0:T(8,128)}, u32[]{:S(2)}) copy-start(f32[72,8,128]{2,1,0:T(8,128)} %get-tuple-element.43.own.refs_0_) | copy-start | bytes 884740
  17.9 19.3 %collective-permute-start = (f32[30,8,128]{2,1,0:T(8,128)S(1)}, f32[30,8,128]{2,1,0:T(8,128)S(1)}, u32[]{:S(2)}, u32[]{:S(2)}) collective-permute-start(f32[30,8,128]{2,1,0:T(8,128)S(1)} %copy-done.23), channel_id=1, source_target_pairs={{0,16},{16,0},{32,48},{48,32},{64,80},{80,64},{96,112},{112,96},{1... | collective-permute-start | bytes 368648 | tf_op jit(solution)/shard_map/ppermute | solution.py:565
  18.5 18.7 %collective-permute-start.1 = (f32[30,8,128]{2,1,0:T(8,128)S(1)}, f32[30,8,128]{2,1,0:T(8,128)S(1)}, u32[]{:S(2)}, u32[]{:S(2)}) collective-permute-start(f32[30,8,128]{2,1,0:T(8,128)S(1)} %copy-done.22), channel_id=1, source_target_pairs={{16,32},{32,16},{48,64},{64,48},{80,96},{96,80},{17,33},{33,17},{4... | collective-permute-start | bytes 368648 | tf_op jit(solution)/shard_map/ppermute | solution.py:565
  34.7 20.5 %copy-start = (f32[128,8,128]{2,1,0:T(8,128)}, f32[128,8,128]{2,1,0:T(8,128)S(1)}, u32[]{:S(2)}) copy-start(f32[128,8,128]{2,1,0:T(8,128)S(1)} %all-to-all-done.r3_a) | copy-start | bytes 1572868
  34.7 20.4 %collective-permute-start.9 = (f32[128,8,128]{2,1,0:T(8,128)S(1)}, f32[128,8,128]{2,1,0:T(8,128)S(1)}, u32[]{:S(2)}, u32[]{:S(2)}) collective-permute-start(f32[128,8,128]{2,1,0:T(8,128)S(1)} %all-to-all-done.r3_a), channel_id=1, source_target_pairs={{0,128},{128,0},{1,129},{129,1},{2,130},{130,2},{3,131},{131,3},{4... | collective-permute-start | bytes 1572872 | tf_op jit(solution)/shard_map/ppermute | solution.py:569
  39.9 9.1 %collective-permute-start.2 = (f32[76,8,128]{2,1,0:T(8,128)}, f32[76,8,128]{2,1,0:T(8,128)S(1)}, u32[]{:S(2)}, u32[]{:S(2)}) collective-permute-start(f32[76,8,128]{2,1,0:T(8,128)} %get-tuple-element.46), channel_id=1, source_target_pairs={{0,1},{1,0},{2,3},{3,2},{4,5},{5,4},{6,7},{7,6},{8,9},{9,8},{10,11... | collective-permute-start | bytes 933896 | tf_op jit(solution)/shard_map/ppermute | solution.py:565
  40.6 12.8 %collective-permute-start.3 = (f32[76,8,128]{2,1,0:T(8,128)}, f32[76,8,128]{2,1,0:T(8,128)S(1)}, u32[]{:S(2)}, u32[]{:S(2)}) collective-permute-start(f32[76,8,128]{2,1,0:T(8,128)} %get-tuple-element.47), channel_id=1, source_target_pairs={{1,2},{2,1},{3,4},{4,3},{5,6},{6,5},{7,8},{8,7},{9,10},{10,9},{11,... | collective-permute-start | bytes 933896 | tf_op jit(solution)/shard_map/ppermute | solution.py:565
  48.9 12.9 %collective-permute-start.7 = (f32[76,8,128]{2,1,0:T(8,128)S(1)}, f32[76,8,128]{2,1,0:T(8,128)S(1)}, u32[]{:S(2)}, u32[]{:S(2)}) collective-permute-start(f32[76,8,128]{2,1,0:T(8,128)S(1)} %collective-permute-done.2.refs_3_), channel_id=1, source_target_pairs={{0,128},{128,0},{1,129},{129,1},{2,130},{130,2},{3,131},{131,3},{4... | collective-permute-start | bytes 933896 | tf_op jit(solution)/shard_map/ppermute | solution.py:569
  53.4 8.5 %collective-permute-start.8 = (f32[76,8,128]{2,1,0:T(8,128)S(1)}, f32[76,8,128]{2,1,0:T(8,128)S(1)}, u32[]{:S(2)}, u32[]{:S(2)}) collective-permute-start(f32[76,8,128]{2,1,0:T(8,128)S(1)} %collective-permute-done.3.refs_4_), channel_id=1, source_target_pairs={{0,128},{128,0},{1,129},{129,1},{2,130},{130,2},{3,131},{131,3},{4... | collective-permute-start | bytes 933896 | tf_op jit(solution)/shard_map/ppermute | solution.py:569
  54.6 7.2 %collective-permute-start.4 = (f32[72,8,128]{2,1,0:T(8,128)S(1)}, f32[72,8,128]{2,1,0:T(8,128)S(1)}, u32[]{:S(2)}, u32[]{:S(2)}) collective-permute-start(f32[72,8,128]{2,1,0:T(8,128)S(1)} %copy-done.3), channel_id=1, source_target_pairs={{0,128},{128,0},{1,129},{129,1},{2,130},{130,2},{3,131},{131,3},{4... | collective-permute-start | bytes 884744 | tf_op jit(solution)/shard_map/ppermute | solution.py:569
  54.7 7.1 %collective-permute-start.5 = (f32[30,8,128]{2,1,0:T(8,128)}, f32[30,8,128]{2,1,0:T(8,128)S(1)}, u32[]{:S(2)}, u32[]{:S(2)}) collective-permute-start(f32[30,8,128]{2,1,0:T(8,128)} %copy-done.5), channel_id=1, source_target_pairs={{0,128},{128,0},{1,129},{129,1},{2,130},{130,2},{3,131},{131,3},{4... | collective-permute-start | bytes 368648 | tf_op jit(solution)/shard_map/ppermute | solution.py:569
  55.1 6.7 %collective-permute-start.6 = (f32[30,8,128]{2,1,0:T(8,128)}, f32[30,8,128]{2,1,0:T(8,128)S(1)}, u32[]{:S(2)}, u32[]{:S(2)}) collective-permute-start(f32[30,8,128]{2,1,0:T(8,128)} %copy-done.6), channel_id=1, source_target_pairs={{0,128},{128,0},{1,129},{129,1},{2,130},{130,2},{3,131},{131,3},{4... | collective-permute-start | bytes 368648 | tf_op jit(solution)/shard_map/ppermute | solution.py:569
  80.4 24.5 %all-to-all-start.1 = ((f32[128,4,128]{2,1,0:T(4,128)}), f32[128,4,128]{2,1,0:T(4,128)S(1)}, u32[]{:S(2)}, u32[]{:S(2)}) async-start(f32[128,4,128]{2,1,0:T(4,128)} %get-tuple-element.55), calls=%async_computation.1 | async-start | bytes 524288 | tf_op jit(solution)/shard_map/all_to_all | solution.py:573
  87.5 5.2 %collective-permute-start.10 = (f32[15,8,128]{2,1,0:T(8,128)S(1)}, f32[15,8,128]{2,1,0:T(8,128)S(1)}, u32[]{:S(2)}, u32[]{:S(2)}) collective-permute-start(f32[15,8,128]{2,1,0:T(8,128)S(1)} %copy-done.25), channel_id=1, source_target_pairs={{0,16},{16,0},{32,48},{48,32},{64,80},{80,64},{96,112},{112,96},{1... | collective-permute-start | bytes 184328 | tf_op jit(solution)/shard_map/ppermute | solution.py:565
  88.1 9.0 %collective-permute-start.11 = (f32[15,8,128]{2,1,0:T(8,128)S(1)}, f32[15,8,128]{2,1,0:T(8,128)S(1)}, u32[]{:S(2)}, u32[]{:S(2)}) collective-permute-start(f32[15,8,128]{2,1,0:T(8,128)S(1)} %copy-done.24), channel_id=1, source_target_pairs={{16,32},{32,16},{48,64},{64,48},{80,96},{96,80},{17,33},{33,17},{4... | collective-permute-start | bytes 184328 | tf_op jit(solution)/shard_map/ppermute | solution.py:565
  99.5 7.9 %collective-permute-start.12 = (f32[38,8,128]{2,1,0:T(8,128)}, f32[38,8,128]{2,1,0:T(8,128)S(1)}, u32[]{:S(2)}, u32[]{:S(2)}) collective-permute-start(f32[38,8,128]{2,1,0:T(8,128)} %get-tuple-element.53), channel_id=1, source_target_pairs={{0,1},{1,0},{2,3},{3,2},{4,5},{5,4},{6,7},{7,6},{8,9},{9,8},{10,11... | collective-permute-start | bytes 466952 | tf_op jit(solution)/shard_map/ppermute | solution.py:565
  100.6 8.3 %collective-permute-start.13 = (f32[38,8,128]{2,1,0:T(8,128)}, f32[38,8,128]{2,1,0:T(8,128)S(1)}, u32[]{:S(2)}, u32[]{:S(2)}) collective-permute-start(f32[38,8,128]{2,1,0:T(8,128)} %get-tuple-element.54), channel_id=1, source_target_pairs={{1,2},{2,1},{3,4},{4,3},{5,6},{6,5},{7,8},{8,7},{9,10},{10,9},{11,... | collective-permute-start | bytes 466952 | tf_op jit(solution)/shard_map/ppermute | solution.py:565
  104.9 7.7 %collective-permute-start.18 = (f32[128,4,128]{2,1,0:T(4,128)S(1)}, f32[128,4,128]{2,1,0:T(4,128)S(1)}, u32[]{:S(2)}, u32[]{:S(2)}) collective-permute-start(f32[128,4,128]{2,1,0:T(4,128)S(1)} %all-to-all-done.1.r3_a), channel_id=1, source_target_pairs={{0,128},{128,0},{1,129},{129,1},{2,130},{130,2},{3,131},{131,3},{4... | collective-permute-start | bytes 786440 | tf_op jit(solution)/shard_map/ppermute | solution.py:569
  107.3 11.7 %collective-permute-start.16 = (f32[38,8,128]{2,1,0:T(8,128)S(1)}, f32[38,8,128]{2,1,0:T(8,128)S(1)}, u32[]{:S(2)}, u32[]{:S(2)}) collective-permute-start(f32[38,8,128]{2,1,0:T(8,128)S(1)} %collective-permute-done.12.refs_3_), channel_id=1, source_target_pairs={{0,128},{128,0},{1,129},{129,1},{2,130},{130,2},{3,131},{131,3},{4... | collective-permute-start | bytes 466952 | tf_op jit(solution)/shard_map/ppermute | solution.py:569
  108.9 10.2 %collective-permute-start.17 = (f32[38,8,128]{2,1,0:T(8,128)S(1)}, f32[38,8,128]{2,1,0:T(8,128)S(1)}, u32[]{:S(2)}, u32[]{:S(2)}) collective-permute-start(f32[38,8,128]{2,1,0:T(8,128)S(1)} %collective-permute-done.13.refs_4_), channel_id=1, source_target_pairs={{0,128},{128,0},{1,129},{129,1},{2,130},{130,2},{3,131},{131,3},{4... | collective-permute-start | bytes 466952 | tf_op jit(solution)/shard_map/ppermute | solution.py:569
  112.1 6.9 %collective-permute-start.14 = (f32[15,8,128]{2,1,0:T(8,128)}, f32[15,8,128]{2,1,0:T(8,128)S(1)}, u32[]{:S(2)}, u32[]{:S(2)}) collective-permute-start(f32[15,8,128]{2,1,0:T(8,128)} %copy-done.12), channel_id=1, source_target_pairs={{0,128},{128,0},{1,129},{129,1},{2,130},{130,2},{3,131},{131,3},{4... | collective-permute-start | bytes 184328 | tf_op jit(solution)/shard_map/ppermute | solution.py:569
  112.1 6.9 %collective-permute-start.15 = (f32[15,8,128]{2,1,0:T(8,128)}, f32[15,8,128]{2,1,0:T(8,128)S(1)}, u32[]{:S(2)}, u32[]{:S(2)}) collective-permute-start(f32[15,8,128]{2,1,0:T(8,128)} %copy-done.13), channel_id=1, source_target_pairs={{0,128},{128,0},{1,129},{129,1},{2,130},{130,2},{3,131},{131,3},{4... | collective-permute-start | bytes 184328 | tf_op jit(solution)/shard_map/ppermute | solution.py:569
  (23 other events, 95.0 us)

commit v3 on v2

--- a/solution.py
+++ b/solution.py
@@ -7,6 +7,7 @@
 from jax.experimental.pallas import tpu as pltpu
 from jax.sharding import PartitionSpec as P
 
+
 FINE_DEGREE = 5
 COARSE_DEGREE = 16
 LOW_FINE = 0.2
@@ -17,7 +18,6 @@
 F32 = jnp.float32
 INTERPRET = False
 LANES_X = {1: 1, 2: 2, 3: 4}
-ROWS = {1: 32, 2: 24, 3: 24}
 HELD = {1: (1, 27), 2: (0, 10), 3: (0, 5)}
 STEPS = {
     1: ((2, 26), (3, 25), (4, 24), (5, 23)),
@@ -36,7 +36,7 @@
     rho = 1.0 / sigma
     keeps = []
     pushes = []
-    for step in range(degree - 1):
+    for _ in range(degree - 1):
         rho_new = 1.0 / (2.0 * sigma - rho)
         keeps.append(rho_new * rho)
         pushes.append(2.0 * rho_new / delta)
@@ -155,6 +155,9 @@
         x[:, at] = ev * first
 
     blocks(*HELD[level], 5 if level == 3 else 2, start)
+    if level > 1:
+        for i in (HELD[level][0], HELD[level][1] - 1):
+            other[:, i] = jnp.zeros_like(other[:, i])
     for n in range(FINE_DEGREE - 1):
         src, dst = (d, other) if n % 2 == 0 else (other, d)
 
@@ -283,7 +286,6 @@
 
 def prepare_kernel(a, b, own, first, second, slots):
     even = is_even(position()[1])
-    slot = None
     for f, src in enumerate((a, b)):
         for t in range(2):
             own[pl.ds(f * 32 + t, 16, 2)] = src[:, t * 8:t * 8 + 8, :]
@@ -405,7 +407,7 @@
     return mul(high) + (mul(mid) + mul(low))
 
 
-def combine(sum3, x2, tmp3, tmp2):
+def combine(sum3, c2, x2, tmp3, tmp2):
     for c in range(2):
         for bx in range(3):
             tmp3[c, bx, pl.ds(0, 12, 2), :] = sum3[c, bx, 4:16, :]
@@ -415,17 +417,17 @@
         for i in [i for i in range(2, 8) if (i + 5) % 4 == low]:
             bx = (i + 5) // 4 - 1
             part = dot(tmp3[:, bx].reshape(48, 128), mat).reshape(2, 24, 128)
-            x2[:, i] = x2[:, i] + part
+            x2[:, i - 2] = c2[:, i] + part
     for low in range(2):
         mat = select_matrix(lambda r, k: r == low * 64 + k // 2, 1.0)
-        part = dot(x2[:, 2:8].reshape(2 * 6 * 24, 128), mat).reshape(2, 6, 24, 128)
+        part = dot(x2[...].reshape(2 * 6 * 24, 128), mat).reshape(2, 6, 24, 128)
         for i in range(6):
             piece = part[:, i, 4:20, :]
             tmp2[:, 2 * i + low, pl.ds(0, 16, 2), :] = piece
             tmp2[:, 2 * i + low, pl.ds(1, 16, 2), :] = piece
 
 
-def coarse_kernel(gx_n, gy_n, build, table, r3_a, r3_b, r3f_a, r3f_b, *refs):
+def coarse_kernel(gx_n, gy_n, build, table, _, r3_a, r3_b, r3f_a, r3f_b, *refs):
     pos = position()
     core = pos[0]
     *weights3, inv3, fx4, fy4, fz4, inv4 = refs[:11]
@@ -454,11 +456,10 @@
 def first_kernel(*refs):
     core, gx, gy = position()
     halves = ((core, refs[:5]), (1 - core, refs[5:10]))
-    sum3 = refs[10]
-    weights1, inv1, diag1 = refs[11:17], refs[17], refs[18]
-    weights2, inv2 = refs[19:25], refs[25]
-    x1, right, own, first, second, slots = refs[26:32]
-    a1, b1, e1, d1, o1, a2, b2, e2, d2, o2, c2, tmp3, tmp2, rest = refs[32:]
+    weights1, inv1, diag1 = refs[10:16], refs[16], refs[17]
+    weights2, inv2 = refs[18:24], refs[24]
+    c1, c2, right, token = refs[25:29]
+    a1, b1, e1, d1, o1, a2, b2, e2, d2, o2 = refs[29:]
     even_x, even_y = is_even(gx), is_even(gy)
     for c in range(2):
         a2[c, 0] = jnp.zeros((24, 128), F32)
@@ -469,22 +470,30 @@
     faces(1, a1, weights1, inv1, diag1)
     faces(2, a2, weights2, inv2, None)
     smooth(2, b2, weights2, inv2, e2, d2, o2, c2)
-    smooth(1, b1, weights1, inv1, e1, d1, o1, x1)
-    combine(sum3, c2, tmp3, tmp2)
+    smooth(1, b1, weights1, inv1, e1, d1, o1, c1)
+    right[...] = b1[:, 6:22, 8:24, :]
+    token[...] = jnp.zeros_like(token)
+
+
+def join_kernel(*refs):
+    core, gx, _ = position()
+    even_x = is_even(gx)
+    sum3, weights1, diag1, c1, c2, right = refs[0], refs[1:7], refs[7], refs[8], refs[9], refs[10]
+    x1, own, first, second, slots = refs[11:16]
+    s2, tmp3, tmp2, rest = refs[16:]
+    combine(sum3, c2, s2, tmp3, tmp2)
 
     def finish(i, _):
-        x1[:, i] = DAMPING * (x1[:, i] + tmp2[:, i // 2 - 1])
+        x1[:, i] = DAMPING * (c1[:, i] + tmp2[:, i // 2 - 1])
         return 0
 
     lax.fori_loop(5, 23, finish, 0)
 
     def residual(i):
         mid, near = weighted(1, i, 2, x1, weights1)
-        at = pl.ds(i, 2)
-        bv = b1[:, at]
-        right[:, pl.ds(i - 6, 2)] = bv[:, :, 8:24, :]
-        res = bv - diag1[:, at] * (mid - near)
-        rest[:, pl.ds(i - 6, 2)] = res[:, :, 8:24, :]
+        res = diag1[:, pl.ds(i, 2)] * (mid - near)
+        at = pl.ds(i - 6, 2)
+        rest[:, at] = right[:, at] - res[:, :, 8:24, :]
 
     blocks(6, 22, 2, residual)
     for c in range(2):
@@ -518,13 +527,13 @@
     weights1, inv1, diag1 = refs[10:16], refs[16], refs[17]
     weights2, inv2 = refs[18:24], refs[24]
     x1, right, out_x, out_r = refs[25:29]
-    b1, e1, d1, o1, c1, b2, e2, d2, o2, c2, tmp3, tmp2, rest = refs[29:]
+    b1, e1, d1, o1, c1, b2, e2, d2, o2, c2, s2, tmp3, tmp2, rest = refs[29:]
     even_x, even_y = is_even(gx), is_even(gy)
     for c, parts in ((core, mine), (1 - core, theirs)):
         spread(1, 0, c, even_x, even_y, own.at[c], *parts, b1, b2, 0)
     smooth(2, b2, weights2, inv2, e2, d2, o2, c2)
     smooth(1, b1, weights1, inv1, e1, d1, o1, c1)
-    combine(sum3, c2, tmp3, tmp2)
+    combine(sum3, c2, s2, tmp3, tmp2)
 
     def finish(i, _):
         c1[:, i] = x1[:, i] + DAMPING * (c1[:, i] + tmp2[:, i // 2 - 1])
@@ -543,7 +552,7 @@
     out_x[...] = c1[core, 6:22, 8:24, :]
 
 
-def call(name, kernel, outs, scratch, *args):
+def call(kernel, outs, scratch, *args):
     smem = pl.BlockSpec(memory_space=pltpu.SMEM)
     vmem = pl.BlockSpec(memory_space=pltpu.VMEM)
     return pl.pallas_call(
@@ -554,7 +563,6 @@
         scratch_shapes=[pltpu.VMEM(s, F32) for s in scratch],
         compiler_params=pltpu.CompilerParams(vmem_limit_bytes=56 * 1024 * 1024),
         interpret=INTERPRET,
-        name=name,
     )(*args)
 
 
@@ -562,7 +570,9 @@
     size = lax.axis_size(axis)
     pairs = [(i, i ^ 1) for i in range(size)]
     others = [(i, i - 1 if i % 2 == 0 else i + 1) for i in range(1, size - 1)]
-    return lax.ppermute(first, axis, pairs), lax.ppermute(second, axis, others)
+    one = lax.ppermute(first, axis, pairs)
+    two = lax.ppermute(second, axis, others)
+    return one, two
 
 
 def swap(x):
@@ -582,10 +592,10 @@
     p2, p3 = (2, 12, 24, 128), (2, 7, 24, 128)
     s4 = (gx_n // 2, gy_n * 2, 128)
     sum3 = (2, 3, 24, 128)
-    tmps = [sum3, (2, 12, 32, 128), (2, 16, 16, 128)]
+    tmps = [(2, 6, 24, 128), sum3, (2, 12, 32, 128), (2, 16, 16, 128)]
 
     own, first, second, slots = call(
-        "prepare", prepare_kernel,
+        prepare_kernel,
         [(72, 8, 128), (30, 8, 128), (30, 8, 128), (count, 8, 128)], [], coefficient, right_side,
     )
     own_o = swap(own)
@@ -594,40 +604,43 @@
     x_one_o, x_two_o = swap(x_one), swap(x_two)
     r3_o = swap(r3)
     first, second = call(
-        "sides_a", functools.partial(sides_kernel, 2), [(76, 8, 128)] * 2, [], own, x_one, x_two
+        functools.partial(sides_kernel, 2), [(76, 8, 128)] * 2, [], own, x_one, x_two
     )
     y_one, y_two = trade(first, second, "gy")
+    y_one_o, y_two_o = swap(y_one), swap(y_two)
+    *coefs, c1, c2, right, token = call(
+        first_kernel, [s1] * 8 + [s2] * 7 + [s1, s2, (2, 16, 16, 128), (8, 128)],
+        [s1, s1, s1, s1, s1, p2, s2, s2, s2, s2],
+        own, x_one, x_two, y_one, y_two, own_o, x_one_o, x_two_o, y_one_o, y_two_o,
+    )
     flat = (count * 8, 128)
     *coarse, c3 = call(
-        "coarse_a", functools.partial(coarse_kernel, gx_n, gy_n, True),
+        functools.partial(coarse_kernel, gx_n, gy_n, True),
         [s3] * 7 + [s4] * 4 + [sum3], [p3, s3, s3, s3, s3, s3, s4],
-        table, r3, r3_o, r3.reshape(flat), r3_o.reshape(flat),
-    )
-    y_one_o, y_two_o = swap(y_one), swap(y_two)
-    outs = [s1] * 8 + [s2] * 7
-    outs += [s1, (2, 16, 16, 128), (2, 36, 8, 128), (15, 8, 128), (15, 8, 128), (count, 4, 128)]
-    *coefs, x1, right, own, first, second, slots = call(
-        "fine_a", first_kernel, outs,
-        [s1, s1, s1, s1, s1, p2, s2, s2, s2, s2, s2] + tmps,
-        own, x_one, x_two, y_one, y_two, own_o, x_one_o, x_two_o, y_one_o, y_two_o, c3,
+        table, token, r3, r3_o, r3.reshape(flat), r3_o.reshape(flat),
+    )
+    x1, own, first, second, slots = call(
+        join_kernel,
+        [s1, (2, 36, 8, 128), (15, 8, 128), (15, 8, 128), (count, 4, 128)], tmps,
+        c3, *coefs[:6], coefs[7], c1, c2, right,
     )
     x_one, x_two = trade(first, second, "gx")
     r3 = everywhere(slots)
     x_one_o, x_two_o = swap(x_one), swap(x_two)
     r3_o = swap(r3)
     first, second = call(
-        "sides_b", functools.partial(sides_kernel, 1), [(38, 8, 128)] * 2, [], own, x_one, x_two
+        functools.partial(sides_kernel, 1), [(38, 8, 128)] * 2, [], own, x_one, x_two
     )
     y_one, y_two = trade(first, second, "gy")
     flat = (count * 4, 128)
     (c3,) = call(
-        "coarse_b", functools.partial(coarse_kernel, gx_n, gy_n, False),
+        functools.partial(coarse_kernel, gx_n, gy_n, False),
         [sum3], [s3, s3, s3, s3, s3, s4],
-        table, r3, r3_o, r3.reshape(flat), r3_o.reshape(flat), *coarse,
+        table, token, r3, r3_o, r3.reshape(flat), r3_o.reshape(flat), *coarse,
     )
     y_one_o, y_two_o = swap(y_one), swap(y_two)
     solution_field, residual = call(
-        "fine_b", second_kernel, [(16, 16, 128)] * 2,
+        second_kernel, [(16, 16, 128)] * 2,
         [s1, s1, s1, s1, s1, s2, s2, s2, s2, s2] + tmps,
         own, x_one, x_two, y_one, y_two, x_one_o, x_two_o, y_one_o, y_two_o, c3,
         *coefs, x1, right,
@@ -637,6 +650,7 @@
 
 def solution(mesh):
     placed = P("gx", "gy", "grp")
+
     return jax.shard_map(
         on_device, mesh=mesh, in_specs=(placed, placed), out_specs=(placed, placed),
         check_vma=False,

time: 136 us -> 139 us (1.022)
  waiting for transfers between devices: 26.6 us -> 15.9 us
  starting transfers between devices: 52.8 us -> 61.8 us
  Pallas kernels: 49.2 us -> 53.7 us
    all_to_all x2, waiting for transfers between devices: 11.6 us -> 0.01 us  [everywhere(): return lax.all_to_all(slots, ('gx', 'gy'), 0, 0, tiled=True)]
    pallas_call x7 -> x8, Pallas kernels: 49.2 us -> 53.7 us  [call(): pl.pallas_call(kernel, out_shape=[jax.ShapeDtypeStruct(s, F32) for s in o...]
    ppermute x11, starting transfers between devices: 11.5 us -> 15.1 us  [swap(): return lax.ppermute(x, 'grp', [(0, 1), (1, 0)])]
    all_to_all x2, starting transfers between devices: 22 us -> 24.8 us  [everywhere(): return lax.all_to_all(slots, ('gx', 'gy'), 0, 0, tiled=True)]
    ppermute x8, starting transfers between devices: 19.3 us -> 21.9 us  [the longest x4 18.1 us: trade(): two = lax.ppermute(second, axis, others)]
    ppermute x11, waiting for transfers between devices: 0.03 us -> 2.53 us  [swap(): return lax.ppermute(x, 'grp', [(0, 1), (1, 0)])]
    ppermute x8, waiting for transfers between devices: 14.9 us -> 13.4 us  [the longest x4 12.8 us: trade(): two = lax.ppermute(second, axis, others)]
  transfers between devices with their start and end apart: 21 -> 21, of which waited for: 5 -> 7; matrix products, arithmetic and copies ran while one was open for 0% -> 0% of each run, Pallas kernels for 11% -> 18%
where the time goes in v3:
time: 139 us; the launch traced here: 138 us
  starting transfers between devices  61.8 us (44%)
  Pallas kernels  53.7 us (39%)
  waiting for transfers between devices  15.9 us (11%)
  local copies, waits for them, and re-layouts  5.08 us (4%)
    pallas_call x8, Pallas kernels, call(): pl.pallas_call(kernel, out_shape=[jax.ShapeDtypeStruct(s, F32) for s in o...  53.7 us
    all_to_all x2, starting transfers between devices, everywhere(): return lax.all_to_all(slots, ('gx', 'gy'), 0, 0, tiled=True)  24.8 us
    ppermute x4, starting transfers between devices, trade(): two = lax.ppermute(second, axis, others)  18.1 us
    ppermute x11, starting transfers between devices, swap(): return lax.ppermute(x, 'grp', [(0, 1), (1, 0)])  15.1 us
    ppermute x4, waiting for transfers between devices, trade(): two = lax.ppermute(second, axis, others)  12.8 us
    unnamed x52, local copies, waits for them, and re-layouts  5.08 us
    ppermute x4, starting transfers between devices, trade(): one = lax.ppermute(first, axis, pairs)  3.82 us
  transfers between devices with their start and end apart: 21, of which 7 were waited for; matrix products, arithmetic and copies ran while one was open for 0% of the time, Pallas kernels for 18%

profile of v3, /device:TPU:27, one launch (start us, length us, event | category | flops | bytes accessed | tf_op | source)
XLA Modules:
  0.0 137.5 jit_solution(3679723774270252267)
XLA Ops:
  0.6 2.4 %shard_map.50 = (f32[72,8,128]{2,1,0:T(8,128)}, f32[30,8,128]{2,1,0:T(8,128)}, f32[30,8,128]{2,1,0:T(8,128)}, f32[128,8,128]{2,1,0:T(8,128)}) custom-call(f32[16,16,128]{2,1,0:T(8,128)} %a.1, f32[16,16,128]{2,1,0:T(8,128)} %b.1), custom_call_target="tpu_custom_call" | custom-call | tf_op jit(solution)/shard_map/pallas_call | solution.py:558
  3.0 14.9 %all-to-all-start = ((f32[128,8,128]{2,1,0:T(8,128)}), f32[128,8,128]{2,1,0:T(8,128)S(1)}, u32[]{:S(2)}, u32[]{:S(2)}) async-start(f32[128,8,128]{2,1,0:T(8,128)} %get-tuple-element.52), calls=%async_computation | async-start | bytes 1048576 | tf_op jit(solution)/shard_map/all_to_all | solution.py:583
  18.5 4.6 %collective-permute-start.1 = (f32[30,8,128]{2,1,0:T(8,128)S(1)}, f32[30,8,128]{2,1,0:T(8,128)S(1)}, u32[]{:S(2)}, u32[]{:S(2)}) collective-permute-start(f32[30,8,128]{2,1,0:T(8,128)S(1)} %copy-done.22), channel_id=1, source_target_pairs={{16,32},{32,16},{48,64},{64,48},{80,96},{96,80},{17,33},{33,17},{4... | collective-permute-start | bytes 368648 | tf_op jit(solution)/shard_map/ppermute | solution.py:574
  23.8 5.2 %collective-permute-done.1.two.refs_2_ = f32[30,8,128]{2,1,0:T(8,128)S(1)} collective-permute-done((f32[30,8,128]{2,1,0:T(8,128)S(1)}, f32[30,8,128]{2,1,0:T(8,128)S(1)}, u32[]{:S(2)}, u32[]{:S(2)}) %collective-permute-start.1) | collective-permute-done | bytes 122912 | tf_op jit(solution)/shard_map/ppermute | solution.py:574
  29.6 1.9 %shard_map.51 = (f32[76,8,128]{2,1,0:T(8,128)}, f32[76,8,128]{2,1,0:T(8,128)}) custom-call(f32[72,8,128]{2,1,0:T(8,128)} %get-tuple-element.46.own.refs_0_, f32[30,8,128]{2,1,0:T(8,128)} %copy-done.5, f32[30,8,128]{2,1,0:T(8,128)} %copy-done.6), custom_call_target="tpu_custom_call" | custom-call | tf_op jit(solution)/shard_map/pallas_call | solution.py:558
  31.6 1.6 %collective-permute-start.2 = (f32[76,8,128]{2,1,0:T(8,128)}, f32[76,8,128]{2,1,0:T(8,128)S(1)}, u32[]{:S(2)}, u32[]{:S(2)}) collective-permute-start(f32[76,8,128]{2,1,0:T(8,128)} %get-tuple-element.49), channel_id=1, source_target_pairs={{0,1},{1,0},{2,3},{3,2},{4,5},{5,4},{6,7},{7,6},{8,9},{9,8},{10,11... | collective-permute-start | bytes 933896 | tf_op jit(solution)/shard_map/ppermute | solution.py:573
  33.1 4.5 %collective-permute-start.3 = (f32[76,8,128]{2,1,0:T(8,128)}, f32[76,8,128]{2,1,0:T(8,128)S(1)}, u32[]{:S(2)}, u32[]{:S(2)}) collective-permute-start(f32[76,8,128]{2,1,0:T(8,128)} %get-tuple-element.50), channel_id=1, source_target_pairs={{1,2},{2,1},{3,4},{4,3},{5,6},{6,5},{7,8},{8,7},{9,10},{10,9},{11,... | collective-permute-start | bytes 933896 | tf_op jit(solution)/shard_map/ppermute | solution.py:574
  37.7 3.0 %collective-permute-start.9 = (f32[128,8,128]{2,1,0:T(8,128)S(1)}, f32[128,8,128]{2,1,0:T(8,128)S(1)}, u32[]{:S(2)}, u32[]{:S(2)}) collective-permute-start(f32[128,8,128]{2,1,0:T(8,128)S(1)} %all-to-all-done.r3_a), channel_id=1, source_target_pairs={{0,128},{128,0},{1,129},{129,1},{2,130},{130,2},{3,131},{131,3},{4... | collective-permute-start | bytes 1572872 | tf_op jit(solution)/shard_map/ppermute | solution.py:579
  41.7 2.0 %collective-permute-done.3.refs_4_ = f32[76,8,128]{2,1,0:T(8,128)S(1)} collective-permute-done((f32[76,8,128]{2,1,0:T(8,128)}, f32[76,8,128]{2,1,0:T(8,128)S(1)}, u32[]{:S(2)}, u32[]{:S(2)}) %collective-permute-start.3) | collective-permute-done | bytes 311328 | tf_op jit(solution)/shard_map/ppermute | solution.py:574
  43.6 3.5 %collective-permute-start.8 = (f32[76,8,128]{2,1,0:T(8,128)S(1)}, f32[76,8,128]{2,1,0:T(8,128)S(1)}, u32[]{:S(2)}, u32[]{:S(2)}) collective-permute-start(f32[76,8,128]{2,1,0:T(8,128)S(1)} %collective-permute-done.3.refs_4_), channel_id=1, source_target_pairs={{0,128},{128,0},{1,129},{129,1},{2,130},{130,2},{3,131},{131,3},{4... | collective-permute-start | bytes 933896 | tf_op jit(solution)/shard_map/ppermute | solution.py:579
  47.6 1.3 collective-permute-done.5.refs_6_
  49.3 1.2 collective-permute-done.6.refs_7_
  52.1 15.8 %shard_map.52 = (f32[2,28,32,128]{3,2,1,0:T(8,128)}, f32[2,28,32,128]{3,2,1,0:T(8,128)}, f32[2,28,32,128]{3,2,1,0:T(8,128)}, f32[2,28,32,128]{3,2,1,0:T(8,128)},...) custom-call(f32[72,8,128]{2,1,0:T(8,128)} %get-tuple-element.46.own., ...), custom_call_target="tpu_custom_call" | custom-call | tf_op jit(solution)/shard_map/pallas_call | solution.py:558
  68.7 5.9 %shard_map.53 = (f32[2,5,24,128]{3,2,1,0:T(8,128)}, f32[2,5,24,128]{3,2,1,0:T(8,128)}, f32[2,5,24,128]{3,2,1,0:T(8,128)}, f32[2,5,24,128]{3,2,1,0:T(8,128)}, f32...) custom-call(f32[2,15]{1,0:T(2,128)} %constant.2.clone.table, ...), custom_call_target="tpu_custom_call" | custom-call | tf_op jit(solution)/shard_map/pallas_call | solution.py:558
  74.6 6.1 %shard_map.54 = (f32[2,28,32,128]{3,2,1,0:T(8,128)}, f32[2,36,8,128]{3,2,1,0:T(8,128)}, f32[15,8,128]{2,1,0:T(8,128)}, f32[15,8,128]{2,1,0:T(8,128)}, f32[128,4,128]{2,1,0:T(4,128)}) custom-call(f32[2,3,24,128]{3,2,1,0:T(8,128)} %get-tuple-element.53.refs_0_, f32[2,28,32,128]{3,2,1,0:T(8,128)} %get-tuple-element.54.refs_1_.refs_10_, ...), custom_call_target="tpu_custom_call" | custom-call | tf_op jit(solution)/shard_map/pallas_call | solution.py:558
  80.8 9.9 %all-to-all-start.1 = ((f32[128,4,128]{2,1,0:T(4,128)}), f32[128,4,128]{2,1,0:T(4,128)S(1)}, u32[]{:S(2)}, u32[]{:S(2)}) async-start(f32[128,4,128]{2,1,0:T(4,128)} %get-tuple-element.69), calls=%async_computation.1 | async-start | bytes 524288 | tf_op jit(solution)/shard_map/all_to_all | solution.py:583
  91.2 4.6 %collective-permute-start.11 = (f32[15,8,128]{2,1,0:T(8,128)S(1)}, f32[15,8,128]{2,1,0:T(8,128)S(1)}, u32[]{:S(2)}, u32[]{:S(2)}) collective-permute-start(f32[15,8,128]{2,1,0:T(8,128)S(1)} %copy-done.24), channel_id=1, source_target_pairs={{16,32},{32,16},{48,64},{64,48},{80,96},{96,80},{17,33},{33,17},{4... | collective-permute-start | bytes 184328 | tf_op jit(solution)/shard_map/ppermute | solution.py:574
  95.8 4.4 %collective-permute-done.11.two.refs_2_ = f32[15,8,128]{2,1,0:T(8,128)S(1)} collective-permute-done((f32[15,8,128]{2,1,0:T(8,128)S(1)}, f32[15,8,128]{2,1,0:T(8,128)S(1)}, u32[]{:S(2)}, u32[]{:S(2)}) %collective-permute-start.11) | collective-permute-done | bytes 61472 | tf_op jit(solution)/shard_map/ppermute | solution.py:574
  100.9 1.8 %shard_map.55 = (f32[38,8,128]{2,1,0:T(8,128)}, f32[38,8,128]{2,1,0:T(8,128)}) custom-call(f32[2,36,8,128]{3,2,1,0:T(8,128)} %get-tuple-element.64.own.refs_0_, f32[15,8,128]{2,1,0:T(8,128)} %copy-done.12, f32[15,8,128]{2,1,0:T(8,128)} %copy-done.13), custom_call_target="tpu_custom_call" | custom-call | tf_op jit(solution)/shard_map/pallas_call | solution.py:558
  103.8 4.4 %collective-permute-start.13 = (f32[38,8,128]{2,1,0:T(8,128)}, f32[38,8,128]{2,1,0:T(8,128)S(1)}, u32[]{:S(2)}, u32[]{:S(2)}) collective-permute-start(f32[38,8,128]{2,1,0:T(8,128)} %get-tuple-element.68), channel_id=1, source_target_pairs={{1,2},{2,1},{3,4},{4,3},{5,6},{6,5},{7,8},{8,7},{9,10},{10,9},{11,... | collective-permute-start | bytes 466952 | tf_op jit(solution)/shard_map/ppermute | solution.py:574
  108.2 2.6 %collective-permute-start.18 = (f32[128,4,128]{2,1,0:T(4,128)S(1)}, f32[128,4,128]{2,1,0:T(4,128)S(1)}, u32[]{:S(2)}, u32[]{:S(2)}) collective-permute-start(f32[128,4,128]{2,1,0:T(4,128)S(1)} %all-to-all-done.1.r3_a), channel_id=1, source_target_pairs={{0,128},{128,0},{1,129},{129,1},{2,130},{130,2},{3,131},{131,3},{4... | collective-permute-start | bytes 786440 | tf_op jit(solution)/shard_map/ppermute | solution.py:579
  112.1 3.5 %collective-permute-start.17 = (f32[38,8,128]{2,1,0:T(8,128)S(1)}, f32[38,8,128]{2,1,0:T(8,128)S(1)}, u32[]{:S(2)}, u32[]{:S(2)}) collective-permute-start(f32[38,8,128]{2,1,0:T(8,128)S(1)} %collective-permute-done.13.refs_4_), channel_id=1, source_target_pairs={{0,128},{128,0},{1,129},{129,1},{2,130},{130,2},{3,131},{131,3},{4... | collective-permute-start | bytes 466952 | tf_op jit(solution)/shard_map/ppermute | solution.py:579
  116.8 5.6 %shard_map.56.refs_9_ = f32[2,3,24,128]{3,2,1,0:T(8,128)} custom-call(f32[2,15]{1,0:T(2,128)} %constant.2.clone.table, f32[8,128]{1,0:T(8,128)} %get-tuple-element.51._, f32[128,4,128]{2,1,0:T(4,128)} %copy-done.1, f32[128,4,128]{2,1,0:T(4,128)} %copy-done.4, f32[512,128]{1,0:T(8,128)} %bitcast.5, f32[512,128]{1,0:T(8,128)} %bitcast.7, ...), custom_call_target="tpu_custom_call" | custom-call | tf_op jit(solution)/shard_map/pallas_call | solution.py:558
  123.2 14.1 %shard_map.57 = (f32[16,16,128]{2,1,0:T(8,128)}, f32[16,16,128]{2,1,0:T(8,128)}) custom-call(f32[2,36,8,128]{3,2,1,0:T(8,128)} %get-tuple-element.64.own.refs_0_, f32[15,8,128]{2,1,0:T(8,128)} %copy-done.12, f32[15,8,128]{2,1,0:T(8,128)} %copy-done.13, f32[38,8,128]{2,1,0:T(8,128)} %copy-done.14, f32[38,8,128]{2,1,0:T(8,128)} %copy-done.15, ...), custom_call_target="tpu_custom_call" | custom-call | tf_op jit(solution)/shard_map/pallas_call | solution.py:558
  (78 shorter events, 11.7 us)
Async XLA Ops:
  3.0 15.5 %copy-start.22 = (f32[30,8,128]{2,1,0:T(8,128)S(1)}, f32[30,8,128]{2,1,0:T(8,128)}, u32[]{:S(2)}) copy-start(f32[30,8,128]{2,1,0:T(8,128)} %get-tuple-element.48) | copy-start | bytes 368644
  3.0 34.6 %all-to-all-start = ((f32[128,8,128]{2,1,0:T(8,128)}), f32[128,8,128]{2,1,0:T(8,128)S(1)}, u32[]{:S(2)}, u32[]{:S(2)}) async-start(f32[128,8,128]{2,1,0:T(8,128)} %get-tuple-element.52), calls=%async_computation | async-start | bytes 1048576 | tf_op jit(solution)/shard_map/all_to_all | solution.py:583
  17.9 29.2 %copy-start.3 = (f32[72,8,128]{2,1,0:T(8,128)S(1)}, f32[72,8,128]{2,1,0:T(8,128)}, u32[]{:S(2)}) copy-start(f32[72,8,128]{2,1,0:T(8,128)} %get-tuple-element.46.own.refs_0_) | copy-start | bytes 884740
  18.0 5.8 %collective-permute-start = (f32[30,8,128]{2,1,0:T(8,128)S(1)}, f32[30,8,128]{2,1,0:T(8,128)S(1)}, u32[]{:S(2)}, u32[]{:S(2)}) collective-permute-start(f32[30,8,128]{2,1,0:T(8,128)S(1)} %copy-done.23), channel_id=1, source_target_pairs={{0,16},{16,0},{32,48},{48,32},{64,80},{80,64},{96,112},{112,96},{1... | collective-permute-start | bytes 368648 | tf_op jit(solution)/shard_map/ppermute | solution.py:573
  18.5 10.5 %collective-permute-start.1 = (f32[30,8,128]{2,1,0:T(8,128)S(1)}, f32[30,8,128]{2,1,0:T(8,128)S(1)}, u32[]{:S(2)}, u32[]{:S(2)}) collective-permute-start(f32[30,8,128]{2,1,0:T(8,128)S(1)} %copy-done.22), channel_id=1, source_target_pairs={{16,32},{32,16},{48,64},{64,48},{80,96},{96,80},{17,33},{33,17},{4... | collective-permute-start | bytes 368648 | tf_op jit(solution)/shard_map/ppermute | solution.py:574
  31.6 9.1 %collective-permute-start.2 = (f32[76,8,128]{2,1,0:T(8,128)}, f32[76,8,128]{2,1,0:T(8,128)S(1)}, u32[]{:S(2)}, u32[]{:S(2)}) collective-permute-start(f32[76,8,128]{2,1,0:T(8,128)} %get-tuple-element.49), channel_id=1, source_target_pairs={{0,1},{1,0},{2,3},{3,2},{4,5},{5,4},{6,7},{7,6},{8,9},{9,8},{10,11... | collective-permute-start | bytes 933896 | tf_op jit(solution)/shard_map/ppermute | solution.py:573
  33.1 10.5 %collective-permute-start.3 = (f32[76,8,128]{2,1,0:T(8,128)}, f32[76,8,128]{2,1,0:T(8,128)S(1)}, u32[]{:S(2)}, u32[]{:S(2)}) collective-permute-start(f32[76,8,128]{2,1,0:T(8,128)} %get-tuple-element.50), channel_id=1, source_target_pairs={{1,2},{2,1},{3,4},{4,3},{5,6},{6,5},{7,8},{8,7},{9,10},{10,9},{11,... | collective-permute-start | bytes 933896 | tf_op jit(solution)/shard_map/ppermute | solution.py:574
  37.6 30.2 %copy-start = (f32[128,8,128]{2,1,0:T(8,128)}, f32[128,8,128]{2,1,0:T(8,128)S(1)}, u32[]{:S(2)}) copy-start(f32[128,8,128]{2,1,0:T(8,128)S(1)} %all-to-all-done.r3_a) | copy-start | bytes 1572868
  37.7 30.2 %collective-permute-start.9 = (f32[128,8,128]{2,1,0:T(8,128)S(1)}, f32[128,8,128]{2,1,0:T(8,128)S(1)}, u32[]{:S(2)}, u32[]{:S(2)}) collective-permute-start(f32[128,8,128]{2,1,0:T(8,128)S(1)} %all-to-all-done.r3_a), channel_id=1, source_target_pairs={{0,128},{128,0},{1,129},{129,1},{2,130},{130,2},{3,131},{131,3},{4... | collective-permute-start | bytes 1572872 | tf_op jit(solution)/shard_map/ppermute | solution.py:579
  40.7 9.9 %collective-permute-start.7 = (f32[76,8,128]{2,1,0:T(8,128)S(1)}, f32[76,8,128]{2,1,0:T(8,128)S(1)}, u32[]{:S(2)}, u32[]{:S(2)}) collective-permute-start(f32[76,8,128]{2,1,0:T(8,128)S(1)} %collective-permute-done.2.refs_3_), channel_id=1, source_target_pairs={{0,128},{128,0},{1,129},{129,1},{2,130},{130,2},{3,131},{131,3},{4... | collective-permute-start | bytes 933896 | tf_op jit(solution)/shard_map/ppermute | solution.py:579
  43.6 6.9 %collective-permute-start.8 = (f32[76,8,128]{2,1,0:T(8,128)S(1)}, f32[76,8,128]{2,1,0:T(8,128)S(1)}, u32[]{:S(2)}, u32[]{:S(2)}) collective-permute-start(f32[76,8,128]{2,1,0:T(8,128)S(1)} %collective-permute-done.3.refs_4_), channel_id=1, source_target_pairs={{0,128},{128,0},{1,129},{129,1},{2,130},{130,2},{3,131},{131,3},{4... | collective-permute-start | bytes 933896 | tf_op jit(solution)/shard_map/ppermute | solution.py:579
  47.1 3.4 %collective-permute-start.4 = (f32[72,8,128]{2,1,0:T(8,128)S(1)}, f32[72,8,128]{2,1,0:T(8,128)S(1)}, u32[]{:S(2)}, u32[]{:S(2)}) collective-permute-start(f32[72,8,128]{2,1,0:T(8,128)S(1)} %copy-done.3), channel_id=1, source_target_pairs={{0,128},{128,0},{1,129},{129,1},{2,130},{130,2},{3,131},{131,3},{4... | collective-permute-start | bytes 884744 | tf_op jit(solution)/shard_map/ppermute | solution.py:579
  47.2 1.7 %collective-permute-start.5 = (f32[30,8,128]{2,1,0:T(8,128)}, f32[30,8,128]{2,1,0:T(8,128)S(1)}, u32[]{:S(2)}, u32[]{:S(2)}) collective-permute-start(f32[30,8,128]{2,1,0:T(8,128)} %copy-done.5), channel_id=1, source_target_pairs={{0,128},{128,0},{1,129},{129,1},{2,130},{130,2},{3,131},{131,3},{4... | collective-permute-start | bytes 368648 | tf_op jit(solution)/shard_map/ppermute | solution.py:579
  49.0 1.6 %collective-permute-start.6 = (f32[30,8,128]{2,1,0:T(8,128)}, f32[30,8,128]{2,1,0:T(8,128)S(1)}, u32[]{:S(2)}, u32[]{:S(2)}) collective-permute-start(f32[30,8,128]{2,1,0:T(8,128)} %copy-done.6), channel_id=1, source_target_pairs={{0,128},{128,0},{1,129},{129,1},{2,130},{130,2},{3,131},{131,3},{4... | collective-permute-start | bytes 368648 | tf_op jit(solution)/shard_map/ppermute | solution.py:579
  80.8 27.4 %all-to-all-start.1 = ((f32[128,4,128]{2,1,0:T(4,128)}), f32[128,4,128]{2,1,0:T(4,128)S(1)}, u32[]{:S(2)}, u32[]{:S(2)}) async-start(f32[128,4,128]{2,1,0:T(4,128)} %get-tuple-element.69), calls=%async_computation.1 | async-start | bytes 524288 | tf_op jit(solution)/shard_map/all_to_all | solution.py:583
  90.6 5.2 %collective-permute-start.10 = (f32[15,8,128]{2,1,0:T(8,128)S(1)}, f32[15,8,128]{2,1,0:T(8,128)S(1)}, u32[]{:S(2)}, u32[]{:S(2)}) collective-permute-start(f32[15,8,128]{2,1,0:T(8,128)S(1)} %copy-done.25), channel_id=1, source_target_pairs={{0,16},{16,0},{32,48},{48,32},{64,80},{80,64},{96,112},{112,96},{1... | collective-permute-start | bytes 184328 | tf_op jit(solution)/shard_map/ppermute | solution.py:573
  91.2 9.1 %collective-permute-start.11 = (f32[15,8,128]{2,1,0:T(8,128)S(1)}, f32[15,8,128]{2,1,0:T(8,128)S(1)}, u32[]{:S(2)}, u32[]{:S(2)}) collective-permute-start(f32[15,8,128]{2,1,0:T(8,128)S(1)} %copy-done.24), channel_id=1, source_target_pairs={{16,32},{32,16},{48,64},{64,48},{80,96},{96,80},{17,33},{33,17},{4... | collective-permute-start | bytes 184328 | tf_op jit(solution)/shard_map/ppermute | solution.py:574
  102.6 8.1 %collective-permute-start.12 = (f32[38,8,128]{2,1,0:T(8,128)}, f32[38,8,128]{2,1,0:T(8,128)S(1)}, u32[]{:S(2)}, u32[]{:S(2)}) collective-permute-start(f32[38,8,128]{2,1,0:T(8,128)} %get-tuple-element.67), channel_id=1, source_target_pairs={{0,1},{1,0},{2,3},{3,2},{4,5},{5,4},{6,7},{7,6},{8,9},{9,8},{10,11... | collective-permute-start | bytes 466952 | tf_op jit(solution)/shard_map/ppermute | solution.py:573
  103.8 8.3 %collective-permute-start.13 = (f32[38,8,128]{2,1,0:T(8,128)}, f32[38,8,128]{2,1,0:T(8,128)S(1)}, u32[]{:S(2)}, u32[]{:S(2)}) collective-permute-start(f32[38,8,128]{2,1,0:T(8,128)} %get-tuple-element.68), channel_id=1, source_target_pairs={{1,2},{2,1},{3,4},{4,3},{5,6},{6,5},{7,8},{8,7},{9,10},{10,9},{11,... | collective-permute-start | bytes 466952 | tf_op jit(solution)/shard_map/ppermute | solution.py:574
  108.2 7.9 %collective-permute-start.18 = (f32[128,4,128]{2,1,0:T(4,128)S(1)}, f32[128,4,128]{2,1,0:T(4,128)S(1)}, u32[]{:S(2)}, u32[]{:S(2)}) collective-permute-start(f32[128,4,128]{2,1,0:T(4,128)S(1)} %all-to-all-done.1.r3_a), channel_id=1, source_target_pairs={{0,128},{128,0},{1,129},{129,1},{2,130},{130,2},{3,131},{131,3},{4... | collective-permute-start | bytes 786440 | tf_op jit(solution)/shard_map/ppermute | solution.py:579
  110.8 11.7 %collective-permute-start.16 = (f32[38,8,128]{2,1,0:T(8,128)S(1)}, f32[38,8,128]{2,1,0:T(8,128)S(1)}, u32[]{:S(2)}, u32[]{:S(2)}) collective-permute-start(f32[38,8,128]{2,1,0:T(8,128)S(1)} %collective-permute-done.12.refs_3_), channel_id=1, source_target_pairs={{0,128},{128,0},{1,129},{129,1},{2,130},{130,2},{3,131},{131,3},{4... | collective-permute-start | bytes 466952 | tf_op jit(solution)/shard_map/ppermute | solution.py:579
  112.1 10.4 %collective-permute-start.17 = (f32[38,8,128]{2,1,0:T(8,128)S(1)}, f32[38,8,128]{2,1,0:T(8,128)S(1)}, u32[]{:S(2)}, u32[]{:S(2)}) collective-permute-start(f32[38,8,128]{2,1,0:T(8,128)S(1)} %collective-permute-done.13.refs_4_), channel_id=1, source_target_pairs={{0,128},{128,0},{1,129},{129,1},{2,130},{130,2},{3,131},{131,3},{4... | collective-permute-start | bytes 466952 | tf_op jit(solution)/shard_map/ppermute | solution.py:579
  115.5 6.8 %collective-permute-start.14 = (f32[15,8,128]{2,1,0:T(8,128)}, f32[15,8,128]{2,1,0:T(8,128)S(1)}, u32[]{:S(2)}, u32[]{:S(2)}) collective-permute-start(f32[15,8,128]{2,1,0:T(8,128)} %copy-done.12), channel_id=1, source_target_pairs={{0,128},{128,0},{1,129},{129,1},{2,130},{130,2},{3,131},{131,3},{4... | collective-permute-start | bytes 184328 | tf_op jit(solution)/shard_map/ppermute | solution.py:579
  115.5 6.9 %collective-permute-start.15 = (f32[15,8,128]{2,1,0:T(8,128)}, f32[15,8,128]{2,1,0:T(8,128)S(1)}, u32[]{:S(2)}, u32[]{:S(2)}) collective-permute-start(f32[15,8,128]{2,1,0:T(8,128)} %copy-done.13), channel_id=1, source_target_pairs={{0,128},{128,0},{1,129},{129,1},{2,130},{130,2},{3,131},{131,3},{4... | collective-permute-start | bytes 184328 | tf_op jit(solution)/shard_map/ppermute | solution.py:579
  (23 other events, 101.6 us)

commit v4 on v3

--- a/solution.py
+++ b/solution.py
@@ -427,7 +427,7 @@
             tmp2[:, 2 * i + low, pl.ds(1, 16, 2), :] = piece
 
 
-def coarse_kernel(gx_n, gy_n, build, table, _, r3_a, r3_b, r3f_a, r3f_b, *refs):
+def coarse(gx_n, gy_n, build, table, r3_a, r3_b, r3f_a, r3f_b, *refs):
     pos = position()
     core = pos[0]
     *weights3, inv3, fx4, fy4, fz4, inv4 = refs[:11]
@@ -453,13 +453,17 @@
     add_coarsest(pos, gx_n, gy_n, x4, c3, sum3)
 
 
+def coarse_kernel(gx_n, gy_n, *refs):
+    coarse(gx_n, gy_n, False, *refs)
+
+
 def first_kernel(*refs):
     core, gx, gy = position()
     halves = ((core, refs[:5]), (1 - core, refs[5:10]))
     weights1, inv1, diag1 = refs[10:16], refs[16], refs[17]
     weights2, inv2 = refs[18:24], refs[24]
-    c1, c2, right, token = refs[25:29]
-    a1, b1, e1, d1, o1, a2, b2, e2, d2, o2 = refs[29:]
+    b1, c2 = refs[25:27]
+    a1, a2, b2, e2, d2, o2 = refs[27:]
     even_x, even_y = is_even(gx), is_even(gy)
     for c in range(2):
         a2[c, 0] = jnp.zeros((24, 128), F32)
@@ -470,17 +474,20 @@
     faces(1, a1, weights1, inv1, diag1)
     faces(2, a2, weights2, inv2, None)
     smooth(2, b2, weights2, inv2, e2, d2, o2, c2)
+
+
+def smooth_kernel(*refs):
+    weights1, inv1, b1, c1, e1, d1, o1 = refs[:6], *refs[6:]
     smooth(1, b1, weights1, inv1, e1, d1, o1, c1)
-    right[...] = b1[:, 6:22, 8:24, :]
-    token[...] = jnp.zeros_like(token)
-
-
-def join_kernel(*refs):
+
+
+def join_kernel(gx_n, gy_n, *refs):
     core, gx, _ = position()
     even_x = is_even(gx)
-    sum3, weights1, diag1, c1, c2, right = refs[0], refs[1:7], refs[7], refs[8], refs[9], refs[10]
-    x1, own, first, second, slots = refs[11:16]
-    s2, tmp3, tmp2, rest = refs[16:]
+    weights1, diag1, b1, c1, c2 = refs[5:11], *refs[11:15]
+    x1, right, own, first, second, slots = refs[26:32]
+    sum3, s2, tmp3, tmp2, rest = refs[32:37]
+    coarse(gx_n, gy_n, True, *refs[:5], *refs[15:26], sum3, *refs[37:])
     combine(sum3, c2, s2, tmp3, tmp2)
 
     def finish(i, _):
@@ -491,9 +498,11 @@
 
     def residual(i):
         mid, near = weighted(1, i, 2, x1, weights1)
-        res = diag1[:, pl.ds(i, 2)] * (mid - near)
+        bv = b1[:, pl.ds(i, 2)]
+        res = bv - diag1[:, pl.ds(i, 2)] * (mid - near)
         at = pl.ds(i - 6, 2)
-        rest[:, at] = right[:, at] - res[:, :, 8:24, :]
+        right[:, at] = bv[:, :, 8:24, :]
+        rest[:, at] = res[:, :, 8:24, :]
 
     blocks(6, 22, 2, residual)
     for c in range(2):
@@ -561,7 +570,7 @@
         in_specs=[smem if a.shape[-1] != 128 else vmem for a in args],
         out_specs=[vmem for _ in outs],
         scratch_shapes=[pltpu.VMEM(s, F32) for s in scratch],
-        compiler_params=pltpu.CompilerParams(vmem_limit_bytes=56 * 1024 * 1024),
+        compiler_params=pltpu.CompilerParams(vmem_limit_bytes=24 * 1024 * 1024),
         interpret=INTERPRET,
     )(*args)
 
@@ -608,21 +617,18 @@
     )
     y_one, y_two = trade(first, second, "gy")
     y_one_o, y_two_o = swap(y_one), swap(y_two)
-    *coefs, c1, c2, right, token = call(
-        first_kernel, [s1] * 8 + [s2] * 7 + [s1, s2, (2, 16, 16, 128), (8, 128)],
-        [s1, s1, s1, s1, s1, p2, s2, s2, s2, s2],
+    *coefs, b1, c2 = call(
+        first_kernel, [s1] * 8 + [s2] * 7 + [s1, s2], [s1, p2, s2, s2, s2, s2],
         own, x_one, x_two, y_one, y_two, own_o, x_one_o, x_two_o, y_one_o, y_two_o,
     )
+    (c1,) = call(smooth_kernel, [s1], [s1, s1, s1], *coefs[:7], b1)
     flat = (count * 8, 128)
-    *coarse, c3 = call(
-        functools.partial(coarse_kernel, gx_n, gy_n, True),
-        [s3] * 7 + [s4] * 4 + [sum3], [p3, s3, s3, s3, s3, s3, s4],
-        table, token, r3, r3_o, r3.reshape(flat), r3_o.reshape(flat),
-    )
-    x1, own, first, second, slots = call(
-        join_kernel,
-        [s1, (2, 36, 8, 128), (15, 8, 128), (15, 8, 128), (count, 4, 128)], tmps,
-        c3, *coefs[:6], coefs[7], c1, c2, right,
+    *coarse, x1, right, own, first, second, slots = call(
+        functools.partial(join_kernel, gx_n, gy_n),
+        [s3] * 7 + [s4] * 4
+        + [s1, (2, 16, 16, 128), (2, 36, 8, 128), (15, 8, 128), (15, 8, 128), (count, 4, 128)],
+        [sum3] + tmps + [p3, s3, s3, s3, s3, s3, s4],
+        table, r3, r3_o, r3.reshape(flat), r3_o.reshape(flat), *coefs[:6], coefs[7], b1, c1, c2,
     )
     x_one, x_two = trade(first, second, "gx")
     r3 = everywhere(slots)
@@ -634,9 +640,9 @@
     y_one, y_two = trade(first, second, "gy")
     flat = (count * 4, 128)
     (c3,) = call(
-        functools.partial(coarse_kernel, gx_n, gy_n, False),
+        functools.partial(coarse_kernel, gx_n, gy_n),
         [sum3], [s3, s3, s3, s3, s3, s4],
-        table, token, r3, r3_o, r3.reshape(flat), r3_o.reshape(flat), *coarse,
+        table, r3, r3_o, r3.reshape(flat), r3_o.reshape(flat), *coarse,
     )
     y_one_o, y_two_o = swap(y_one), swap(y_two)
     solution_field, residual = call(

time: 139 us -> 152 us (1.094)
  local copies, waits for them, and re-layouts: 5.08 us -> 37.8 us
  Pallas kernels: 53.7 us -> 34 us
    unnamed x52 -> x124, local copies, waits for them, and re-layouts: 5.08 us -> 37.8 us
    pallas_call x8, Pallas kernels: 53.7 us -> 34 us  [call(): pl.pallas_call(kernel, out_shape=[jax.ShapeDtypeStruct(s, F32) for s in o...]
  transfers between devices with their start and end apart: 21 -> 21, of which waited for: 7 -> 7; matrix products, arithmetic and copies ran while one was open for 0% -> 0% of each run, Pallas kernels for 18% -> 10%
where the time goes in v4:
time: 152 us; the launch traced here: 149 us
  starting transfers between devices  60.9 us (40%)
  local copies, waits for them, and re-layouts  37.8 us (25%)
  Pallas kernels  34 us (22%)
  waiting for transfers between devices  15.6 us (10%)
    unnamed x124, local copies, waits for them, and re-layouts  37.8 us
    pallas_call x8, Pallas kernels, call(): pl.pallas_call(kernel, out_shape=[jax.ShapeDtypeStruct(s, F32) for s in o...  34 us
    all_to_all x2, starting transfers between devices, everywhere(): return lax.all_to_all(slots, ('gx', 'gy'), 0, 0, tiled=True)  24.6 us
    ppermute x4, starting transfers between devices, trade(): two = lax.ppermute(second, axis, others)  18.1 us
    ppermute x11, starting transfers between devices, swap(): return lax.ppermute(x, 'grp', [(0, 1), (1, 0)])  14.3 us
    ppermute x4, waiting for transfers between devices, trade(): two = lax.ppermute(second, axis, others)  12.5 us
    ppermute x4, starting transfers between devices, trade(): one = lax.ppermute(first, axis, pairs)  3.89 us
  transfers between devices with their start and end apart: 21, of which 7 were waited for; matrix products, arithmetic and copies ran while one was open for 0% of the time, Pallas kernels for 10%

profile of v4, /device:TPU:27, one launch (start us, length us, event | category | flops | bytes accessed | tf_op | source)
XLA Modules:
  0.0 149.5 jit_solution(11028615886110240927)
XLA Ops:
  2.4 1.4 shard_map.50
  3.8 14.8 %all-to-all-start = ((f32[128,8,128]{2,1,0:T(8,128)}), f32[128,8,128]{2,1,0:T(8,128)S(1)}, u32[]{:S(2)}, u32[]{:S(2)}) async-start(f32[128,8,128]{2,1,0:T(8,128)} %get-tuple-element.44), calls=%async_computation | async-start | bytes 1048576 | tf_op jit(solution)/shard_map/all_to_all | solution.py:592
  19.2 4.6 %collective-permute-start.2 = (f32[30,8,128]{2,1,0:T(8,128)S(1)}, f32[30,8,128]{2,1,0:T(8,128)S(1)}, u32[]{:S(2)}, u32[]{:S(2)}) collective-permute-start(f32[30,8,128]{2,1,0:T(8,128)S(1)} %get-tuple-element.47), channel_id=1, source_target_pairs={{16,32},{32,16},{48,64},{64,48},{80,96},{96,80},{17,33},{33,17},{4... | collective-permute-start | bytes 368648 | tf_op jit(solution)/shard_map/ppermute | solution.py:583
  24.4 5.2 %collective-permute-done.2.two.refs_2_ = f32[30,8,128]{2,1,0:T(8,128)S(1)} collective-permute-done((f32[30,8,128]{2,1,0:T(8,128)S(1)}, f32[30,8,128]{2,1,0:T(8,128)S(1)}, u32[]{:S(2)}, u32[]{:S(2)}) %collective-permute-start.2) | collective-permute-done | bytes 122912 | tf_op jit(solution)/shard_map/ppermute | solution.py:583
  29.7 1.7 %collective-permute-start.3 = (f32[76,8,128]{2,1,0:T(8,128)S(1)}, f32[76,8,128]{2,1,0:T(8,128)S(1)}, u32[]{:S(2)}, u32[]{:S(2)}) collective-permute-start(f32[76,8,128]{2,1,0:T(8,128)S(1)} %get-tuple-element.48), channel_id=1, source_target_pairs={{0,1},{1,0},{2,3},{3,2},{4,5},{5,4},{6,7},{7,6},{8,9},{9,8},{10,11... | collective-permute-start | bytes 933896 | tf_op jit(solution)/shard_map/ppermute | solution.py:582
  31.4 4.4 %collective-permute-start.4 = (f32[76,8,128]{2,1,0:T(8,128)S(1)}, f32[76,8,128]{2,1,0:T(8,128)S(1)}, u32[]{:S(2)}, u32[]{:S(2)}) collective-permute-start(f32[76,8,128]{2,1,0:T(8,128)S(1)} %get-tuple-element.49), channel_id=1, source_target_pairs={{1,2},{2,1},{3,4},{4,3},{5,6},{6,5},{7,8},{8,7},{9,10},{10,9},{11,... | collective-permute-start | bytes 933896 | tf_op jit(solution)/shard_map/ppermute | solution.py:583
  35.8 3.0 %collective-permute-start = (f32[128,8,128]{2,1,0:T(8,128)S(1)}, f32[128,8,128]{2,1,0:T(8,128)S(1)}, u32[]{:S(2)}, u32[]{:S(2)}) collective-permute-start(f32[128,8,128]{2,1,0:T(8,128)S(1)} %all-to-all-done.refs_1_), channel_id=1, source_target_pairs={{0,128},{128,0},{1,129},{129,1},{2,130},{130,2},{3,131},{131,3},{4... | collective-permute-start | bytes 1572872 | tf_op jit(solution)/shard_map/ppermute | solution.py:588
  40.4 1.2 collective-permute-done.4.refs_4_
  41.7 3.5 %collective-permute-start.9 = (f32[76,8,128]{2,1,0:T(8,128)S(1)}, f32[76,8,128]{2,1,0:T(8,128)S(1)}, u32[]{:S(2)}, u32[]{:S(2)}) collective-permute-start(f32[76,8,128]{2,1,0:T(8,128)S(1)} %collective-permute-done.4.refs_4_), channel_id=1, source_target_pairs={{0,128},{128,0},{1,129},{129,1},{2,130},{130,2},{3,131},{131,3},{4... | collective-permute-start | bytes 933896 | tf_op jit(solution)/shard_map/ppermute | solution.py:588
  46.4 1.2 collective-permute-done.6.refs_6_
  47.8 1.2 collective-permute-done.7.refs_7_
  51.9 5.4 %shard_map.52 = (f32[2,28,32,128]{3,2,1,0:T(8,128)S(1)}, f32[2,28,32,128]{3,2,1,0:T(8,128)S(1)}, f32[2,28,32,128]{3,2,1,0:T(8,128)S(1)}, f32[2,28,32,128]{3,2,1,...) custom-call(f32[72,8,128]{2,1,0:T(8,128)S(1)} %copy-done.13, ...), custom_call_target="tpu_custom_call" | custom-call | tf_op jit(solution)/shard_map/pallas_call | solution.py:567
  57.4 4.9 %shard_map.53.refs_13_ = f32[2,28,32,128]{3,2,1,0:T(8,128)S(1)} custom-call(f32[2,28,32,128]{3,2,1,0:T(8,128)S(1)} %get-tuple-element.50.refs_0_.refs_5_.refs_10_, f32[2,28,32,128]{3,2,1,0:T(8,128)S(1)} %get-tuple-element.51.refs_1_.refs_6_.refs_11_, f32[2,28,32,128]{3,2,1,0:T(8,128)S(1)} %get-tuple-element.52.refs_2_.refs_7_.refs_12_, ...), custom_call_target="tpu_custom_call" | custom-call | tf_op jit(solution)/shard_map/pallas_call | solution.py:567
  63.1 6.6 %shard_map.54 = (f32[2,5,24,128]{3,2,1,0:T(8,128)S(1)}, f32[2,5,24,128]{3,2,1,0:T(8,128)S(1)}, f32[2,5,24,128]{3,2,1,0:T(8,128)S(1)}, f32[2,5,24,128]{3,2,1,0:T(...) custom-call(f32[2,15]{1,0:T(2,128)S(1)} %copy-done.59, ...), custom_call_target="tpu_custom_call" | custom-call | tf_op jit(solution)/shard_map/pallas_call | solution.py:567
  79.9 9.8 %all-to-all-start.1 = ((f32[128,4,128]{2,1,0:T(4,128)}), f32[128,4,128]{2,1,0:T(4,128)S(1)}, u32[]{:S(2)}, u32[]{:S(2)}) async-start(f32[128,4,128]{2,1,0:T(4,128)} %copy-done.22), calls=%async_computation.1 | async-start | bytes 524288 | tf_op jit(solution)/shard_map/all_to_all | solution.py:592
  90.2 4.6 %collective-permute-start.11 = (f32[15,8,128]{2,1,0:T(8,128)}, f32[15,8,128]{2,1,0:T(8,128)S(1)}, u32[]{:S(2)}, u32[]{:S(2)}) collective-permute-start(f32[15,8,128]{2,1,0:T(8,128)} %copy-done.61), channel_id=1, source_target_pairs={{16,32},{32,16},{48,64},{64,48},{80,96},{96,80},{17,33},{33,17},{4... | collective-permute-start | bytes 184328 | tf_op jit(solution)/shard_map/ppermute | solution.py:583
  94.9 4.6 %collective-permute-done.11.two.refs_2_ = f32[15,8,128]{2,1,0:T(8,128)S(1)} collective-permute-done((f32[15,8,128]{2,1,0:T(8,128)}, f32[15,8,128]{2,1,0:T(8,128)S(1)}, u32[]{:S(2)}, u32[]{:S(2)}) %collective-permute-start.11) | collective-permute-done | bytes 61472 | tf_op jit(solution)/shard_map/ppermute | solution.py:583
  101.3 4.4 %collective-permute-start.13 = (f32[38,8,128]{2,1,0:T(8,128)}, f32[38,8,128]{2,1,0:T(8,128)}, u32[]{:S(2)}, u32[]{:S(2)}) collective-permute-start(f32[38,8,128]{2,1,0:T(8,128)} %get-tuple-element.64), channel_id=1, source_target_pairs={{1,2},{2,1},{3,4},{4,3},{5,6},{6,5},{7,8},{8,7},{9,10},{10,9},{11,... | collective-permute-start | bytes 466952 | tf_op jit(solution)/shard_map/ppermute | solution.py:583
  105.8 2.4 %collective-permute-start.18 = (f32[128,4,128]{2,1,0:T(4,128)S(1)}, f32[128,4,128]{2,1,0:T(4,128)S(1)}, u32[]{:S(2)}, u32[]{:S(2)}) collective-permute-start(f32[128,4,128]{2,1,0:T(4,128)S(1)} %all-to-all-done.1.refs_1_), channel_id=1, source_target_pairs={{0,128},{128,0},{1,129},{129,1},{2,130},{130,2},{3,131},{131,3},{4... | collective-permute-start | bytes 786440 | tf_op jit(solution)/shard_map/ppermute | solution.py:588
  108.3 1.5 collective-permute-done.13.refs_4_
  109.7 3.4 %collective-permute-start.17 = (f32[38,8,128]{2,1,0:T(8,128)}, f32[38,8,128]{2,1,0:T(8,128)S(1)}, u32[]{:S(2)}, u32[]{:S(2)}) collective-permute-start(f32[38,8,128]{2,1,0:T(8,128)} %collective-permute-done.13.refs_4_), channel_id=1, source_target_pairs={{0,128},{128,0},{1,129},{129,1},{2,130},{130,2},{3,131},{131,3},{4... | collective-permute-start | bytes 466952 | tf_op jit(solution)/shard_map/ppermute | solution.py:588
  123.1 4.1 %shard_map.56.refs_9_ = f32[2,3,24,128]{3,2,1,0:T(8,128)S(1)} custom-call(f32[2,15]{1,0:T(2,128)S(1)} %copy-done.60, f32[128,4,128]{2,1,0:T(4,128)S(1)} %all-to-all-done.1.refs_1_, f32[128,4,128]{2,1,0:T(4,128)S(1)} %collective-permute-done.18.refs_2_, f32[512,128]{1,0:T(8,128)S(1)} %bitcast.5, f32[512,128]{1,0:T(8,128)S(1)} %bitcast.7, ...), custom_call_target="tpu_custom_call" | custom-call | tf_op jit(solution)/shard_map/pallas_call | solution.py:567
  128.4 1.2 copy-done.7
  138.5 10.9 %shard_map.57 = (f32[16,16,128]{2,1,0:T(8,128)}, f32[16,16,128]{2,1,0:T(8,128)}) custom-call(f32[2,36,8,128]{3,2,1,0:T(8,128)S(1)} %copy-done.11, f32[15,8,128]{2,1,0:T(8,128)S(1)} %collective-permute-done.10.one.refs_1_, f32[15,8,128]{2,1,0:T(8,128)S(1)} %collective-permute-done.11.two.refs_2_, f32[38,8,128]{2,1,0:T(8,128)} %collective-permute-done.12.refs_3_, ...), custom_call_target="tpu_custom_call" | custom-call | tf_op jit(solution)/shard_map/pallas_call | solution.py:567
  (150 shorter events, 42.4 us)
Async XLA Ops:
  3.8 41.3 %copy-start.12 = (f32[72,8,128]{2,1,0:T(8,128)}, f32[72,8,128]{2,1,0:T(8,128)S(1)}, u32[]{:S(2)}) copy-start(f32[72,8,128]{2,1,0:T(8,128)S(1)} %get-tuple-element.45.own.refs_0_) | copy-start | bytes 884740
  3.8 32.0 %all-to-all-start = ((f32[128,8,128]{2,1,0:T(8,128)}), f32[128,8,128]{2,1,0:T(8,128)S(1)}, u32[]{:S(2)}, u32[]{:S(2)}) async-start(f32[128,8,128]{2,1,0:T(8,128)} %get-tuple-element.44), calls=%async_computation | async-start | bytes 1048576 | tf_op jit(solution)/shard_map/all_to_all | solution.py:592
  18.6 5.8 %collective-permute-start.1 = (f32[30,8,128]{2,1,0:T(8,128)S(1)}, f32[30,8,128]{2,1,0:T(8,128)S(1)}, u32[]{:S(2)}, u32[]{:S(2)}) collective-permute-start(f32[30,8,128]{2,1,0:T(8,128)S(1)} %get-tuple-element.46), channel_id=1, source_target_pairs={{0,16},{16,0},{32,48},{48,32},{64,80},{80,64},{96,112},{112,96},{1... | collective-permute-start | bytes 368648 | tf_op jit(solution)/shard_map/ppermute | solution.py:582
  19.2 10.5 %collective-permute-start.2 = (f32[30,8,128]{2,1,0:T(8,128)S(1)}, f32[30,8,128]{2,1,0:T(8,128)S(1)}, u32[]{:S(2)}, u32[]{:S(2)}) collective-permute-start(f32[30,8,128]{2,1,0:T(8,128)S(1)} %get-tuple-element.47), channel_id=1, source_target_pairs={{16,32},{32,16},{48,64},{64,48},{80,96},{96,80},{17,33},{33,17},{4... | collective-permute-start | bytes 368648 | tf_op jit(solution)/shard_map/ppermute | solution.py:583
  29.7 9.2 %collective-permute-start.3 = (f32[76,8,128]{2,1,0:T(8,128)S(1)}, f32[76,8,128]{2,1,0:T(8,128)S(1)}, u32[]{:S(2)}, u32[]{:S(2)}) collective-permute-start(f32[76,8,128]{2,1,0:T(8,128)S(1)} %get-tuple-element.48), channel_id=1, source_target_pairs={{0,1},{1,0},{2,3},{3,2},{4,5},{5,4},{6,7},{7,6},{8,9},{9,8},{10,11... | collective-permute-start | bytes 933896 | tf_op jit(solution)/shard_map/ppermute | solution.py:582
  31.4 10.3 %collective-permute-start.4 = (f32[76,8,128]{2,1,0:T(8,128)S(1)}, f32[76,8,128]{2,1,0:T(8,128)S(1)}, u32[]{:S(2)}, u32[]{:S(2)}) collective-permute-start(f32[76,8,128]{2,1,0:T(8,128)S(1)} %get-tuple-element.49), channel_id=1, source_target_pairs={{1,2},{2,1},{3,4},{4,3},{5,6},{6,5},{7,8},{8,7},{9,10},{10,9},{11,... | collective-permute-start | bytes 933896 | tf_op jit(solution)/shard_map/ppermute | solution.py:583
  35.8 26.6 %collective-permute-start = (f32[128,8,128]{2,1,0:T(8,128)S(1)}, f32[128,8,128]{2,1,0:T(8,128)S(1)}, u32[]{:S(2)}, u32[]{:S(2)}) collective-permute-start(f32[128,8,128]{2,1,0:T(8,128)S(1)} %all-to-all-done.refs_1_), channel_id=1, source_target_pairs={{0,128},{128,0},{1,129},{129,1},{2,130},{130,2},{3,131},{131,3},{4... | collective-permute-start | bytes 1572872 | tf_op jit(solution)/shard_map/ppermute | solution.py:588
  38.8 10.2 %collective-permute-start.8 = (f32[76,8,128]{2,1,0:T(8,128)S(1)}, f32[76,8,128]{2,1,0:T(8,128)S(1)}, u32[]{:S(2)}, u32[]{:S(2)}) collective-permute-start(f32[76,8,128]{2,1,0:T(8,128)S(1)} %collective-permute-done.3.refs_3_), channel_id=1, source_target_pairs={{0,128},{128,0},{1,129},{129,1},{2,130},{130,2},{3,131},{131,3},{4... | collective-permute-start | bytes 933896 | tf_op jit(solution)/shard_map/ppermute | solution.py:588
  41.7 7.3 %collective-permute-start.9 = (f32[76,8,128]{2,1,0:T(8,128)S(1)}, f32[76,8,128]{2,1,0:T(8,128)S(1)}, u32[]{:S(2)}, u32[]{:S(2)}) collective-permute-start(f32[76,8,128]{2,1,0:T(8,128)S(1)} %collective-permute-done.4.refs_4_), channel_id=1, source_target_pairs={{0,128},{128,0},{1,129},{129,1},{2,130},{130,2},{3,131},{131,3},{4... | collective-permute-start | bytes 933896 | tf_op jit(solution)/shard_map/ppermute | solution.py:588
  45.9 3.1 %collective-permute-start.5 = (f32[72,8,128]{2,1,0:T(8,128)S(1)}, f32[72,8,128]{2,1,0:T(8,128)S(1)}, u32[]{:S(2)}, u32[]{:S(2)}) collective-permute-start(f32[72,8,128]{2,1,0:T(8,128)S(1)} %get-tuple-element.45.own.refs_0_), channel_id=1, source_target_pairs={{0,128},{128,0},{1,129},{129,1},{2,130},{130,2},{3,131},{131,3},{4... | collective-permute-start | bytes 884744 | tf_op jit(solution)/shard_map/ppermute | solution.py:588
  45.9 1.8 %collective-permute-start.6 = (f32[30,8,128]{2,1,0:T(8,128)S(1)}, f32[30,8,128]{2,1,0:T(8,128)S(1)}, u32[]{:S(2)}, u32[]{:S(2)}) collective-permute-start(f32[30,8,128]{2,1,0:T(8,128)S(1)} %collective-permute-done.1.one.refs_1_), channel_id=1, source_target_pairs={{0,128},{128,0},{1,129},{129,1},{2,130},{130,2},{3,131},{131,3},{4... | collective-permute-start | bytes 368648 | tf_op jit(solution)/shard_map/ppermute | solution.py:588
  47.7 1.3 collective-permute-start.7
  57.4 5.1 %copy-start = (f32[2,28,32,128]{3,2,1,0:T(8,128)}, f32[2,28,32,128]{3,2,1,0:T(8,128)S(1)}, u32[]{:S(2)}) copy-start(f32[2,28,32,128]{3,2,1,0:T(8,128)S(1)} %get-tuple-element.53.refs_3_.refs_8_.refs_13_) | copy-start | bytes 2752516
  79.8 19.6 %copy-start.11 = (f32[2,36,8,128]{3,2,1,0:T(8,128)S(1)}, f32[2,36,8,128]{3,2,1,0:T(8,128)}, u32[]{:S(2)}) copy-start(f32[2,36,8,128]{3,2,1,0:T(8,128)} %copy-done.10) | copy-start | bytes 884740
  79.9 25.9 %all-to-all-start.1 = ((f32[128,4,128]{2,1,0:T(4,128)}), f32[128,4,128]{2,1,0:T(4,128)S(1)}, u32[]{:S(2)}, u32[]{:S(2)}) async-start(f32[128,4,128]{2,1,0:T(4,128)} %copy-done.22), calls=%async_computation.1 | async-start | bytes 524288 | tf_op jit(solution)/shard_map/all_to_all | solution.py:592
  89.7 5.2 %collective-permute-start.10 = (f32[15,8,128]{2,1,0:T(8,128)}, f32[15,8,128]{2,1,0:T(8,128)S(1)}, u32[]{:S(2)}, u32[]{:S(2)}) collective-permute-start(f32[15,8,128]{2,1,0:T(8,128)} %get-tuple-element.61), channel_id=1, source_target_pairs={{0,16},{16,0},{32,48},{48,32},{64,80},{80,64},{96,112},{112,96},{1... | collective-permute-start | bytes 184328 | tf_op jit(solution)/shard_map/ppermute | solution.py:582
  90.2 9.3 %collective-permute-start.11 = (f32[15,8,128]{2,1,0:T(8,128)}, f32[15,8,128]{2,1,0:T(8,128)S(1)}, u32[]{:S(2)}, u32[]{:S(2)}) collective-permute-start(f32[15,8,128]{2,1,0:T(8,128)} %copy-done.61), channel_id=1, source_target_pairs={{16,32},{32,16},{48,64},{64,48},{80,96},{96,80},{17,33},{33,17},{4... | collective-permute-start | bytes 184328 | tf_op jit(solution)/shard_map/ppermute | solution.py:583
  100.2 7.9 %collective-permute-start.12 = (f32[38,8,128]{2,1,0:T(8,128)}, f32[38,8,128]{2,1,0:T(8,128)}, u32[]{:S(2)}, u32[]{:S(2)}) collective-permute-start(f32[38,8,128]{2,1,0:T(8,128)} %get-tuple-element.63), channel_id=1, source_target_pairs={{0,1},{1,0},{2,3},{3,2},{4,5},{5,4},{6,7},{7,6},{8,9},{9,8},{10,11... | collective-permute-start | bytes 466952 | tf_op jit(solution)/shard_map/ppermute | solution.py:582
  101.3 8.4 %collective-permute-start.13 = (f32[38,8,128]{2,1,0:T(8,128)}, f32[38,8,128]{2,1,0:T(8,128)}, u32[]{:S(2)}, u32[]{:S(2)}) collective-permute-start(f32[38,8,128]{2,1,0:T(8,128)} %get-tuple-element.64), channel_id=1, source_target_pairs={{1,2},{2,1},{3,4},{4,3},{5,6},{6,5},{7,8},{8,7},{9,10},{10,9},{11,... | collective-permute-start | bytes 466952 | tf_op jit(solution)/shard_map/ppermute | solution.py:583
  105.8 7.8 %collective-permute-start.18 = (f32[128,4,128]{2,1,0:T(4,128)S(1)}, f32[128,4,128]{2,1,0:T(4,128)S(1)}, u32[]{:S(2)}, u32[]{:S(2)}) collective-permute-start(f32[128,4,128]{2,1,0:T(4,128)S(1)} %all-to-all-done.1.refs_1_), channel_id=1, source_target_pairs={{0,128},{128,0},{1,129},{129,1},{2,130},{130,2},{3,131},{131,3},{4... | collective-permute-start | bytes 786440 | tf_op jit(solution)/shard_map/ppermute | solution.py:588
  108.2 19.0 %collective-permute-start.16 = (f32[38,8,128]{2,1,0:T(8,128)}, f32[38,8,128]{2,1,0:T(8,128)S(1)}, u32[]{:S(2)}, u32[]{:S(2)}) collective-permute-start(f32[38,8,128]{2,1,0:T(8,128)} %collective-permute-done.12.refs_3_), channel_id=1, source_target_pairs={{0,128},{128,0},{1,129},{129,1},{2,130},{130,2},{3,131},{131,3},{4... | collective-permute-start | bytes 466952 | tf_op jit(solution)/shard_map/ppermute | solution.py:588
  109.7 17.4 %collective-permute-start.17 = (f32[38,8,128]{2,1,0:T(8,128)}, f32[38,8,128]{2,1,0:T(8,128)S(1)}, u32[]{:S(2)}, u32[]{:S(2)}) collective-permute-start(f32[38,8,128]{2,1,0:T(8,128)} %collective-permute-done.13.refs_4_), channel_id=1, source_target_pairs={{0,128},{128,0},{1,129},{129,1},{2,130},{130,2},{3,131},{131,3},{4... | collective-permute-start | bytes 466952 | tf_op jit(solution)/shard_map/ppermute | solution.py:588
  113.1 14.1 %collective-permute-start.14 = (f32[15,8,128]{2,1,0:T(8,128)S(1)}, f32[15,8,128]{2,1,0:T(8,128)S(1)}, u32[]{:S(2)}, u32[]{:S(2)}) collective-permute-start(f32[15,8,128]{2,1,0:T(8,128)S(1)} %collective-permute-done.10.one.refs_1_), channel_id=1, source_target_pairs={{0,128},{128,0},{1,129},{129,1},{2,130},{130,2},{3,131},{131,3},{4... | collective-permute-start | bytes 184328 | tf_op jit(solution)/shard_map/ppermute | solution.py:588
  113.1 14.1 %collective-permute-start.15 = (f32[15,8,128]{2,1,0:T(8,128)S(1)}, f32[15,8,128]{2,1,0:T(8,128)S(1)}, u32[]{:S(2)}, u32[]{:S(2)}) collective-permute-start(f32[15,8,128]{2,1,0:T(8,128)S(1)} %collective-permute-done.11.two.refs_2_), channel_id=1, source_target_pairs={{0,128},{128,0},{1,129},{129,1},{2,130},{130,2},{3,131},{131,3},{4... | collective-permute-start | bytes 184328 | tf_op jit(solution)/shard_map/ppermute | solution.py:588
  (59 other events, 105.7 us)

commit v5 on v3

--- a/solution.py
+++ b/solution.py
@@ -205,22 +205,19 @@
     inv[...] = 1.0 / total
 
 
-def smooth4(table, b, fx, fy, fz, inv):
-    first = cheb_steps(COARSE_DEGREE, LOW_COARSE, HIGH_BOUND)[0]
+def smooth4(b, fx, fy, fz, inv):
+    first, keeps, pushes = cheb_steps(COARSE_DEGREE, LOW_COARSE, HIGH_BOUND)
     e = b * inv[...] * (1.0 / SCALE[4])
-    d = e * first
-
-    def body(step, carry):
-        e, d, x = carry
+    x = d = e * first
+    for keep, push in zip(keeps, pushes):
         gx, gy, gz = fx[...], fy[...], fz[...]
         near = gx * x_up4(d) + x_dn4(gx * d)
         near = near + gy * roll(d, -1, 1) + roll(gy * d, 1, 1)
         near = near + gz * roll(d, -1, 2) + roll(gz * d, 1, 2)
         e = e - d + inv[...] * near
-        d = table[0, step] * d + table[1, step] * e
-        return e, d, x + d
-
-    return lax.fori_loop(0, COARSE_DEGREE - 1, body, (e, d, d))[2]
+        d = keep * d + push * e
+        x = x + d
+    return x
 
 
 def build4(src, stride, offset, core, gx_n, gy_n):
@@ -271,6 +268,21 @@
     return total
 
 
+class Copies:
+    def __init__(self, sems):
+        self.sems, self.made = sems, []
+
+    def start(self, src, dst):
+        copy = pltpu.make_async_copy(src, dst, self.sems.at[len(self.made)])
+        copy.start()
+        self.made.append(copy)
+        return copy
+
+    def finish(self):
+        for copy in self.made:
+            copy.wait()
+
+
 def position():
     return tuple(lax.axis_index(name) for name in ("grp", "gx", "gy"))
 
@@ -284,9 +296,13 @@
     return lax.rem(index, 2) == 0
 
 
-def prepare_kernel(a, b, own, first, second, slots):
+def prepare_kernel(a_hbm, b_hbm, own, own_hbm, first, second, slots, a, b, sems):
     even = is_even(position()[1])
+    copies = Copies(sems)
+    copies.start(a_hbm, a)
+    copies.start(b_hbm, b)
     for f, src in enumerate((a, b)):
+        copies.made[f].wait()
         for t in range(2):
             own[pl.ds(f * 32 + t, 16, 2)] = src[:, t * 8:t * 8 + 8, :]
             put_pair(
@@ -313,7 +329,9 @@
         slots[0, pl.ds(f, 4, 2), :] = restrict_to3(
             lambda k: own[64 + f * 4 + k, pl.ds(0, 4, 2), :] + own[64 + f * 4 + k, pl.ds(1, 4, 2), :]
         )
+    keep = copies.start(own, own_hbm)
     slots[1:] = jnp.broadcast_to(slots[0:1], (slots.shape[0] - 1, 8, 128))
+    keep.wait()
 
 
 def sides_kernel(nf, own, one, two, first, second):
@@ -350,7 +368,7 @@
             second[nf * 28 + f * 10 + i] = tile
 
 
-def spread(nf, f, core, even_x, even_y, own, x_one, x_two, y_one, y_two, fine, mid, pad):
+def spread(nf, f, core, even_x, even_y, x_one, x_two, y_one, y_two, fine, mid, pad):
     lower = lambda i: jnp.where(even_x, x_two[i], x_one[i])
     upper = lambda i: jnp.where(even_x, x_one[i], x_two[i])
     below = lambda i: jnp.where(even_y, y_two[i], y_one[i])
@@ -364,7 +382,7 @@
             elif i >= 22:
                 tile = upper(f * 12 + 2 * (i - 22) + t)
             else:
-                tile = own[f * 32 + 2 * (i - 6) + t]
+                continue
             fine[core, i, 8 + 8 * t:16 + 8 * t, :] = tile
     base = nf * 28 + f * 10
     for i in range(10):
@@ -375,8 +393,16 @@
         elif i >= 7:
             tile = upper(nf * 12 + f * 3 + i - 7)
         else:
-            tile = own[nf * 32 + f * 4 + i - 3]
+            continue
         mid[core, i + pad, 8:16, :] = tile
+
+
+def spread_own(nf, f, core, own, fine, mid, pad):
+    for i in range(16):
+        for t in range(2):
+            fine[core, i + 6, 8 + 8 * t:16 + 8 * t, :] = own[f * 32 + 2 * i + t]
+    for i in range(4):
+        mid[core, i + 3 + pad, 8:16, :] = own[nf * 32 + f * 4 + i]
 
 
 def add_coarsest(pos, gx_n, gy_n, x4, x3, out):
@@ -427,73 +453,106 @@
             tmp2[:, 2 * i + low, pl.ds(1, 16, 2), :] = piece
 
 
-def coarse_kernel(gx_n, gy_n, build, table, _, r3_a, r3_b, r3f_a, r3f_b, *refs):
+def split3(ref):
+    return [ref.at[k] for k in range(6)], ref.at[6]
+
+
+def coarse_first_kernel(
+    gx_n, gy_n, r3_a, r3_b, r3f_a, r3f_b, sum3, w3_hbm, w4_hbm,
+    w3, w4, a3, b3, e3, d3, o3, c3, x4, sems,
+):
     pos = position()
     core = pos[0]
-    *weights3, inv3, fx4, fy4, fz4, inv4 = refs[:11]
-    if build:
-        sum3, a3, b3, e3, d3, o3, c3, x4 = refs[11:]
-        for c in range(2):
-            a3[c, 0] = jnp.zeros((24, 128), F32)
-            a3[c, 6] = jnp.zeros((24, 128), F32)
-        for c, src in ((core, r3_a), (1 - core, r3_b)):
-            window3(src, a3, 0, 2, c, pos, gx_n, gy_n, 1)
-            window3(src, b3, 1, 2, c, pos, gx_n, gy_n, 0)
-        a4 = build4(r3f_a, 4, 0, core, gx_n, gy_n) + build4(r3f_b, 4, 0, 1 - core, gx_n, gy_n)
-        b4 = build4(r3f_a, 4, 1, core, gx_n, gy_n) + build4(r3f_b, 4, 1, 1 - core, gx_n, gy_n)
-        faces4(a4, fx4, fy4, fz4, inv4)
-        faces(3, a3, weights3, inv3, None)
-    else:
-        sum3, b3, e3, d3, o3, c3, x4 = refs[11:]
-        window3(r3_a, b3, 0, 1, core, pos, gx_n, gy_n, 0)
-        window3(r3_b, b3, 0, 1, 1 - core, pos, gx_n, gy_n, 0)
-        b4 = build4(r3f_a, 2, 0, core, gx_n, gy_n) + build4(r3f_b, 2, 0, 1 - core, gx_n, gy_n)
-    x4[...] = smooth4(table, b4, fx4, fy4, fz4, inv4)
+    weights3, inv3 = split3(w3)
+    fx4, fy4, fz4, inv4 = (w4.at[k] for k in range(4))
+    copies = Copies(sems)
+    for c in range(2):
+        a3[c, 0] = jnp.zeros((24, 128), F32)
+        a3[c, 6] = jnp.zeros((24, 128), F32)
+    for c, src in ((core, r3_a), (1 - core, r3_b)):
+        window3(src, a3, 0, 2, c, pos, gx_n, gy_n, 1)
+        window3(src, b3, 1, 2, c, pos, gx_n, gy_n, 0)
+    a4 = build4(r3f_a, 4, 0, core, gx_n, gy_n) + build4(r3f_b, 4, 0, 1 - core, gx_n, gy_n)
+    b4 = build4(r3f_a, 4, 1, core, gx_n, gy_n) + build4(r3f_b, 4, 1, 1 - core, gx_n, gy_n)
+    faces4(a4, fx4, fy4, fz4, inv4)
+    copies.start(w4, w4_hbm)
+    faces(3, a3, weights3, inv3, None)
+    copies.start(w3, w3_hbm)
+    x4[...] = smooth4(b4, fx4, fy4, fz4, inv4)
     smooth(3, b3, weights3, inv3, e3, d3, o3, c3)
     add_coarsest(pos, gx_n, gy_n, x4, c3, sum3)
-
-
-def first_kernel(*refs):
+    copies.finish()
+
+
+def coarse_second_kernel(
+    gx_n, gy_n, r3_a, r3_b, r3f_a, r3f_b, w3_hbm, w4_hbm, sum3,
+    w3, w4, b3, e3, d3, o3, c3, x4, sems,
+):
+    pos = position()
+    core = pos[0]
+    copies = Copies(sems)
+    copies.start(w4_hbm, w4)
+    copies.start(w3_hbm, w3)
+    weights3, inv3 = split3(w3)
+    window3(r3_a, b3, 0, 1, core, pos, gx_n, gy_n, 0)
+    window3(r3_b, b3, 0, 1, 1 - core, pos, gx_n, gy_n, 0)
+    b4 = build4(r3f_a, 2, 0, core, gx_n, gy_n) + build4(r3f_b, 2, 0, 1 - core, gx_n, gy_n)
+    copies.made[0].wait()
+    x4[...] = smooth4(b4, *(w4.at[k] for k in range(4)))
+    copies.made[1].wait()
+    smooth(3, b3, weights3, inv3, e3, d3, o3, c3)
+    add_coarsest(pos, gx_n, gy_n, x4, c3, sum3)
+
+
+def first_kernel(
+    own_a, x_one_a, x_two_a, y_one_a, y_two_a, own_b, x_one_b, x_two_b, y_one_b, y_two_b, sum3,
+    w1_hbm, w2_hbm, x1_hbm, right_hbm, own_hbm, own, first, second, slots,
+    w1, w2, x1, own_s, a1, b1, e1, d1, o1, a2, b2, e2, d2, o2, c2, s2, tmp3, tmp2, rest, sems,
+):
     core, gx, gy = position()
-    halves = ((core, refs[:5]), (1 - core, refs[5:10]))
-    weights1, inv1, diag1 = refs[10:16], refs[16], refs[17]
-    weights2, inv2 = refs[18:24], refs[24]
-    c1, c2, right, token = refs[25:29]
-    a1, b1, e1, d1, o1, a2, b2, e2, d2, o2 = refs[29:]
     even_x, even_y = is_even(gx), is_even(gy)
+    copies = Copies(sems)
+    copies.start(own_a, own_s)
+    halves = (
+        (core, (x_one_a, x_two_a, y_one_a, y_two_a)),
+        (1 - core, (x_one_b, x_two_b, y_one_b, y_two_b)),
+    )
+    weights1, inv1 = split3(w1)
+    diag1 = w1.at[7]
+    weights2, inv2 = split3(w2)
     for c in range(2):
         a2[c, 0] = jnp.zeros((24, 128), F32)
         a2[c, 11] = jnp.zeros((24, 128), F32)
     for c, parts in halves:
         spread(2, 0, c, even_x, even_y, *parts, a1, a2, 1)
         spread(2, 1, c, even_x, even_y, *parts, b1, b2, 0)
+    spread_own(2, 0, 1 - core, own_b, a1, a2, 1)
+    spread_own(2, 1, 1 - core, own_b, b1, b2, 0)
+    copies.finish()
+    spread_own(2, 0, core, own_s, a1, a2, 1)
+    spread_own(2, 1, core, own_s, b1, b2, 0)
+    out = Copies(sems.at[pl.ds(1, 5)])
+    out.start(b1.at[:, 6:22, 8:24, :], right_hbm)
+    faces(2, a2, weights2, inv2, None)
+    out.start(w2, w2_hbm)
     faces(1, a1, weights1, inv1, diag1)
-    faces(2, a2, weights2, inv2, None)
+    out.start(w1, w1_hbm)
     smooth(2, b2, weights2, inv2, e2, d2, o2, c2)
-    smooth(1, b1, weights1, inv1, e1, d1, o1, c1)
-    right[...] = b1[:, 6:22, 8:24, :]
-    token[...] = jnp.zeros_like(token)
-
-
-def join_kernel(*refs):
-    core, gx, _ = position()
-    even_x = is_even(gx)
-    sum3, weights1, diag1, c1, c2, right = refs[0], refs[1:7], refs[7], refs[8], refs[9], refs[10]
-    x1, own, first, second, slots = refs[11:16]
-    s2, tmp3, tmp2, rest = refs[16:]
+    smooth(1, b1, weights1, inv1, e1, d1, o1, x1)
     combine(sum3, c2, s2, tmp3, tmp2)
 
     def finish(i, _):
-        x1[:, i] = DAMPING * (c1[:, i] + tmp2[:, i // 2 - 1])
+        x1[:, i] = DAMPING * (x1[:, i] + tmp2[:, i // 2 - 1])
         return 0
 
     lax.fori_loop(5, 23, finish, 0)
+    out.start(x1, x1_hbm)
 
     def residual(i):
         mid, near = weighted(1, i, 2, x1, weights1)
-        res = diag1[:, pl.ds(i, 2)] * (mid - near)
-        at = pl.ds(i - 6, 2)
-        rest[:, at] = right[:, at] - res[:, :, 8:24, :]
+        at = pl.ds(i, 2)
+        res = b1[:, at] - diag1[:, at] * (mid - near)
+        rest[:, pl.ds(i - 6, 2)] = res[:, :, 8:24, :]
 
     blocks(6, 22, 2, residual)
     for c in range(2):
@@ -507,10 +566,11 @@
                 total = part if total is None else total + part
             return total
 
-        def out(k, value):
+        def put(k, value):
             own[c, 32 + k] = value
 
-        restrict_to2(read_pair, out)
+        restrict_to2(read_pair, put)
+    out.start(own, own_hbm)
     for i in range(12):
         put_pair(even_x, first, second, i, own[core, 20 + i], own[core, i])
     for i in range(3):
@@ -519,20 +579,36 @@
         lambda k: own[core, 32 + k, pl.ds(0, 4, 2), :] + own[core, 32 + k, pl.ds(1, 4, 2), :]
     )
     slots[1:] = jnp.broadcast_to(slots[0:1], (slots.shape[0] - 1, 4, 128))
-
-
-def second_kernel(*refs):
+    out.finish()
+
+
+def second_kernel(
+    own_hbm, w1_hbm, w2_hbm, x1_hbm, right_hbm,
+    x_one_a, x_two_a, y_one_a, y_two_a, x_one_b, x_two_b, y_one_b, y_two_b, sum3,
+    out_x, out_r,
+    w1, w2, x1, right, own, b1, e1, d1, o1, c1, b2, e2, d2, o2, c2, s2, tmp3, tmp2, rest, sems,
+):
     core, gx, gy = position()
-    own, mine, theirs, sum3 = refs[0], refs[1:5], refs[5:9], refs[9]
-    weights1, inv1, diag1 = refs[10:16], refs[16], refs[17]
-    weights2, inv2 = refs[18:24], refs[24]
-    x1, right, out_x, out_r = refs[25:29]
-    b1, e1, d1, o1, c1, b2, e2, d2, o2, c2, s2, tmp3, tmp2, rest = refs[29:]
     even_x, even_y = is_even(gx), is_even(gy)
-    for c, parts in ((core, mine), (1 - core, theirs)):
-        spread(1, 0, c, even_x, even_y, own.at[c], *parts, b1, b2, 0)
+    copies = Copies(sems)
+    for src, dst in (
+        (own_hbm, own), (w2_hbm, w2), (w1_hbm, w1), (x1_hbm, x1), (right_hbm, right)
+    ):
+        copies.start(src, dst)
+    weights1, inv1 = split3(w1)
+    diag1 = w1.at[7]
+    weights2, inv2 = split3(w2)
+    spread(1, 0, core, even_x, even_y, x_one_a, x_two_a, y_one_a, y_two_a, b1, b2, 0)
+    spread(1, 0, 1 - core, even_x, even_y, x_one_b, x_two_b, y_one_b, y_two_b, b1, b2, 0)
+    copies.made[0].wait()
+    for c in range(2):
+        spread_own(1, 0, c, own.at[c], b1, b2, 0)
+    copies.made[1].wait()
     smooth(2, b2, weights2, inv2, e2, d2, o2, c2)
+    copies.made[2].wait()
     smooth(1, b1, weights1, inv1, e1, d1, o1, c1)
+    copies.made[3].wait()
+    copies.made[4].wait()
     combine(sum3, c2, s2, tmp3, tmp2)
 
     def finish(i, _):
@@ -540,6 +616,7 @@
         return 0
 
     lax.fori_loop(5, 23, finish, 0)
+    field = copies.start(c1.at[core, 6:22, 8:24, :], out_x)
 
     def residual(i):
         mid, near = weighted(1, i, 2, c1, weights1)
@@ -548,20 +625,32 @@
         rest[:, at] = right[:, at] - res[:, :, 8:24, :]
 
     blocks(6, 22, 2, residual)
-    out_r[...] = rest[core]
-    out_x[...] = c1[core, 6:22, 8:24, :]
-
-
-def call(kernel, outs, scratch, *args):
-    smem = pl.BlockSpec(memory_space=pltpu.SMEM)
+    done = copies.start(rest.at[core], out_r)
+    field.wait()
+    done.wait()
+
+
+def call(kernel, outs, scratch, *args, hbm_in=(), hbm_out=(), sems=0, limit=8):
     vmem = pl.BlockSpec(memory_space=pltpu.VMEM)
+    hbm = pl.BlockSpec(memory_space=pltpu.HBM)
+    specs = [vmem for _ in args]
+    args = list(args)
+    for i in hbm_in:
+        specs[i] = hbm
+        args[i] = pltpu.with_memory_space_constraint(args[i], pltpu.HBM)
+    scratch = [pltpu.VMEM(s, F32) for s in scratch]
+    if sems:
+        scratch.append(pltpu.SemaphoreType.DMA((sems,)))
     return pl.pallas_call(
         kernel,
-        out_shape=[jax.ShapeDtypeStruct(s, F32) for s in outs],
-        in_specs=[smem if a.shape[-1] != 128 else vmem for a in args],
-        out_specs=[vmem for _ in outs],
-        scratch_shapes=[pltpu.VMEM(s, F32) for s in scratch],
-        compiler_params=pltpu.CompilerParams(vmem_limit_bytes=56 * 1024 * 1024),
+        out_shape=[
+            pltpu.HBM(s, F32) if i in hbm_out else jax.ShapeDtypeStruct(s, F32)
+            for i, s in enumerate(outs)
+        ],
+        in_specs=specs,
+        out_specs=[hbm if i in hbm_out else vmem for i in range(len(outs))],
+        scratch_shapes=scratch,
+        compiler_params=pltpu.CompilerParams(vmem_limit_bytes=limit * 1024 * 1024),
         interpret=INTERPRET,
     )(*args)
 
@@ -586,19 +675,18 @@
 def on_device(right_side, coefficient):
     gx_n, gy_n = lax.axis_size("gx"), lax.axis_size("gy")
     count = gx_n * gy_n
-    _, keeps, pushes = cheb_steps(COARSE_DEGREE, LOW_COARSE, HIGH_BOUND)
-    table = jnp.array([keeps, pushes], F32)
     s1, s2, s3 = (2, 28, 32, 128), (2, 10, 24, 128), (2, 5, 24, 128)
     p2, p3 = (2, 12, 24, 128), (2, 7, 24, 128)
     s4 = (gx_n // 2, gy_n * 2, 128)
     sum3 = (2, 3, 24, 128)
     tmps = [(2, 6, 24, 128), sum3, (2, 12, 32, 128), (2, 16, 16, 128)]
 
-    own, first, second, slots = call(
+    own, own_kept, first, second, slots = call(
         prepare_kernel,
-        [(72, 8, 128), (30, 8, 128), (30, 8, 128), (count, 8, 128)], [], coefficient, right_side,
-    )
-    own_o = swap(own)
+        [(72, 8, 128), (72, 8, 128), (30, 8, 128), (30, 8, 128), (count, 8, 128)],
+        [(16, 16, 128)] * 2, coefficient, right_side, hbm_in=(0, 1), hbm_out=(1,), sems=3,
+    )
+    own_o = swap(own_kept)
     x_one, x_two = trade(first, second, "gx")
     r3 = everywhere(slots)
     x_one_o, x_two_o = swap(x_one), swap(x_two)
@@ -608,21 +696,20 @@
     )
     y_one, y_two = trade(first, second, "gy")
     y_one_o, y_two_o = swap(y_one), swap(y_two)
-    *coefs, c1, c2, right, token = call(
-        first_kernel, [s1] * 8 + [s2] * 7 + [s1, s2, (2, 16, 16, 128), (8, 128)],
-        [s1, s1, s1, s1, s1, p2, s2, s2, s2, s2],
-        own, x_one, x_two, y_one, y_two, own_o, x_one_o, x_two_o, y_one_o, y_two_o,
-    )
     flat = (count * 8, 128)
-    *coarse, c3 = call(
-        functools.partial(coarse_kernel, gx_n, gy_n, True),
-        [s3] * 7 + [s4] * 4 + [sum3], [p3, s3, s3, s3, s3, s3, s4],
-        table, token, r3, r3_o, r3.reshape(flat), r3_o.reshape(flat),
-    )
-    x1, own, first, second, slots = call(
-        join_kernel,
-        [s1, (2, 36, 8, 128), (15, 8, 128), (15, 8, 128), (count, 4, 128)], tmps,
-        c3, *coefs[:6], coefs[7], c1, c2, right,
+    w1s, w2s, w3s, w4s = (8,) + s1, (7,) + s2, (7,) + s3, (4,) + s4
+    c3, w3, w4 = call(
+        functools.partial(coarse_first_kernel, gx_n, gy_n), [sum3, w3s, w4s],
+        [w3s, w4s, p3, s3, s3, s3, s3, s3, s4],
+        r3, r3_o, r3.reshape(flat), r3_o.reshape(flat), hbm_out=(1, 2), sems=2, limit=12,
+    )
+    w1, w2, x1, right, own_kept, own, first, second, slots = call(
+        first_kernel,
+        [w1s, w2s, s1, (2, 16, 16, 128), (2, 36, 8, 128), (2, 36, 8, 128), (15, 8, 128),
+         (15, 8, 128), (count, 4, 128)],
+        [w1s, w2s, s1, (72, 8, 128), s1, s1, s1, s1, s1, p2, s2, s2, s2, s2, s2] + tmps,
+        own_kept, x_one, x_two, y_one, y_two, own_o, x_one_o, x_two_o, y_one_o, y_two_o, c3,
+        hbm_in=(0,), hbm_out=(0, 1, 2, 3, 4), sems=6, limit=28,
     )
     x_one, x_two = trade(first, second, "gx")
     r3 = everywhere(slots)
@@ -632,18 +719,21 @@
         functools.partial(sides_kernel, 1), [(38, 8, 128)] * 2, [], own, x_one, x_two
     )
     y_one, y_two = trade(first, second, "gy")
+    y_one_o, y_two_o = swap(y_one), swap(y_two)
     flat = (count * 4, 128)
     (c3,) = call(
-        functools.partial(coarse_kernel, gx_n, gy_n, False),
-        [sum3], [s3, s3, s3, s3, s3, s4],
-        table, token, r3, r3_o, r3.reshape(flat), r3_o.reshape(flat), *coarse,
-    )
-    y_one_o, y_two_o = swap(y_one), swap(y_two)
+        functools.partial(coarse_second_kernel, gx_n, gy_n),
+        [sum3], [w3s, w4s, s3, s3, s3, s3, s3, s4],
+        r3, r3_o, r3.reshape(flat), r3_o.reshape(flat), w3, w4,
+        hbm_in=(4, 5), sems=2, limit=12,
+    )
     solution_field, residual = call(
         second_kernel, [(16, 16, 128)] * 2,
-        [s1, s1, s1, s1, s1, s2, s2, s2, s2, s2] + tmps,
-        own, x_one, x_two, y_one, y_two, x_one_o, x_two_o, y_one_o, y_two_o, c3,
-        *coefs, x1, right,
+        [w1s, w2s, s1, (2, 16, 16, 128), (2, 36, 8, 128), s1, s1, s1, s1, s1, s2, s2, s2, s2, s2]
+        + tmps,
+        own_kept, w1, w2, x1, right,
+        x_one, x_two, y_one, y_two, x_one_o, x_two_o, y_one_o, y_two_o, c3,
+        hbm_in=(0, 1, 2, 3, 4), hbm_out=(0, 1), sems=7, limit=28,
     )
     return solution_field, residual
 

time: 139 us -> 120 us (0.86)
  Pallas kernels: 53.7 us -> 37.5 us
  waiting for transfers between devices: 15.9 us -> 25.9 us
  starting transfers between devices: 61.8 us -> 53.6 us
  local copies, waits for them, and re-layouts: 5.08 us -> 0 us
    pallas_call x8 -> x7, Pallas kernels: 53.7 us -> 37.5 us  [call(): pl.pallas_call(kernel, out_shape=[pltpu.HBM(s, F32) if i in hbm_out else...]
    all_to_all x2, waiting for transfers between devices: 0.01 us -> 11.6 us  [everywhere(): return lax.all_to_all(slots, ('gx', 'gy'), 0, 0, tiled=True)]
    unnamed x52 -> x0, local copies, waits for them, and re-layouts: 5.08 us -> none
    ppermute x4, waiting for transfers between devices: 0.62 us -> 5.37 us  [trade(): one = lax.ppermute(first, axis, pairs)]
    ppermute x4, waiting for transfers between devices: 12.8 us -> 8.86 us  [trade(): two = lax.ppermute(second, axis, others)]
    ppermute x11, starting transfers between devices: 15.1 us -> 12.1 us  [swap(): return lax.ppermute(x, 'grp', [(0, 1), (1, 0)])]
    all_to_all x2, starting transfers between devices: 24.8 us -> 22 us  [everywhere(): return lax.all_to_all(slots, ('gx', 'gy'), 0, 0, tiled=True)]
    ppermute x11, waiting for transfers between devices: 2.53 us -> 0.03 us  [swap(): return lax.ppermute(x, 'grp', [(0, 1), (1, 0)])]
  transfers between devices with their start and end apart: 21 -> 21, of which waited for: 7 -> 5; matrix products, arithmetic and copies ran while one was open for 0% -> 0% of each run, Pallas kernels for 18% -> 7%
where the time goes in v5:
time: 120 us; the launch traced here: 118 us
  starting transfers between devices  53.6 us (45%)
  Pallas kernels  37.5 us (31%)
  waiting for transfers between devices  25.9 us (22%)
    pallas_call x7, Pallas kernels, call(): pl.pallas_call(kernel, out_shape=[pltpu.HBM(s, F32) if i in hbm_out else...  37.5 us
    all_to_all x2, starting transfers between devices, everywhere(): return lax.all_to_all(slots, ('gx', 'gy'), 0, 0, tiled=True)  22 us
    ppermute x4, starting transfers between devices, trade(): two = lax.ppermute(second, axis, others)  16.3 us
    ppermute x11, starting transfers between devices, swap(): return lax.ppermute(x, 'grp', [(0, 1), (1, 0)])  12.1 us
    all_to_all x2, waiting for transfers between devices, everywhere(): return lax.all_to_all(slots, ('gx', 'gy'), 0, 0, tiled=True)  11.6 us
    ppermute x4, waiting for transfers between devices, trade(): two = lax.ppermute(second, axis, others)  8.86 us
    ppermute x4, waiting for transfers between devices, trade(): one = lax.ppermute(first, axis, pairs)  5.37 us
    ppermute x4, starting transfers between devices, trade(): one = lax.ppermute(first, axis, pairs)  3.22 us
  transfers between devices with their start and end apart: 21, of which 5 were waited for; matrix products, arithmetic and copies ran while one was open for 0% of the time, Pallas kernels for 7%

profile of v5, /device:TPU:27, one launch (start us, length us, event | category | flops | bytes accessed | tf_op | source)
XLA Modules:
  0.0 118.0 jit_solution(5917617402192565649)
XLA Ops:
  0.6 3.4 %shard_map.41 = (f32[72,8,128]{2,1,0:T(8,128)S(1)}, f32[72,8,128]{2,1,0:T(8,128)}, f32[30,8,128]{2,1,0:T(8,128)S(1)}, f32[30,8,128]{2,1,0:T(8,128)S(1)}, f32[128,8,128]{2,1,0:T(8,128)}) custom-call(f32[16,16,128]{2,1,0:T(8,128)} %a_hbm.1, f32[16,16,128]{2,1,0:T(8,128)} %b_hbm.1), custom_call_target="tpu_custom_call" | custom-call | tf_op jit(solution)/shard_map/pallas_call | solution.py:644
  4.0 14.8 %all-to-all-start = ((f32[128,8,128]{2,1,0:T(8,128)}), f32[128,8,128]{2,1,0:T(8,128)S(1)}, u32[]{:S(2)}, u32[]{:S(2)}) async-start(f32[128,8,128]{2,1,0:T(8,128)} %get-tuple-element.29), calls=%async_computation | async-start | bytes 1048576 | tf_op jit(solution)/shard_map/all_to_all | solution.py:672
  18.9 0.6 collective-permute-start
  19.4 4.6 %collective-permute-start.1 = (f32[30,8,128]{2,1,0:T(8,128)S(1)}, f32[30,8,128]{2,1,0:T(8,128)S(1)}, u32[]{:S(2)}, u32[]{:S(2)}) collective-permute-start(f32[30,8,128]{2,1,0:T(8,128)S(1)} %get-tuple-element.25), channel_id=1, source_target_pairs={{16,32},{32,16},{48,64},{64,48},{80,96},{96,80},{17,33},{33,17},{4... | collective-permute-start | bytes 368648 | tf_op jit(solution)/shard_map/ppermute | solution.py:663
  24.0 11.6 %all-to-all-done.r3_a = f32[128,8,128]{2,1,0:T(8,128)S(1)} async-done(((f32[128,8,128]{2,1,0:T(8,128)}), f32[128,8,128]{2,1,0:T(8,128)S(1)}, u32[]{:S(2)}, u32[]{:S(2)}) %all-to-all-start) | async-done | bytes 524320 | tf_op jit(solution)/shard_map/all_to_all | solution.py:672
  35.6 2.5 %collective-permute-start.9 = (f32[128,8,128]{2,1,0:T(8,128)S(1)}, f32[128,8,128]{2,1,0:T(8,128)S(1)}, u32[]{:S(2)}, u32[]{:S(2)}) collective-permute-start(f32[128,8,128]{2,1,0:T(8,128)S(1)} %all-to-all-done.r3_a), channel_id=1, source_target_pairs={{0,128},{128,0},{1,129},{129,1},{2,130},{130,2},{3,131},{131,3},{4... | collective-permute-start | bytes 1572872 | tf_op jit(solution)/shard_map/ppermute | solution.py:668
  38.2 0.9 collective-permute-start.2
  39.1 2.8 %collective-permute-start.3 = (f32[76,8,128]{2,1,0:T(8,128)S(1)}, f32[76,8,128]{2,1,0:T(8,128)S(1)}, u32[]{:S(2)}, u32[]{:S(2)}) collective-permute-start(f32[76,8,128]{2,1,0:T(8,128)S(1)} %get-tuple-element.28), channel_id=1, source_target_pairs={{1,2},{2,1},{3,4},{4,3},{5,6},{6,5},{7,8},{8,7},{9,10},{10,9},{11,... | collective-permute-start | bytes 933896 | tf_op jit(solution)/shard_map/ppermute | solution.py:663
  41.8 5.4 %collective-permute-done.2.y_one_a = f32[76,8,128]{2,1,0:T(8,128)S(1)} collective-permute-done((f32[76,8,128]{2,1,0:T(8,128)S(1)}, f32[76,8,128]{2,1,0:T(8,128)S(1)}, u32[]{:S(2)}, u32[]{:S(2)}) %collective-permute-start.2) | collective-permute-done | bytes 311328 | tf_op jit(solution)/shard_map/ppermute | solution.py:662
  47.2 0.9 collective-permute-start.7
  48.1 3.6 %collective-permute-done.3.y_two_a = f32[76,8,128]{2,1,0:T(8,128)S(1)} collective-permute-done((f32[76,8,128]{2,1,0:T(8,128)S(1)}, f32[76,8,128]{2,1,0:T(8,128)S(1)}, u32[]{:S(2)}, u32[]{:S(2)}) %collective-permute-start.3) | collective-permute-done | bytes 311328 | tf_op jit(solution)/shard_map/ppermute | solution.py:663
  51.7 1.1 collective-permute-start.8
  53.4 4.2 %shard_map.43 = (f32[2,3,24,128]{3,2,1,0:T(8,128)S(1)}, f32[7,2,5,24,128]{4,3,2,1,0:T(8,128)}, f32[4,4,32,128]{3,2,1,0:T(8,128)}) custom-call(f32[128,8,128]{2,1,0:T(8,128)S(1)} %all-to-all-done.r3_a, f32[128,8,128]{2,1,0:T(8,128)S(1)} %collective-permute-done.9.r3_b, f32[1024,128]{1,0:T(8,128)S(1)} %bitcast.4, f32[1024,128]{1,0:T(8,128)S(1)} %bitcast.6), custom_call_target="tpu_custom_call" | custom-call | tf_op jit(solution)/shard_map/pallas_call | solution.py:644
  57.6 14.6 %shard_map.44 = (f32[8,2,28,32,128]{4,3,2,1,0:T(8,128)}, f32[7,2,10,24,128]{4,3,2,1,0:T(8,128)}, f32[2,28,32,128]{3,2,1,0:T(8,128)}, f32[2,16,16,128]{3,2,1,0:T(...) custom-call(f32[72,8,128]{2,1,0:T(8,128)} %get-tuple-element.23.own_, ...), custom_call_target="tpu_custom_call" | custom-call | tf_op jit(solution)/shard_map/pallas_call | solution.py:644
  72.2 7.2 %all-to-all-start.1 = ((f32[128,4,128]{2,1,0:T(4,128)}), f32[128,4,128]{2,1,0:T(4,128)S(1)}, u32[]{:S(2)}, u32[]{:S(2)}) async-start(f32[128,4,128]{2,1,0:T(4,128)} %get-tuple-element.41), calls=%async_computation.1 | async-start | bytes 524288 | tf_op jit(solution)/shard_map/all_to_all | solution.py:672
  79.9 4.6 %collective-permute-start.11 = (f32[15,8,128]{2,1,0:T(8,128)S(1)}, f32[15,8,128]{2,1,0:T(8,128)S(1)}, u32[]{:S(2)}, u32[]{:S(2)}) collective-permute-start(f32[15,8,128]{2,1,0:T(8,128)S(1)} %get-tuple-element.37), channel_id=1, source_target_pairs={{16,32},{32,16},{48,64},{64,48},{80,96},{96,80},{17,33},{33,17},{4... | collective-permute-start | bytes 184328 | tf_op jit(solution)/shard_map/ppermute | solution.py:663
  84.5 4.4 %collective-permute-done.11.two.x_two_a = f32[15,8,128]{2,1,0:T(8,128)S(1)} collective-permute-done((f32[15,8,128]{2,1,0:T(8,128)S(1)}, f32[15,8,128]{2,1,0:T(8,128)S(1)}, u32[]{:S(2)}, u32[]{:S(2)}) %collective-permute-start.11) | collective-permute-done | bytes 61472 | tf_op jit(solution)/shard_map/ppermute | solution.py:663
  89.0 1.3 %collective-permute-start.12 = (f32[38,8,128]{2,1,0:T(8,128)S(1)}, f32[38,8,128]{2,1,0:T(8,128)S(1)}, u32[]{:S(2)}, u32[]{:S(2)}) collective-permute-start(f32[38,8,128]{2,1,0:T(8,128)S(1)} %get-tuple-element.39), channel_id=1, source_target_pairs={{0,1},{1,0},{2,3},{3,2},{4,5},{5,4},{6,7},{7,6},{8,9},{9,8},{10,11... | collective-permute-start | bytes 466952 | tf_op jit(solution)/shard_map/ppermute | solution.py:662
  90.2 4.3 %collective-permute-start.13 = (f32[38,8,128]{2,1,0:T(8,128)S(1)}, f32[38,8,128]{2,1,0:T(8,128)S(1)}, u32[]{:S(2)}, u32[]{:S(2)}) collective-permute-start(f32[38,8,128]{2,1,0:T(8,128)S(1)} %get-tuple-element.40), channel_id=1, source_target_pairs={{1,2},{2,1},{3,4},{4,3},{5,6},{6,5},{7,8},{8,7},{9,10},{10,9},{11,... | collective-permute-start | bytes 466952 | tf_op jit(solution)/shard_map/ppermute | solution.py:663
  94.6 2.8 %collective-permute-start.18 = (f32[128,4,128]{2,1,0:T(4,128)S(1)}, f32[128,4,128]{2,1,0:T(4,128)S(1)}, u32[]{:S(2)}, u32[]{:S(2)}) collective-permute-start(f32[128,4,128]{2,1,0:T(4,128)S(1)} %all-to-all-done.1.r3_a), channel_id=1, source_target_pairs={{0,128},{128,0},{1,129},{129,1},{2,130},{130,2},{3,131},{131,3},{4... | collective-permute-start | bytes 786440 | tf_op jit(solution)/shard_map/ppermute | solution.py:668
  97.5 0.8 collective-permute-done.13.y_two_a
  98.3 3.7 %collective-permute-start.17 = (f32[38,8,128]{2,1,0:T(8,128)S(1)}, f32[38,8,128]{2,1,0:T(8,128)S(1)}, u32[]{:S(2)}, u32[]{:S(2)}) collective-permute-start(f32[38,8,128]{2,1,0:T(8,128)S(1)} %collective-permute-done.13.y_two_a), channel_id=1, source_target_pairs={{0,128},{128,0},{1,129},{129,1},{2,130},{130,2},{3,131},{131,3},{4... | collective-permute-start | bytes 466952 | tf_op jit(solution)/shard_map/ppermute | solution.py:668
  102.5 4.0 %shard_map.46.sum3 = f32[2,3,24,128]{3,2,1,0:T(8,128)S(1)} custom-call(f32[128,4,128]{2,1,0:T(4,128)S(1)} %all-to-all-done.1.r3_a, f32[128,4,128]{2,1,0:T(4,128)S(1)} %collective-permute-done.18.r3_b, f32[512,128]{1,0:T(8,128)S(1)} %bitcast.5, f32[512,128]{1,0:T(8,128)S(1)} %bitcast.7, f32[7,2,5,24,128]{4,3,2,1,0:T(8,128)} %get-tuple-element.42.w3_hbm, ...), custom_call_target="tpu_custom_call" | custom-call | tf_op jit(solution)/shard_map/pallas_call | solution.py:644
  106.5 11.3 %shard_map.47 = (f32[16,16,128]{2,1,0:T(8,128)}, f32[16,16,128]{2,1,0:T(8,128)}) custom-call(f32[2,36,8,128]{3,2,1,0:T(8,128)} %get-tuple-element.31.own_hbm, f32[8,2,28,32,128]{4,3,2,1,0:T(8,128)} %get-tuple-element.32.w1_hbm, f32[7,2,10,24,128]{4,3,2,1,0:T(8,128)} %get-tuple-element.33.w2_hbm, f32[2,28,32,128]{3,2,1,0:T(8,128)} %get-tuple-element.34.x1_hbm, ...), custom_call_target="tpu_custom_call" | custom-call | tf_op jit(solution)/shard_map/pallas_call | solution.py:644
  (25 shorter events, 1.8 us)
Async XLA Ops:
  4.0 31.6 %all-to-all-start = ((f32[128,8,128]{2,1,0:T(8,128)}), f32[128,8,128]{2,1,0:T(8,128)S(1)}, u32[]{:S(2)}, u32[]{:S(2)}) async-start(f32[128,8,128]{2,1,0:T(8,128)} %get-tuple-element.29), calls=%async_computation | async-start | bytes 1048576 | tf_op jit(solution)/shard_map/all_to_all | solution.py:672
  18.9 19.3 %collective-permute-start = (f32[30,8,128]{2,1,0:T(8,128)S(1)}, f32[30,8,128]{2,1,0:T(8,128)S(1)}, u32[]{:S(2)}, u32[]{:S(2)}) collective-permute-start(f32[30,8,128]{2,1,0:T(8,128)S(1)} %get-tuple-element.24), channel_id=1, source_target_pairs={{0,16},{16,0},{32,48},{48,32},{64,80},{80,64},{96,112},{112,96},{1... | collective-permute-start | bytes 368648 | tf_op jit(solution)/shard_map/ppermute | solution.py:662
  19.4 18.7 %collective-permute-start.1 = (f32[30,8,128]{2,1,0:T(8,128)S(1)}, f32[30,8,128]{2,1,0:T(8,128)S(1)}, u32[]{:S(2)}, u32[]{:S(2)}) collective-permute-start(f32[30,8,128]{2,1,0:T(8,128)S(1)} %get-tuple-element.25), channel_id=1, source_target_pairs={{16,32},{32,16},{48,64},{64,48},{80,96},{96,80},{17,33},{33,17},{4... | collective-permute-start | bytes 368648 | tf_op jit(solution)/shard_map/ppermute | solution.py:663
  35.6 17.7 %collective-permute-start.9 = (f32[128,8,128]{2,1,0:T(8,128)S(1)}, f32[128,8,128]{2,1,0:T(8,128)S(1)}, u32[]{:S(2)}, u32[]{:S(2)}) collective-permute-start(f32[128,8,128]{2,1,0:T(8,128)S(1)} %all-to-all-done.r3_a), channel_id=1, source_target_pairs={{0,128},{128,0},{1,129},{129,1},{2,130},{130,2},{3,131},{131,3},{4... | collective-permute-start | bytes 1572872 | tf_op jit(solution)/shard_map/ppermute | solution.py:668
  38.2 9.0 %collective-permute-start.2 = (f32[76,8,128]{2,1,0:T(8,128)S(1)}, f32[76,8,128]{2,1,0:T(8,128)S(1)}, u32[]{:S(2)}, u32[]{:S(2)}) collective-permute-start(f32[76,8,128]{2,1,0:T(8,128)S(1)} %get-tuple-element.27), channel_id=1, source_target_pairs={{0,1},{1,0},{2,3},{3,2},{4,5},{5,4},{6,7},{7,6},{8,9},{9,8},{10,11... | collective-permute-start | bytes 933896 | tf_op jit(solution)/shard_map/ppermute | solution.py:662
  39.1 12.6 %collective-permute-start.3 = (f32[76,8,128]{2,1,0:T(8,128)S(1)}, f32[76,8,128]{2,1,0:T(8,128)S(1)}, u32[]{:S(2)}, u32[]{:S(2)}) collective-permute-start(f32[76,8,128]{2,1,0:T(8,128)S(1)} %get-tuple-element.28), channel_id=1, source_target_pairs={{1,2},{2,1},{3,4},{4,3},{5,6},{6,5},{7,8},{8,7},{9,10},{10,9},{11,... | collective-permute-start | bytes 933896 | tf_op jit(solution)/shard_map/ppermute | solution.py:663
  47.2 10.4 %collective-permute-start.7 = (f32[76,8,128]{2,1,0:T(8,128)S(1)}, f32[76,8,128]{2,1,0:T(8,128)S(1)}, u32[]{:S(2)}, u32[]{:S(2)}) collective-permute-start(f32[76,8,128]{2,1,0:T(8,128)S(1)} %collective-permute-done.2.y_one_a), channel_id=1, source_target_pairs={{0,128},{128,0},{1,129},{129,1},{2,130},{130,2},{3,131},{131,3},{4... | collective-permute-start | bytes 933896 | tf_op jit(solution)/shard_map/ppermute | solution.py:668
  51.7 5.9 %collective-permute-start.8 = (f32[76,8,128]{2,1,0:T(8,128)S(1)}, f32[76,8,128]{2,1,0:T(8,128)S(1)}, u32[]{:S(2)}, u32[]{:S(2)}) collective-permute-start(f32[76,8,128]{2,1,0:T(8,128)S(1)} %collective-permute-done.3.y_two_a), channel_id=1, source_target_pairs={{0,128},{128,0},{1,129},{129,1},{2,130},{130,2},{3,131},{131,3},{4... | collective-permute-start | bytes 933896 | tf_op jit(solution)/shard_map/ppermute | solution.py:668
  52.8 4.7 %collective-permute-start.4 = (f32[72,8,128]{2,1,0:T(8,128)}, f32[72,8,128]{2,1,0:T(8,128)S(1)}, u32[]{:S(2)}, u32[]{:S(2)}) collective-permute-start(f32[72,8,128]{2,1,0:T(8,128)} %get-tuple-element.23.own_a), channel_id=1, source_target_pairs={{0,128},{128,0},{1,129},{129,1},{2,130},{130,2},{3,131},{131,3},{4... | collective-permute-start | bytes 884744 | tf_op jit(solution)/shard_map/ppermute | solution.py:668
  52.8 4.7 %collective-permute-start.5 = (f32[30,8,128]{2,1,0:T(8,128)S(1)}, f32[30,8,128]{2,1,0:T(8,128)S(1)}, u32[]{:S(2)}, u32[]{:S(2)}) collective-permute-start(f32[30,8,128]{2,1,0:T(8,128)S(1)} %collective-permute-done.one.x_one_a), channel_id=1, source_target_pairs={{0,128},{128,0},{1,129},{129,1},{2,130},{130,2},{3,131},{131,3},{4... | collective-permute-start | bytes 368648 | tf_op jit(solution)/shard_map/ppermute | solution.py:668
  53.4 4.2 %collective-permute-start.6 = (f32[30,8,128]{2,1,0:T(8,128)S(1)}, f32[30,8,128]{2,1,0:T(8,128)S(1)}, u32[]{:S(2)}, u32[]{:S(2)}) collective-permute-start(f32[30,8,128]{2,1,0:T(8,128)S(1)} %collective-permute-done.1.two.x_two_a), channel_id=1, source_target_pairs={{0,128},{128,0},{1,129},{129,1},{2,130},{130,2},{3,131},{131,3},{4... | collective-permute-start | bytes 368648 | tf_op jit(solution)/shard_map/ppermute | solution.py:668
  72.2 22.4 %all-to-all-start.1 = ((f32[128,4,128]{2,1,0:T(4,128)}), f32[128,4,128]{2,1,0:T(4,128)S(1)}, u32[]{:S(2)}, u32[]{:S(2)}) async-start(f32[128,4,128]{2,1,0:T(4,128)} %get-tuple-element.41), calls=%async_computation.1 | async-start | bytes 524288 | tf_op jit(solution)/shard_map/all_to_all | solution.py:672
  79.4 5.2 %collective-permute-start.10 = (f32[15,8,128]{2,1,0:T(8,128)S(1)}, f32[15,8,128]{2,1,0:T(8,128)S(1)}, u32[]{:S(2)}, u32[]{:S(2)}) collective-permute-start(f32[15,8,128]{2,1,0:T(8,128)S(1)} %get-tuple-element.36), channel_id=1, source_target_pairs={{0,16},{16,0},{32,48},{48,32},{64,80},{80,64},{96,112},{112,96},{1... | collective-permute-start | bytes 184328 | tf_op jit(solution)/shard_map/ppermute | solution.py:662
  79.9 9.0 %collective-permute-start.11 = (f32[15,8,128]{2,1,0:T(8,128)S(1)}, f32[15,8,128]{2,1,0:T(8,128)S(1)}, u32[]{:S(2)}, u32[]{:S(2)}) collective-permute-start(f32[15,8,128]{2,1,0:T(8,128)S(1)} %get-tuple-element.37), channel_id=1, source_target_pairs={{16,32},{32,16},{48,64},{64,48},{80,96},{96,80},{17,33},{33,17},{4... | collective-permute-start | bytes 184328 | tf_op jit(solution)/shard_map/ppermute | solution.py:663
  89.0 8.4 %collective-permute-start.12 = (f32[38,8,128]{2,1,0:T(8,128)S(1)}, f32[38,8,128]{2,1,0:T(8,128)S(1)}, u32[]{:S(2)}, u32[]{:S(2)}) collective-permute-start(f32[38,8,128]{2,1,0:T(8,128)S(1)} %get-tuple-element.39), channel_id=1, source_target_pairs={{0,1},{1,0},{2,3},{3,2},{4,5},{5,4},{6,7},{7,6},{8,9},{9,8},{10,11... | collective-permute-start | bytes 466952 | tf_op jit(solution)/shard_map/ppermute | solution.py:662
  90.2 8.1 %collective-permute-start.13 = (f32[38,8,128]{2,1,0:T(8,128)S(1)}, f32[38,8,128]{2,1,0:T(8,128)S(1)}, u32[]{:S(2)}, u32[]{:S(2)}) collective-permute-start(f32[38,8,128]{2,1,0:T(8,128)S(1)} %get-tuple-element.40), channel_id=1, source_target_pairs={{1,2},{2,1},{3,4},{4,3},{5,6},{6,5},{7,8},{8,7},{9,10},{10,9},{11,... | collective-permute-start | bytes 466952 | tf_op jit(solution)/shard_map/ppermute | solution.py:663
  94.6 7.9 %collective-permute-start.18 = (f32[128,4,128]{2,1,0:T(4,128)S(1)}, f32[128,4,128]{2,1,0:T(4,128)S(1)}, u32[]{:S(2)}, u32[]{:S(2)}) collective-permute-start(f32[128,4,128]{2,1,0:T(4,128)S(1)} %all-to-all-done.1.r3_a), channel_id=1, source_target_pairs={{0,128},{128,0},{1,129},{129,1},{2,130},{130,2},{3,131},{131,3},{4... | collective-permute-start | bytes 786440 | tf_op jit(solution)/shard_map/ppermute | solution.py:668
  97.4 9.1 %collective-permute-start.16 = (f32[38,8,128]{2,1,0:T(8,128)S(1)}, f32[38,8,128]{2,1,0:T(8,128)S(1)}, u32[]{:S(2)}, u32[]{:S(2)}) collective-permute-start(f32[38,8,128]{2,1,0:T(8,128)S(1)} %collective-permute-done.12.y_one_a), channel_id=1, source_target_pairs={{0,128},{128,0},{1,129},{129,1},{2,130},{130,2},{3,131},{131,3},{4... | collective-permute-start | bytes 466952 | tf_op jit(solution)/shard_map/ppermute | solution.py:668
  98.3 8.2 %collective-permute-start.17 = (f32[38,8,128]{2,1,0:T(8,128)S(1)}, f32[38,8,128]{2,1,0:T(8,128)S(1)}, u32[]{:S(2)}, u32[]{:S(2)}) collective-permute-start(f32[38,8,128]{2,1,0:T(8,128)S(1)} %collective-permute-done.13.y_two_a), channel_id=1, source_target_pairs={{0,128},{128,0},{1,129},{129,1},{2,130},{130,2},{3,131},{131,3},{4... | collective-permute-start | bytes 466952 | tf_op jit(solution)/shard_map/ppermute | solution.py:668
  102.0 4.5 %collective-permute-start.14 = (f32[15,8,128]{2,1,0:T(8,128)S(1)}, f32[15,8,128]{2,1,0:T(8,128)S(1)}, u32[]{:S(2)}, u32[]{:S(2)}) collective-permute-start(f32[15,8,128]{2,1,0:T(8,128)S(1)} %collective-permute-done.10.one.x_one_a), channel_id=1, source_target_pairs={{0,128},{128,0},{1,129},{129,1},{2,130},{130,2},{3,131},{131,3},{4... | collective-permute-start | bytes 184328 | tf_op jit(solution)/shard_map/ppermute | solution.py:668
  102.0 4.5 %collective-permute-start.15 = (f32[15,8,128]{2,1,0:T(8,128)S(1)}, f32[15,8,128]{2,1,0:T(8,128)S(1)}, u32[]{:S(2)}, u32[]{:S(2)}) collective-permute-start(f32[15,8,128]{2,1,0:T(8,128)S(1)} %collective-permute-done.11.two.x_two_a), channel_id=1, source_target_pairs={{0,128},{128,0},{1,129},{129,1},{2,130},{130,2},{3,131},{131,3},{4... | collective-permute-start | bytes 184328 | tf_op jit(solution)/shard_map/ppermute | solution.py:668

commit v6 on v5

--- a/solution.py
+++ b/solution.py
@@ -296,40 +296,41 @@
     return lax.rem(index, 2) == 0
 
 
-def prepare_kernel(a_hbm, b_hbm, own, own_hbm, first, second, slots, a, b, sems):
+def prepare_kernel(a_hbm, b_hbm, own, mid_hbm, first, second, slots, a, b, sems):
     even = is_even(position()[1])
     copies = Copies(sems)
     copies.start(a_hbm, a)
     copies.start(b_hbm, b)
     for f, src in enumerate((a, b)):
         copies.made[f].wait()
+
+        def read_pair(k):
+            total = None
+            for x in (2 * k, 2 * k + 1):
+                part = src[x, pl.ds(0, 8, 2), :] + src[x, pl.ds(1, 8, 2), :]
+                total = part if total is None else total + part
+            return total
+
+        values = []
+
+        def out(k, value):
+            own[64 + f * 4 + k] = value
+            values.append(value)
+
+        restrict_to2(read_pair, out)
+        for k in range(3):
+            put_pair(even, first, second, 24 + f * 3 + k, values[k + 1], values[k])
+    keep = copies.start(own.at[64:72], mid_hbm)
+    for f, src in enumerate((a, b)):
         for t in range(2):
             own[pl.ds(f * 32 + t, 16, 2)] = src[:, t * 8:t * 8 + 8, :]
             put_pair(
                 even, first, second, pl.ds(f * 12 + t, 6, 2),
                 src[10:16, t * 8:t * 8 + 8, :], src[0:6, t * 8:t * 8 + 8, :],
             )
-
-        def read_pair(k):
-            total = None
-            for x in (2 * k, 2 * k + 1):
-                part = src[x, pl.ds(0, 8, 2), :] + src[x, pl.ds(1, 8, 2), :]
-                total = part if total is None else total + part
-            return total
-
-        values = []
-
-        def out(k, value):
-            own[64 + f * 4 + k] = value
-            values.append(value)
-
-        restrict_to2(read_pair, out)
-        for k in range(3):
-            put_pair(even, first, second, 24 + f * 3 + k, values[k + 1], values[k])
         slots[0, pl.ds(f, 4, 2), :] = restrict_to3(
             lambda k: own[64 + f * 4 + k, pl.ds(0, 4, 2), :] + own[64 + f * 4 + k, pl.ds(1, 4, 2), :]
         )
-    keep = copies.start(own, own_hbm)
     slots[1:] = jnp.broadcast_to(slots[0:1], (slots.shape[0] - 1, 8, 128))
     keep.wait()
 
@@ -505,14 +506,18 @@
 
 
 def first_kernel(
-    own_a, x_one_a, x_two_a, y_one_a, y_two_a, own_b, x_one_b, x_two_b, y_one_b, y_two_b, sum3,
+    a_hbm, b_hbm, mid_hbm,
+    x_one_a, x_two_a, y_one_a, y_two_a, own_b, x_one_b, x_two_b, y_one_b, y_two_b, sum3,
     w1_hbm, w2_hbm, x1_hbm, right_hbm, own_hbm, own, first, second, slots,
-    w1, w2, x1, own_s, a1, b1, e1, d1, o1, a2, b2, e2, d2, o2, c2, s2, tmp3, tmp2, rest, sems,
+    w1, w2, x1, a1, b1, e1, d1, o1, a2, b2, e2, d2, o2, c2, s2, tmp3, tmp2, rest, sems,
 ):
     core, gx, gy = position()
     even_x, even_y = is_even(gx), is_even(gy)
     copies = Copies(sems)
-    copies.start(own_a, own_s)
+    copies.start(a_hbm, a1.at[core, 6:22, 8:24, :])
+    copies.start(b_hbm, b1.at[core, 6:22, 8:24, :])
+    copies.start(mid_hbm.at[0:4], a2.at[core, 4:8, 8:16, :])
+    copies.start(mid_hbm.at[4:8], b2.at[core, 3:7, 8:16, :])
     halves = (
         (core, (x_one_a, x_two_a, y_one_a, y_two_a)),
         (1 - core, (x_one_b, x_two_b, y_one_b, y_two_b)),
@@ -529,9 +534,7 @@
     spread_own(2, 0, 1 - core, own_b, a1, a2, 1)
     spread_own(2, 1, 1 - core, own_b, b1, b2, 0)
     copies.finish()
-    spread_own(2, 0, core, own_s, a1, a2, 1)
-    spread_own(2, 1, core, own_s, b1, b2, 0)
-    out = Copies(sems.at[pl.ds(1, 5)])
+    out = Copies(sems.at[pl.ds(4, 5)])
     out.start(b1.at[:, 6:22, 8:24, :], right_hbm)
     faces(2, a2, weights2, inv2, None)
     out.start(w2, w2_hbm)
@@ -681,12 +684,12 @@
     sum3 = (2, 3, 24, 128)
     tmps = [(2, 6, 24, 128), sum3, (2, 12, 32, 128), (2, 16, 16, 128)]
 
-    own, own_kept, first, second, slots = call(
+    own, middle, first, second, slots = call(
         prepare_kernel,
-        [(72, 8, 128), (72, 8, 128), (30, 8, 128), (30, 8, 128), (count, 8, 128)],
+        [(72, 8, 128), (8, 8, 128), (30, 8, 128), (30, 8, 128), (count, 8, 128)],
         [(16, 16, 128)] * 2, coefficient, right_side, hbm_in=(0, 1), hbm_out=(1,), sems=3,
     )
-    own_o = swap(own_kept)
+    own_o = swap(own)
     x_one, x_two = trade(first, second, "gx")
     r3 = everywhere(slots)
     x_one_o, x_two_o = swap(x_one), swap(x_two)
@@ -707,9 +710,10 @@
         first_kernel,
         [w1s, w2s, s1, (2, 16, 16, 128), (2, 36, 8, 128), (2, 36, 8, 128), (15, 8, 128),
          (15, 8, 128), (count, 4, 128)],
-        [w1s, w2s, s1, (72, 8, 128), s1, s1, s1, s1, s1, p2, s2, s2, s2, s2, s2] + tmps,
-        own_kept, x_one, x_two, y_one, y_two, own_o, x_one_o, x_two_o, y_one_o, y_two_o, c3,
-        hbm_in=(0,), hbm_out=(0, 1, 2, 3, 4), sems=6, limit=28,
+        [w1s, w2s, s1, s1, s1, s1, s1, s1, p2, s2, s2, s2, s2, s2] + tmps,
+        coefficient, right_side, middle,
+        x_one, x_two, y_one, y_two, own_o, x_one_o, x_two_o, y_one_o, y_two_o, c3,
+        hbm_in=(0, 1, 2), hbm_out=(0, 1, 2, 3, 4), sems=9, limit=28,
     )
     x_one, x_two = trade(first, second, "gx")
     r3 = everywhere(slots)

time: 120 us -> 119 us (level)
  no operation moved by 1% of the time
where the time goes in v6:
time: 119 us; the launch traced here: 117 us
  starting transfers between devices  53.6 us (45%)
  Pallas kernels  37 us (31%)
  waiting for transfers between devices  25.9 us (22%)
    pallas_call x7, Pallas kernels, call(): pl.pallas_call(kernel, out_shape=[pltpu.HBM(s, F32) if i in hbm_out else...  37 us
    all_to_all x2, starting transfers between devices, everywhere(): return lax.all_to_all(slots, ('gx', 'gy'), 0, 0, tiled=True)  22 us
    ppermute x4, starting transfers between devices, trade(): two = lax.ppermute(second, axis, others)  16.4 us
    ppermute x11, starting transfers between devices, swap(): return lax.ppermute(x, 'grp', [(0, 1), (1, 0)])  12.1 us
    all_to_all x2, waiting for transfers between devices, everywhere(): return lax.all_to_all(slots, ('gx', 'gy'), 0, 0, tiled=True)  11.6 us
    ppermute x4, waiting for transfers between devices, trade(): two = lax.ppermute(second, axis, others)  8.88 us
    ppermute x4, waiting for transfers between devices, trade(): one = lax.ppermute(first, axis, pairs)  5.37 us
    ppermute x4, starting transfers between devices, trade(): one = lax.ppermute(first, axis, pairs)  3.2 us
  transfers between devices with their start and end apart: 21, of which 5 were waited for; matrix products, arithmetic and copies ran while one was open for 0% of the time, Pallas kernels for 7%

profile of v6, /device:TPU:27, one launch (start us, length us, event | category | flops | bytes accessed | tf_op | source)
XLA Modules:
  0.0 117.4 jit_solution(542126730461029792)
XLA Ops:
  0.6 2.8 %shard_map.41 = (f32[72,8,128]{2,1,0:T(8,128)S(1)}, f32[8,8,128]{2,1,0:T(8,128)}, f32[30,8,128]{2,1,0:T(8,128)S(1)}, f32[30,8,128]{2,1,0:T(8,128)S(1)}, f32[128,8,128]{2,1,0:T(8,128)}) custom-call(f32[16,16,128]{2,1,0:T(8,128)} %a_hbm.3, f32[16,16,128]{2,1,0:T(8,128)} %b_hbm.3), custom_call_target="tpu_custom_call" | custom-call | tf_op jit(solution)/shard_map/pallas_call | solution.py:647
  3.4 14.8 %all-to-all-start = ((f32[128,8,128]{2,1,0:T(8,128)}), f32[128,8,128]{2,1,0:T(8,128)S(1)}, u32[]{:S(2)}, u32[]{:S(2)}) async-start(f32[128,8,128]{2,1,0:T(8,128)} %get-tuple-element.29), calls=%async_computation | async-start | bytes 1048576 | tf_op jit(solution)/shard_map/all_to_all | solution.py:675
  18.3 0.6 collective-permute-start
  18.8 4.6 %collective-permute-start.1 = (f32[30,8,128]{2,1,0:T(8,128)S(1)}, f32[30,8,128]{2,1,0:T(8,128)S(1)}, u32[]{:S(2)}, u32[]{:S(2)}) collective-permute-start(f32[30,8,128]{2,1,0:T(8,128)S(1)} %get-tuple-element.25), channel_id=1, source_target_pairs={{16,32},{32,16},{48,64},{64,48},{80,96},{96,80},{17,33},{33,17},{4... | collective-permute-start | bytes 368648 | tf_op jit(solution)/shard_map/ppermute | solution.py:666
  23.4 11.6 %all-to-all-done.r3_a = f32[128,8,128]{2,1,0:T(8,128)S(1)} async-done(((f32[128,8,128]{2,1,0:T(8,128)}), f32[128,8,128]{2,1,0:T(8,128)S(1)}, u32[]{:S(2)}, u32[]{:S(2)}) %all-to-all-start) | async-done | bytes 524320 | tf_op jit(solution)/shard_map/all_to_all | solution.py:675
  35.1 2.5 %collective-permute-start.9 = (f32[128,8,128]{2,1,0:T(8,128)S(1)}, f32[128,8,128]{2,1,0:T(8,128)S(1)}, u32[]{:S(2)}, u32[]{:S(2)}) collective-permute-start(f32[128,8,128]{2,1,0:T(8,128)S(1)} %all-to-all-done.r3_a), channel_id=1, source_target_pairs={{0,128},{128,0},{1,129},{129,1},{2,130},{130,2},{3,131},{131,3},{4... | collective-permute-start | bytes 1572872 | tf_op jit(solution)/shard_map/ppermute | solution.py:671
  37.6 0.9 collective-permute-start.2
  38.5 2.8 %collective-permute-start.3 = (f32[76,8,128]{2,1,0:T(8,128)S(1)}, f32[76,8,128]{2,1,0:T(8,128)S(1)}, u32[]{:S(2)}, u32[]{:S(2)}) collective-permute-start(f32[76,8,128]{2,1,0:T(8,128)S(1)} %get-tuple-element.28), channel_id=1, source_target_pairs={{1,2},{2,1},{3,4},{4,3},{5,6},{6,5},{7,8},{8,7},{9,10},{10,9},{11,... | collective-permute-start | bytes 933896 | tf_op jit(solution)/shard_map/ppermute | solution.py:666
  41.3 5.4 %collective-permute-done.2.y_one_a = f32[76,8,128]{2,1,0:T(8,128)S(1)} collective-permute-done((f32[76,8,128]{2,1,0:T(8,128)S(1)}, f32[76,8,128]{2,1,0:T(8,128)S(1)}, u32[]{:S(2)}, u32[]{:S(2)}) %collective-permute-start.2) | collective-permute-done | bytes 311328 | tf_op jit(solution)/shard_map/ppermute | solution.py:665
  46.6 0.9 collective-permute-start.7
  47.5 3.6 %collective-permute-done.3.y_two_a = f32[76,8,128]{2,1,0:T(8,128)S(1)} collective-permute-done((f32[76,8,128]{2,1,0:T(8,128)S(1)}, f32[76,8,128]{2,1,0:T(8,128)S(1)}, u32[]{:S(2)}, u32[]{:S(2)}) %collective-permute-start.3) | collective-permute-done | bytes 311328 | tf_op jit(solution)/shard_map/ppermute | solution.py:666
  51.1 1.1 collective-permute-start.8
  52.8 4.2 %shard_map.43 = (f32[2,3,24,128]{3,2,1,0:T(8,128)S(1)}, f32[7,2,5,24,128]{4,3,2,1,0:T(8,128)}, f32[4,4,32,128]{3,2,1,0:T(8,128)}) custom-call(f32[128,8,128]{2,1,0:T(8,128)S(1)} %all-to-all-done.r3_a, f32[128,8,128]{2,1,0:T(8,128)S(1)} %collective-permute-done.9.r3_b, f32[1024,128]{1,0:T(8,128)S(1)} %bitcast.4, f32[1024,128]{1,0:T(8,128)S(1)} %bitcast.6), custom_call_target="tpu_custom_call" | custom-call | tf_op jit(solution)/shard_map/pallas_call | solution.py:647
  57.0 14.6 %shard_map.44 = (f32[8,2,28,32,128]{4,3,2,1,0:T(8,128)}, f32[7,2,10,24,128]{4,3,2,1,0:T(8,128)}, f32[2,28,32,128]{3,2,1,0:T(8,128)}, f32[2,16,16,128]{3,2,1,0:T(...) custom-call(f32[16,16,128]{2,1,0:T(8,128)} %a_hbm.3, ...), custom_call_target="tpu_custom_call" | custom-call | tf_op jit(solution)/shard_map/pallas_call | solution.py:647
  71.6 7.2 %all-to-all-start.1 = ((f32[128,4,128]{2,1,0:T(4,128)}), f32[128,4,128]{2,1,0:T(4,128)S(1)}, u32[]{:S(2)}, u32[]{:S(2)}) async-start(f32[128,4,128]{2,1,0:T(4,128)} %get-tuple-element.41), calls=%async_computation.1 | async-start | bytes 524288 | tf_op jit(solution)/shard_map/all_to_all | solution.py:675
  79.4 4.6 %collective-permute-start.11 = (f32[15,8,128]{2,1,0:T(8,128)S(1)}, f32[15,8,128]{2,1,0:T(8,128)S(1)}, u32[]{:S(2)}, u32[]{:S(2)}) collective-permute-start(f32[15,8,128]{2,1,0:T(8,128)S(1)} %get-tuple-element.37), channel_id=1, source_target_pairs={{16,32},{32,16},{48,64},{64,48},{80,96},{96,80},{17,33},{33,17},{4... | collective-permute-start | bytes 184328 | tf_op jit(solution)/shard_map/ppermute | solution.py:666
  84.0 4.4 %collective-permute-done.11.two.x_two_a = f32[15,8,128]{2,1,0:T(8,128)S(1)} collective-permute-done((f32[15,8,128]{2,1,0:T(8,128)S(1)}, f32[15,8,128]{2,1,0:T(8,128)S(1)}, u32[]{:S(2)}, u32[]{:S(2)}) %collective-permute-start.11) | collective-permute-done | bytes 61472 | tf_op jit(solution)/shard_map/ppermute | solution.py:666
  88.4 1.2 %collective-permute-start.12 = (f32[38,8,128]{2,1,0:T(8,128)S(1)}, f32[38,8,128]{2,1,0:T(8,128)S(1)}, u32[]{:S(2)}, u32[]{:S(2)}) collective-permute-start(f32[38,8,128]{2,1,0:T(8,128)S(1)} %get-tuple-element.39), channel_id=1, source_target_pairs={{0,1},{1,0},{2,3},{3,2},{4,5},{5,4},{6,7},{7,6},{8,9},{9,8},{10,11... | collective-permute-start | bytes 466952 | tf_op jit(solution)/shard_map/ppermute | solution.py:665
  89.7 4.4 %collective-permute-start.13 = (f32[38,8,128]{2,1,0:T(8,128)S(1)}, f32[38,8,128]{2,1,0:T(8,128)S(1)}, u32[]{:S(2)}, u32[]{:S(2)}) collective-permute-start(f32[38,8,128]{2,1,0:T(8,128)S(1)} %get-tuple-element.40), channel_id=1, source_target_pairs={{1,2},{2,1},{3,4},{4,3},{5,6},{6,5},{7,8},{8,7},{9,10},{10,9},{11,... | collective-permute-start | bytes 466952 | tf_op jit(solution)/shard_map/ppermute | solution.py:666
  94.1 2.7 %collective-permute-start.18 = (f32[128,4,128]{2,1,0:T(4,128)S(1)}, f32[128,4,128]{2,1,0:T(4,128)S(1)}, u32[]{:S(2)}, u32[]{:S(2)}) collective-permute-start(f32[128,4,128]{2,1,0:T(4,128)S(1)} %all-to-all-done.1.r3_a), channel_id=1, source_target_pairs={{0,128},{128,0},{1,129},{129,1},{2,130},{130,2},{3,131},{131,3},{4... | collective-permute-start | bytes 786440 | tf_op jit(solution)/shard_map/ppermute | solution.py:671
  96.9 0.8 collective-permute-done.13.y_two_a
  97.8 3.7 %collective-permute-start.17 = (f32[38,8,128]{2,1,0:T(8,128)S(1)}, f32[38,8,128]{2,1,0:T(8,128)S(1)}, u32[]{:S(2)}, u32[]{:S(2)}) collective-permute-start(f32[38,8,128]{2,1,0:T(8,128)S(1)} %collective-permute-done.13.y_two_a), channel_id=1, source_target_pairs={{0,128},{128,0},{1,129},{129,1},{2,130},{130,2},{3,131},{131,3},{4... | collective-permute-start | bytes 466952 | tf_op jit(solution)/shard_map/ppermute | solution.py:671
  101.9 4.0 %shard_map.46.sum3 = f32[2,3,24,128]{3,2,1,0:T(8,128)S(1)} custom-call(f32[128,4,128]{2,1,0:T(4,128)S(1)} %all-to-all-done.1.r3_a, f32[128,4,128]{2,1,0:T(4,128)S(1)} %collective-permute-done.18.r3_b, f32[512,128]{1,0:T(8,128)S(1)} %bitcast.5, f32[512,128]{1,0:T(8,128)S(1)} %bitcast.7, f32[7,2,5,24,128]{4,3,2,1,0:T(8,128)} %get-tuple-element.42.w3_hbm, ...), custom_call_target="tpu_custom_call" | custom-call | tf_op jit(solution)/shard_map/pallas_call | solution.py:647
  106.0 11.3 %shard_map.47 = (f32[16,16,128]{2,1,0:T(8,128)}, f32[16,16,128]{2,1,0:T(8,128)}) custom-call(f32[2,36,8,128]{3,2,1,0:T(8,128)} %get-tuple-element.31.own_hbm, f32[8,2,28,32,128]{4,3,2,1,0:T(8,128)} %get-tuple-element.32.w1_hbm, f32[7,2,10,24,128]{4,3,2,1,0:T(8,128)} %get-tuple-element.33.w2_hbm, f32[2,28,32,128]{3,2,1,0:T(8,128)} %get-tuple-element.34.x1_hbm, ...), custom_call_target="tpu_custom_call" | custom-call | tf_op jit(solution)/shard_map/pallas_call | solution.py:647
  (25 shorter events, 1.8 us)
Async XLA Ops:
  3.4 31.6 %all-to-all-start = ((f32[128,8,128]{2,1,0:T(8,128)}), f32[128,8,128]{2,1,0:T(8,128)S(1)}, u32[]{:S(2)}, u32[]{:S(2)}) async-start(f32[128,8,128]{2,1,0:T(8,128)} %get-tuple-element.29), calls=%async_computation | async-start | bytes 1048576 | tf_op jit(solution)/shard_map/all_to_all | solution.py:675
  18.3 19.3 %collective-permute-start = (f32[30,8,128]{2,1,0:T(8,128)S(1)}, f32[30,8,128]{2,1,0:T(8,128)S(1)}, u32[]{:S(2)}, u32[]{:S(2)}) collective-permute-start(f32[30,8,128]{2,1,0:T(8,128)S(1)} %get-tuple-element.24), channel_id=1, source_target_pairs={{0,16},{16,0},{32,48},{48,32},{64,80},{80,64},{96,112},{112,96},{1... | collective-permute-start | bytes 368648 | tf_op jit(solution)/shard_map/ppermute | solution.py:665
  18.8 18.7 %collective-permute-start.1 = (f32[30,8,128]{2,1,0:T(8,128)S(1)}, f32[30,8,128]{2,1,0:T(8,128)S(1)}, u32[]{:S(2)}, u32[]{:S(2)}) collective-permute-start(f32[30,8,128]{2,1,0:T(8,128)S(1)} %get-tuple-element.25), channel_id=1, source_target_pairs={{16,32},{32,16},{48,64},{64,48},{80,96},{96,80},{17,33},{33,17},{4... | collective-permute-start | bytes 368648 | tf_op jit(solution)/shard_map/ppermute | solution.py:666
  35.1 17.7 %collective-permute-start.9 = (f32[128,8,128]{2,1,0:T(8,128)S(1)}, f32[128,8,128]{2,1,0:T(8,128)S(1)}, u32[]{:S(2)}, u32[]{:S(2)}) collective-permute-start(f32[128,8,128]{2,1,0:T(8,128)S(1)} %all-to-all-done.r3_a), channel_id=1, source_target_pairs={{0,128},{128,0},{1,129},{129,1},{2,130},{130,2},{3,131},{131,3},{4... | collective-permute-start | bytes 1572872 | tf_op jit(solution)/shard_map/ppermute | solution.py:671
  37.6 9.0 %collective-permute-start.2 = (f32[76,8,128]{2,1,0:T(8,128)S(1)}, f32[76,8,128]{2,1,0:T(8,128)S(1)}, u32[]{:S(2)}, u32[]{:S(2)}) collective-permute-start(f32[76,8,128]{2,1,0:T(8,128)S(1)} %get-tuple-element.27), channel_id=1, source_target_pairs={{0,1},{1,0},{2,3},{3,2},{4,5},{5,4},{6,7},{7,6},{8,9},{9,8},{10,11... | collective-permute-start | bytes 933896 | tf_op jit(solution)/shard_map/ppermute | solution.py:665
  38.5 12.6 %collective-permute-start.3 = (f32[76,8,128]{2,1,0:T(8,128)S(1)}, f32[76,8,128]{2,1,0:T(8,128)S(1)}, u32[]{:S(2)}, u32[]{:S(2)}) collective-permute-start(f32[76,8,128]{2,1,0:T(8,128)S(1)} %get-tuple-element.28), channel_id=1, source_target_pairs={{1,2},{2,1},{3,4},{4,3},{5,6},{6,5},{7,8},{8,7},{9,10},{10,9},{11,... | collective-permute-start | bytes 933896 | tf_op jit(solution)/shard_map/ppermute | solution.py:666
  46.6 10.4 %collective-permute-start.7 = (f32[76,8,128]{2,1,0:T(8,128)S(1)}, f32[76,8,128]{2,1,0:T(8,128)S(1)}, u32[]{:S(2)}, u32[]{:S(2)}) collective-permute-start(f32[76,8,128]{2,1,0:T(8,128)S(1)} %collective-permute-done.2.y_one_a), channel_id=1, source_target_pairs={{0,128},{128,0},{1,129},{129,1},{2,130},{130,2},{3,131},{131,3},{4... | collective-permute-start | bytes 933896 | tf_op jit(solution)/shard_map/ppermute | solution.py:671
  51.1 5.9 %collective-permute-start.8 = (f32[76,8,128]{2,1,0:T(8,128)S(1)}, f32[76,8,128]{2,1,0:T(8,128)S(1)}, u32[]{:S(2)}, u32[]{:S(2)}) collective-permute-start(f32[76,8,128]{2,1,0:T(8,128)S(1)} %collective-permute-done.3.y_two_a), channel_id=1, source_target_pairs={{0,128},{128,0},{1,129},{129,1},{2,130},{130,2},{3,131},{131,3},{4... | collective-permute-start | bytes 933896 | tf_op jit(solution)/shard_map/ppermute | solution.py:671
  52.2 4.7 %collective-permute-start.4 = (f32[72,8,128]{2,1,0:T(8,128)S(1)}, f32[72,8,128]{2,1,0:T(8,128)S(1)}, u32[]{:S(2)}, u32[]{:S(2)}) collective-permute-start(f32[72,8,128]{2,1,0:T(8,128)S(1)} %get-tuple-element.26.own), channel_id=1, source_target_pairs={{0,128},{128,0},{1,129},{129,1},{2,130},{130,2},{3,131},{131,3},{4... | collective-permute-start | bytes 884744 | tf_op jit(solution)/shard_map/ppermute | solution.py:671
  52.2 4.7 %collective-permute-start.5 = (f32[30,8,128]{2,1,0:T(8,128)S(1)}, f32[30,8,128]{2,1,0:T(8,128)S(1)}, u32[]{:S(2)}, u32[]{:S(2)}) collective-permute-start(f32[30,8,128]{2,1,0:T(8,128)S(1)} %collective-permute-done.one.x_one_a), channel_id=1, source_target_pairs={{0,128},{128,0},{1,129},{129,1},{2,130},{130,2},{3,131},{131,3},{4... | collective-permute-start | bytes 368648 | tf_op jit(solution)/shard_map/ppermute | solution.py:671
  52.8 4.2 %collective-permute-start.6 = (f32[30,8,128]{2,1,0:T(8,128)S(1)}, f32[30,8,128]{2,1,0:T(8,128)S(1)}, u32[]{:S(2)}, u32[]{:S(2)}) collective-permute-start(f32[30,8,128]{2,1,0:T(8,128)S(1)} %collective-permute-done.1.two.x_two_a), channel_id=1, source_target_pairs={{0,128},{128,0},{1,129},{129,1},{2,130},{130,2},{3,131},{131,3},{4... | collective-permute-start | bytes 368648 | tf_op jit(solution)/shard_map/ppermute | solution.py:671
  71.6 22.4 %all-to-all-start.1 = ((f32[128,4,128]{2,1,0:T(4,128)}), f32[128,4,128]{2,1,0:T(4,128)S(1)}, u32[]{:S(2)}, u32[]{:S(2)}) async-start(f32[128,4,128]{2,1,0:T(4,128)} %get-tuple-element.41), calls=%async_computation.1 | async-start | bytes 524288 | tf_op jit(solution)/shard_map/all_to_all | solution.py:675
  78.8 5.2 %collective-permute-start.10 = (f32[15,8,128]{2,1,0:T(8,128)S(1)}, f32[15,8,128]{2,1,0:T(8,128)S(1)}, u32[]{:S(2)}, u32[]{:S(2)}) collective-permute-start(f32[15,8,128]{2,1,0:T(8,128)S(1)} %get-tuple-element.36), channel_id=1, source_target_pairs={{0,16},{16,0},{32,48},{48,32},{64,80},{80,64},{96,112},{112,96},{1... | collective-permute-start | bytes 184328 | tf_op jit(solution)/shard_map/ppermute | solution.py:665
  79.4 9.1 %collective-permute-start.11 = (f32[15,8,128]{2,1,0:T(8,128)S(1)}, f32[15,8,128]{2,1,0:T(8,128)S(1)}, u32[]{:S(2)}, u32[]{:S(2)}) collective-permute-start(f32[15,8,128]{2,1,0:T(8,128)S(1)} %get-tuple-element.37), channel_id=1, source_target_pairs={{16,32},{32,16},{48,64},{64,48},{80,96},{96,80},{17,33},{33,17},{4... | collective-permute-start | bytes 184328 | tf_op jit(solution)/shard_map/ppermute | solution.py:666
  88.4 8.4 %collective-permute-start.12 = (f32[38,8,128]{2,1,0:T(8,128)S(1)}, f32[38,8,128]{2,1,0:T(8,128)S(1)}, u32[]{:S(2)}, u32[]{:S(2)}) collective-permute-start(f32[38,8,128]{2,1,0:T(8,128)S(1)} %get-tuple-element.39), channel_id=1, source_target_pairs={{0,1},{1,0},{2,3},{3,2},{4,5},{5,4},{6,7},{7,6},{8,9},{9,8},{10,11... | collective-permute-start | bytes 466952 | tf_op jit(solution)/shard_map/ppermute | solution.py:665
  89.7 8.1 %collective-permute-start.13 = (f32[38,8,128]{2,1,0:T(8,128)S(1)}, f32[38,8,128]{2,1,0:T(8,128)S(1)}, u32[]{:S(2)}, u32[]{:S(2)}) collective-permute-start(f32[38,8,128]{2,1,0:T(8,128)S(1)} %get-tuple-element.40), channel_id=1, source_target_pairs={{1,2},{2,1},{3,4},{4,3},{5,6},{6,5},{7,8},{8,7},{9,10},{10,9},{11,... | collective-permute-start | bytes 466952 | tf_op jit(solution)/shard_map/ppermute | solution.py:666
  94.1 7.9 %collective-permute-start.18 = (f32[128,4,128]{2,1,0:T(4,128)S(1)}, f32[128,4,128]{2,1,0:T(4,128)S(1)}, u32[]{:S(2)}, u32[]{:S(2)}) collective-permute-start(f32[128,4,128]{2,1,0:T(4,128)S(1)} %all-to-all-done.1.r3_a), channel_id=1, source_target_pairs={{0,128},{128,0},{1,129},{129,1},{2,130},{130,2},{3,131},{131,3},{4... | collective-permute-start | bytes 786440 | tf_op jit(solution)/shard_map/ppermute | solution.py:671
  96.8 9.2 %collective-permute-start.16 = (f32[38,8,128]{2,1,0:T(8,128)S(1)}, f32[38,8,128]{2,1,0:T(8,128)S(1)}, u32[]{:S(2)}, u32[]{:S(2)}) collective-permute-start(f32[38,8,128]{2,1,0:T(8,128)S(1)} %collective-permute-done.12.y_one_a), channel_id=1, source_target_pairs={{0,128},{128,0},{1,129},{129,1},{2,130},{130,2},{3,131},{131,3},{4... | collective-permute-start | bytes 466952 | tf_op jit(solution)/shard_map/ppermute | solution.py:671
  97.8 8.2 %collective-permute-start.17 = (f32[38,8,128]{2,1,0:T(8,128)S(1)}, f32[38,8,128]{2,1,0:T(8,128)S(1)}, u32[]{:S(2)}, u32[]{:S(2)}) collective-permute-start(f32[38,8,128]{2,1,0:T(8,128)S(1)} %collective-permute-done.13.y_two_a), channel_id=1, source_target_pairs={{0,128},{128,0},{1,129},{129,1},{2,130},{130,2},{3,131},{131,3},{4... | collective-permute-start | bytes 466952 | tf_op jit(solution)/shard_map/ppermute | solution.py:671
  101.4 4.5 %collective-permute-start.14 = (f32[15,8,128]{2,1,0:T(8,128)S(1)}, f32[15,8,128]{2,1,0:T(8,128)S(1)}, u32[]{:S(2)}, u32[]{:S(2)}) collective-permute-start(f32[15,8,128]{2,1,0:T(8,128)S(1)} %collective-permute-done.10.one.x_one_a), channel_id=1, source_target_pairs={{0,128},{128,0},{1,129},{129,1},{2,130},{130,2},{3,131},{131,3},{4... | collective-permute-start | bytes 184328 | tf_op jit(solution)/shard_map/ppermute | solution.py:671
  101.4 4.5 %collective-permute-start.15 = (f32[15,8,128]{2,1,0:T(8,128)S(1)}, f32[15,8,128]{2,1,0:T(8,128)S(1)}, u32[]{:S(2)}, u32[]{:S(2)}) collective-permute-start(f32[15,8,128]{2,1,0:T(8,128)S(1)} %collective-permute-done.11.two.x_two_a), channel_id=1, source_target_pairs={{0,128},{128,0},{1,129},{129,1},{2,130},{130,2},{3,131},{131,3},{4... | collective-permute-start | bytes 184328 | tf_op jit(solution)/shard_map/ppermute | solution.py:671

commit v7 on v6

--- a/solution.py
+++ b/solution.py
@@ -507,9 +507,9 @@
 
 def first_kernel(
     a_hbm, b_hbm, mid_hbm,
-    x_one_a, x_two_a, y_one_a, y_two_a, own_b, x_one_b, x_two_b, y_one_b, y_two_b, sum3,
-    w1_hbm, w2_hbm, x1_hbm, right_hbm, own_hbm, own, first, second, slots,
-    w1, w2, x1, a1, b1, e1, d1, o1, a2, b2, e2, d2, o2, c2, s2, tmp3, tmp2, rest, sems,
+    x_one_a, x_two_a, y_one_a, y_two_a, own_b, x_one_b, x_two_b, y_one_b, y_two_b,
+    w1_hbm, w2_hbm, c1_hbm, c2_hbm, right_hbm,
+    w1, w2, c1, a1, b1, e1, d1, o1, a2, b2, e2, d2, o2, c2, sems,
 ):
     core, gx, gy = position()
     even_x, even_y = is_even(gx), is_even(gy)
@@ -541,21 +541,48 @@
     faces(1, a1, weights1, inv1, diag1)
     out.start(w1, w1_hbm)
     smooth(2, b2, weights2, inv2, e2, d2, o2, c2)
-    smooth(1, b1, weights1, inv1, e1, d1, o1, x1)
+    out.start(c2, c2_hbm)
+    smooth(1, b1, weights1, inv1, e1, d1, o1, c1)
+    out.start(c1, c1_hbm)
+    out.finish()
+
+
+def join_first_kernel(
+    gx_n, gy_n, r3_a, r3_b, r3f_a, r3f_b, w1_hbm, right_hbm, c1_hbm, c2_hbm,
+    w3_hbm, w4_hbm, x1_hbm, own_hbm, own, first, second, slots,
+    sum3, w3, w4, a3, b3, e3, d3, o3, c3, x4, w1, right, x1, c2, s2, tmp3, tmp2, rest, sems,
+):
+    core, gx, _ = position()
+    even_x = is_even(gx)
+    weights1, diag1 = split3(w1)[0], w1.at[7]
+    copies = Copies(sems.at[pl.ds(2, 4)])
+    copies.start(c2_hbm, c2)
+    copies.start(c1_hbm, x1)
+    copies.start(w1_hbm.at[:, :, 6:22], w1.at[:, :, 6:22])
+    copies.start(right_hbm, right)
+    coarse_first_kernel(
+        gx_n, gy_n, r3_a, r3_b, r3f_a, r3f_b, sum3, w3_hbm, w4_hbm,
+        w3, w4, a3, b3, e3, d3, o3, c3, x4, sems.at[pl.ds(0, 2)],
+    )
+    copies.made[0].wait()
     combine(sum3, c2, s2, tmp3, tmp2)
+    copies.made[1].wait()
 
     def finish(i, _):
         x1[:, i] = DAMPING * (x1[:, i] + tmp2[:, i // 2 - 1])
         return 0
 
     lax.fori_loop(5, 23, finish, 0)
+    out = Copies(sems.at[pl.ds(6, 2)])
     out.start(x1, x1_hbm)
+    copies.made[2].wait()
+    copies.made[3].wait()
 
     def residual(i):
         mid, near = weighted(1, i, 2, x1, weights1)
-        at = pl.ds(i, 2)
-        res = b1[:, at] - diag1[:, at] * (mid - near)
-        rest[:, pl.ds(i - 6, 2)] = res[:, :, 8:24, :]
+        res = diag1[:, pl.ds(i, 2)] * (mid - near)
+        at = pl.ds(i - 6, 2)
+        rest[:, at] = right[:, at] - res[:, :, 8:24, :]
 
     blocks(6, 22, 2, residual)
     for c in range(2):
@@ -586,20 +613,16 @@
 
 
 def second_kernel(
-    own_hbm, w1_hbm, w2_hbm, x1_hbm, right_hbm,
-    x_one_a, x_two_a, y_one_a, y_two_a, x_one_b, x_two_b, y_one_b, y_two_b, sum3,
-    out_x, out_r,
-    w1, w2, x1, right, own, b1, e1, d1, o1, c1, b2, e2, d2, o2, c2, s2, tmp3, tmp2, rest, sems,
+    own_hbm, w1_hbm, w2_hbm,
+    x_one_a, x_two_a, y_one_a, y_two_a, x_one_b, x_two_b, y_one_b, y_two_b, c1_hbm, c2_hbm,
+    w1, w2, own, b1, e1, d1, o1, c1, b2, e2, d2, o2, c2, sems,
 ):
     core, gx, gy = position()
     even_x, even_y = is_even(gx), is_even(gy)
     copies = Copies(sems)
-    for src, dst in (
-        (own_hbm, own), (w2_hbm, w2), (w1_hbm, w1), (x1_hbm, x1), (right_hbm, right)
-    ):
+    for src, dst in ((own_hbm, own), (w2_hbm, w2), (w1_hbm.at[0:7], w1)):
         copies.start(src, dst)
     weights1, inv1 = split3(w1)
-    diag1 = w1.at[7]
     weights2, inv2 = split3(w2)
     spread(1, 0, core, even_x, even_y, x_one_a, x_two_a, y_one_a, y_two_a, b1, b2, 0)
     spread(1, 0, 1 - core, even_x, even_y, x_one_b, x_two_b, y_one_b, y_two_b, b1, b2, 0)
@@ -608,11 +631,36 @@
         spread_own(1, 0, c, own.at[c], b1, b2, 0)
     copies.made[1].wait()
     smooth(2, b2, weights2, inv2, e2, d2, o2, c2)
+    middle = copies.start(c2, c2_hbm)
     copies.made[2].wait()
     smooth(1, b1, weights1, inv1, e1, d1, o1, c1)
-    copies.made[3].wait()
-    copies.made[4].wait()
+    last = copies.start(c1, c1_hbm)
+    middle.wait()
+    last.wait()
+
+
+def join_second_kernel(
+    gx_n, gy_n, r3_a, r3_b, r3f_a, r3f_b, w3_hbm, w4_hbm, w1_hbm, x1_hbm, right_hbm,
+    c1_hbm, c2_hbm, out_x, out_r,
+    sum3, w3, w4, b3, e3, d3, o3, c3, x4, w1, x1, right, c1, c2, s2, tmp3, tmp2, rest, sems,
+):
+    core = position()[0]
+    weights1, diag1 = split3(w1)[0], w1.at[7]
+    copies = Copies(sems.at[pl.ds(2, 7)])
+    own = pl.ds(6, 16)
+    for src, dst in (
+        (c2_hbm, c2), (c1_hbm, c1), (x1_hbm, x1), (w1_hbm.at[:, :, own], w1.at[:, :, own]),
+        (right_hbm, right),
+    ):
+        copies.start(src, dst)
+    coarse_second_kernel(
+        gx_n, gy_n, r3_a, r3_b, r3f_a, r3f_b, w3_hbm, w4_hbm, sum3,
+        w3, w4, b3, e3, d3, o3, c3, x4, sems.at[pl.ds(0, 2)],
+    )
+    copies.made[0].wait()
     combine(sum3, c2, s2, tmp3, tmp2)
+    copies.made[1].wait()
+    copies.made[2].wait()
 
     def finish(i, _):
         c1[:, i] = x1[:, i] + DAMPING * (c1[:, i] + tmp2[:, i // 2 - 1])
@@ -620,6 +668,8 @@
 
     lax.fori_loop(5, 23, finish, 0)
     field = copies.start(c1.at[core, 6:22, 8:24, :], out_x)
+    copies.made[3].wait()
+    copies.made[4].wait()
 
     def residual(i):
         mid, near = weighted(1, i, 2, c1, weights1)
@@ -699,21 +749,23 @@
     )
     y_one, y_two = trade(first, second, "gy")
     y_one_o, y_two_o = swap(y_one), swap(y_two)
+    w1s, w2s, w3s, w4s = (8,) + s1, (7,) + s2, (7,) + s3, (4,) + s4
+    block = (2, 16, 16, 128)
+    w1, w2, c1, c2, right = call(
+        first_kernel, [w1s, w2s, s1, s2, block],
+        [w1s, w2s, s1, s1, s1, s1, s1, s1, p2, s2, s2, s2, s2, s2],
+        coefficient, right_side, middle,
+        x_one, x_two, y_one, y_two, own_o, x_one_o, x_two_o, y_one_o, y_two_o,
+        hbm_in=(0, 1, 2), hbm_out=(0, 1, 2, 3, 4), sems=9, limit=28,
+    )
     flat = (count * 8, 128)
-    w1s, w2s, w3s, w4s = (8,) + s1, (7,) + s2, (7,) + s3, (4,) + s4
-    c3, w3, w4 = call(
-        functools.partial(coarse_first_kernel, gx_n, gy_n), [sum3, w3s, w4s],
-        [w3s, w4s, p3, s3, s3, s3, s3, s3, s4],
-        r3, r3_o, r3.reshape(flat), r3_o.reshape(flat), hbm_out=(1, 2), sems=2, limit=12,
-    )
-    w1, w2, x1, right, own_kept, own, first, second, slots = call(
-        first_kernel,
-        [w1s, w2s, s1, (2, 16, 16, 128), (2, 36, 8, 128), (2, 36, 8, 128), (15, 8, 128),
-         (15, 8, 128), (count, 4, 128)],
-        [w1s, w2s, s1, s1, s1, s1, s1, s1, p2, s2, s2, s2, s2, s2] + tmps,
-        coefficient, right_side, middle,
-        x_one, x_two, y_one, y_two, own_o, x_one_o, x_two_o, y_one_o, y_two_o, c3,
-        hbm_in=(0, 1, 2), hbm_out=(0, 1, 2, 3, 4), sems=9, limit=28,
+    w3, w4, x1, own_kept, own, first, second, slots = call(
+        functools.partial(join_first_kernel, gx_n, gy_n),
+        [w3s, w4s, s1, (2, 36, 8, 128), (2, 36, 8, 128), (15, 8, 128), (15, 8, 128),
+         (count, 4, 128)],
+        [sum3, w3s, w4s, p3, s3, s3, s3, s3, s3, s4, w1s, block, s1, s2] + tmps,
+        r3, r3_o, r3.reshape(flat), r3_o.reshape(flat), w1, right, c1, c2,
+        hbm_in=(4, 5, 6, 7), hbm_out=(0, 1, 2, 3), sems=8, limit=28,
     )
     x_one, x_two = trade(first, second, "gx")
     r3 = everywhere(slots)
@@ -725,19 +777,17 @@
     y_one, y_two = trade(first, second, "gy")
     y_one_o, y_two_o = swap(y_one), swap(y_two)
     flat = (count * 4, 128)
-    (c3,) = call(
-        functools.partial(coarse_second_kernel, gx_n, gy_n),
-        [sum3], [w3s, w4s, s3, s3, s3, s3, s3, s4],
-        r3, r3_o, r3.reshape(flat), r3_o.reshape(flat), w3, w4,
-        hbm_in=(4, 5), sems=2, limit=12,
+    c1, c2 = call(
+        second_kernel, [s1, s2],
+        [(7,) + s1, w2s, (2, 36, 8, 128), s1, s1, s1, s1, s1, s2, s2, s2, s2, s2],
+        own_kept, w1, w2, x_one, x_two, y_one, y_two, x_one_o, x_two_o, y_one_o, y_two_o,
+        hbm_in=(0, 1, 2), hbm_out=(0, 1), sems=5, limit=28,
     )
     solution_field, residual = call(
-        second_kernel, [(16, 16, 128)] * 2,
-        [w1s, w2s, s1, (2, 16, 16, 128), (2, 36, 8, 128), s1, s1, s1, s1, s1, s2, s2, s2, s2, s2]
-        + tmps,
-        own_kept, w1, w2, x1, right,
-        x_one, x_two, y_one, y_two, x_one_o, x_two_o, y_one_o, y_two_o, c3,
-        hbm_in=(0, 1, 2, 3, 4), hbm_out=(0, 1), sems=7, limit=28,
+        functools.partial(join_second_kernel, gx_n, gy_n), [(16, 16, 128)] * 2,
+        [sum3, w3s, w4s, s3, s3, s3, s3, s3, s4, w1s, s1, block, s1, s2] + tmps,
+        r3, r3_o, r3.reshape(flat), r3_o.reshape(flat), w3, w4, w1, x1, right, c1, c2,
+        hbm_in=(4, 5, 6, 7, 8, 9, 10), hbm_out=(0, 1), sems=9, limit=28,
     )
     return solution_field, residual
 

time: 119 us -> 123 us (1.034)
  waiting for transfers between devices: 25.9 us -> 16.4 us
  starting transfers between devices: 53.6 us -> 61.6 us
  Pallas kernels: 37 us -> 42.2 us
    all_to_all x2, waiting for transfers between devices: 11.6 us -> 0.01 us  [everywhere(): return lax.all_to_all(slots, ('gx', 'gy'), 0, 0, tiled=True)]
    pallas_call x7, Pallas kernels: 37 us -> 42.2 us  [call(): pl.pallas_call(kernel, out_shape=[pltpu.HBM(s, F32) if i in hbm_out else...]
    ppermute x4, waiting for transfers between devices: 5.37 us -> 0.62 us  [trade(): one = lax.ppermute(first, axis, pairs)]
    ppermute x4, waiting for transfers between devices: 8.88 us -> 12.6 us  [trade(): two = lax.ppermute(second, axis, others)]
    ppermute x11, waiting for transfers between devices: 0.03 us -> 3.21 us  [swap(): return lax.ppermute(x, 'grp', [(0, 1), (1, 0)])]
    ppermute x11, starting transfers between devices: 12.1 us -> 15 us  [swap(): return lax.ppermute(x, 'grp', [(0, 1), (1, 0)])]
    all_to_all x2, starting transfers between devices: 22 us -> 24.7 us  [everywhere(): return lax.all_to_all(slots, ('gx', 'gy'), 0, 0, tiled=True)]
    ppermute x4, starting transfers between devices: 16.4 us -> 18 us  [trade(): two = lax.ppermute(second, axis, others)]
  transfers between devices with their start and end apart: 21 -> 21, of which waited for: 5 -> 9; matrix products, arithmetic and copies ran while one was open for 0% -> 0% of each run, Pallas kernels for 7% -> 18%
where the time goes in v7:
time: 123 us; the launch traced here: 121 us
  starting transfers between devices  61.6 us (50%)
  Pallas kernels  42.2 us (34%)
  waiting for transfers between devices  16.4 us (13%)
    pallas_call x7, Pallas kernels, call(): pl.pallas_call(kernel, out_shape=[pltpu.HBM(s, F32) if i in hbm_out else...  42.2 us
    all_to_all x2, starting transfers between devices, everywhere(): return lax.all_to_all(slots, ('gx', 'gy'), 0, 0, tiled=True)  24.7 us
    ppermute x4, starting transfers between devices, trade(): two = lax.ppermute(second, axis, others)  18 us
    ppermute x11, starting transfers between devices, swap(): return lax.ppermute(x, 'grp', [(0, 1), (1, 0)])  15 us
    ppermute x4, waiting for transfers between devices, trade(): two = lax.ppermute(second, axis, others)  12.6 us
    ppermute x4, starting transfers between devices, trade(): one = lax.ppermute(first, axis, pairs)  4 us
    ppermute x11, waiting for transfers between devices, swap(): return lax.ppermute(x, 'grp', [(0, 1), (1, 0)])  3.21 us
  transfers between devices with their start and end apart: 21, of which 9 were waited for; matrix products, arithmetic and copies ran while one was open for 0% of the time, Pallas kernels for 18%

profile of v7, /device:TPU:27, one launch (start us, length us, event | category | flops | bytes accessed | tf_op | source)
XLA Modules:
  0.0 121.2 jit_solution(816267491710645522)
XLA Ops:
  0.6 2.8 %shard_map.41 = (f32[72,8,128]{2,1,0:T(8,128)S(1)}, f32[8,8,128]{2,1,0:T(8,128)}, f32[30,8,128]{2,1,0:T(8,128)S(1)}, f32[30,8,128]{2,1,0:T(8,128)S(1)}, f32[128,8,128]{2,1,0:T(8,128)}) custom-call(f32[16,16,128]{2,1,0:T(8,128)} %a_hbm.3, f32[16,16,128]{2,1,0:T(8,128)} %b_hbm.3), custom_call_target="tpu_custom_call" | custom-call | tf_op jit(solution)/shard_map/pallas_call | solution.py:697
  3.4 14.8 %all-to-all-start = ((f32[128,8,128]{2,1,0:T(8,128)}), f32[128,8,128]{2,1,0:T(8,128)S(1)}, u32[]{:S(2)}, u32[]{:S(2)}) async-start(f32[128,8,128]{2,1,0:T(8,128)} %get-tuple-element.26), calls=%async_computation | async-start | bytes 1048576 | tf_op jit(solution)/shard_map/all_to_all | solution.py:725
  18.8 4.6 %collective-permute-start.2 = (f32[30,8,128]{2,1,0:T(8,128)S(1)}, f32[30,8,128]{2,1,0:T(8,128)S(1)}, u32[]{:S(2)}, u32[]{:S(2)}) collective-permute-start(f32[30,8,128]{2,1,0:T(8,128)S(1)} %get-tuple-element.29), channel_id=1, source_target_pairs={{16,32},{32,16},{48,64},{64,48},{80,96},{96,80},{17,33},{33,17},{4... | collective-permute-start | bytes 368648 | tf_op jit(solution)/shard_map/ppermute | solution.py:716
  24.1 5.2 %collective-permute-done.2.two.x_two_a = f32[30,8,128]{2,1,0:T(8,128)S(1)} collective-permute-done((f32[30,8,128]{2,1,0:T(8,128)S(1)}, f32[30,8,128]{2,1,0:T(8,128)S(1)}, u32[]{:S(2)}, u32[]{:S(2)}) %collective-permute-start.2) | collective-permute-done | bytes 122912 | tf_op jit(solution)/shard_map/ppermute | solution.py:716
  29.3 1.7 %collective-permute-start.3 = (f32[76,8,128]{2,1,0:T(8,128)S(1)}, f32[76,8,128]{2,1,0:T(8,128)S(1)}, u32[]{:S(2)}, u32[]{:S(2)}) collective-permute-start(f32[76,8,128]{2,1,0:T(8,128)S(1)} %get-tuple-element.31), channel_id=1, source_target_pairs={{0,1},{1,0},{2,3},{3,2},{4,5},{5,4},{6,7},{7,6},{8,9},{9,8},{10,11... | collective-permute-start | bytes 933896 | tf_op jit(solution)/shard_map/ppermute | solution.py:715
  31.0 4.4 %collective-permute-start.4 = (f32[76,8,128]{2,1,0:T(8,128)S(1)}, f32[76,8,128]{2,1,0:T(8,128)S(1)}, u32[]{:S(2)}, u32[]{:S(2)}) collective-permute-start(f32[76,8,128]{2,1,0:T(8,128)S(1)} %get-tuple-element.32), channel_id=1, source_target_pairs={{1,2},{2,1},{3,4},{4,3},{5,6},{6,5},{7,8},{8,7},{9,10},{10,9},{11,... | collective-permute-start | bytes 933896 | tf_op jit(solution)/shard_map/ppermute | solution.py:716
  35.5 3.0 %collective-permute-start = (f32[128,8,128]{2,1,0:T(8,128)S(1)}, f32[128,8,128]{2,1,0:T(8,128)S(1)}, u32[]{:S(2)}, u32[]{:S(2)}) collective-permute-start(f32[128,8,128]{2,1,0:T(8,128)S(1)} %all-to-all-done.r3_a), channel_id=1, source_target_pairs={{0,128},{128,0},{1,129},{129,1},{2,130},{130,2},{3,131},{131,3},{4... | collective-permute-start | bytes 1572872 | tf_op jit(solution)/shard_map/ppermute | solution.py:721
  38.5 0.8 collective-permute-start.8
  39.3 2.0 %collective-permute-done.4.y_two_a = f32[76,8,128]{2,1,0:T(8,128)S(1)} collective-permute-done((f32[76,8,128]{2,1,0:T(8,128)S(1)}, f32[76,8,128]{2,1,0:T(8,128)S(1)}, u32[]{:S(2)}, u32[]{:S(2)}) %collective-permute-start.4) | collective-permute-done | bytes 311328 | tf_op jit(solution)/shard_map/ppermute | solution.py:716
  41.3 3.5 %collective-permute-start.9 = (f32[76,8,128]{2,1,0:T(8,128)S(1)}, f32[76,8,128]{2,1,0:T(8,128)S(1)}, u32[]{:S(2)}, u32[]{:S(2)}) collective-permute-start(f32[76,8,128]{2,1,0:T(8,128)S(1)} %collective-permute-done.4.y_two_a), channel_id=1, source_target_pairs={{0,128},{128,0},{1,129},{129,1},{2,130},{130,2},{3,131},{131,3},{4... | collective-permute-start | bytes 933896 | tf_op jit(solution)/shard_map/ppermute | solution.py:721
  45.3 1.3 %collective-permute-done.6.x_one_b = f32[30,8,128]{2,1,0:T(8,128)S(1)} collective-permute-done((f32[30,8,128]{2,1,0:T(8,128)S(1)}, f32[30,8,128]{2,1,0:T(8,128)S(1)}, u32[]{:S(2)}, u32[]{:S(2)}) %collective-permute-start.6) | collective-permute-done | bytes 122912 | tf_op jit(solution)/shard_map/ppermute | solution.py:721
  47.0 1.0 collective-permute-done.7.x_two_b
  48.0 12.1 %shard_map.43 = (f32[8,2,28,32,128]{4,3,2,1,0:T(8,128)}, f32[7,2,10,24,128]{4,3,2,1,0:T(8,128)}, f32[2,28,32,128]{3,2,1,0:T(8,128)}, f32[2,10,24,128]{3,2,1,0:T(8,128)}, f32[2,16,16,128]{3,2,1,0:T(8,128)}) custom-call(f32[16,16,128]{2,1,0:T(8,128)} %a_hbm.3, f32[16,16,128]{2,1,0:T(8,128)} %b_hbm.3, f32[8,8,128]{2,1,0:T(8,128)} %get-tuple-element.27.mid_hbm, ...), custom_call_target="tpu_custom_call" | custom-call | tf_op jit(solution)/shard_map/pallas_call | solution.py:697
  60.1 9.0 %shard_map.44 = (f32[7,2,5,24,128]{4,3,2,1,0:T(8,128)}, f32[4,4,32,128]{3,2,1,0:T(8,128)}, f32[2,28,32,128]{3,2,1,0:T(8,128)}, f32[2,36,8,128]{3,2,1,0:T(8,128)}...) custom-call(f32[128,8,128]{2,1,0:T(8,128)S(1)} %all-to-all-done.r3_a, ...), custom_call_target="tpu_custom_call" | custom-call | tf_op jit(solution)/shard_map/pallas_call | solution.py:697
  69.1 9.9 %all-to-all-start.1 = ((f32[128,4,128]{2,1,0:T(4,128)}), f32[128,4,128]{2,1,0:T(4,128)S(1)}, u32[]{:S(2)}, u32[]{:S(2)}) async-start(f32[128,4,128]{2,1,0:T(4,128)} %get-tuple-element.37), calls=%async_computation.1 | async-start | bytes 524288 | tf_op jit(solution)/shard_map/all_to_all | solution.py:725
  79.5 4.6 %collective-permute-start.12 = (f32[15,8,128]{2,1,0:T(8,128)S(1)}, f32[15,8,128]{2,1,0:T(8,128)S(1)}, u32[]{:S(2)}, u32[]{:S(2)}) collective-permute-start(f32[15,8,128]{2,1,0:T(8,128)S(1)} %get-tuple-element.44), channel_id=1, source_target_pairs={{16,32},{32,16},{48,64},{64,48},{80,96},{96,80},{17,33},{33,17},{4... | collective-permute-start | bytes 184328 | tf_op jit(solution)/shard_map/ppermute | solution.py:716
  84.1 4.4 %collective-permute-done.12.two.x_two_a = f32[15,8,128]{2,1,0:T(8,128)S(1)} collective-permute-done((f32[15,8,128]{2,1,0:T(8,128)S(1)}, f32[15,8,128]{2,1,0:T(8,128)S(1)}, u32[]{:S(2)}, u32[]{:S(2)}) %collective-permute-start.12) | collective-permute-done | bytes 61472 | tf_op jit(solution)/shard_map/ppermute | solution.py:716
  88.6 1.2 collective-permute-start.13
  89.8 4.3 %collective-permute-start.14 = (f32[38,8,128]{2,1,0:T(8,128)S(1)}, f32[38,8,128]{2,1,0:T(8,128)S(1)}, u32[]{:S(2)}, u32[]{:S(2)}) collective-permute-start(f32[38,8,128]{2,1,0:T(8,128)S(1)} %get-tuple-element.47), channel_id=1, source_target_pairs={{1,2},{2,1},{3,4},{4,3},{5,6},{6,5},{7,8},{8,7},{9,10},{10,9},{11,... | collective-permute-start | bytes 466952 | tf_op jit(solution)/shard_map/ppermute | solution.py:716
  94.1 2.7 %collective-permute-start.10 = (f32[128,4,128]{2,1,0:T(4,128)S(1)}, f32[128,4,128]{2,1,0:T(4,128)S(1)}, u32[]{:S(2)}, u32[]{:S(2)}) collective-permute-start(f32[128,4,128]{2,1,0:T(4,128)S(1)} %all-to-all-done.1.r3_a), channel_id=1, source_target_pairs={{0,128},{128,0},{1,129},{129,1},{2,130},{130,2},{3,131},{131,3},{4... | collective-permute-start | bytes 786440 | tf_op jit(solution)/shard_map/ppermute | solution.py:721
  96.9 1.0 collective-permute-done.14.y_two_a
  97.9 3.5 %collective-permute-start.18 = (f32[38,8,128]{2,1,0:T(8,128)S(1)}, f32[38,8,128]{2,1,0:T(8,128)S(1)}, u32[]{:S(2)}, u32[]{:S(2)}) collective-permute-start(f32[38,8,128]{2,1,0:T(8,128)S(1)} %collective-permute-done.14.y_two_a), channel_id=1, source_target_pairs={{0,128},{128,0},{1,129},{129,1},{2,130},{130,2},{3,131},{131,3},{4... | collective-permute-start | bytes 466952 | tf_op jit(solution)/shard_map/ppermute | solution.py:721
  102.8 10.0 %shard_map.46 = (f32[2,28,32,128]{3,2,1,0:T(8,128)}, f32[2,10,24,128]{3,2,1,0:T(8,128)}) custom-call(f32[2,36,8,128]{3,2,1,0:T(8,128)} %get-tuple-element.41.own_hbm, f32[8,2,28,32,128]{4,3,2,1,0:T(8,128)} %get-tuple-element.33.w1_hbm, f32[7,2,10,24,128]{4,3,2,1,0:T(8,128)} %get-tuple-element.42.w2_hbm, ...), custom_call_target="tpu_custom_call" | custom-call | tf_op jit(solution)/shard_map/pallas_call | solution.py:697
  112.8 8.2 %shard_map.47 = (f32[16,16,128]{2,1,0:T(8,128)}, f32[16,16,128]{2,1,0:T(8,128)}) custom-call(f32[128,4,128]{2,1,0:T(4,128)S(1)} %all-to-all-done.1.r3_a, f32[128,4,128]{2,1,0:T(4,128)S(1)} %collective-permute-done.10.r3_b, f32[512,128]{1,0:T(8,128)S(1)} %bitcast.5, f32[512,128]{1,0:T(8,128)S(1)} %bitcast.7, f32[7,2,5,24,128]{4,3,2,1,0:T(8,128)} %get-tuple-element.38.w3_hbm, ...), custom_call_target="tpu_custom_call" | custom-call | tf_op jit(solution)/shard_map/pallas_call | solution.py:697
  (25 shorter events, 4.2 us)
Async XLA Ops:
  3.4 32.0 %all-to-all-start = ((f32[128,8,128]{2,1,0:T(8,128)}), f32[128,8,128]{2,1,0:T(8,128)S(1)}, u32[]{:S(2)}, u32[]{:S(2)}) async-start(f32[128,8,128]{2,1,0:T(8,128)} %get-tuple-element.26), calls=%async_computation | async-start | bytes 1048576 | tf_op jit(solution)/shard_map/all_to_all | solution.py:725
  18.3 5.8 %collective-permute-start.1 = (f32[30,8,128]{2,1,0:T(8,128)S(1)}, f32[30,8,128]{2,1,0:T(8,128)S(1)}, u32[]{:S(2)}, u32[]{:S(2)}) collective-permute-start(f32[30,8,128]{2,1,0:T(8,128)S(1)} %get-tuple-element.28), channel_id=1, source_target_pairs={{0,16},{16,0},{32,48},{48,32},{64,80},{80,64},{96,112},{112,96},{1... | collective-permute-start | bytes 368648 | tf_op jit(solution)/shard_map/ppermute | solution.py:715
  18.8 10.5 %collective-permute-start.2 = (f32[30,8,128]{2,1,0:T(8,128)S(1)}, f32[30,8,128]{2,1,0:T(8,128)S(1)}, u32[]{:S(2)}, u32[]{:S(2)}) collective-permute-start(f32[30,8,128]{2,1,0:T(8,128)S(1)} %get-tuple-element.29), channel_id=1, source_target_pairs={{16,32},{32,16},{48,64},{64,48},{80,96},{96,80},{17,33},{33,17},{4... | collective-permute-start | bytes 368648 | tf_op jit(solution)/shard_map/ppermute | solution.py:716
  29.3 9.2 %collective-permute-start.3 = (f32[76,8,128]{2,1,0:T(8,128)S(1)}, f32[76,8,128]{2,1,0:T(8,128)S(1)}, u32[]{:S(2)}, u32[]{:S(2)}) collective-permute-start(f32[76,8,128]{2,1,0:T(8,128)S(1)} %get-tuple-element.31), channel_id=1, source_target_pairs={{0,1},{1,0},{2,3},{3,2},{4,5},{5,4},{6,7},{7,6},{8,9},{9,8},{10,11... | collective-permute-start | bytes 933896 | tf_op jit(solution)/shard_map/ppermute | solution.py:715
  31.0 10.3 %collective-permute-start.4 = (f32[76,8,128]{2,1,0:T(8,128)S(1)}, f32[76,8,128]{2,1,0:T(8,128)S(1)}, u32[]{:S(2)}, u32[]{:S(2)}) collective-permute-start(f32[76,8,128]{2,1,0:T(8,128)S(1)} %get-tuple-element.32), channel_id=1, source_target_pairs={{1,2},{2,1},{3,4},{4,3},{5,6},{6,5},{7,8},{8,7},{9,10},{10,9},{11,... | collective-permute-start | bytes 933896 | tf_op jit(solution)/shard_map/ppermute | solution.py:716
  35.5 24.6 %collective-permute-start = (f32[128,8,128]{2,1,0:T(8,128)S(1)}, f32[128,8,128]{2,1,0:T(8,128)S(1)}, u32[]{:S(2)}, u32[]{:S(2)}) collective-permute-start(f32[128,8,128]{2,1,0:T(8,128)S(1)} %all-to-all-done.r3_a), channel_id=1, source_target_pairs={{0,128},{128,0},{1,129},{129,1},{2,130},{130,2},{3,131},{131,3},{4... | collective-permute-start | bytes 1572872 | tf_op jit(solution)/shard_map/ppermute | solution.py:721
  38.5 9.5 %collective-permute-start.8 = (f32[76,8,128]{2,1,0:T(8,128)S(1)}, f32[76,8,128]{2,1,0:T(8,128)S(1)}, u32[]{:S(2)}, u32[]{:S(2)}) collective-permute-start(f32[76,8,128]{2,1,0:T(8,128)S(1)} %collective-permute-done.3.y_one_a), channel_id=1, source_target_pairs={{0,128},{128,0},{1,129},{129,1},{2,130},{130,2},{3,131},{131,3},{4... | collective-permute-start | bytes 933896 | tf_op jit(solution)/shard_map/ppermute | solution.py:721
  41.3 6.7 %collective-permute-start.9 = (f32[76,8,128]{2,1,0:T(8,128)S(1)}, f32[76,8,128]{2,1,0:T(8,128)S(1)}, u32[]{:S(2)}, u32[]{:S(2)}) collective-permute-start(f32[76,8,128]{2,1,0:T(8,128)S(1)} %collective-permute-done.4.y_two_a), channel_id=1, source_target_pairs={{0,128},{128,0},{1,129},{129,1},{2,130},{130,2},{3,131},{131,3},{4... | collective-permute-start | bytes 933896 | tf_op jit(solution)/shard_map/ppermute | solution.py:721
  44.8 3.2 %collective-permute-start.5 = (f32[72,8,128]{2,1,0:T(8,128)S(1)}, f32[72,8,128]{2,1,0:T(8,128)S(1)}, u32[]{:S(2)}, u32[]{:S(2)}) collective-permute-start(f32[72,8,128]{2,1,0:T(8,128)S(1)} %get-tuple-element.30.own), channel_id=1, source_target_pairs={{0,128},{128,0},{1,129},{129,1},{2,130},{130,2},{3,131},{131,3},{4... | collective-permute-start | bytes 884744 | tf_op jit(solution)/shard_map/ppermute | solution.py:721
  44.8 1.8 %collective-permute-start.6 = (f32[30,8,128]{2,1,0:T(8,128)S(1)}, f32[30,8,128]{2,1,0:T(8,128)S(1)}, u32[]{:S(2)}, u32[]{:S(2)}) collective-permute-start(f32[30,8,128]{2,1,0:T(8,128)S(1)} %collective-permute-done.1.one.x_one_a), channel_id=1, source_target_pairs={{0,128},{128,0},{1,129},{129,1},{2,130},{130,2},{3,131},{131,3},{4... | collective-permute-start | bytes 368648 | tf_op jit(solution)/shard_map/ppermute | solution.py:721
  46.6 1.3 %collective-permute-start.7 = (f32[30,8,128]{2,1,0:T(8,128)S(1)}, f32[30,8,128]{2,1,0:T(8,128)S(1)}, u32[]{:S(2)}, u32[]{:S(2)}) collective-permute-start(f32[30,8,128]{2,1,0:T(8,128)S(1)} %collective-permute-done.2.two.x_two_a), channel_id=1, source_target_pairs={{0,128},{128,0},{1,129},{129,1},{2,130},{130,2},{3,131},{131,3},{4... | collective-permute-start | bytes 368648 | tf_op jit(solution)/shard_map/ppermute | solution.py:721
  69.1 25.0 %all-to-all-start.1 = ((f32[128,4,128]{2,1,0:T(4,128)}), f32[128,4,128]{2,1,0:T(4,128)S(1)}, u32[]{:S(2)}, u32[]{:S(2)}) async-start(f32[128,4,128]{2,1,0:T(4,128)} %get-tuple-element.37), calls=%async_computation.1 | async-start | bytes 524288 | tf_op jit(solution)/shard_map/all_to_all | solution.py:725
  78.9 5.2 %collective-permute-start.11 = (f32[15,8,128]{2,1,0:T(8,128)S(1)}, f32[15,8,128]{2,1,0:T(8,128)S(1)}, u32[]{:S(2)}, u32[]{:S(2)}) collective-permute-start(f32[15,8,128]{2,1,0:T(8,128)S(1)} %get-tuple-element.43), channel_id=1, source_target_pairs={{0,16},{16,0},{32,48},{48,32},{64,80},{80,64},{96,112},{112,96},{1... | collective-permute-start | bytes 184328 | tf_op jit(solution)/shard_map/ppermute | solution.py:715
  79.5 9.1 %collective-permute-start.12 = (f32[15,8,128]{2,1,0:T(8,128)S(1)}, f32[15,8,128]{2,1,0:T(8,128)S(1)}, u32[]{:S(2)}, u32[]{:S(2)}) collective-permute-start(f32[15,8,128]{2,1,0:T(8,128)S(1)} %get-tuple-element.44), channel_id=1, source_target_pairs={{16,32},{32,16},{48,64},{64,48},{80,96},{96,80},{17,33},{33,17},{4... | collective-permute-start | bytes 184328 | tf_op jit(solution)/shard_map/ppermute | solution.py:716
  88.6 8.2 %collective-permute-start.13 = (f32[38,8,128]{2,1,0:T(8,128)S(1)}, f32[38,8,128]{2,1,0:T(8,128)S(1)}, u32[]{:S(2)}, u32[]{:S(2)}) collective-permute-start(f32[38,8,128]{2,1,0:T(8,128)S(1)} %get-tuple-element.46), channel_id=1, source_target_pairs={{0,1},{1,0},{2,3},{3,2},{4,5},{5,4},{6,7},{7,6},{8,9},{9,8},{10,11... | collective-permute-start | bytes 466952 | tf_op jit(solution)/shard_map/ppermute | solution.py:715
  89.8 8.1 %collective-permute-start.14 = (f32[38,8,128]{2,1,0:T(8,128)S(1)}, f32[38,8,128]{2,1,0:T(8,128)S(1)}, u32[]{:S(2)}, u32[]{:S(2)}) collective-permute-start(f32[38,8,128]{2,1,0:T(8,128)S(1)} %get-tuple-element.47), channel_id=1, source_target_pairs={{1,2},{2,1},{3,4},{4,3},{5,6},{6,5},{7,8},{8,7},{9,10},{10,9},{11,... | collective-permute-start | bytes 466952 | tf_op jit(solution)/shard_map/ppermute | solution.py:716
  94.1 18.7 %collective-permute-start.10 = (f32[128,4,128]{2,1,0:T(4,128)S(1)}, f32[128,4,128]{2,1,0:T(4,128)S(1)}, u32[]{:S(2)}, u32[]{:S(2)}) collective-permute-start(f32[128,4,128]{2,1,0:T(4,128)S(1)} %all-to-all-done.1.r3_a), channel_id=1, source_target_pairs={{0,128},{128,0},{1,129},{129,1},{2,130},{130,2},{3,131},{131,3},{4... | collective-permute-start | bytes 786440 | tf_op jit(solution)/shard_map/ppermute | solution.py:721
  96.8 6.0 %collective-permute-start.17 = (f32[38,8,128]{2,1,0:T(8,128)S(1)}, f32[38,8,128]{2,1,0:T(8,128)S(1)}, u32[]{:S(2)}, u32[]{:S(2)}) collective-permute-start(f32[38,8,128]{2,1,0:T(8,128)S(1)} %collective-permute-done.13.y_one_a), channel_id=1, source_target_pairs={{0,128},{128,0},{1,129},{129,1},{2,130},{130,2},{3,131},{131,3},{4... | collective-permute-start | bytes 466952 | tf_op jit(solution)/shard_map/ppermute | solution.py:721
  97.9 4.9 %collective-permute-start.18 = (f32[38,8,128]{2,1,0:T(8,128)S(1)}, f32[38,8,128]{2,1,0:T(8,128)S(1)}, u32[]{:S(2)}, u32[]{:S(2)}) collective-permute-start(f32[38,8,128]{2,1,0:T(8,128)S(1)} %collective-permute-done.14.y_two_a), channel_id=1, source_target_pairs={{0,128},{128,0},{1,129},{129,1},{2,130},{130,2},{3,131},{131,3},{4... | collective-permute-start | bytes 466952 | tf_op jit(solution)/shard_map/ppermute | solution.py:721
  101.4 1.2 %collective-permute-start.15 = (f32[15,8,128]{2,1,0:T(8,128)S(1)}, f32[15,8,128]{2,1,0:T(8,128)S(1)}, u32[]{:S(2)}, u32[]{:S(2)}) collective-permute-start(f32[15,8,128]{2,1,0:T(8,128)S(1)} %collective-permute-done.11.one.x_one_a), channel_id=1, source_target_pairs={{0,128},{128,0},{1,129},{129,1},{2,130},{130,2},{3,131},{131,3},{4... | collective-permute-start | bytes 184328 | tf_op jit(solution)/shard_map/ppermute | solution.py:721
  101.4 1.4 %collective-permute-start.16 = (f32[15,8,128]{2,1,0:T(8,128)S(1)}, f32[15,8,128]{2,1,0:T(8,128)S(1)}, u32[]{:S(2)}, u32[]{:S(2)}) collective-permute-start(f32[15,8,128]{2,1,0:T(8,128)S(1)} %collective-permute-done.12.two.x_two_a), channel_id=1, source_target_pairs={{0,128},{128,0},{1,129},{129,1},{2,130},{130,2},{3,131},{131,3},{4... | collective-permute-start | bytes 184328 | tf_op jit(solution)/shard_map/ppermute | solution.py:721

commit v8 on v7

--- a/solution.py
+++ b/solution.py
@@ -543,7 +543,7 @@
     smooth(2, b2, weights2, inv2, e2, d2, o2, c2)
     out.start(c2, c2_hbm)
     smooth(1, b1, weights1, inv1, e1, d1, o1, c1)
-    out.start(c1, c1_hbm)
+    out.start(c1.at[:, 5:23], c1_hbm.at[:, 5:23])
     out.finish()
 
 
@@ -557,7 +557,7 @@
     weights1, diag1 = split3(w1)[0], w1.at[7]
     copies = Copies(sems.at[pl.ds(2, 4)])
     copies.start(c2_hbm, c2)
-    copies.start(c1_hbm, x1)
+    copies.start(c1_hbm.at[:, 5:23], x1.at[:, 5:23])
     copies.start(w1_hbm.at[:, :, 6:22], w1.at[:, :, 6:22])
     copies.start(right_hbm, right)
     coarse_first_kernel(
@@ -613,16 +613,20 @@
 
 
 def second_kernel(
-    own_hbm, w1_hbm, w2_hbm,
-    x_one_a, x_two_a, y_one_a, y_two_a, x_one_b, x_two_b, y_one_b, y_two_b, c1_hbm, c2_hbm,
-    w1, w2, own, b1, e1, d1, o1, c1, b2, e2, d2, o2, c2, sems,
+    own_hbm, w1_hbm, w2_hbm, x1_hbm, right_hbm,
+    x_one_a, x_two_a, y_one_a, y_two_a, x_one_b, x_two_b, y_one_b, y_two_b, sum3,
+    out_x, out_r,
+    w1, w2, x1, right, own, b1, e1, d1, o1, c1, b2, e2, d2, o2, c2, s2, tmp3, tmp2, rest, sems,
 ):
     core, gx, gy = position()
     even_x, even_y = is_even(gx), is_even(gy)
     copies = Copies(sems)
-    for src, dst in ((own_hbm, own), (w2_hbm, w2), (w1_hbm.at[0:7], w1)):
+    for src, dst in (
+        (own_hbm, own), (w2_hbm, w2), (w1_hbm, w1), (x1_hbm, x1), (right_hbm, right)
+    ):
         copies.start(src, dst)
     weights1, inv1 = split3(w1)
+    diag1 = w1.at[7]
     weights2, inv2 = split3(w2)
     spread(1, 0, core, even_x, even_y, x_one_a, x_two_a, y_one_a, y_two_a, b1, b2, 0)
     spread(1, 0, 1 - core, even_x, even_y, x_one_b, x_two_b, y_one_b, y_two_b, b1, b2, 0)
@@ -631,36 +635,11 @@
         spread_own(1, 0, c, own.at[c], b1, b2, 0)
     copies.made[1].wait()
     smooth(2, b2, weights2, inv2, e2, d2, o2, c2)
-    middle = copies.start(c2, c2_hbm)
     copies.made[2].wait()
     smooth(1, b1, weights1, inv1, e1, d1, o1, c1)
-    last = copies.start(c1, c1_hbm)
-    middle.wait()
-    last.wait()
-
-
-def join_second_kernel(
-    gx_n, gy_n, r3_a, r3_b, r3f_a, r3f_b, w3_hbm, w4_hbm, w1_hbm, x1_hbm, right_hbm,
-    c1_hbm, c2_hbm, out_x, out_r,
-    sum3, w3, w4, b3, e3, d3, o3, c3, x4, w1, x1, right, c1, c2, s2, tmp3, tmp2, rest, sems,
-):
-    core = position()[0]
-    weights1, diag1 = split3(w1)[0], w1.at[7]
-    copies = Copies(sems.at[pl.ds(2, 7)])
-    own = pl.ds(6, 16)
-    for src, dst in (
-        (c2_hbm, c2), (c1_hbm, c1), (x1_hbm, x1), (w1_hbm.at[:, :, own], w1.at[:, :, own]),
-        (right_hbm, right),
-    ):
-        copies.start(src, dst)
-    coarse_second_kernel(
-        gx_n, gy_n, r3_a, r3_b, r3f_a, r3f_b, w3_hbm, w4_hbm, sum3,
-        w3, w4, b3, e3, d3, o3, c3, x4, sems.at[pl.ds(0, 2)],
-    )
-    copies.made[0].wait()
+    copies.made[3].wait()
+    copies.made[4].wait()
     combine(sum3, c2, s2, tmp3, tmp2)
-    copies.made[1].wait()
-    copies.made[2].wait()
 
     def finish(i, _):
         c1[:, i] = x1[:, i] + DAMPING * (c1[:, i] + tmp2[:, i // 2 - 1])
@@ -668,8 +647,6 @@
 
     lax.fori_loop(5, 23, finish, 0)
     field = copies.start(c1.at[core, 6:22, 8:24, :], out_x)
-    copies.made[3].wait()
-    copies.made[4].wait()
 
     def residual(i):
         mid, near = weighted(1, i, 2, c1, weights1)
@@ -777,17 +754,19 @@
     y_one, y_two = trade(first, second, "gy")
     y_one_o, y_two_o = swap(y_one), swap(y_two)
     flat = (count * 4, 128)
-    c1, c2 = call(
-        second_kernel, [s1, s2],
-        [(7,) + s1, w2s, (2, 36, 8, 128), s1, s1, s1, s1, s1, s2, s2, s2, s2, s2],
-        own_kept, w1, w2, x_one, x_two, y_one, y_two, x_one_o, x_two_o, y_one_o, y_two_o,
-        hbm_in=(0, 1, 2), hbm_out=(0, 1), sems=5, limit=28,
+    (c3,) = call(
+        functools.partial(coarse_second_kernel, gx_n, gy_n),
+        [sum3], [w3s, w4s, s3, s3, s3, s3, s3, s4],
+        r3, r3_o, r3.reshape(flat), r3_o.reshape(flat), w3, w4,
+        hbm_in=(4, 5), sems=2, limit=12,
     )
     solution_field, residual = call(
-        functools.partial(join_second_kernel, gx_n, gy_n), [(16, 16, 128)] * 2,
-        [sum3, w3s, w4s, s3, s3, s3, s3, s3, s4, w1s, s1, block, s1, s2] + tmps,
-        r3, r3_o, r3.reshape(flat), r3_o.reshape(flat), w3, w4, w1, x1, right, c1, c2,
-        hbm_in=(4, 5, 6, 7, 8, 9, 10), hbm_out=(0, 1), sems=9, limit=28,
+        second_kernel, [(16, 16, 128)] * 2,
+        [w1s, w2s, s1, (2, 16, 16, 128), (2, 36, 8, 128), s1, s1, s1, s1, s1, s2, s2, s2, s2, s2]
+        + tmps,
+        own_kept, w1, w2, x1, right,
+        x_one, x_two, y_one, y_two, x_one_o, x_two_o, y_one_o, y_two_o, c3,
+        hbm_in=(0, 1, 2, 3, 4), hbm_out=(0, 1), sems=7, limit=28,
     )
     return solution_field, residual
 

time: 123 us -> 118 us (0.959)
  Pallas kernels: 42.2 us -> 38.3 us
    pallas_call x7, Pallas kernels: 42.2 us -> 38.3 us  [call(): pl.pallas_call(kernel, out_shape=[pltpu.HBM(s, F32) if i in hbm_out else...]
  transfers between devices with their start and end apart: 21 -> 21, of which waited for: 9 -> 7; matrix products, arithmetic and copies ran while one was open for 0% -> 0% of each run, Pallas kernels for 18% -> 14%
where the time goes in v8:
time: 118 us; the launch traced here: 116 us
  starting transfers between devices  61.6 us (52%)
  Pallas kernels  38.3 us (32%)
  waiting for transfers between devices  15.6 us (13%)
    pallas_call x7, Pallas kernels, call(): pl.pallas_call(kernel, out_shape=[pltpu.HBM(s, F32) if i in hbm_out else...  38.3 us
    all_to_all x2, starting transfers between devices, everywhere(): return lax.all_to_all(slots, ('gx', 'gy'), 0, 0, tiled=True)  24.7 us
    ppermute x4, starting transfers between devices, trade(): two = lax.ppermute(second, axis, others)  18 us
    ppermute x11, starting transfers between devices, swap(): return lax.ppermute(x, 'grp', [(0, 1), (1, 0)])  14.9 us
    ppermute x4, waiting for transfers between devices, trade(): two = lax.ppermute(second, axis, others)  12.6 us
    ppermute x4, starting transfers between devices, trade(): one = lax.ppermute(first, axis, pairs)  4 us
  transfers between devices with their start and end apart: 21, of which 7 were waited for; matrix products, arithmetic and copies ran while one was open for 0% of the time, Pallas kernels for 14%

profile of v8, /device:TPU:27, one launch (start us, length us, event | category | flops | bytes accessed | tf_op | source)
XLA Modules:
  0.0 116.4 jit_solution(12205597723071715027)
XLA Ops:
  0.6 2.8 %shard_map.41 = (f32[72,8,128]{2,1,0:T(8,128)S(1)}, f32[8,8,128]{2,1,0:T(8,128)}, f32[30,8,128]{2,1,0:T(8,128)S(1)}, f32[30,8,128]{2,1,0:T(8,128)S(1)}, f32[128,8,128]{2,1,0:T(8,128)}) custom-call(f32[16,16,128]{2,1,0:T(8,128)} %a_hbm.3, f32[16,16,128]{2,1,0:T(8,128)} %b_hbm.3), custom_call_target="tpu_custom_call" | custom-call | tf_op jit(solution)/shard_map/pallas_call | solution.py:674
  3.4 14.8 %all-to-all-start = ((f32[128,8,128]{2,1,0:T(8,128)}), f32[128,8,128]{2,1,0:T(8,128)S(1)}, u32[]{:S(2)}, u32[]{:S(2)}) async-start(f32[128,8,128]{2,1,0:T(8,128)} %get-tuple-element.24), calls=%async_computation | async-start | bytes 1048576 | tf_op jit(solution)/shard_map/all_to_all | solution.py:702
  18.8 4.6 %collective-permute-start.2 = (f32[30,8,128]{2,1,0:T(8,128)S(1)}, f32[30,8,128]{2,1,0:T(8,128)S(1)}, u32[]{:S(2)}, u32[]{:S(2)}) collective-permute-start(f32[30,8,128]{2,1,0:T(8,128)S(1)} %get-tuple-element.27), channel_id=1, source_target_pairs={{16,32},{32,16},{48,64},{64,48},{80,96},{96,80},{17,33},{33,17},{4... | collective-permute-start | bytes 368648 | tf_op jit(solution)/shard_map/ppermute | solution.py:693
  24.1 5.2 %collective-permute-done.2.two.x_two_a = f32[30,8,128]{2,1,0:T(8,128)S(1)} collective-permute-done((f32[30,8,128]{2,1,0:T(8,128)S(1)}, f32[30,8,128]{2,1,0:T(8,128)S(1)}, u32[]{:S(2)}, u32[]{:S(2)}) %collective-permute-start.2) | collective-permute-done | bytes 122912 | tf_op jit(solution)/shard_map/ppermute | solution.py:693
  29.3 1.7 %collective-permute-start.3 = (f32[76,8,128]{2,1,0:T(8,128)S(1)}, f32[76,8,128]{2,1,0:T(8,128)S(1)}, u32[]{:S(2)}, u32[]{:S(2)}) collective-permute-start(f32[76,8,128]{2,1,0:T(8,128)S(1)} %get-tuple-element.29), channel_id=1, source_target_pairs={{0,1},{1,0},{2,3},{3,2},{4,5},{5,4},{6,7},{7,6},{8,9},{9,8},{10,11... | collective-permute-start | bytes 933896 | tf_op jit(solution)/shard_map/ppermute | solution.py:692
  31.0 4.4 %collective-permute-start.4 = (f32[76,8,128]{2,1,0:T(8,128)S(1)}, f32[76,8,128]{2,1,0:T(8,128)S(1)}, u32[]{:S(2)}, u32[]{:S(2)}) collective-permute-start(f32[76,8,128]{2,1,0:T(8,128)S(1)} %get-tuple-element.30), channel_id=1, source_target_pairs={{1,2},{2,1},{3,4},{4,3},{5,6},{6,5},{7,8},{8,7},{9,10},{10,9},{11,... | collective-permute-start | bytes 933896 | tf_op jit(solution)/shard_map/ppermute | solution.py:693
  35.5 3.0 %collective-permute-start = (f32[128,8,128]{2,1,0:T(8,128)S(1)}, f32[128,8,128]{2,1,0:T(8,128)S(1)}, u32[]{:S(2)}, u32[]{:S(2)}) collective-permute-start(f32[128,8,128]{2,1,0:T(8,128)S(1)} %all-to-all-done.r3_a), channel_id=1, source_target_pairs={{0,128},{128,0},{1,129},{129,1},{2,130},{130,2},{3,131},{131,3},{4... | collective-permute-start | bytes 1572872 | tf_op jit(solution)/shard_map/ppermute | solution.py:698
  38.5 0.8 collective-permute-start.8
  39.3 2.0 %collective-permute-done.4.y_two_a = f32[76,8,128]{2,1,0:T(8,128)S(1)} collective-permute-done((f32[76,8,128]{2,1,0:T(8,128)S(1)}, f32[76,8,128]{2,1,0:T(8,128)S(1)}, u32[]{:S(2)}, u32[]{:S(2)}) %collective-permute-start.4) | collective-permute-done | bytes 311328 | tf_op jit(solution)/shard_map/ppermute | solution.py:693
  41.3 3.5 %collective-permute-start.9 = (f32[76,8,128]{2,1,0:T(8,128)S(1)}, f32[76,8,128]{2,1,0:T(8,128)S(1)}, u32[]{:S(2)}, u32[]{:S(2)}) collective-permute-start(f32[76,8,128]{2,1,0:T(8,128)S(1)} %collective-permute-done.4.y_two_a), channel_id=1, source_target_pairs={{0,128},{128,0},{1,129},{129,1},{2,130},{130,2},{3,131},{131,3},{4... | collective-permute-start | bytes 933896 | tf_op jit(solution)/shard_map/ppermute | solution.py:698
  45.3 1.3 %collective-permute-done.6.x_one_b = f32[30,8,128]{2,1,0:T(8,128)S(1)} collective-permute-done((f32[30,8,128]{2,1,0:T(8,128)S(1)}, f32[30,8,128]{2,1,0:T(8,128)S(1)}, u32[]{:S(2)}, u32[]{:S(2)}) %collective-permute-start.6) | collective-permute-done | bytes 122912 | tf_op jit(solution)/shard_map/ppermute | solution.py:698
  47.0 1.0 collective-permute-done.7.x_two_b
  48.0 12.0 %shard_map.43 = (f32[8,2,28,32,128]{4,3,2,1,0:T(8,128)}, f32[7,2,10,24,128]{4,3,2,1,0:T(8,128)}, f32[2,28,32,128]{3,2,1,0:T(8,128)}, f32[2,10,24,128]{3,2,1,0:T(8,128)}, f32[2,16,16,128]{3,2,1,0:T(8,128)}) custom-call(f32[16,16,128]{2,1,0:T(8,128)} %a_hbm.3, f32[16,16,128]{2,1,0:T(8,128)} %b_hbm.3, f32[8,8,128]{2,1,0:T(8,128)} %get-tuple-element.25.mid_hbm, ...), custom_call_target="tpu_custom_call" | custom-call | tf_op jit(solution)/shard_map/pallas_call | solution.py:674
  60.0 8.1 %shard_map.44 = (f32[7,2,5,24,128]{4,3,2,1,0:T(8,128)}, f32[4,4,32,128]{3,2,1,0:T(8,128)}, f32[2,28,32,128]{3,2,1,0:T(8,128)}, f32[2,36,8,128]{3,2,1,0:T(8,128)}...) custom-call(f32[128,8,128]{2,1,0:T(8,128)S(1)} %all-to-all-done.r3_a, ...), custom_call_target="tpu_custom_call" | custom-call | tf_op jit(solution)/shard_map/pallas_call | solution.py:674
  68.1 9.9 %all-to-all-start.1 = ((f32[128,4,128]{2,1,0:T(4,128)}), f32[128,4,128]{2,1,0:T(4,128)S(1)}, u32[]{:S(2)}, u32[]{:S(2)}) async-start(f32[128,4,128]{2,1,0:T(4,128)} %get-tuple-element.43), calls=%async_computation.1 | async-start | bytes 524288 | tf_op jit(solution)/shard_map/all_to_all | solution.py:702
  78.5 4.6 %collective-permute-start.11 = (f32[15,8,128]{2,1,0:T(8,128)S(1)}, f32[15,8,128]{2,1,0:T(8,128)S(1)}, u32[]{:S(2)}, u32[]{:S(2)}) collective-permute-start(f32[15,8,128]{2,1,0:T(8,128)S(1)} %get-tuple-element.39), channel_id=1, source_target_pairs={{16,32},{32,16},{48,64},{64,48},{80,96},{96,80},{17,33},{33,17},{4... | collective-permute-start | bytes 184328 | tf_op jit(solution)/shard_map/ppermute | solution.py:693
  83.2 4.4 %collective-permute-done.11.two.x_two_a = f32[15,8,128]{2,1,0:T(8,128)S(1)} collective-permute-done((f32[15,8,128]{2,1,0:T(8,128)S(1)}, f32[15,8,128]{2,1,0:T(8,128)S(1)}, u32[]{:S(2)}, u32[]{:S(2)}) %collective-permute-start.11) | collective-permute-done | bytes 61472 | tf_op jit(solution)/shard_map/ppermute | solution.py:693
  87.6 1.2 %collective-permute-start.12 = (f32[38,8,128]{2,1,0:T(8,128)S(1)}, f32[38,8,128]{2,1,0:T(8,128)S(1)}, u32[]{:S(2)}, u32[]{:S(2)}) collective-permute-start(f32[38,8,128]{2,1,0:T(8,128)S(1)} %get-tuple-element.41), channel_id=1, source_target_pairs={{0,1},{1,0},{2,3},{3,2},{4,5},{5,4},{6,7},{7,6},{8,9},{9,8},{10,11... | collective-permute-start | bytes 466952 | tf_op jit(solution)/shard_map/ppermute | solution.py:692
  88.8 4.4 %collective-permute-start.13 = (f32[38,8,128]{2,1,0:T(8,128)S(1)}, f32[38,8,128]{2,1,0:T(8,128)S(1)}, u32[]{:S(2)}, u32[]{:S(2)}) collective-permute-start(f32[38,8,128]{2,1,0:T(8,128)S(1)} %get-tuple-element.42), channel_id=1, source_target_pairs={{1,2},{2,1},{3,4},{4,3},{5,6},{6,5},{7,8},{8,7},{9,10},{10,9},{11,... | collective-permute-start | bytes 466952 | tf_op jit(solution)/shard_map/ppermute | solution.py:693
  93.2 2.6 %collective-permute-start.18 = (f32[128,4,128]{2,1,0:T(4,128)S(1)}, f32[128,4,128]{2,1,0:T(4,128)S(1)}, u32[]{:S(2)}, u32[]{:S(2)}) collective-permute-start(f32[128,4,128]{2,1,0:T(4,128)S(1)} %all-to-all-done.1.r3_a), channel_id=1, source_target_pairs={{0,128},{128,0},{1,129},{129,1},{2,130},{130,2},{3,131},{131,3},{4... | collective-permute-start | bytes 786440 | tf_op jit(solution)/shard_map/ppermute | solution.py:698
  95.9 1.0 collective-permute-done.13.y_two_a
  96.9 3.5 %collective-permute-start.17 = (f32[38,8,128]{2,1,0:T(8,128)S(1)}, f32[38,8,128]{2,1,0:T(8,128)S(1)}, u32[]{:S(2)}, u32[]{:S(2)}) collective-permute-start(f32[38,8,128]{2,1,0:T(8,128)S(1)} %collective-permute-done.13.y_two_a), channel_id=1, source_target_pairs={{0,128},{128,0},{1,129},{129,1},{2,130},{130,2},{3,131},{131,3},{4... | collective-permute-start | bytes 466952 | tf_op jit(solution)/shard_map/ppermute | solution.py:698
  100.9 4.0 %shard_map.46.sum3 = f32[2,3,24,128]{3,2,1,0:T(8,128)S(1)} custom-call(f32[128,4,128]{2,1,0:T(4,128)S(1)} %all-to-all-done.1.r3_a, f32[128,4,128]{2,1,0:T(4,128)S(1)} %collective-permute-done.18.r3_b, f32[512,128]{1,0:T(8,128)S(1)} %bitcast.5, f32[512,128]{1,0:T(8,128)S(1)} %bitcast.7, f32[7,2,5,24,128]{4,3,2,1,0:T(8,128)} %get-tuple-element.44.w3_hbm, ...), custom_call_target="tpu_custom_call" | custom-call | tf_op jit(solution)/shard_map/pallas_call | solution.py:674
  104.9 11.3 %shard_map.47 = (f32[16,16,128]{2,1,0:T(8,128)}, f32[16,16,128]{2,1,0:T(8,128)}) custom-call(f32[2,36,8,128]{3,2,1,0:T(8,128)} %get-tuple-element.35.own_hbm, f32[8,2,28,32,128]{4,3,2,1,0:T(8,128)} %get-tuple-element.31.w1_hbm, f32[7,2,10,24,128]{4,3,2,1,0:T(8,128)} %get-tuple-element.36.w2_hbm, f32[2,28,32,128]{3,2,1,0:T(8,128)} %get-tuple-element.37.x1_hbm, ...), custom_call_target="tpu_custom_call" | custom-call | tf_op jit(solution)/shard_map/pallas_call | solution.py:674
  (25 shorter events, 3.3 us)
Async XLA Ops:
  3.4 32.0 %all-to-all-start = ((f32[128,8,128]{2,1,0:T(8,128)}), f32[128,8,128]{2,1,0:T(8,128)S(1)}, u32[]{:S(2)}, u32[]{:S(2)}) async-start(f32[128,8,128]{2,1,0:T(8,128)} %get-tuple-element.24), calls=%async_computation | async-start | bytes 1048576 | tf_op jit(solution)/shard_map/all_to_all | solution.py:702
  18.3 5.8 %collective-permute-start.1 = (f32[30,8,128]{2,1,0:T(8,128)S(1)}, f32[30,8,128]{2,1,0:T(8,128)S(1)}, u32[]{:S(2)}, u32[]{:S(2)}) collective-permute-start(f32[30,8,128]{2,1,0:T(8,128)S(1)} %get-tuple-element.26), channel_id=1, source_target_pairs={{0,16},{16,0},{32,48},{48,32},{64,80},{80,64},{96,112},{112,96},{1... | collective-permute-start | bytes 368648 | tf_op jit(solution)/shard_map/ppermute | solution.py:692
  18.8 10.5 %collective-permute-start.2 = (f32[30,8,128]{2,1,0:T(8,128)S(1)}, f32[30,8,128]{2,1,0:T(8,128)S(1)}, u32[]{:S(2)}, u32[]{:S(2)}) collective-permute-start(f32[30,8,128]{2,1,0:T(8,128)S(1)} %get-tuple-element.27), channel_id=1, source_target_pairs={{16,32},{32,16},{48,64},{64,48},{80,96},{96,80},{17,33},{33,17},{4... | collective-permute-start | bytes 368648 | tf_op jit(solution)/shard_map/ppermute | solution.py:693
  29.3 9.2 %collective-permute-start.3 = (f32[76,8,128]{2,1,0:T(8,128)S(1)}, f32[76,8,128]{2,1,0:T(8,128)S(1)}, u32[]{:S(2)}, u32[]{:S(2)}) collective-permute-start(f32[76,8,128]{2,1,0:T(8,128)S(1)} %get-tuple-element.29), channel_id=1, source_target_pairs={{0,1},{1,0},{2,3},{3,2},{4,5},{5,4},{6,7},{7,6},{8,9},{9,8},{10,11... | collective-permute-start | bytes 933896 | tf_op jit(solution)/shard_map/ppermute | solution.py:692
  31.0 10.3 %collective-permute-start.4 = (f32[76,8,128]{2,1,0:T(8,128)S(1)}, f32[76,8,128]{2,1,0:T(8,128)S(1)}, u32[]{:S(2)}, u32[]{:S(2)}) collective-permute-start(f32[76,8,128]{2,1,0:T(8,128)S(1)} %get-tuple-element.30), channel_id=1, source_target_pairs={{1,2},{2,1},{3,4},{4,3},{5,6},{6,5},{7,8},{8,7},{9,10},{10,9},{11,... | collective-permute-start | bytes 933896 | tf_op jit(solution)/shard_map/ppermute | solution.py:693
  35.5 24.5 %collective-permute-start = (f32[128,8,128]{2,1,0:T(8,128)S(1)}, f32[128,8,128]{2,1,0:T(8,128)S(1)}, u32[]{:S(2)}, u32[]{:S(2)}) collective-permute-start(f32[128,8,128]{2,1,0:T(8,128)S(1)} %all-to-all-done.r3_a), channel_id=1, source_target_pairs={{0,128},{128,0},{1,129},{129,1},{2,130},{130,2},{3,131},{131,3},{4... | collective-permute-start | bytes 1572872 | tf_op jit(solution)/shard_map/ppermute | solution.py:698
  38.5 9.5 %collective-permute-start.8 = (f32[76,8,128]{2,1,0:T(8,128)S(1)}, f32[76,8,128]{2,1,0:T(8,128)S(1)}, u32[]{:S(2)}, u32[]{:S(2)}) collective-permute-start(f32[76,8,128]{2,1,0:T(8,128)S(1)} %collective-permute-done.3.y_one_a), channel_id=1, source_target_pairs={{0,128},{128,0},{1,129},{129,1},{2,130},{130,2},{3,131},{131,3},{4... | collective-permute-start | bytes 933896 | tf_op jit(solution)/shard_map/ppermute | solution.py:698
  41.3 6.7 %collective-permute-start.9 = (f32[76,8,128]{2,1,0:T(8,128)S(1)}, f32[76,8,128]{2,1,0:T(8,128)S(1)}, u32[]{:S(2)}, u32[]{:S(2)}) collective-permute-start(f32[76,8,128]{2,1,0:T(8,128)S(1)} %collective-permute-done.4.y_two_a), channel_id=1, source_target_pairs={{0,128},{128,0},{1,129},{129,1},{2,130},{130,2},{3,131},{131,3},{4... | collective-permute-start | bytes 933896 | tf_op jit(solution)/shard_map/ppermute | solution.py:698
  44.8 3.2 %collective-permute-start.5 = (f32[72,8,128]{2,1,0:T(8,128)S(1)}, f32[72,8,128]{2,1,0:T(8,128)S(1)}, u32[]{:S(2)}, u32[]{:S(2)}) collective-permute-start(f32[72,8,128]{2,1,0:T(8,128)S(1)} %get-tuple-element.28.own), channel_id=1, source_target_pairs={{0,128},{128,0},{1,129},{129,1},{2,130},{130,2},{3,131},{131,3},{4... | collective-permute-start | bytes 884744 | tf_op jit(solution)/shard_map/ppermute | solution.py:698
  44.8 1.8 %collective-permute-start.6 = (f32[30,8,128]{2,1,0:T(8,128)S(1)}, f32[30,8,128]{2,1,0:T(8,128)S(1)}, u32[]{:S(2)}, u32[]{:S(2)}) collective-permute-start(f32[30,8,128]{2,1,0:T(8,128)S(1)} %collective-permute-done.1.one.x_one_a), channel_id=1, source_target_pairs={{0,128},{128,0},{1,129},{129,1},{2,130},{130,2},{3,131},{131,3},{4... | collective-permute-start | bytes 368648 | tf_op jit(solution)/shard_map/ppermute | solution.py:698
  46.6 1.3 %collective-permute-start.7 = (f32[30,8,128]{2,1,0:T(8,128)S(1)}, f32[30,8,128]{2,1,0:T(8,128)S(1)}, u32[]{:S(2)}, u32[]{:S(2)}) collective-permute-start(f32[30,8,128]{2,1,0:T(8,128)S(1)} %collective-permute-done.2.two.x_two_a), channel_id=1, source_target_pairs={{0,128},{128,0},{1,129},{129,1},{2,130},{130,2},{3,131},{131,3},{4... | collective-permute-start | bytes 368648 | tf_op jit(solution)/shard_map/ppermute | solution.py:698
  68.1 25.1 %all-to-all-start.1 = ((f32[128,4,128]{2,1,0:T(4,128)}), f32[128,4,128]{2,1,0:T(4,128)S(1)}, u32[]{:S(2)}, u32[]{:S(2)}) async-start(f32[128,4,128]{2,1,0:T(4,128)} %get-tuple-element.43), calls=%async_computation.1 | async-start | bytes 524288 | tf_op jit(solution)/shard_map/all_to_all | solution.py:702
  78.0 5.2 %collective-permute-start.10 = (f32[15,8,128]{2,1,0:T(8,128)S(1)}, f32[15,8,128]{2,1,0:T(8,128)S(1)}, u32[]{:S(2)}, u32[]{:S(2)}) collective-permute-start(f32[15,8,128]{2,1,0:T(8,128)S(1)} %get-tuple-element.38), channel_id=1, source_target_pairs={{0,16},{16,0},{32,48},{48,32},{64,80},{80,64},{96,112},{112,96},{1... | collective-permute-start | bytes 184328 | tf_op jit(solution)/shard_map/ppermute | solution.py:692
  78.5 9.1 %collective-permute-start.11 = (f32[15,8,128]{2,1,0:T(8,128)S(1)}, f32[15,8,128]{2,1,0:T(8,128)S(1)}, u32[]{:S(2)}, u32[]{:S(2)}) collective-permute-start(f32[15,8,128]{2,1,0:T(8,128)S(1)} %get-tuple-element.39), channel_id=1, source_target_pairs={{16,32},{32,16},{48,64},{64,48},{80,96},{96,80},{17,33},{33,17},{4... | collective-permute-start | bytes 184328 | tf_op jit(solution)/shard_map/ppermute | solution.py:693
  87.6 8.2 %collective-permute-start.12 = (f32[38,8,128]{2,1,0:T(8,128)S(1)}, f32[38,8,128]{2,1,0:T(8,128)S(1)}, u32[]{:S(2)}, u32[]{:S(2)}) collective-permute-start(f32[38,8,128]{2,1,0:T(8,128)S(1)} %get-tuple-element.41), channel_id=1, source_target_pairs={{0,1},{1,0},{2,3},{3,2},{4,5},{5,4},{6,7},{7,6},{8,9},{9,8},{10,11... | collective-permute-start | bytes 466952 | tf_op jit(solution)/shard_map/ppermute | solution.py:692
  88.8 8.1 %collective-permute-start.13 = (f32[38,8,128]{2,1,0:T(8,128)S(1)}, f32[38,8,128]{2,1,0:T(8,128)S(1)}, u32[]{:S(2)}, u32[]{:S(2)}) collective-permute-start(f32[38,8,128]{2,1,0:T(8,128)S(1)} %get-tuple-element.42), channel_id=1, source_target_pairs={{1,2},{2,1},{3,4},{4,3},{5,6},{6,5},{7,8},{8,7},{9,10},{10,9},{11,... | collective-permute-start | bytes 466952 | tf_op jit(solution)/shard_map/ppermute | solution.py:693
  93.2 7.7 %collective-permute-start.18 = (f32[128,4,128]{2,1,0:T(4,128)S(1)}, f32[128,4,128]{2,1,0:T(4,128)S(1)}, u32[]{:S(2)}, u32[]{:S(2)}) collective-permute-start(f32[128,4,128]{2,1,0:T(4,128)S(1)} %all-to-all-done.1.r3_a), channel_id=1, source_target_pairs={{0,128},{128,0},{1,129},{129,1},{2,130},{130,2},{3,131},{131,3},{4... | collective-permute-start | bytes 786440 | tf_op jit(solution)/shard_map/ppermute | solution.py:698
  95.8 9.1 %collective-permute-start.16 = (f32[38,8,128]{2,1,0:T(8,128)S(1)}, f32[38,8,128]{2,1,0:T(8,128)S(1)}, u32[]{:S(2)}, u32[]{:S(2)}) collective-permute-start(f32[38,8,128]{2,1,0:T(8,128)S(1)} %collective-permute-done.12.y_one_a), channel_id=1, source_target_pairs={{0,128},{128,0},{1,129},{129,1},{2,130},{130,2},{3,131},{131,3},{4... | collective-permute-start | bytes 466952 | tf_op jit(solution)/shard_map/ppermute | solution.py:698
  96.9 8.0 %collective-permute-start.17 = (f32[38,8,128]{2,1,0:T(8,128)S(1)}, f32[38,8,128]{2,1,0:T(8,128)S(1)}, u32[]{:S(2)}, u32[]{:S(2)}) collective-permute-start(f32[38,8,128]{2,1,0:T(8,128)S(1)} %collective-permute-done.13.y_two_a), channel_id=1, source_target_pairs={{0,128},{128,0},{1,129},{129,1},{2,130},{130,2},{3,131},{131,3},{4... | collective-permute-start | bytes 466952 | tf_op jit(solution)/shard_map/ppermute | solution.py:698
  100.4 4.5 %collective-permute-start.14 = (f32[15,8,128]{2,1,0:T(8,128)S(1)}, f32[15,8,128]{2,1,0:T(8,128)S(1)}, u32[]{:S(2)}, u32[]{:S(2)}) collective-permute-start(f32[15,8,128]{2,1,0:T(8,128)S(1)} %collective-permute-done.10.one.x_one_a), channel_id=1, source_target_pairs={{0,128},{128,0},{1,129},{129,1},{2,130},{130,2},{3,131},{131,3},{4... | collective-permute-start | bytes 184328 | tf_op jit(solution)/shard_map/ppermute | solution.py:698
  100.4 4.5 %collective-permute-start.15 = (f32[15,8,128]{2,1,0:T(8,128)S(1)}, f32[15,8,128]{2,1,0:T(8,128)S(1)}, u32[]{:S(2)}, u32[]{:S(2)}) collective-permute-start(f32[15,8,128]{2,1,0:T(8,128)S(1)} %collective-permute-done.11.two.x_two_a), channel_id=1, source_target_pairs={{0,128},{128,0},{1,129},{129,1},{2,130},{130,2},{3,131},{131,3},{4... | collective-permute-start | bytes 184328 | tf_op jit(solution)/shard_map/ppermute | solution.py:698

commit v9 on v8

--- a/solution.py
+++ b/solution.py
@@ -26,6 +26,7 @@
 }
 CHUNK = {1: 2, 2: 2, 3: 3}
 PAD = {1: 0, 2: 1, 3: 1}
+UNROLL = 6
 SCALE = {1: 1.0, 2: 0.25, 3: 0.0625, 4: 0.015625}
 
 
@@ -90,15 +91,18 @@
 
 
 def blocks(start, stop, step, body):
-    if stop - start == step:
-        body(start)
-        return
+    count = (stop - start) // step
+    turns = count // UNROLL if count > UNROLL else 0
 
     def run(n, _):
-        body(start + n * step)
+        for k in range(UNROLL):
+            body(start + (n * UNROLL + k) * step)
         return 0
 
-    lax.fori_loop(0, (stop - start) // step, run, 0)
+    if turns:
+        lax.fori_loop(0, turns, run, 0)
+    for k in range(turns * UNROLL, count):
+        body(start + k * step)
 
 
 def faces(level, a, weights, inv, diag_ref):
@@ -568,11 +572,10 @@
     combine(sum3, c2, s2, tmp3, tmp2)
     copies.made[1].wait()
 
-    def finish(i, _):
+    def finish(i):
         x1[:, i] = DAMPING * (x1[:, i] + tmp2[:, i // 2 - 1])
-        return 0
-
-    lax.fori_loop(5, 23, finish, 0)
+
+    blocks(5, 23, 1, finish)
     out = Copies(sems.at[pl.ds(6, 2)])
     out.start(x1, x1_hbm)
     copies.made[2].wait()
@@ -641,11 +644,10 @@
     copies.made[4].wait()
     combine(sum3, c2, s2, tmp3, tmp2)
 
-    def finish(i, _):
+    def finish(i):
         c1[:, i] = x1[:, i] + DAMPING * (c1[:, i] + tmp2[:, i // 2 - 1])
-        return 0
-
-    lax.fori_loop(5, 23, finish, 0)
+
+    blocks(5, 23, 1, finish)
     field = copies.start(c1.at[core, 6:22, 8:24, :], out_x)
 
     def residual(i):

time: 118 us -> 109 us (0.924)
  Pallas kernels: 38.3 us -> 29.5 us
    pallas_call x7, Pallas kernels: 38.3 us -> 29.5 us  [call(): pl.pallas_call(kernel, out_shape=[pltpu.HBM(s, F32) if i in hbm_out else...]
  transfers between devices with their start and end apart: 21 -> 21, of which waited for: 7 -> 7; matrix products, arithmetic and copies ran while one was open for 0% -> 0% of each run, Pallas kernels for 14% -> 11%
where the time goes in v9:
time: 109 us; the launch traced here: 107 us
  starting transfers between devices  61.7 us (57%)
  Pallas kernels  29.5 us (27%)
  waiting for transfers between devices  15.3 us (14%)
    pallas_call x7, Pallas kernels, call(): pl.pallas_call(kernel, out_shape=[pltpu.HBM(s, F32) if i in hbm_out else...  29.5 us
    all_to_all x2, starting transfers between devices, everywhere(): return lax.all_to_all(slots, ('gx', 'gy'), 0, 0, tiled=True)  24.5 us
    ppermute x4, starting transfers between devices, trade(): two = lax.ppermute(second, axis, others)  18 us
    ppermute x11, starting transfers between devices, swap(): return lax.ppermute(x, 'grp', [(0, 1), (1, 0)])  15.1 us
    ppermute x4, waiting for transfers between devices, trade(): two = lax.ppermute(second, axis, others)  12.4 us
    ppermute x4, starting transfers between devices, trade(): one = lax.ppermute(first, axis, pairs)  4.01 us
    ppermute x11, waiting for transfers between devices, swap(): return lax.ppermute(x, 'grp', [(0, 1), (1, 0)])  2.32 us
  transfers between devices with their start and end apart: 21, of which 7 were waited for; matrix products, arithmetic and copies ran while one was open for 0% of the time, Pallas kernels for 11%

profile of v9, /device:TPU:27, one launch (start us, length us, event | category | flops | bytes accessed | tf_op | source)
XLA Modules:
  0.0 107.4 jit_solution(14940618949372676045)
XLA Ops:
  0.6 2.8 %shard_map.41 = (f32[72,8,128]{2,1,0:T(8,128)S(1)}, f32[8,8,128]{2,1,0:T(8,128)}, f32[30,8,128]{2,1,0:T(8,128)S(1)}, f32[30,8,128]{2,1,0:T(8,128)S(1)}, f32[128,8,128]{2,1,0:T(8,128)}) custom-call(f32[16,16,128]{2,1,0:T(8,128)} %a_hbm.3, f32[16,16,128]{2,1,0:T(8,128)} %b_hbm.3), custom_call_target="tpu_custom_call" | custom-call | tf_op jit(solution)/shard_map/pallas_call | solution.py:676
  3.4 14.8 %all-to-all-start = ((f32[128,8,128]{2,1,0:T(8,128)}), f32[128,8,128]{2,1,0:T(8,128)S(1)}, u32[]{:S(2)}, u32[]{:S(2)}) async-start(f32[128,8,128]{2,1,0:T(8,128)} %get-tuple-element.24), calls=%async_computation | async-start | bytes 1048576 | tf_op jit(solution)/shard_map/all_to_all | solution.py:704
  18.8 4.6 %collective-permute-start.2 = (f32[30,8,128]{2,1,0:T(8,128)S(1)}, f32[30,8,128]{2,1,0:T(8,128)S(1)}, u32[]{:S(2)}, u32[]{:S(2)}) collective-permute-start(f32[30,8,128]{2,1,0:T(8,128)S(1)} %get-tuple-element.27), channel_id=1, source_target_pairs={{16,32},{32,16},{48,64},{64,48},{80,96},{96,80},{17,33},{33,17},{4... | collective-permute-start | bytes 368648 | tf_op jit(solution)/shard_map/ppermute | solution.py:695
  24.1 5.2 %collective-permute-done.2.two.x_two_a = f32[30,8,128]{2,1,0:T(8,128)S(1)} collective-permute-done((f32[30,8,128]{2,1,0:T(8,128)S(1)}, f32[30,8,128]{2,1,0:T(8,128)S(1)}, u32[]{:S(2)}, u32[]{:S(2)}) %collective-permute-start.2) | collective-permute-done | bytes 122912 | tf_op jit(solution)/shard_map/ppermute | solution.py:695
  29.3 1.7 %collective-permute-start.3 = (f32[76,8,128]{2,1,0:T(8,128)S(1)}, f32[76,8,128]{2,1,0:T(8,128)S(1)}, u32[]{:S(2)}, u32[]{:S(2)}) collective-permute-start(f32[76,8,128]{2,1,0:T(8,128)S(1)} %get-tuple-element.29), channel_id=1, source_target_pairs={{0,1},{1,0},{2,3},{3,2},{4,5},{5,4},{6,7},{7,6},{8,9},{9,8},{10,11... | collective-permute-start | bytes 933896 | tf_op jit(solution)/shard_map/ppermute | solution.py:694
  31.0 4.4 %collective-permute-start.4 = (f32[76,8,128]{2,1,0:T(8,128)S(1)}, f32[76,8,128]{2,1,0:T(8,128)S(1)}, u32[]{:S(2)}, u32[]{:S(2)}) collective-permute-start(f32[76,8,128]{2,1,0:T(8,128)S(1)} %get-tuple-element.30), channel_id=1, source_target_pairs={{1,2},{2,1},{3,4},{4,3},{5,6},{6,5},{7,8},{8,7},{9,10},{10,9},{11,... | collective-permute-start | bytes 933896 | tf_op jit(solution)/shard_map/ppermute | solution.py:695
  35.5 3.0 %collective-permute-start = (f32[128,8,128]{2,1,0:T(8,128)S(1)}, f32[128,8,128]{2,1,0:T(8,128)S(1)}, u32[]{:S(2)}, u32[]{:S(2)}) collective-permute-start(f32[128,8,128]{2,1,0:T(8,128)S(1)} %all-to-all-done.r3_a), channel_id=1, source_target_pairs={{0,128},{128,0},{1,129},{129,1},{2,130},{130,2},{3,131},{131,3},{4... | collective-permute-start | bytes 1572872 | tf_op jit(solution)/shard_map/ppermute | solution.py:700
  38.5 0.8 collective-permute-start.8
  39.3 2.0 %collective-permute-done.4.y_two_a = f32[76,8,128]{2,1,0:T(8,128)S(1)} collective-permute-done((f32[76,8,128]{2,1,0:T(8,128)S(1)}, f32[76,8,128]{2,1,0:T(8,128)S(1)}, u32[]{:S(2)}, u32[]{:S(2)}) %collective-permute-start.4) | collective-permute-done | bytes 311328 | tf_op jit(solution)/shard_map/ppermute | solution.py:695
  41.3 3.5 %collective-permute-start.9 = (f32[76,8,128]{2,1,0:T(8,128)S(1)}, f32[76,8,128]{2,1,0:T(8,128)S(1)}, u32[]{:S(2)}, u32[]{:S(2)}) collective-permute-start(f32[76,8,128]{2,1,0:T(8,128)S(1)} %collective-permute-done.4.y_two_a), channel_id=1, source_target_pairs={{0,128},{128,0},{1,129},{129,1},{2,130},{130,2},{3,131},{131,3},{4... | collective-permute-start | bytes 933896 | tf_op jit(solution)/shard_map/ppermute | solution.py:700
  45.3 1.3 %collective-permute-done.6.x_one_b = f32[30,8,128]{2,1,0:T(8,128)S(1)} collective-permute-done((f32[30,8,128]{2,1,0:T(8,128)S(1)}, f32[30,8,128]{2,1,0:T(8,128)S(1)}, u32[]{:S(2)}, u32[]{:S(2)}) %collective-permute-start.6) | collective-permute-done | bytes 122912 | tf_op jit(solution)/shard_map/ppermute | solution.py:700
  47.0 1.0 collective-permute-done.7.x_two_b
  48.0 7.3 %shard_map.43 = (f32[8,2,28,32,128]{4,3,2,1,0:T(8,128)}, f32[7,2,10,24,128]{4,3,2,1,0:T(8,128)}, f32[2,28,32,128]{3,2,1,0:T(8,128)}, f32[2,10,24,128]{3,2,1,0:T(8,128)}, f32[2,16,16,128]{3,2,1,0:T(8,128)}) custom-call(f32[16,16,128]{2,1,0:T(8,128)} %a_hbm.3, f32[16,16,128]{2,1,0:T(8,128)} %b_hbm.3, f32[8,8,128]{2,1,0:T(8,128)} %get-tuple-element.25.mid_hbm, ...), custom_call_target="tpu_custom_call" | custom-call | tf_op jit(solution)/shard_map/pallas_call | solution.py:676
  55.3 7.5 %shard_map.44 = (f32[7,2,5,24,128]{4,3,2,1,0:T(8,128)}, f32[4,4,32,128]{3,2,1,0:T(8,128)}, f32[2,28,32,128]{3,2,1,0:T(8,128)}, f32[2,36,8,128]{3,2,1,0:T(8,128)}...) custom-call(f32[128,8,128]{2,1,0:T(8,128)S(1)} %all-to-all-done.r3_a, ...), custom_call_target="tpu_custom_call" | custom-call | tf_op jit(solution)/shard_map/pallas_call | solution.py:676
  62.8 9.7 %all-to-all-start.1 = ((f32[128,4,128]{2,1,0:T(4,128)}), f32[128,4,128]{2,1,0:T(4,128)S(1)}, u32[]{:S(2)}, u32[]{:S(2)}) async-start(f32[128,4,128]{2,1,0:T(4,128)} %get-tuple-element.43), calls=%async_computation.1 | async-start | bytes 524288 | tf_op jit(solution)/shard_map/all_to_all | solution.py:704
  73.0 4.6 %collective-permute-start.11 = (f32[15,8,128]{2,1,0:T(8,128)S(1)}, f32[15,8,128]{2,1,0:T(8,128)S(1)}, u32[]{:S(2)}, u32[]{:S(2)}) collective-permute-start(f32[15,8,128]{2,1,0:T(8,128)S(1)} %get-tuple-element.39), channel_id=1, source_target_pairs={{16,32},{32,16},{48,64},{64,48},{80,96},{96,80},{17,33},{33,17},{4... | collective-permute-start | bytes 184328 | tf_op jit(solution)/shard_map/ppermute | solution.py:695
  77.7 4.4 %collective-permute-done.11.two.x_two_a = f32[15,8,128]{2,1,0:T(8,128)S(1)} collective-permute-done((f32[15,8,128]{2,1,0:T(8,128)S(1)}, f32[15,8,128]{2,1,0:T(8,128)S(1)}, u32[]{:S(2)}, u32[]{:S(2)}) %collective-permute-start.11) | collective-permute-done | bytes 61472 | tf_op jit(solution)/shard_map/ppermute | solution.py:695
  82.1 1.2 %collective-permute-start.12 = (f32[38,8,128]{2,1,0:T(8,128)S(1)}, f32[38,8,128]{2,1,0:T(8,128)S(1)}, u32[]{:S(2)}, u32[]{:S(2)}) collective-permute-start(f32[38,8,128]{2,1,0:T(8,128)S(1)} %get-tuple-element.41), channel_id=1, source_target_pairs={{0,1},{1,0},{2,3},{3,2},{4,5},{5,4},{6,7},{7,6},{8,9},{9,8},{10,11... | collective-permute-start | bytes 466952 | tf_op jit(solution)/shard_map/ppermute | solution.py:694
  83.3 4.4 %collective-permute-start.13 = (f32[38,8,128]{2,1,0:T(8,128)S(1)}, f32[38,8,128]{2,1,0:T(8,128)S(1)}, u32[]{:S(2)}, u32[]{:S(2)}) collective-permute-start(f32[38,8,128]{2,1,0:T(8,128)S(1)} %get-tuple-element.42), channel_id=1, source_target_pairs={{1,2},{2,1},{3,4},{4,3},{5,6},{6,5},{7,8},{8,7},{9,10},{10,9},{11,... | collective-permute-start | bytes 466952 | tf_op jit(solution)/shard_map/ppermute | solution.py:695
  87.7 2.6 %collective-permute-start.18 = (f32[128,4,128]{2,1,0:T(4,128)S(1)}, f32[128,4,128]{2,1,0:T(4,128)S(1)}, u32[]{:S(2)}, u32[]{:S(2)}) collective-permute-start(f32[128,4,128]{2,1,0:T(4,128)S(1)} %all-to-all-done.1.r3_a), channel_id=1, source_target_pairs={{0,128},{128,0},{1,129},{129,1},{2,130},{130,2},{3,131},{131,3},{4... | collective-permute-start | bytes 786440 | tf_op jit(solution)/shard_map/ppermute | solution.py:700
  90.6 0.8 collective-permute-done.13.y_two_a
  91.4 3.5 %collective-permute-start.17 = (f32[38,8,128]{2,1,0:T(8,128)S(1)}, f32[38,8,128]{2,1,0:T(8,128)S(1)}, u32[]{:S(2)}, u32[]{:S(2)}) collective-permute-start(f32[38,8,128]{2,1,0:T(8,128)S(1)} %collective-permute-done.13.y_two_a), channel_id=1, source_target_pairs={{0,128},{128,0},{1,129},{129,1},{2,130},{130,2},{3,131},{131,3},{4... | collective-permute-start | bytes 466952 | tf_op jit(solution)/shard_map/ppermute | solution.py:700
  95.4 4.0 %shard_map.46.sum3 = f32[2,3,24,128]{3,2,1,0:T(8,128)S(1)} custom-call(f32[128,4,128]{2,1,0:T(4,128)S(1)} %all-to-all-done.1.r3_a, f32[128,4,128]{2,1,0:T(4,128)S(1)} %collective-permute-done.18.r3_b, f32[512,128]{1,0:T(8,128)S(1)} %bitcast.5, f32[512,128]{1,0:T(8,128)S(1)} %bitcast.7, f32[7,2,5,24,128]{4,3,2,1,0:T(8,128)} %get-tuple-element.44.w3_hbm, ...), custom_call_target="tpu_custom_call" | custom-call | tf_op jit(solution)/shard_map/pallas_call | solution.py:676
  99.4 7.8 %shard_map.47 = (f32[16,16,128]{2,1,0:T(8,128)}, f32[16,16,128]{2,1,0:T(8,128)}) custom-call(f32[2,36,8,128]{3,2,1,0:T(8,128)} %get-tuple-element.35.own_hbm, f32[8,2,28,32,128]{4,3,2,1,0:T(8,128)} %get-tuple-element.31.w1_hbm, f32[7,2,10,24,128]{4,3,2,1,0:T(8,128)} %get-tuple-element.36.w2_hbm, f32[2,28,32,128]{3,2,1,0:T(8,128)} %get-tuple-element.37.x1_hbm, ...), custom_call_target="tpu_custom_call" | custom-call | tf_op jit(solution)/shard_map/pallas_call | solution.py:676
  (25 shorter events, 3.6 us)
Async XLA Ops:
  3.4 32.0 %all-to-all-start = ((f32[128,8,128]{2,1,0:T(8,128)}), f32[128,8,128]{2,1,0:T(8,128)S(1)}, u32[]{:S(2)}, u32[]{:S(2)}) async-start(f32[128,8,128]{2,1,0:T(8,128)} %get-tuple-element.24), calls=%async_computation | async-start | bytes 1048576 | tf_op jit(solution)/shard_map/all_to_all | solution.py:704
  18.3 5.8 %collective-permute-start.1 = (f32[30,8,128]{2,1,0:T(8,128)S(1)}, f32[30,8,128]{2,1,0:T(8,128)S(1)}, u32[]{:S(2)}, u32[]{:S(2)}) collective-permute-start(f32[30,8,128]{2,1,0:T(8,128)S(1)} %get-tuple-element.26), channel_id=1, source_target_pairs={{0,16},{16,0},{32,48},{48,32},{64,80},{80,64},{96,112},{112,96},{1... | collective-permute-start | bytes 368648 | tf_op jit(solution)/shard_map/ppermute | solution.py:694
  18.8 10.5 %collective-permute-start.2 = (f32[30,8,128]{2,1,0:T(8,128)S(1)}, f32[30,8,128]{2,1,0:T(8,128)S(1)}, u32[]{:S(2)}, u32[]{:S(2)}) collective-permute-start(f32[30,8,128]{2,1,0:T(8,128)S(1)} %get-tuple-element.27), channel_id=1, source_target_pairs={{16,32},{32,16},{48,64},{64,48},{80,96},{96,80},{17,33},{33,17},{4... | collective-permute-start | bytes 368648 | tf_op jit(solution)/shard_map/ppermute | solution.py:695
  29.3 9.2 %collective-permute-start.3 = (f32[76,8,128]{2,1,0:T(8,128)S(1)}, f32[76,8,128]{2,1,0:T(8,128)S(1)}, u32[]{:S(2)}, u32[]{:S(2)}) collective-permute-start(f32[76,8,128]{2,1,0:T(8,128)S(1)} %get-tuple-element.29), channel_id=1, source_target_pairs={{0,1},{1,0},{2,3},{3,2},{4,5},{5,4},{6,7},{7,6},{8,9},{9,8},{10,11... | collective-permute-start | bytes 933896 | tf_op jit(solution)/shard_map/ppermute | solution.py:694
  31.0 10.3 %collective-permute-start.4 = (f32[76,8,128]{2,1,0:T(8,128)S(1)}, f32[76,8,128]{2,1,0:T(8,128)S(1)}, u32[]{:S(2)}, u32[]{:S(2)}) collective-permute-start(f32[76,8,128]{2,1,0:T(8,128)S(1)} %get-tuple-element.30), channel_id=1, source_target_pairs={{1,2},{2,1},{3,4},{4,3},{5,6},{6,5},{7,8},{8,7},{9,10},{10,9},{11,... | collective-permute-start | bytes 933896 | tf_op jit(solution)/shard_map/ppermute | solution.py:695
  35.5 19.8 %collective-permute-start = (f32[128,8,128]{2,1,0:T(8,128)S(1)}, f32[128,8,128]{2,1,0:T(8,128)S(1)}, u32[]{:S(2)}, u32[]{:S(2)}) collective-permute-start(f32[128,8,128]{2,1,0:T(8,128)S(1)} %all-to-all-done.r3_a), channel_id=1, source_target_pairs={{0,128},{128,0},{1,129},{129,1},{2,130},{130,2},{3,131},{131,3},{4... | collective-permute-start | bytes 1572872 | tf_op jit(solution)/shard_map/ppermute | solution.py:700
  38.5 9.5 %collective-permute-start.8 = (f32[76,8,128]{2,1,0:T(8,128)S(1)}, f32[76,8,128]{2,1,0:T(8,128)S(1)}, u32[]{:S(2)}, u32[]{:S(2)}) collective-permute-start(f32[76,8,128]{2,1,0:T(8,128)S(1)} %collective-permute-done.3.y_one_a), channel_id=1, source_target_pairs={{0,128},{128,0},{1,129},{129,1},{2,130},{130,2},{3,131},{131,3},{4... | collective-permute-start | bytes 933896 | tf_op jit(solution)/shard_map/ppermute | solution.py:700
  41.3 6.7 %collective-permute-start.9 = (f32[76,8,128]{2,1,0:T(8,128)S(1)}, f32[76,8,128]{2,1,0:T(8,128)S(1)}, u32[]{:S(2)}, u32[]{:S(2)}) collective-permute-start(f32[76,8,128]{2,1,0:T(8,128)S(1)} %collective-permute-done.4.y_two_a), channel_id=1, source_target_pairs={{0,128},{128,0},{1,129},{129,1},{2,130},{130,2},{3,131},{131,3},{4... | collective-permute-start | bytes 933896 | tf_op jit(solution)/shard_map/ppermute | solution.py:700
  44.8 3.2 %collective-permute-start.5 = (f32[72,8,128]{2,1,0:T(8,128)S(1)}, f32[72,8,128]{2,1,0:T(8,128)S(1)}, u32[]{:S(2)}, u32[]{:S(2)}) collective-permute-start(f32[72,8,128]{2,1,0:T(8,128)S(1)} %get-tuple-element.28.own), channel_id=1, source_target_pairs={{0,128},{128,0},{1,129},{129,1},{2,130},{130,2},{3,131},{131,3},{4... | collective-permute-start | bytes 884744 | tf_op jit(solution)/shard_map/ppermute | solution.py:700
  44.8 1.8 %collective-permute-start.6 = (f32[30,8,128]{2,1,0:T(8,128)S(1)}, f32[30,8,128]{2,1,0:T(8,128)S(1)}, u32[]{:S(2)}, u32[]{:S(2)}) collective-permute-start(f32[30,8,128]{2,1,0:T(8,128)S(1)} %collective-permute-done.1.one.x_one_a), channel_id=1, source_target_pairs={{0,128},{128,0},{1,129},{129,1},{2,130},{130,2},{3,131},{131,3},{4... | collective-permute-start | bytes 368648 | tf_op jit(solution)/shard_map/ppermute | solution.py:700
  46.6 1.4 %collective-permute-start.7 = (f32[30,8,128]{2,1,0:T(8,128)S(1)}, f32[30,8,128]{2,1,0:T(8,128)S(1)}, u32[]{:S(2)}, u32[]{:S(2)}) collective-permute-start(f32[30,8,128]{2,1,0:T(8,128)S(1)} %collective-permute-done.2.two.x_two_a), channel_id=1, source_target_pairs={{0,128},{128,0},{1,129},{129,1},{2,130},{130,2},{3,131},{131,3},{4... | collective-permute-start | bytes 368648 | tf_op jit(solution)/shard_map/ppermute | solution.py:700
  62.8 24.9 %all-to-all-start.1 = ((f32[128,4,128]{2,1,0:T(4,128)}), f32[128,4,128]{2,1,0:T(4,128)S(1)}, u32[]{:S(2)}, u32[]{:S(2)}) async-start(f32[128,4,128]{2,1,0:T(4,128)} %get-tuple-element.43), calls=%async_computation.1 | async-start | bytes 524288 | tf_op jit(solution)/shard_map/all_to_all | solution.py:704
  72.5 5.2 %collective-permute-start.10 = (f32[15,8,128]{2,1,0:T(8,128)S(1)}, f32[15,8,128]{2,1,0:T(8,128)S(1)}, u32[]{:S(2)}, u32[]{:S(2)}) collective-permute-start(f32[15,8,128]{2,1,0:T(8,128)S(1)} %get-tuple-element.38), channel_id=1, source_target_pairs={{0,16},{16,0},{32,48},{48,32},{64,80},{80,64},{96,112},{112,96},{1... | collective-permute-start | bytes 184328 | tf_op jit(solution)/shard_map/ppermute | solution.py:694
  73.0 9.1 %collective-permute-start.11 = (f32[15,8,128]{2,1,0:T(8,128)S(1)}, f32[15,8,128]{2,1,0:T(8,128)S(1)}, u32[]{:S(2)}, u32[]{:S(2)}) collective-permute-start(f32[15,8,128]{2,1,0:T(8,128)S(1)} %get-tuple-element.39), channel_id=1, source_target_pairs={{16,32},{32,16},{48,64},{64,48},{80,96},{96,80},{17,33},{33,17},{4... | collective-permute-start | bytes 184328 | tf_op jit(solution)/shard_map/ppermute | solution.py:695
  82.1 8.2 %collective-permute-start.12 = (f32[38,8,128]{2,1,0:T(8,128)S(1)}, f32[38,8,128]{2,1,0:T(8,128)S(1)}, u32[]{:S(2)}, u32[]{:S(2)}) collective-permute-start(f32[38,8,128]{2,1,0:T(8,128)S(1)} %get-tuple-element.41), channel_id=1, source_target_pairs={{0,1},{1,0},{2,3},{3,2},{4,5},{5,4},{6,7},{7,6},{8,9},{9,8},{10,11... | collective-permute-start | bytes 466952 | tf_op jit(solution)/shard_map/ppermute | solution.py:694
  83.3 8.1 %collective-permute-start.13 = (f32[38,8,128]{2,1,0:T(8,128)S(1)}, f32[38,8,128]{2,1,0:T(8,128)S(1)}, u32[]{:S(2)}, u32[]{:S(2)}) collective-permute-start(f32[38,8,128]{2,1,0:T(8,128)S(1)} %get-tuple-element.42), channel_id=1, source_target_pairs={{1,2},{2,1},{3,4},{4,3},{5,6},{6,5},{7,8},{8,7},{9,10},{10,9},{11,... | collective-permute-start | bytes 466952 | tf_op jit(solution)/shard_map/ppermute | solution.py:695
  87.7 7.7 %collective-permute-start.18 = (f32[128,4,128]{2,1,0:T(4,128)S(1)}, f32[128,4,128]{2,1,0:T(4,128)S(1)}, u32[]{:S(2)}, u32[]{:S(2)}) collective-permute-start(f32[128,4,128]{2,1,0:T(4,128)S(1)} %all-to-all-done.1.r3_a), channel_id=1, source_target_pairs={{0,128},{128,0},{1,129},{129,1},{2,130},{130,2},{3,131},{131,3},{4... | collective-permute-start | bytes 786440 | tf_op jit(solution)/shard_map/ppermute | solution.py:700
  90.3 9.1 %collective-permute-start.16 = (f32[38,8,128]{2,1,0:T(8,128)S(1)}, f32[38,8,128]{2,1,0:T(8,128)S(1)}, u32[]{:S(2)}, u32[]{:S(2)}) collective-permute-start(f32[38,8,128]{2,1,0:T(8,128)S(1)} %collective-permute-done.12.y_one_a), channel_id=1, source_target_pairs={{0,128},{128,0},{1,129},{129,1},{2,130},{130,2},{3,131},{131,3},{4... | collective-permute-start | bytes 466952 | tf_op jit(solution)/shard_map/ppermute | solution.py:700
  91.4 8.0 %collective-permute-start.17 = (f32[38,8,128]{2,1,0:T(8,128)S(1)}, f32[38,8,128]{2,1,0:T(8,128)S(1)}, u32[]{:S(2)}, u32[]{:S(2)}) collective-permute-start(f32[38,8,128]{2,1,0:T(8,128)S(1)} %collective-permute-done.13.y_two_a), channel_id=1, source_target_pairs={{0,128},{128,0},{1,129},{129,1},{2,130},{130,2},{3,131},{131,3},{4... | collective-permute-start | bytes 466952 | tf_op jit(solution)/shard_map/ppermute | solution.py:700
  94.9 4.5 %collective-permute-start.14 = (f32[15,8,128]{2,1,0:T(8,128)S(1)}, f32[15,8,128]{2,1,0:T(8,128)S(1)}, u32[]{:S(2)}, u32[]{:S(2)}) collective-permute-start(f32[15,8,128]{2,1,0:T(8,128)S(1)} %collective-permute-done.10.one.x_one_a), channel_id=1, source_target_pairs={{0,128},{128,0},{1,129},{129,1},{2,130},{130,2},{3,131},{131,3},{4... | collective-permute-start | bytes 184328 | tf_op jit(solution)/shard_map/ppermute | solution.py:700
  94.9 4.5 %collective-permute-start.15 = (f32[15,8,128]{2,1,0:T(8,128)S(1)}, f32[15,8,128]{2,1,0:T(8,128)S(1)}, u32[]{:S(2)}, u32[]{:S(2)}) collective-permute-start(f32[15,8,128]{2,1,0:T(8,128)S(1)} %collective-permute-done.11.two.x_two_a), channel_id=1, source_target_pairs={{0,128},{128,0},{1,129},{129,1},{2,130},{130,2},{3,131},{131,3},{4... | collective-permute-start | bytes 184328 | tf_op jit(solution)/shard_map/ppermute | solution.py:700

commit v10 on v6

--- a/solution.py
+++ b/solution.py
@@ -26,6 +26,7 @@
 }
 CHUNK = {1: 2, 2: 2, 3: 3}
 PAD = {1: 0, 2: 1, 3: 1}
+UNROLL = 6
 SCALE = {1: 1.0, 2: 0.25, 3: 0.0625, 4: 0.015625}
 
 
@@ -90,15 +91,18 @@
 
 
 def blocks(start, stop, step, body):
-    if stop - start == step:
-        body(start)
-        return
+    count = (stop - start) // step
+    turns = count // UNROLL if count > UNROLL else 0
 
     def run(n, _):
-        body(start + n * step)
+        for k in range(UNROLL):
+            body(start + (n * UNROLL + k) * step)
         return 0
 
-    lax.fori_loop(0, (stop - start) // step, run, 0)
+    if turns:
+        lax.fori_loop(0, turns, run, 0)
+    for k in range(turns * UNROLL, count):
+        body(start + k * step)
 
 
 def faces(level, a, weights, inv, diag_ref):
@@ -544,11 +548,10 @@
     smooth(1, b1, weights1, inv1, e1, d1, o1, x1)
     combine(sum3, c2, s2, tmp3, tmp2)
 
-    def finish(i, _):
+    def finish(i):
         x1[:, i] = DAMPING * (x1[:, i] + tmp2[:, i // 2 - 1])
-        return 0
-
-    lax.fori_loop(5, 23, finish, 0)
+
+    blocks(5, 23, 1, finish)
     out.start(x1, x1_hbm)
 
     def residual(i):
@@ -614,11 +617,10 @@
     copies.made[4].wait()
     combine(sum3, c2, s2, tmp3, tmp2)
 
-    def finish(i, _):
+    def finish(i):
         c1[:, i] = x1[:, i] + DAMPING * (c1[:, i] + tmp2[:, i // 2 - 1])
-        return 0
-
-    lax.fori_loop(5, 23, finish, 0)
+
+    blocks(5, 23, 1, finish)
     field = copies.start(c1.at[core, 6:22, 8:24, :], out_x)
 
     def residual(i):

time: 119 us -> 109 us (0.916)
  Pallas kernels: 37 us -> 27.6 us
    pallas_call x7, Pallas kernels: 37 us -> 27.6 us  [call(): pl.pallas_call(kernel, out_shape=[pltpu.HBM(s, F32) if i in hbm_out else...]
  transfers between devices with their start and end apart: 21 -> 21, of which waited for: 5 -> 5; matrix products, arithmetic and copies ran while one was open for 0% -> 0% of each run, Pallas kernels for 7% -> 8%
where the time goes in v10:
time: 109 us; the launch traced here: 108 us
  starting transfers between devices  53.6 us (49%)
  Pallas kernels  27.6 us (25%)
  waiting for transfers between devices  25.7 us (24%)
    pallas_call x7, Pallas kernels, call(): pl.pallas_call(kernel, out_shape=[pltpu.HBM(s, F32) if i in hbm_out else...  27.6 us
    all_to_all x2, starting transfers between devices, everywhere(): return lax.all_to_all(slots, ('gx', 'gy'), 0, 0, tiled=True)  21.8 us
    ppermute x4, starting transfers between devices, trade(): two = lax.ppermute(second, axis, others)  16.4 us
    ppermute x11, starting transfers between devices, swap(): return lax.ppermute(x, 'grp', [(0, 1), (1, 0)])  12.3 us
    all_to_all x2, waiting for transfers between devices, everywhere(): return lax.all_to_all(slots, ('gx', 'gy'), 0, 0, tiled=True)  11.6 us
    ppermute x4, waiting for transfers between devices, trade(): two = lax.ppermute(second, axis, others)  8.67 us
    ppermute x4, waiting for transfers between devices, trade(): one = lax.ppermute(first, axis, pairs)  5.37 us
    ppermute x4, starting transfers between devices, trade(): one = lax.ppermute(first, axis, pairs)  3.2 us
  transfers between devices with their start and end apart: 21, of which 5 were waited for; matrix products, arithmetic and copies ran while one was open for 0% of the time, Pallas kernels for 8%

profile of v10, /device:TPU:27, one launch (start us, length us, event | category | flops | bytes accessed | tf_op | source)
XLA Modules:
  0.0 107.9 jit_solution(15000201389984421278)
XLA Ops:
  0.6 2.8 %shard_map.41 = (f32[72,8,128]{2,1,0:T(8,128)S(1)}, f32[8,8,128]{2,1,0:T(8,128)}, f32[30,8,128]{2,1,0:T(8,128)S(1)}, f32[30,8,128]{2,1,0:T(8,128)S(1)}, f32[128,8,128]{2,1,0:T(8,128)}) custom-call(f32[16,16,128]{2,1,0:T(8,128)} %a_hbm.3, f32[16,16,128]{2,1,0:T(8,128)} %b_hbm.3), custom_call_target="tpu_custom_call" | custom-call | tf_op jit(solution)/shard_map/pallas_call | solution.py:649
  3.4 14.8 %all-to-all-start = ((f32[128,8,128]{2,1,0:T(8,128)}), f32[128,8,128]{2,1,0:T(8,128)S(1)}, u32[]{:S(2)}, u32[]{:S(2)}) async-start(f32[128,8,128]{2,1,0:T(8,128)} %get-tuple-element.29), calls=%async_computation | async-start | bytes 1048576 | tf_op jit(solution)/shard_map/all_to_all | solution.py:677
  18.3 0.6 collective-permute-start
  18.8 4.6 %collective-permute-start.1 = (f32[30,8,128]{2,1,0:T(8,128)S(1)}, f32[30,8,128]{2,1,0:T(8,128)S(1)}, u32[]{:S(2)}, u32[]{:S(2)}) collective-permute-start(f32[30,8,128]{2,1,0:T(8,128)S(1)} %get-tuple-element.25), channel_id=1, source_target_pairs={{16,32},{32,16},{48,64},{64,48},{80,96},{96,80},{17,33},{33,17},{4... | collective-permute-start | bytes 368648 | tf_op jit(solution)/shard_map/ppermute | solution.py:668
  23.4 11.6 %all-to-all-done.r3_a = f32[128,8,128]{2,1,0:T(8,128)S(1)} async-done(((f32[128,8,128]{2,1,0:T(8,128)}), f32[128,8,128]{2,1,0:T(8,128)S(1)}, u32[]{:S(2)}, u32[]{:S(2)}) %all-to-all-start) | async-done | bytes 524320 | tf_op jit(solution)/shard_map/all_to_all | solution.py:677
  35.1 2.5 %collective-permute-start.9 = (f32[128,8,128]{2,1,0:T(8,128)S(1)}, f32[128,8,128]{2,1,0:T(8,128)S(1)}, u32[]{:S(2)}, u32[]{:S(2)}) collective-permute-start(f32[128,8,128]{2,1,0:T(8,128)S(1)} %all-to-all-done.r3_a), channel_id=1, source_target_pairs={{0,128},{128,0},{1,129},{129,1},{2,130},{130,2},{3,131},{131,3},{4... | collective-permute-start | bytes 1572872 | tf_op jit(solution)/shard_map/ppermute | solution.py:673
  37.6 0.9 collective-permute-start.2
  38.5 2.8 %collective-permute-start.3 = (f32[76,8,128]{2,1,0:T(8,128)S(1)}, f32[76,8,128]{2,1,0:T(8,128)S(1)}, u32[]{:S(2)}, u32[]{:S(2)}) collective-permute-start(f32[76,8,128]{2,1,0:T(8,128)S(1)} %get-tuple-element.28), channel_id=1, source_target_pairs={{1,2},{2,1},{3,4},{4,3},{5,6},{6,5},{7,8},{8,7},{9,10},{10,9},{11,... | collective-permute-start | bytes 933896 | tf_op jit(solution)/shard_map/ppermute | solution.py:668
  41.3 5.4 %collective-permute-done.2.y_one_a = f32[76,8,128]{2,1,0:T(8,128)S(1)} collective-permute-done((f32[76,8,128]{2,1,0:T(8,128)S(1)}, f32[76,8,128]{2,1,0:T(8,128)S(1)}, u32[]{:S(2)}, u32[]{:S(2)}) %collective-permute-start.2) | collective-permute-done | bytes 311328 | tf_op jit(solution)/shard_map/ppermute | solution.py:667
  46.6 0.9 collective-permute-start.7
  47.5 3.6 %collective-permute-done.3.y_two_a = f32[76,8,128]{2,1,0:T(8,128)S(1)} collective-permute-done((f32[76,8,128]{2,1,0:T(8,128)S(1)}, f32[76,8,128]{2,1,0:T(8,128)S(1)}, u32[]{:S(2)}, u32[]{:S(2)}) %collective-permute-start.3) | collective-permute-done | bytes 311328 | tf_op jit(solution)/shard_map/ppermute | solution.py:668
  51.1 1.1 %collective-permute-start.8 = (f32[76,8,128]{2,1,0:T(8,128)S(1)}, f32[76,8,128]{2,1,0:T(8,128)S(1)}, u32[]{:S(2)}, u32[]{:S(2)}) collective-permute-start(f32[76,8,128]{2,1,0:T(8,128)S(1)} %collective-permute-done.3.y_two_a), channel_id=1, source_target_pairs={{0,128},{128,0},{1,129},{129,1},{2,130},{130,2},{3,131},{131,3},{4... | collective-permute-start | bytes 933896 | tf_op jit(solution)/shard_map/ppermute | solution.py:673
  52.8 4.2 %shard_map.43 = (f32[2,3,24,128]{3,2,1,0:T(8,128)S(1)}, f32[7,2,5,24,128]{4,3,2,1,0:T(8,128)}, f32[4,4,32,128]{3,2,1,0:T(8,128)}) custom-call(f32[128,8,128]{2,1,0:T(8,128)S(1)} %all-to-all-done.r3_a, f32[128,8,128]{2,1,0:T(8,128)S(1)} %collective-permute-done.9.r3_b, f32[1024,128]{1,0:T(8,128)S(1)} %bitcast.4, f32[1024,128]{1,0:T(8,128)S(1)} %bitcast.6), custom_call_target="tpu_custom_call" | custom-call | tf_op jit(solution)/shard_map/pallas_call | solution.py:649
  57.0 8.7 %shard_map.44 = (f32[8,2,28,32,128]{4,3,2,1,0:T(8,128)}, f32[7,2,10,24,128]{4,3,2,1,0:T(8,128)}, f32[2,28,32,128]{3,2,1,0:T(8,128)}, f32[2,16,16,128]{3,2,1,0:T(...) custom-call(f32[16,16,128]{2,1,0:T(8,128)} %a_hbm.3, ...), custom_call_target="tpu_custom_call" | custom-call | tf_op jit(solution)/shard_map/pallas_call | solution.py:649
  65.7 7.0 %all-to-all-start.1 = ((f32[128,4,128]{2,1,0:T(4,128)}), f32[128,4,128]{2,1,0:T(4,128)S(1)}, u32[]{:S(2)}, u32[]{:S(2)}) async-start(f32[128,4,128]{2,1,0:T(4,128)} %get-tuple-element.41), calls=%async_computation.1 | async-start | bytes 524288 | tf_op jit(solution)/shard_map/all_to_all | solution.py:677
  73.2 4.6 %collective-permute-start.11 = (f32[15,8,128]{2,1,0:T(8,128)S(1)}, f32[15,8,128]{2,1,0:T(8,128)S(1)}, u32[]{:S(2)}, u32[]{:S(2)}) collective-permute-start(f32[15,8,128]{2,1,0:T(8,128)S(1)} %get-tuple-element.37), channel_id=1, source_target_pairs={{16,32},{32,16},{48,64},{64,48},{80,96},{96,80},{17,33},{33,17},{4... | collective-permute-start | bytes 184328 | tf_op jit(solution)/shard_map/ppermute | solution.py:668
  77.9 4.4 %collective-permute-done.11.two.x_two_a = f32[15,8,128]{2,1,0:T(8,128)S(1)} collective-permute-done((f32[15,8,128]{2,1,0:T(8,128)S(1)}, f32[15,8,128]{2,1,0:T(8,128)S(1)}, u32[]{:S(2)}, u32[]{:S(2)}) %collective-permute-start.11) | collective-permute-done | bytes 61472 | tf_op jit(solution)/shard_map/ppermute | solution.py:668
  82.3 1.2 %collective-permute-start.12 = (f32[38,8,128]{2,1,0:T(8,128)S(1)}, f32[38,8,128]{2,1,0:T(8,128)S(1)}, u32[]{:S(2)}, u32[]{:S(2)}) collective-permute-start(f32[38,8,128]{2,1,0:T(8,128)S(1)} %get-tuple-element.39), channel_id=1, source_target_pairs={{0,1},{1,0},{2,3},{3,2},{4,5},{5,4},{6,7},{7,6},{8,9},{9,8},{10,11... | collective-permute-start | bytes 466952 | tf_op jit(solution)/shard_map/ppermute | solution.py:667
  83.6 4.4 %collective-permute-start.13 = (f32[38,8,128]{2,1,0:T(8,128)S(1)}, f32[38,8,128]{2,1,0:T(8,128)S(1)}, u32[]{:S(2)}, u32[]{:S(2)}) collective-permute-start(f32[38,8,128]{2,1,0:T(8,128)S(1)} %get-tuple-element.40), channel_id=1, source_target_pairs={{1,2},{2,1},{3,4},{4,3},{5,6},{6,5},{7,8},{8,7},{9,10},{10,9},{11,... | collective-permute-start | bytes 466952 | tf_op jit(solution)/shard_map/ppermute | solution.py:668
  87.9 2.7 %collective-permute-start.18 = (f32[128,4,128]{2,1,0:T(4,128)S(1)}, f32[128,4,128]{2,1,0:T(4,128)S(1)}, u32[]{:S(2)}, u32[]{:S(2)}) collective-permute-start(f32[128,4,128]{2,1,0:T(4,128)S(1)} %all-to-all-done.1.r3_a), channel_id=1, source_target_pairs={{0,128},{128,0},{1,129},{129,1},{2,130},{130,2},{3,131},{131,3},{4... | collective-permute-start | bytes 786440 | tf_op jit(solution)/shard_map/ppermute | solution.py:673
  91.0 0.6 collective-permute-done.13.y_two_a
  91.6 3.7 %collective-permute-start.17 = (f32[38,8,128]{2,1,0:T(8,128)S(1)}, f32[38,8,128]{2,1,0:T(8,128)S(1)}, u32[]{:S(2)}, u32[]{:S(2)}) collective-permute-start(f32[38,8,128]{2,1,0:T(8,128)S(1)} %collective-permute-done.13.y_two_a), channel_id=1, source_target_pairs={{0,128},{128,0},{1,129},{129,1},{2,130},{130,2},{3,131},{131,3},{4... | collective-permute-start | bytes 466952 | tf_op jit(solution)/shard_map/ppermute | solution.py:673
  95.8 4.0 %shard_map.46.sum3 = f32[2,3,24,128]{3,2,1,0:T(8,128)S(1)} custom-call(f32[128,4,128]{2,1,0:T(4,128)S(1)} %all-to-all-done.1.r3_a, f32[128,4,128]{2,1,0:T(4,128)S(1)} %collective-permute-done.18.r3_b, f32[512,128]{1,0:T(8,128)S(1)} %bitcast.5, f32[512,128]{1,0:T(8,128)S(1)} %bitcast.7, f32[7,2,5,24,128]{4,3,2,1,0:T(8,128)} %get-tuple-element.42.w3_hbm, ...), custom_call_target="tpu_custom_call" | custom-call | tf_op jit(solution)/shard_map/pallas_call | solution.py:649
  99.9 7.8 %shard_map.47 = (f32[16,16,128]{2,1,0:T(8,128)}, f32[16,16,128]{2,1,0:T(8,128)}) custom-call(f32[2,36,8,128]{3,2,1,0:T(8,128)} %get-tuple-element.31.own_hbm, f32[8,2,28,32,128]{4,3,2,1,0:T(8,128)} %get-tuple-element.32.w1_hbm, f32[7,2,10,24,128]{4,3,2,1,0:T(8,128)} %get-tuple-element.33.w2_hbm, f32[2,28,32,128]{3,2,1,0:T(8,128)} %get-tuple-element.34.x1_hbm, ...), custom_call_target="tpu_custom_call" | custom-call | tf_op jit(solution)/shard_map/pallas_call | solution.py:649
  (25 shorter events, 2.0 us)
Async XLA Ops:
  3.4 31.6 %all-to-all-start = ((f32[128,8,128]{2,1,0:T(8,128)}), f32[128,8,128]{2,1,0:T(8,128)S(1)}, u32[]{:S(2)}, u32[]{:S(2)}) async-start(f32[128,8,128]{2,1,0:T(8,128)} %get-tuple-element.29), calls=%async_computation | async-start | bytes 1048576 | tf_op jit(solution)/shard_map/all_to_all | solution.py:677
  18.3 19.3 %collective-permute-start = (f32[30,8,128]{2,1,0:T(8,128)S(1)}, f32[30,8,128]{2,1,0:T(8,128)S(1)}, u32[]{:S(2)}, u32[]{:S(2)}) collective-permute-start(f32[30,8,128]{2,1,0:T(8,128)S(1)} %get-tuple-element.24), channel_id=1, source_target_pairs={{0,16},{16,0},{32,48},{48,32},{64,80},{80,64},{96,112},{112,96},{1... | collective-permute-start | bytes 368648 | tf_op jit(solution)/shard_map/ppermute | solution.py:667
  18.8 18.7 %collective-permute-start.1 = (f32[30,8,128]{2,1,0:T(8,128)S(1)}, f32[30,8,128]{2,1,0:T(8,128)S(1)}, u32[]{:S(2)}, u32[]{:S(2)}) collective-permute-start(f32[30,8,128]{2,1,0:T(8,128)S(1)} %get-tuple-element.25), channel_id=1, source_target_pairs={{16,32},{32,16},{48,64},{64,48},{80,96},{96,80},{17,33},{33,17},{4... | collective-permute-start | bytes 368648 | tf_op jit(solution)/shard_map/ppermute | solution.py:668
  35.1 17.7 %collective-permute-start.9 = (f32[128,8,128]{2,1,0:T(8,128)S(1)}, f32[128,8,128]{2,1,0:T(8,128)S(1)}, u32[]{:S(2)}, u32[]{:S(2)}) collective-permute-start(f32[128,8,128]{2,1,0:T(8,128)S(1)} %all-to-all-done.r3_a), channel_id=1, source_target_pairs={{0,128},{128,0},{1,129},{129,1},{2,130},{130,2},{3,131},{131,3},{4... | collective-permute-start | bytes 1572872 | tf_op jit(solution)/shard_map/ppermute | solution.py:673
  37.6 9.0 %collective-permute-start.2 = (f32[76,8,128]{2,1,0:T(8,128)S(1)}, f32[76,8,128]{2,1,0:T(8,128)S(1)}, u32[]{:S(2)}, u32[]{:S(2)}) collective-permute-start(f32[76,8,128]{2,1,0:T(8,128)S(1)} %get-tuple-element.27), channel_id=1, source_target_pairs={{0,1},{1,0},{2,3},{3,2},{4,5},{5,4},{6,7},{7,6},{8,9},{9,8},{10,11... | collective-permute-start | bytes 933896 | tf_op jit(solution)/shard_map/ppermute | solution.py:667
  38.5 12.6 %collective-permute-start.3 = (f32[76,8,128]{2,1,0:T(8,128)S(1)}, f32[76,8,128]{2,1,0:T(8,128)S(1)}, u32[]{:S(2)}, u32[]{:S(2)}) collective-permute-start(f32[76,8,128]{2,1,0:T(8,128)S(1)} %get-tuple-element.28), channel_id=1, source_target_pairs={{1,2},{2,1},{3,4},{4,3},{5,6},{6,5},{7,8},{8,7},{9,10},{10,9},{11,... | collective-permute-start | bytes 933896 | tf_op jit(solution)/shard_map/ppermute | solution.py:668
  46.6 10.4 %collective-permute-start.7 = (f32[76,8,128]{2,1,0:T(8,128)S(1)}, f32[76,8,128]{2,1,0:T(8,128)S(1)}, u32[]{:S(2)}, u32[]{:S(2)}) collective-permute-start(f32[76,8,128]{2,1,0:T(8,128)S(1)} %collective-permute-done.2.y_one_a), channel_id=1, source_target_pairs={{0,128},{128,0},{1,129},{129,1},{2,130},{130,2},{3,131},{131,3},{4... | collective-permute-start | bytes 933896 | tf_op jit(solution)/shard_map/ppermute | solution.py:673
  51.1 5.9 %collective-permute-start.8 = (f32[76,8,128]{2,1,0:T(8,128)S(1)}, f32[76,8,128]{2,1,0:T(8,128)S(1)}, u32[]{:S(2)}, u32[]{:S(2)}) collective-permute-start(f32[76,8,128]{2,1,0:T(8,128)S(1)} %collective-permute-done.3.y_two_a), channel_id=1, source_target_pairs={{0,128},{128,0},{1,129},{129,1},{2,130},{130,2},{3,131},{131,3},{4... | collective-permute-start | bytes 933896 | tf_op jit(solution)/shard_map/ppermute | solution.py:673
  52.2 4.7 %collective-permute-start.4 = (f32[72,8,128]{2,1,0:T(8,128)S(1)}, f32[72,8,128]{2,1,0:T(8,128)S(1)}, u32[]{:S(2)}, u32[]{:S(2)}) collective-permute-start(f32[72,8,128]{2,1,0:T(8,128)S(1)} %get-tuple-element.26.own), channel_id=1, source_target_pairs={{0,128},{128,0},{1,129},{129,1},{2,130},{130,2},{3,131},{131,3},{4... | collective-permute-start | bytes 884744 | tf_op jit(solution)/shard_map/ppermute | solution.py:673
  52.2 4.7 %collective-permute-start.5 = (f32[30,8,128]{2,1,0:T(8,128)S(1)}, f32[30,8,128]{2,1,0:T(8,128)S(1)}, u32[]{:S(2)}, u32[]{:S(2)}) collective-permute-start(f32[30,8,128]{2,1,0:T(8,128)S(1)} %collective-permute-done.one.x_one_a), channel_id=1, source_target_pairs={{0,128},{128,0},{1,129},{129,1},{2,130},{130,2},{3,131},{131,3},{4... | collective-permute-start | bytes 368648 | tf_op jit(solution)/shard_map/ppermute | solution.py:673
  52.8 4.2 %collective-permute-start.6 = (f32[30,8,128]{2,1,0:T(8,128)S(1)}, f32[30,8,128]{2,1,0:T(8,128)S(1)}, u32[]{:S(2)}, u32[]{:S(2)}) collective-permute-start(f32[30,8,128]{2,1,0:T(8,128)S(1)} %collective-permute-done.1.two.x_two_a), channel_id=1, source_target_pairs={{0,128},{128,0},{1,129},{129,1},{2,130},{130,2},{3,131},{131,3},{4... | collective-permute-start | bytes 368648 | tf_op jit(solution)/shard_map/ppermute | solution.py:673
  65.7 22.2 %all-to-all-start.1 = ((f32[128,4,128]{2,1,0:T(4,128)}), f32[128,4,128]{2,1,0:T(4,128)S(1)}, u32[]{:S(2)}, u32[]{:S(2)}) async-start(f32[128,4,128]{2,1,0:T(4,128)} %get-tuple-element.41), calls=%async_computation.1 | async-start | bytes 524288 | tf_op jit(solution)/shard_map/all_to_all | solution.py:677
  72.7 5.2 %collective-permute-start.10 = (f32[15,8,128]{2,1,0:T(8,128)S(1)}, f32[15,8,128]{2,1,0:T(8,128)S(1)}, u32[]{:S(2)}, u32[]{:S(2)}) collective-permute-start(f32[15,8,128]{2,1,0:T(8,128)S(1)} %get-tuple-element.36), channel_id=1, source_target_pairs={{0,16},{16,0},{32,48},{48,32},{64,80},{80,64},{96,112},{112,96},{1... | collective-permute-start | bytes 184328 | tf_op jit(solution)/shard_map/ppermute | solution.py:667
  73.2 9.1 %collective-permute-start.11 = (f32[15,8,128]{2,1,0:T(8,128)S(1)}, f32[15,8,128]{2,1,0:T(8,128)S(1)}, u32[]{:S(2)}, u32[]{:S(2)}) collective-permute-start(f32[15,8,128]{2,1,0:T(8,128)S(1)} %get-tuple-element.37), channel_id=1, source_target_pairs={{16,32},{32,16},{48,64},{64,48},{80,96},{96,80},{17,33},{33,17},{4... | collective-permute-start | bytes 184328 | tf_op jit(solution)/shard_map/ppermute | solution.py:668
  82.3 8.4 %collective-permute-start.12 = (f32[38,8,128]{2,1,0:T(8,128)S(1)}, f32[38,8,128]{2,1,0:T(8,128)S(1)}, u32[]{:S(2)}, u32[]{:S(2)}) collective-permute-start(f32[38,8,128]{2,1,0:T(8,128)S(1)} %get-tuple-element.39), channel_id=1, source_target_pairs={{0,1},{1,0},{2,3},{3,2},{4,5},{5,4},{6,7},{7,6},{8,9},{9,8},{10,11... | collective-permute-start | bytes 466952 | tf_op jit(solution)/shard_map/ppermute | solution.py:667
  83.6 8.1 %collective-permute-start.13 = (f32[38,8,128]{2,1,0:T(8,128)S(1)}, f32[38,8,128]{2,1,0:T(8,128)S(1)}, u32[]{:S(2)}, u32[]{:S(2)}) collective-permute-start(f32[38,8,128]{2,1,0:T(8,128)S(1)} %get-tuple-element.40), channel_id=1, source_target_pairs={{1,2},{2,1},{3,4},{4,3},{5,6},{6,5},{7,8},{8,7},{9,10},{10,9},{11,... | collective-permute-start | bytes 466952 | tf_op jit(solution)/shard_map/ppermute | solution.py:668
  87.9 7.9 %collective-permute-start.18 = (f32[128,4,128]{2,1,0:T(4,128)S(1)}, f32[128,4,128]{2,1,0:T(4,128)S(1)}, u32[]{:S(2)}, u32[]{:S(2)}) collective-permute-start(f32[128,4,128]{2,1,0:T(4,128)S(1)} %all-to-all-done.1.r3_a), channel_id=1, source_target_pairs={{0,128},{128,0},{1,129},{129,1},{2,130},{130,2},{3,131},{131,3},{4... | collective-permute-start | bytes 786440 | tf_op jit(solution)/shard_map/ppermute | solution.py:673
  90.7 9.2 %collective-permute-start.16 = (f32[38,8,128]{2,1,0:T(8,128)S(1)}, f32[38,8,128]{2,1,0:T(8,128)S(1)}, u32[]{:S(2)}, u32[]{:S(2)}) collective-permute-start(f32[38,8,128]{2,1,0:T(8,128)S(1)} %collective-permute-done.12.y_one_a), channel_id=1, source_target_pairs={{0,128},{128,0},{1,129},{129,1},{2,130},{130,2},{3,131},{131,3},{4... | collective-permute-start | bytes 466952 | tf_op jit(solution)/shard_map/ppermute | solution.py:673
  91.6 8.2 %collective-permute-start.17 = (f32[38,8,128]{2,1,0:T(8,128)S(1)}, f32[38,8,128]{2,1,0:T(8,128)S(1)}, u32[]{:S(2)}, u32[]{:S(2)}) collective-permute-start(f32[38,8,128]{2,1,0:T(8,128)S(1)} %collective-permute-done.13.y_two_a), channel_id=1, source_target_pairs={{0,128},{128,0},{1,129},{129,1},{2,130},{130,2},{3,131},{131,3},{4... | collective-permute-start | bytes 466952 | tf_op jit(solution)/shard_map/ppermute | solution.py:673
  95.3 4.5 %collective-permute-start.14 = (f32[15,8,128]{2,1,0:T(8,128)S(1)}, f32[15,8,128]{2,1,0:T(8,128)S(1)}, u32[]{:S(2)}, u32[]{:S(2)}) collective-permute-start(f32[15,8,128]{2,1,0:T(8,128)S(1)} %collective-permute-done.10.one.x_one_a), channel_id=1, source_target_pairs={{0,128},{128,0},{1,129},{129,1},{2,130},{130,2},{3,131},{131,3},{4... | collective-permute-start | bytes 184328 | tf_op jit(solution)/shard_map/ppermute | solution.py:673
  95.3 4.5 %collective-permute-start.15 = (f32[15,8,128]{2,1,0:T(8,128)S(1)}, f32[15,8,128]{2,1,0:T(8,128)S(1)}, u32[]{:S(2)}, u32[]{:S(2)}) collective-permute-start(f32[15,8,128]{2,1,0:T(8,128)S(1)} %collective-permute-done.11.two.x_two_a), channel_id=1, source_target_pairs={{0,128},{128,0},{1,129},{129,1},{2,130},{130,2},{3,131},{131,3},{4... | collective-permute-start | bytes 184328 | tf_op jit(solution)/shard_map/ppermute | solution.py:673
